TPU v7x, 32 devices: a whole 2x2x4 slice. The times are simulated.
32 devices in a mesh: lag: 4 (over y, x), row: 8 (over z, core).
Axes of the slice: x: 2, y: 2, z: 4, core: 2. Of those that a mesh axis runs over, the one named last changes fastest.
Arguments:
- lag_weights: float32 [16, 4096, 4096], P('lag', 'row'), may hold values from -0.0234375 to 0.0234375
- inverse_head: float32 [4096, 4096], P('row'), may hold values from -0.09375 to 0.09375
- excitation: float32 [3, 4096, 128], P(None, 'row'), may hold values from -6 to 6
- history: float32 [16, 4096, 128], P('lag', 'row'), may hold values from -6 to 6
Outputs:
- densities: float32 [3, 4096, 128], P(None, 'row')
All inputs are finite; a program needn't handle non-finite values.
Results may differ from a plain program's by a relative error of at most 0.0001.
Values sent between devices are 32-bit elements; how exact they have to be, the bound alone decides.
No kernel may reach another device: no remote copies, remote signals or barrier semaphores. Data moves between devices by JAX's collectives and lax.ppermute only.
A program may use at most 128 MiB of HBM per device.

v0:
```python
import jax
import jax.numpy as jnp
from jax import lax
from jax.experimental import pallas as pl
from jax.experimental.pallas import tpu as pltpu
from jax.sharding import PartitionSpec as P


STEPS = 3
HIGHEST = lax.Precision.HIGHEST
F32 = jnp.float32
BF16 = jnp.bfloat16


def split(value):
    high = value.astype(BF16)
    return high, (value - high.astype(F32)).astype(BF16)


def dot(a, b):
    return jnp.dot(a, b, preferred_element_type=F32)


def product(weight, vectors):
    count, width = len(vectors), vectors[0].shape[1]
    wh, wl = split(weight)
    highs, lows = zip(*(split(v) for v in vectors))
    main = dot(wh, jnp.concatenate(highs + lows, axis=1))
    rest = dot(wl, jnp.concatenate(highs, axis=1) if count > 1 else highs[0])
    return main[:, : count * width] + main[:, count * width :] + rest


def ordered(core, near, far):
    return jnp.concatenate([jnp.where(core == 0, near, far), jnp.where(core == 0, far, near)], axis=0)


def chip_kernel(where, weights, near, far, *refs):
    outs, high, low = refs[-STEPS - 2 : -2], *refs[-2:]
    totals = refs[:-STEPS - 2]
    at = pl.program_id(0)
    lags, rows, width = near.shape
    core = where[0]

    @pl.when(at == 0)
    def _():
        for n, out in enumerate(outs):
            out[...] = totals[n][...] if totals else jnp.zeros_like(out)
        for k in range(lags):
            columns = slice((lags - 1 - k) * width, (lags - k) * width)
            for piece, side in ((near, core), (far, 1 - core)):
                here = pl.ds(pl.multiple_of(side * rows, rows), rows)
                high[here, columns], low[here, columns] = split(piece[k])

    for k in range(STEPS):

        @pl.when(at == k if k + 1 < STEPS else at >= k)
        def _():
            size = (k + 1) * width
            columns = pl.ds(pl.multiple_of((lags - 1 - at) * width, width), size)
            wh, wl = split(weights[0])
            h = high[:, columns]
            main = dot(wh, jnp.concatenate([h, low[:, columns]], axis=1))
            result = main[:, :size] + main[:, size:] + dot(wl, h)
            for n in range(k + 1):
                outs[n][...] += result[:, n * width : (n + 1) * width]


def first_kernel(where, weights, near, far, total, out):
    @pl.when(pl.program_id(0) == 0)
    def _():
        out[...] = total[...]

    out[...] += product(weights[0], [ordered(where[0], near[0], far[0])])


def rest_kernel(where, weights, near, near_before, far, far_before, one, two, one_out, two_out):
    at = pl.program_id(0)
    width = near.shape[-1]
    now = ordered(where[0], near[0], far[0])

    @pl.when(at == 0)
    def _():
        one_out[...] = one[...] + product(weights[0], [now])
        two_out[...] = two[...]

    @pl.when(at > 0)
    def _():
        result = product(weights[0], [now, ordered(where[0], near_before[0], far_before[0])])
        one_out[...] += result[:, :width]
        two_out[...] += result[:, width:]


def entered_kernel(where, weights, near, far, one, two, one_out, two_out):
    at = pl.program_id(0)
    width = near.shape[-1]
    last = ordered(where[0], near[1], far[1])

    @pl.when(at == 0)
    def _():
        one_out[...] = one[...]
        two_out[...] = two[...]

    @pl.when(jnp.logical_and(where[1] > 0, at == 0))
    def _():
        result = product(weights[0], [last, ordered(where[0], near[0], far[0])])
        one_out[...] += result[:, :width]
        two_out[...] += result[:, width:]

    @pl.when(jnp.logical_and(where[1] > 0, at == 1))
    def _():
        two_out[...] += product(weights[0], [last])


def second_kernel(where, weights, *refs):
    nears, fars, total, out = refs[: len(refs) // 2 - 1], refs[len(refs) // 2 - 1 : -2], refs[-2], refs[-1]

    @pl.when(pl.program_id(0) == 0)
    def _():
        out[...] = total[...]

    @pl.when(where[1] == 0)
    def _():
        near, far = (jnp.concatenate([p[...] for p in parts], axis=0) for parts in (nears, fars))
        out[...] += product(weights[0], [ordered(where[0], near, far)])


def columns_kernel(where, *refs):
    fold, groups = where.shape[1] - 1, where.shape[2]
    sources, outs = refs[:fold], refs[fold:]
    part = sources[0].shape[2] // groups
    take = lambda j: jnp.concatenate([s[0, :, j * part : (j + 1) * part] for s in sources], axis=1)
    if len(outs) == 1:
        for j in range(groups):

            @pl.when(where[0, fold, 0] == j)
            def _():
                outs[0][...] = take(j)

        return
    for j in range(groups - 1):
        outs[j][...] = take(j)
    for side, out in enumerate(outs[groups - 1 :]):

        @pl.when(pl.program_id(0) == side)
        def _():
            out[...] = take(groups - 1)


def pick_kernel(which, *refs):
    sources, out = refs[:-1], refs[-1]
    groups = len(sources) - 1
    for j, source in enumerate(sources):
        chosen = which[0] == min(j, groups - 1)
        if j >= groups - 1:
            chosen = jnp.logical_and(chosen, pl.program_id(0) == j - groups + 1)

        @pl.when(chosen)
        def _():
            out[...] = source[...]


def call(kernel, where, grid, operands, specs, count, shape, cost, aliases={}, scratch=()):
    return pl.pallas_call(
        kernel,
        out_shape=[jax.ShapeDtypeStruct(shape, F32)] * count,
        grid_spec=pltpu.PrefetchScalarGridSpec(
            num_scalar_prefetch=1, grid=grid, in_specs=specs, out_specs=[all_of(shape)] * count, scratch_shapes=scratch
        ),
        input_output_aliases=aliases,
        cost_estimate=pl.CostEstimate(flops=cost[0], bytes_accessed=cost[1], transcendentals=0),
        compiler_params=pltpu.CompilerParams(dimension_semantics=("arbitrary",) * len(grid)),
    )(where, *operands)


def all_of(shape):
    return pl.BlockSpec(shape, lambda *_: (0,) * len(shape))


def on_device(lag_weights, inverse_head, excitation, history):
    groups, devices = lax.axis_size("lag"), lax.axis_size("row")
    group, at = lax.axis_index("lag"), lax.axis_index("row")
    chips = devices // 2
    chip, core = at // 2, at % 2
    lags, rows, order = lag_weights.shape
    width = history.shape[-1]
    part = rows // groups
    tile = rows * 2 * rows
    square = (rows, width)
    tie = lax.optimization_barrier

    def pairs(axis_size, mask):
        return [(i, i ^ mask) for i in range(axis_size)]

    def other_core(value):
        return lax.ppermute(value, "row", pairs(devices, 1))

    def along(value, step, sources):
        return lax.ppermute(value, "row", [(2 * i + c, 2 * (i + step) + c) for i in sources for c in (0, 1)])

    def go_up(value, hop):
        return along(value, 1, range(hop - 1, chips - 1))

    def go_down(value, hop):
        return along(value, -1, range(1, chips - hop + 1))

    def taken(z, stage):
        both = min(z, chips - 1 - z)
        if stage <= 2 * both:
            return (stage + 1) // 2, stage % 2 == 1
        return stage - both, z >= stage - both

    def by_chip(values):
        result = jnp.int32(values[0])
        for z in range(1, chips):
            result = jnp.where(chip == z, values[z], result)
        return result

    def source_of(stage):
        return by_chip([z + (-h if u else h) for z in range(chips) for h, u in [taken(z, stage)]])

    def choose(stage, ups, downs):
        found = sorted({taken(z, stage) for z in range(chips)})
        arrays = [(ups if u else downs)[h] for h, u in found]
        return lax.select_n(by_chip([found.index(taken(z, stage)) for z in range(chips)]), *arrays) if len(found) > 1 else arrays[0]

    stages = [chip] + [source_of(stage) for stage in range(1, chips)]
    xored = [chip ^ k for k in range(chips)]
    where = jnp.stack([core, group, *stages, *xored]).astype(jnp.int32)

    def weight_spec(stage, first=0):
        return pl.BlockSpec((1, rows, 2 * rows), lambda k, w: (k + first, 0, w[2 + stage]))

    def lag_spec(shift):
        return pl.BlockSpec((1, rows, width), lambda k, w: (jnp.maximum(k + shift, 0), 0, 0))

    def add_chip(totals, near, far, stage):
        return call(
            chip_kernel, where, (lags,), (lag_weights, near, far, *totals),
            [weight_spec(stage)] + [all_of(v.shape) for v in (near, far, *totals)], STEPS, square,
            (18 * lags * tile * width, 4 * lags * tile), {4 + n: n for n in range(len(totals))},
            [pltpu.VMEM((2 * rows, lags * width), BF16)] * 2,
        )

    def add_first(total, near, far, stage):
        return call(
            first_kernel, where, (lags,), (lag_weights, near, far, total),
            [weight_spec(stage), lag_spec(0), lag_spec(0), all_of(square)], 1, square,
            (6 * lags * tile * width, 4 * lags * tile), {4: 0},
        )[0]

    def add_rest(one, two, near, far, stage):
        return call(
            rest_kernel, where, (lags - 1,), (lag_weights, near, near, far, far, one, two),
            [weight_spec(stage, 1), lag_spec(0), lag_spec(-1), lag_spec(0), lag_spec(-1), all_of(square), all_of(square)],
            2, square, (12 * lags * tile * width, 4 * lags * tile), {6: 0, 7: 1},
        )

    def add_entered(one, two, near, stage):
        far = other_core(near)
        spec = pl.BlockSpec((1, rows, 2 * rows), lambda k, w: (jnp.where(w[1] > 0, k, 0), 0, w[2 + stage]))
        return call(
            entered_kernel, where, (STEPS - 1,), (lag_weights, near, far, one, two),
            [spec, all_of(near.shape), all_of(near.shape), all_of(square), all_of(square)],
            2, square, (18 * tile * width, 8 * tile), {4: 0, 5: 1},
        )

    def add_second(total, nears, fars):
        block = pl.BlockSpec((part, width), lambda k, w: (k, 0))
        return call(
            second_kernel, where, (chips,), (lag_weights, *nears, *fars, total),
            [pl.BlockSpec((1, rows, 2 * rows), lambda k, w: (1, 0, jnp.where(w[1] == 0, w[2 + chips + k], 0)))]
            + [block] * 2 * groups + [all_of(square)],
            1, square, (6 * rows * order * width, 4 * rows * order), {2 + 2 * groups: 0},
        )[0]

    slots = jnp.stack([(chip ^ k) * 2 + (core ^ h) for h in (0, 1) for k in range(chips)]).astype(jnp.int32)
    meet = devices * part

    def columns(matrix, every):
        fold = devices // 2
        numbers = jnp.tile(slots.reshape(2, fold, 1), (1, 1, groups))
        numbers = jnp.concatenate([numbers, jnp.full((2, 1, groups), group, jnp.int32)], axis=1)
        whole = pl.BlockSpec((rows, meet // 2), lambda s, w: (0, s))
        half = pl.BlockSpec((rows, meet // 2), lambda s, w: (0, 0))
        shape = lambda size: jax.ShapeDtypeStruct((rows, size), F32)
        return pl.pallas_call(
            columns_kernel,
            out_shape=[shape(meet)] * (groups - 1) + [shape(meet // 2)] * 2 if every else [shape(meet)],
            grid_spec=pltpu.PrefetchScalarGridSpec(
                num_scalar_prefetch=1,
                grid=(2,),
                in_specs=[pl.BlockSpec((1, rows, rows), lambda s, w, i=i: (0, 0, w[s, i, 0])) for i in range(fold)],
                out_specs=[whole] * (groups - 1) + [half] * 2 if every else [whole],
            ),
            cost_estimate=pl.CostEstimate(flops=0, bytes_accessed=8 * rows * order, transcendentals=0),
            compiler_params=pltpu.CompilerParams(dimension_semantics=("arbitrary",)),
            name="columns",
        )(numbers, *[matrix] * fold)

    def pick(matrices):
        spec = lambda j: pl.BlockSpec((rows, meet // 2), lambda s, w: (0, jnp.where(w[0] == j, s, 0)))
        return pl.pallas_call(
            pick_kernel,
            out_shape=jax.ShapeDtypeStruct((rows, meet), F32),
            grid_spec=pltpu.PrefetchScalarGridSpec(
                num_scalar_prefetch=1,
                grid=(2,),
                in_specs=[spec(j) for j in range(groups - 1)] + [all_of((rows, meet // 2))] * 2,
                out_specs=pl.BlockSpec((rows, meet // 2), lambda s, w: (0, s)),
            ),
            cost_estimate=pl.CostEstimate(flops=0, bytes_accessed=16 * rows * meet, transcendentals=0),
            compiler_params=pltpu.CompilerParams(dimension_semantics=("arbitrary",)),
            name="pick",
        )(group.astype(jnp.int32).reshape(1), *matrices)

    def gather_near(value):
        pieces = [value] + [lax.ppermute(value, "row", pairs(devices, 2 * k)) for k in range(1, chips)]
        return jnp.concatenate(pieces, axis=0)

    def gather_far(mine):
        return jnp.concatenate([mine, other_core(mine)], axis=0)

    def own_part(value):
        return lax.dynamic_slice(value, (group * part, 0), (part, value.shape[1]))

    def sum_parts(value):
        result = own_part(value)
        for mask in range(1, groups):
            sent = lax.dynamic_slice(value, ((group ^ mask) * part, 0), (part, width))
            result = result + lax.ppermute(sent, "lag", pairs(groups, mask))
        return result

    def whole_rows(value):
        pieces = [value] + [lax.ppermute(value, "lag", pairs(groups, mask)) for mask in range(1, groups)]
        return jnp.concatenate([lax.select_n(group ^ i, *pieces) for i in range(groups)], axis=1)

    def enter(tail):
        return lax.ppermute(tail, "lag", [(i, i + 1) for i in range(groups - 1)])

    def tails(arrays):
        return {hop: value[lags - (STEPS - 1) :] for hop, value in arrays.items()}

    def multiply(matrix, vector):
        return jnp.dot(matrix, vector, precision=HIGHEST)

    ups, downs = {1: go_up(history, 1)}, {1: go_down(history, 1)}
    tail = history[lags - (STEPS - 1) :]
    entered = [enter(jnp.where(group >= 0, tail, 0.0))]
    own_far = other_core(history)
    *chunks, last_near, last_far = columns(lag_weights, True)
    relayed = lax.ppermute(last_far, "lag", [(0, groups // 2)])
    sent = [lax.ppermute(chunks[j], "lag", [(0, j)]) for j in range(1, groups - 1)]
    (head_columns,) = columns(inverse_head[None], False)
    ups[1], downs[1], entered, own_far, head_columns = tie((ups[1], downs[1], entered, own_far, head_columns))
    totals = []
    for stage in range(1, chips - 1):
        next_up, next_down = go_up(ups[stage], stage + 1), go_down(downs[stage], stage + 1)
        near = choose(stage, ups, downs)
        entered.append(enter(choose(stage, tails(ups), tails(downs))))
        if stage == 1:
            last_near, entered[0] = tie((last_near, entered[0]))
            sent.append(lax.ppermute(last_near, "lag", [(0, groups - 1)]))
            totals = add_chip([], history, own_far, 0)
        if stage == chips - 2:
            relayed, near = tie((relayed, near))
            sent.append(lax.ppermute(relayed, "lag", [(groups // 2, groups - 1)]))
        totals = add_chip(totals, near, other_core(near), stage)
        if stage == chips - 2:
            for early in range(chips - 2):
                entered[early], totals = tie((entered[early], totals))
                totals = [totals[0], *add_entered(totals[1], totals[2], entered[early], early)]
        ups[stage + 1], downs[stage + 1] = next_up, next_down
        ups, downs, totals = tie((ups, downs, totals))
    first, one, two = totals

    near = choose(chips - 1, ups, downs)
    far = other_core(near)
    first = add_first(first, near, far, chips - 1)

    right_side = own_part(excitation[0]) - sum_parts(first)
    right_side, ups, downs, near, far, one, two = tie((right_side, ups, downs, near, far, one, two))
    mine = gather_near(right_side)
    entered.append(enter(choose(chips - 1, tails(ups), tails(downs))))
    one, two = add_rest(one, two, near, far, chips - 1)
    mine, one, two, sent = tie((mine, one, two, sent))
    density = sum_parts(multiply(head_columns, gather_far(mine)))
    first_columns = pick([chunks[0], *sent])
    results = [density]

    density, first_columns, entered, one, two = tie((density, first_columns, entered, one, two))
    mine = gather_near(density)
    for stage in (chips - 2, chips - 1):
        one, two = add_entered(one, two, entered[stage], stage)
    mine, one, two = tie((mine, one, two))
    right_side = own_part(excitation[1]) - sum_parts(one + multiply(first_columns, gather_far(mine)))

    right_side, two, old = tie((right_side, two, mine))
    mine = gather_near(right_side)
    nears = [old] + [lax.ppermute(old, "lag", [(j, 0)]) for j in range(1, groups)]
    mine, two, nears = tie((mine, two, nears))
    spread = gather_far(mine)
    fars = other_core(jnp.stack(nears))
    spread, fars = tie((spread, fars))
    density = sum_parts(multiply(head_columns, spread))
    two = add_second(two, nears, [fars[j] for j in range(groups)])
    results.append(density)

    density, two = tie((density, two))
    mine = gather_near(density)
    right_side = own_part(excitation[2]) - sum_parts(two + multiply(first_columns, gather_far(mine)))

    right_side, results = tie((right_side, results))
    mine = gather_near(right_side)
    early = whole_rows(jnp.stack(results))
    mine, early = tie((mine, early))
    density = sum_parts(multiply(head_columns, gather_far(mine)))
    return jnp.concatenate([early, whole_rows(density[None])], axis=0)


def solution(mesh):
    placed = (P("lag", "row", None), P("row", None), P(None, "row", None), P("lag", "row", None))

    return jax.shard_map(on_device, mesh=mesh, in_specs=placed, out_specs=P(None, "row", None), check_vma=False)
```

profile of v0, /device:TPU:0, one launch (start us, length us, event | category | flops | bytes accessed | tf_op | source)
XLA Modules:
  0.0 366.4 jit_solution(6172682327613354666)
XLA Ops:
  0.0 5.9 %collective-permute-start = (f32[4,512,128]{2,1,0:T(8,128)}, f32[4,512,128]{2,1,0:T(8,128)}, u32[]{:S(2)}, u32[]{:S(2)}) collective-permute-start(f32[4,512,128]{2,1,0:T(8,128)} %near.1), channel_id=1, source_target_pairs={{0,2},{1,3},{2,4},{3,5},{4,6},{5,7},{8,10},{9,11},{10,12},{11,13},... | collective-permute-start | bytes 3145736 | tf_op jit(solution)/shard_map/ppermute | solution.py:198
  8.4 3.4 collective-permute-start.2
  12.7 5.8 %columns.2 = f32[512,1024]{1,0:T(8,128)} custom-call(s32[2,5,4]{2,1,0:T(8,128)} %concatenate.44.where, f32[1,512,4096]{2,1,0:T(8,128)} %bitcast.47, f32[1,512,4096]{2,1,0:T(8,128)} %bitcast.48, f32[1,512,4096]{2,1,0:T(8,128)} %bitcast.49, f32[1,512,4096]{2,1,0:T(8,128)} %bitcast.50), custom_call_target="tpu_custom_call" | custom-call | bytes 16777216 | tf_op jit(solution)/shard_map/columns/pallas_call | solution.py:286
  18.5 5.1 %collective-permute-done.2.near = f32[2,512,128]{2,1,0:T(8,128)S(1)} collective-permute-done((f32[2,512,128]{2,1,0:T(8,128)S(1)}, f32[2,512,128]{2,1,0:T(8,128)S(1)}, u32[]{:S(2)}, u32[]{:S(2)}) %collective-permute-start.2) | collective-permute-done | bytes 524320 | tf_op jit(solution)/shard_map/ppermute | solution.py:338
  23.6 4.1 %collective-permute-done = f32[4,512,128]{2,1,0:T(8,128)} collective-permute-done((f32[4,512,128]{2,1,0:T(8,128)}, f32[4,512,128]{2,1,0:T(8,128)}, u32[]{:S(2)}, u32[]{:S(2)}) %collective-permute-start) | collective-permute-done | bytes 1048608 | tf_op jit(solution)/shard_map/ppermute | solution.py:198
  27.7 5.0 %collective-permute-done.1 = f32[4,512,128]{2,1,0:T(8,128)S(1)} collective-permute-done((f32[4,512,128]{2,1,0:T(8,128)}, f32[4,512,128]{2,1,0:T(8,128)S(1)}, u32[]{:S(2)}, u32[]{:S(2)}) %collective-permute-start.1) | collective-permute-done | bytes 1048608 | tf_op jit(solution)/shard_map/ppermute | solution.py:198
  36.1 7.2 %columns.3 = (f32[512,1024]{1,0:T(8,128)}, f32[512,1024]{1,0:T(8,128)}, f32[512,1024]{1,0:T(8,128)}, f32[512,512]{1,0:T(8,128)}, f32[512,512]{1,0:T(8,128)}) custom-call(s32[2,5,4]{2,1,0:T(8,128)} %concatenate.44.where, f32[4,512,4096]{2,1,0:T(8,128)} %weights.19, f32[4,512,4096]{2,1,0:T(8,128)} %weights.19, f32[4,512,4096]{2,1,0:T(8,128)} %weights.19, ...), custom_call_target="tpu_custom_call" | custom-call | bytes 16777216 | tf_op jit(solution)/shard_map/columns/pallas_call | solution.py:286
  43.2 4.7 %collective-permute-start.10 = (f32[512,512]{1,0:T(8,128)}, f32[512,512]{1,0:T(8,128)}, u32[]{:S(2)}, u32[]{:S(2)}) collective-permute-start(f32[512,512]{1,0:T(8,128)} %get-tuple-element.118), channel_id=1, source_target_pairs={{0,16},{1,17},{2,18},{3,19},{4,20},{5,21},{6,22},{7,23}} | collective-permute-start | bytes 3145736 | tf_op jit(solution)/shard_map/ppermute | solution.py:351
  48.6 9.8 %shard_map.46 = (f32[512,128]{1,0:T(8,128)}, f32[512,128]{1,0:T(8,128)}, f32[512,128]{1,0:T(8,128)}) custom-call(s32[10]{0:T(128)} %stack.100.where, f32[4,512,4096]{2,1,0:T(8,128)} %weights.19, f32[4,512,128]{2,1,0:T(8,128)} %near.1, f32[4,512,128]{2,1,0:T(8,128)} %copy-done.15), custom_call_target="tpu_custom_call" | custom-call | flops 4831838208 | bytes 8388608 | tf_op jit(solution)/shard_map/pallas_call | solution.py:163
  58.4 10.0 %shard_map.47 = (f32[512,128]{1,0:T(8,128)}, f32[512,128]{1,0:T(8,128)}, f32[512,128]{1,0:T(8,128)}) custom-call(s32[10]{0:T(128)} %stack.100.where, f32[4,512,4096]{2,1,0:T(8,128)} %weights.19, f32[4,512,128]{2,1,0:T(8,128)} %broadcast_select_fusion.near, ...), custom_call_target="tpu_custom_call", output_to_operand_aliasing={{0}: (4, {}), {1}: (5, {}), {2}: (6, {})} | custom-call | flops 4831838208 | bytes 8388608 | tf_op jit(solution)/shard_map/pallas_call | solution.py:163
  70.1 2.8 collective-permute-done.11.far
  72.8 10.0 %shard_map.48 = (f32[512,128]{1,0:T(8,128)}, f32[512,128]{1,0:T(8,128)}, f32[512,128]{1,0:T(8,128)}) custom-call(s32[10]{0:T(128)} %stack.100.where, f32[4,512,4096]{2,1,0:T(8,128)} %weights.19, f32[4,512,128]{2,1,0:T(8,128)} %copy-done.11, f32[4,512,128]{2,1,0:T(8,128)} %collective-permute-done.11.far, ...), custom_call_target="tpu_custom_call", output_to_operand_aliasing={{0}: (4, {}), {1}: (5, {}), {2}: (6, {})} | custom-call | flops 4831838208 | bytes 8388608 | tf_op jit(solution)/shard_map/pallas_call | solution.py:163
  83.0 1.9 slice_select_fusion
  84.8 2.1 collective-permute-start.9
  88.6 1.8 collective-permute-start.8
  90.4 3.7 %shard_map.49 = (f32[512,128]{1,0:T(8,128)}, f32[512,128]{1,0:T(8,128)}) custom-call(s32[10]{0:T(128)} %stack.100.where, f32[4,512,4096]{2,1,0:T(8,128)} %weights.19, f32[2,512,128]{2,1,0:T(8,128)} %copy-done.16, f32[2,512,128]{2,1,0:T(8,128)} %collective-permute-done.12.far, ...), custom_call_target="tpu_custom_call", output_to_operand_aliasing={{0}: (4, {}), {1}: (5, {})} | custom-call | flops 1207959552 | bytes 4194304 | tf_op jit(solution)/shard_map/pallas_call | solution.py:163
  94.1 4.3 %collective-permute-done.9.near = f32[2,512,128]{2,1,0:T(8,128)} collective-permute-done((f32[2,512,128]{2,1,0:T(8,128)}, f32[2,512,128]{2,1,0:T(8,128)}, u32[]{:S(2)}, u32[]{:S(2)}) %collective-permute-start.9) | collective-permute-done | bytes 524320 | tf_op jit(solution)/shard_map/ppermute | solution.py:338
  98.4 2.2 collective-permute-done.13.far
  100.7 3.7 %shard_map.50 = (f32[512,128]{1,0:T(8,128)}, f32[512,128]{1,0:T(8,128)}) custom-call(s32[10]{0:T(128)} %stack.100.where, f32[4,512,4096]{2,1,0:T(8,128)} %weights.19, f32[2,512,128]{2,1,0:T(8,128)} %collective-permute-done.9.near, f32[2,512,128]{2,1,0:T(8,128)} %collective-permute-done.13.far, ...), custom_call_target="tpu_custom_call", output_to_operand_aliasing={{0}: (4, {}), {1}: (5, {})} | custom-call | flops 1207959552 | bytes 4194304 | tf_op jit(solution)/shard_map/pallas_call | solution.py:163
  104.4 14.4 %collective-permute-done.8 = f32[4,512,128]{2,1,0:T(8,128)} collective-permute-done((f32[4,512,128]{2,1,0:T(8,128)S(1)}, f32[4,512,128]{2,1,0:T(8,128)}, u32[]{:S(2)}, u32[]{:S(2)}) %collective-permute-start.8) | collective-permute-done | bytes 1048608 | tf_op jit(solution)/shard_map/ppermute | solution.py:198
  120.3 6.7 %collective-permute-start.21 = (f32[512,1024]{1,0:T(8,128)}, f32[512,1024]{1,0:T(8,128)}, u32[]{:S(2)}, u32[]{:S(2)}) collective-permute-start(f32[512,1024]{1,0:T(8,128)} %get-tuple-element.152), channel_id=1, source_target_pairs={{0,8},{1,9},{2,10},{3,11},{4,12},{5,13},{6,14},{7,15}} | collective-permute-start | bytes 6291464 | tf_op jit(solution)/shard_map/ppermute | solution.py:352
  127.0 2.6 collective-permute-start.22
  130.6 7.4 %shard_map.51 = f32[512,128]{1,0:T(8,128)} custom-call(s32[10]{0:T(128)} %stack.100.where, f32[4,512,4096]{2,1,0:T(8,128)} %weights.19, f32[4,512,128]{2,1,0:T(8,128)} %copy-done.3, f32[4,512,128]{2,1,0:T(8,128)} %copy-done.4, f32[512,128]{1,0:T(8,128)} %get-tuple-element.142.total), custom_call_target="tpu_custom_call", output_to_operand_aliasing={{}: (4, {})} | custom-call | flops 1610612736 | bytes 8388608 | tf_op jit(solution)/shard_map/pallas_call | solution.py:163
  139.2 6.3 %collective-permute-start.23 = (f32[512,512]{1,0:T(8,128)}, f32[512,512]{1,0:T(8,128)}, u32[]{:S(2)}, u32[]{:S(2)}) collective-permute-start(f32[512,512]{1,0:T(8,128)} %get-tuple-element.154), channel_id=1, source_target_pairs={{0,24},{1,25},{2,26},{3,27},{4,28},{5,29},{6,30},{7,31}} | collective-permute-start | bytes 3145736 | tf_op jit(solution)/shard_map/ppermute | solution.py:362
  145.5 27.8 %collective-permute-done.15 = f32[128,128]{1,0:T(8,128)S(1)} collective-permute-done((f32[128,128]{1,0:T(8,128)S(1)}, f32[128,128]{1,0:T(8,128)S(1)}, u32[]{:S(2)}, u32[]{:S(2)}) %collective-permute-start.15) | collective-permute-done | bytes 65568 | tf_op jit(solution)/shard_map/ppermute | solution.py:330
  173.3 1.7 collective-permute-start.24
  176.1 2.0 fusion.15
  178.0 18.7 %collective-permute-done.17 = f32[128,128]{1,0:T(8,128)} collective-permute-done((f32[128,128]{1,0:T(8,128)S(1)}, f32[128,128]{1,0:T(8,128)}, u32[]{:S(2)}, u32[]{:S(2)}) %collective-permute-start.17) | collective-permute-done | bytes 65568 | tf_op jit(solution)/shard_map/ppermute | solution.py:330
  197.7 4.3 %collective-permute-done.18 = f32[128,128]{1,0:T(8,128)S(1)} collective-permute-done((f32[128,128]{1,0:T(8,128)S(1)}, f32[128,128]{1,0:T(8,128)S(1)}, u32[]{:S(2)}, u32[]{:S(2)}) %collective-permute-start.18) | collective-permute-done | bytes 65568 | tf_op jit(solution)/shard_map/ppermute | solution.py:317
  202.9 4.8 %collective-permute-done.19 = f32[128,128]{1,0:T(8,128)S(1)} collective-permute-done((f32[128,128]{1,0:T(8,128)S(1)}, f32[128,128]{1,0:T(8,128)S(1)}, u32[]{:S(2)}, u32[]{:S(2)}) %collective-permute-start.19) | collective-permute-done | bytes 65568 | tf_op jit(solution)/shard_map/ppermute | solution.py:317
  209.1 7.7 %shard_map.52 = (f32[512,128]{1,0:T(8,128)}, f32[512,128]{1,0:T(8,128)}) custom-call(s32[10]{0:T(128)} %stack.100.where, f32[4,512,4096]{2,1,0:T(8,128)} %weights.19, f32[4,512,128]{2,1,0:T(8,128)} %copy-done.3, f32[4,512,128]{2,1,0:T(8,128)} %copy-done.3, f32[4,512,128]{2,1,0:T(8,128)} %copy-done.4, ...), custom_call_target="tpu_custom_call", output_to_operand_aliasing={{0}: (6, {}), {1}: (7, {})} | custom-call | flops 3221225472 | bytes 8388608 | tf_op jit(solution)/shard_map/pallas_call | solution.py:163
  216.8 2.2 collective-permute-start.29
  219.2 2.2 select_select_fusion.2
  222.9 1.8 fusion
  224.8 6.0 %collective-permute-start.26 = (f32[128,128]{1,0:T(8,128)S(1)}, f32[128,128]{1,0:T(8,128)S(1)}, u32[]{:S(2)}, u32[]{:S(2)}) collective-permute-start(f32[128,128]{1,0:T(8,128)S(1)} %get-tuple-element.225), channel_id=1, source_target_pairs={{0,8},{8,0},{16,24},{24,16},{1,9},{9,1},{17,25},{25,17},{2,10},{10... | collective-permute-start | bytes 196616 | tf_op jit(solution)/shard_map/ppermute | solution.py:330
  232.3 4.0 %pick.1 = f32[512,1024]{1,0:T(8,128)} custom-call(s32[1]{0:T(128)} %bitcast.13.which, f32[512,1024]{1,0:T(8,128)} %get-tuple-element.157.refs_0_, f32[512,1024]{1,0:T(8,128)} %collective-permute-done.21.refs_1_, f32[512,1024]{1,0:T(8,128)} %collective-permute-done.22.refs_2_, f32[512,512]{1,0:T(8,128)} %collective-permute-done.23.refs_3_, ...), custom_call_target="tpu_custom_call" | custom-call | bytes 8388608 | tf_op jit(solution)/shard_map/pick/pallas_call | solution.py:302
  236.3 6.8 %collective-permute-done.26 = f32[128,128]{1,0:T(8,128)S(1)} collective-permute-done((f32[128,128]{1,0:T(8,128)S(1)}, f32[128,128]{1,0:T(8,128)S(1)}, u32[]{:S(2)}, u32[]{:S(2)}) %collective-permute-start.26) | collective-permute-done | bytes 65568 | tf_op jit(solution)/shard_map/ppermute | solution.py:330
  243.7 3.0 collective-permute-start.32
  249.0 2.5 collective-permute-done.32
  252.9 3.7 %shard_map.53 = (f32[512,128]{1,0:T(8,128)}, f32[512,128]{1,0:T(8,128)}) custom-call(s32[10]{0:T(128)} %stack.100.where, f32[4,512,4096]{2,1,0:T(8,128)} %weights.19, f32[2,512,128]{2,1,0:T(8,128)} %collective-permute-done.29.near, f32[2,512,128]{2,1,0:T(8,128)} %collective-permute-done.35.far, ...), custom_call_target="tpu_custom_call", output_to_operand_aliasing={{0}: (4, {}), {1}: (5, {})} | custom-call | flops 1207959552 | bytes 4194304 | tf_op jit(solution)/shard_map/pallas_call | solution.py:163
  257.4 3.7 %shard_map.54 = (f32[512,128]{1,0:T(8,128)}, f32[512,128]{1,0:T(8,128)}) custom-call(s32[10]{0:T(128)} %stack.100.where, f32[4,512,4096]{2,1,0:T(8,128)} %weights.19, f32[2,512,128]{2,1,0:T(8,128)} %copy-done.17, f32[2,512,128]{2,1,0:T(8,128)} %copy-done.18, f32[512,128]{1,0:T(8,128)} %get-tuple-element.173.one, ...), custom_call_target="tpu_custom_call", output_to_operand_aliasing={{0}: (4, {}), {1}: (5, {})} | custom-call | flops 1207959552 | bytes 4194304 | tf_op jit(solution)/shard_map/pallas_call | solution.py:163
  262.7 3.4 fusion.4
  266.1 7.7 %collective-permute-start.37 = (f32[128,128]{1,0:T(8,128)S(1)}, f32[128,128]{1,0:T(8,128)S(1)}, u32[]{:S(2)}, u32[]{:S(2)}) collective-permute-start(f32[128,128]{1,0:T(8,128)S(1)} %get-tuple-element.222), channel_id=1, source_target_pairs={{0,8},{8,0},{16,24},{24,16},{1,9},{9,1},{17,25},{25,17},{2,10},{10... | collective-permute-start | bytes 196616 | tf_op jit(solution)/shard_map/ppermute | solution.py:330
  276.2 3.1 collective-permute-done.38
  286.6 1.9 collective-permute-done.40
  288.6 2.2 collective-permute-start.42
  291.9 2.8 collective-permute-done.42
  296.3 2.5 collective-permute-done.46
  299.9 1.8 fusion.16
  302.3 2.7 collective-permute-start.49
  305.3 7.5 %shard_map.55 = f32[512,128]{1,0:T(8,128)} custom-call(s32[10]{0:T(128)} %stack.100.where, f32[4,512,4096]{2,1,0:T(8,128)} %weights.19, f32[512,128]{1,0:T(8,128)} %copy-done.10, f32[512,128]{1,0:T(8,128)} %copy-done.12, f32[512,128]{1,0:T(8,128)} %copy-done.13, f32[512,128]{1,0:T(8,128)} %copy-done.14, ...), custom_call_target="tpu_custom_call", output_to_operand_aliasing={{}: (10, {})} | custom-call | flops 1610612736 | bytes 8388608 | tf_op jit(solution)/shard_map/pallas_call | solution.py:163
  315.4 1.9 collective-permute-start.53
  317.7 2.8 collective-permute-done.52
  323.1 3.4 fusion.17
  327.2 3.0 collective-permute-start.57
  335.9 1.8 collective-permute-start.60
  337.7 1.8 collective-permute-start.61
  339.5 1.7 collective-permute-start.62
  345.0 2.1 collective-permute-done.63
  348.9 1.8 fusion.8
  351.3 2.9 collective-permute-start.67
  356.5 2.0 collective-permute-start.68
  361.2 2.0 collective-permute-done.69
  363.2 2.1 collective-permute-done.70
  (182 shorter events, 67.0 us)
Async XLA Ops:
  0.0 27.7 %collective-permute-start = (f32[4,512,128]{2,1,0:T(8,128)}, f32[4,512,128]{2,1,0:T(8,128)}, u32[]{:S(2)}, u32[]{:S(2)}) collective-permute-start(f32[4,512,128]{2,1,0:T(8,128)} %near.1), channel_id=1, source_target_pairs={{0,2},{1,3},{2,4},{3,5},{4,6},{5,7},{8,10},{9,11},{10,12},{11,13},... | collective-permute-start | bytes 3145736 | tf_op jit(solution)/shard_map/ppermute | solution.py:198
  5.9 26.7 %collective-permute-start.1 = (f32[4,512,128]{2,1,0:T(8,128)}, f32[4,512,128]{2,1,0:T(8,128)S(1)}, u32[]{:S(2)}, u32[]{:S(2)}) collective-permute-start(f32[4,512,128]{2,1,0:T(8,128)} %near.1), channel_id=1, source_target_pairs={{2,0},{3,1},{4,2},{5,3},{6,4},{7,5},{10,8},{11,9},{12,10},{13,11},... | collective-permute-start | bytes 3145736 | tf_op jit(solution)/shard_map/ppermute | solution.py:198
  7.2 25.4 %collective-permute-start.3 = (f32[4,512,128]{2,1,0:T(8,128)}, f32[4,512,128]{2,1,0:T(8,128)S(1)}, u32[]{:S(2)}, u32[]{:S(2)}) collective-permute-start(f32[4,512,128]{2,1,0:T(8,128)} %near.1), channel_id=1, source_target_pairs={{0,1},{1,0},{2,3},{3,2},{4,5},{5,4},{6,7},{7,6},{8,9},{9,8},{10,11... | collective-permute-start | bytes 3145736 | tf_op jit(solution)/shard_map/ppermute | solution.py:195
  8.4 15.2 %collective-permute-start.2 = (f32[2,512,128]{2,1,0:T(8,128)S(1)}, f32[2,512,128]{2,1,0:T(8,128)S(1)}, u32[]{:S(2)}, u32[]{:S(2)}) collective-permute-start(f32[2,512,128]{2,1,0:T(8,128)S(1)} %slice_select_fusion.1), channel_id=1, source_target_pairs={{0,8},{8,16},{16,24},{1,9},{9,17},{17,25},{2,10},{10,18},{18,26},{... | collective-permute-start | bytes 1572872 | tf_op jit(solution)/shard_map/ppermute | solution.py:338
  34.0 24.4 %collective-permute-start.6 = (f32[4,512,128]{2,1,0:T(8,128)}, f32[4,512,128]{2,1,0:T(8,128)}, u32[]{:S(2)}, u32[]{:S(2)}) collective-permute-start(f32[4,512,128]{2,1,0:T(8,128)} %broadcast_select_fusion.near), channel_id=1, source_target_pairs={{0,1},{1,0},{2,3},{3,2},{4,5},{5,4},{6,7},{7,6},{8,9},{9,8},{10,11... | collective-permute-start | bytes 3145736 | tf_op jit(solution)/shard_map/ppermute | solution.py:195
  34.0 34.3 %collective-permute-start.4 = (f32[4,512,128]{2,1,0:T(8,128)}, f32[4,512,128]{2,1,0:T(8,128)S(1)}, u32[]{:S(2)}, u32[]{:S(2)}) collective-permute-start(f32[4,512,128]{2,1,0:T(8,128)} %collective-permute-done), channel_id=1, source_target_pairs={{2,4},{3,5},{4,6},{5,7},{10,12},{11,13},{12,14},{13,15},{18,20},{1... | collective-permute-start | bytes 3145736 | tf_op jit(solution)/shard_map/ppermute | solution.py:198
  34.8 33.6 %collective-permute-start.5 = (f32[4,512,128]{2,1,0:T(8,128)S(1)}, f32[4,512,128]{2,1,0:T(8,128)S(1)}, u32[]{:S(2)}, u32[]{:S(2)}) collective-permute-start(f32[4,512,128]{2,1,0:T(8,128)S(1)} %collective-permute-done.1), channel_id=1, source_target_pairs={{2,0},{3,1},{4,2},{5,3},{10,8},{11,9},{12,10},{13,11},{18,16},{19,... | collective-permute-start | bytes 3145736 | tf_op jit(solution)/shard_map/ppermute | solution.py:198
  43.2 26.8 %collective-permute-start.10 = (f32[512,512]{1,0:T(8,128)}, f32[512,512]{1,0:T(8,128)}, u32[]{:S(2)}, u32[]{:S(2)}) collective-permute-start(f32[512,512]{1,0:T(8,128)} %get-tuple-element.118), channel_id=1, source_target_pairs={{0,16},{1,17},{2,18},{3,19},{4,20},{5,21},{6,22},{7,23}} | collective-permute-start | bytes 3145736 | tf_op jit(solution)/shard_map/ppermute | solution.py:351
  82.8 7.6 %collective-permute-start.12 = (f32[2,512,128]{2,1,0:T(8,128)}, f32[2,512,128]{2,1,0:T(8,128)}, u32[]{:S(2)}, u32[]{:S(2)}) collective-permute-start(f32[2,512,128]{2,1,0:T(8,128)} %copy-done.16), channel_id=1, source_target_pairs={{0,1},{1,0},{2,3},{3,2},{4,5},{5,4},{6,7},{7,6},{8,9},{9,8},{10,11... | collective-permute-start | bytes 1572872 | tf_op jit(solution)/shard_map/ppermute | solution.py:195
  84.8 13.6 %collective-permute-start.9 = (f32[2,512,128]{2,1,0:T(8,128)}, f32[2,512,128]{2,1,0:T(8,128)}, u32[]{:S(2)}, u32[]{:S(2)}) collective-permute-start(f32[2,512,128]{2,1,0:T(8,128)} %slice_select_fusion), channel_id=1, source_target_pairs={{0,8},{8,16},{16,24},{1,9},{9,17},{17,25},{2,10},{10,18},{18,26},{... | collective-permute-start | bytes 1572872 | tf_op jit(solution)/shard_map/ppermute | solution.py:338
  86.9 17.4 %collective-permute-start.7 = (f32[4,512,128]{2,1,0:T(8,128)S(1)}, f32[4,512,128]{2,1,0:T(8,128)}, u32[]{:S(2)}, u32[]{:S(2)}) collective-permute-start(f32[4,512,128]{2,1,0:T(8,128)S(1)} %collective-permute-done.4), channel_id=1, source_target_pairs={{4,6},{5,7},{12,14},{13,15},{20,22},{21,23},{28,30},{29,31}} | collective-permute-start | bytes 3145736 | tf_op jit(solution)/shard_map/ppermute | solution.py:198
  88.6 30.2 %collective-permute-start.8 = (f32[4,512,128]{2,1,0:T(8,128)S(1)}, f32[4,512,128]{2,1,0:T(8,128)}, u32[]{:S(2)}, u32[]{:S(2)}) collective-permute-start(f32[4,512,128]{2,1,0:T(8,128)S(1)} %collective-permute-done.5), channel_id=1, source_target_pairs={{2,0},{3,1},{10,8},{11,9},{18,16},{19,17},{26,24},{27,25}} | collective-permute-start | bytes 3145736 | tf_op jit(solution)/shard_map/ppermute | solution.py:198
  120.2 9.5 %collective-permute-start.14 = (f32[4,512,128]{2,1,0:T(8,128)S(1)}, f32[4,512,128]{2,1,0:T(8,128)S(1)}, u32[]{:S(2)}, u32[]{:S(2)}) collective-permute-start(f32[4,512,128]{2,1,0:T(8,128)S(1)} %select_select_fusion.near.near_before), channel_id=1, source_target_pairs={{0,1},{1,0},{2,3},{3,2},{4,5},{5,4},{6,7},{7,6},{8,9},{9,8},{10,11... | collective-permute-start | bytes 3145736 | tf_op jit(solution)/shard_map/ppermute | solution.py:195
  120.3 98.8 %collective-permute-start.21 = (f32[512,1024]{1,0:T(8,128)}, f32[512,1024]{1,0:T(8,128)}, u32[]{:S(2)}, u32[]{:S(2)}) collective-permute-start(f32[512,1024]{1,0:T(8,128)} %get-tuple-element.152), channel_id=1, source_target_pairs={{0,8},{1,9},{2,10},{3,11},{4,12},{5,13},{6,14},{7,15}} | collective-permute-start | bytes 6291464 | tf_op jit(solution)/shard_map/ppermute | solution.py:352
  127.0 92.1 %collective-permute-start.22 = (f32[512,1024]{1,0:T(8,128)}, f32[512,1024]{1,0:T(8,128)}, u32[]{:S(2)}, u32[]{:S(2)}) collective-permute-start(f32[512,1024]{1,0:T(8,128)} %get-tuple-element.153), channel_id=1, source_target_pairs={{0,16},{1,17},{2,18},{3,19},{4,20},{5,21},{6,22},{7,23}} | collective-permute-start | bytes 6291464 | tf_op jit(solution)/shard_map/ppermute | solution.py:352
  139.1 34.2 %collective-permute-start.15 = (f32[128,128]{1,0:T(8,128)S(1)}, f32[128,128]{1,0:T(8,128)S(1)}, u32[]{:S(2)}, u32[]{:S(2)}) collective-permute-start(f32[128,128]{1,0:T(8,128)S(1)} %get-tuple-element.228), channel_id=1, source_target_pairs={{0,8},{8,0},{16,24},{24,16},{1,9},{9,1},{17,25},{25,17},{2,10},{10... | collective-permute-start | bytes 196616 | tf_op jit(solution)/shard_map/ppermute | solution.py:330
  139.2 36.3 %collective-permute-start.16 = (f32[128,128]{1,0:T(8,128)S(1)}, f32[128,128]{1,0:T(8,128)S(1)}, u32[]{:S(2)}, u32[]{:S(2)}) collective-permute-start(f32[128,128]{1,0:T(8,128)S(1)} %get-tuple-element.230), channel_id=1, source_target_pairs={{0,16},{8,24},{16,0},{24,8},{1,17},{9,25},{17,1},{25,9},{2,18},{10... | collective-permute-start | bytes 196616 | tf_op jit(solution)/shard_map/ppermute | solution.py:330
  139.2 79.8 %collective-permute-start.23 = (f32[512,512]{1,0:T(8,128)}, f32[512,512]{1,0:T(8,128)}, u32[]{:S(2)}, u32[]{:S(2)}) collective-permute-start(f32[512,512]{1,0:T(8,128)} %get-tuple-element.154), channel_id=1, source_target_pairs={{0,24},{1,25},{2,26},{3,27},{4,28},{5,29},{6,30},{7,31}} | collective-permute-start | bytes 3145736 | tf_op jit(solution)/shard_map/ppermute | solution.py:362
  173.3 45.8 %collective-permute-start.24 = (f32[512,512]{1,0:T(8,128)}, f32[512,512]{1,0:T(8,128)}, u32[]{:S(2)}, u32[]{:S(2)}) collective-permute-start(f32[512,512]{1,0:T(8,128)} %collective-permute-done.10), channel_id=1, source_target_pairs={{16,24},{17,25},{18,26},{19,27},{20,28},{21,29},{22,30},{23,31}} | collective-permute-start | bytes 3145736 | tf_op jit(solution)/shard_map/ppermute | solution.py:366
  176.1 20.6 %collective-permute-start.17 = (f32[128,128]{1,0:T(8,128)S(1)}, f32[128,128]{1,0:T(8,128)}, u32[]{:S(2)}, u32[]{:S(2)}) collective-permute-start(f32[128,128]{1,0:T(8,128)S(1)} %get-tuple-element.229), channel_id=1, source_target_pairs={{0,24},{8,16},{16,8},{24,0},{1,25},{9,17},{17,9},{25,1},{2,26},{10... | collective-permute-start | bytes 196616 | tf_op jit(solution)/shard_map/ppermute | solution.py:330
  197.6 4.3 %collective-permute-start.18 = (f32[128,128]{1,0:T(8,128)S(1)}, f32[128,128]{1,0:T(8,128)S(1)}, u32[]{:S(2)}, u32[]{:S(2)}) collective-permute-start(f32[128,128]{1,0:T(8,128)S(1)} %bitcast_subtract_fusion), channel_id=1, source_target_pairs={{0,2},{1,3},{2,0},{3,1},{4,6},{5,7},{6,4},{7,5},{8,10},{9,11},{10,... | collective-permute-start | bytes 196616 | tf_op jit(solution)/shard_map/ppermute | solution.py:317
  202.0 5.8 %collective-permute-start.19 = (f32[128,128]{1,0:T(8,128)S(1)}, f32[128,128]{1,0:T(8,128)S(1)}, u32[]{:S(2)}, u32[]{:S(2)}) collective-permute-start(f32[128,128]{1,0:T(8,128)S(1)} %bitcast_subtract_fusion), channel_id=1, source_target_pairs={{0,4},{1,5},{2,6},{3,7},{4,0},{5,1},{6,2},{7,3},{8,12},{9,13},{10,... | collective-permute-start | bytes 196616 | tf_op jit(solution)/shard_map/ppermute | solution.py:317
  207.7 9.1 %collective-permute-start.20 = (f32[128,128]{1,0:T(8,128)S(1)}, f32[128,128]{1,0:T(8,128)S(1)}, u32[]{:S(2)}, u32[]{:S(2)}) collective-permute-start(f32[128,128]{1,0:T(8,128)S(1)} %bitcast_subtract_fusion), channel_id=1, source_target_pairs={{0,6},{1,7},{2,4},{3,5},{4,2},{5,3},{6,0},{7,1},{8,14},{9,15},{10,... | collective-permute-start | bytes 196616 | tf_op jit(solution)/shard_map/ppermute | solution.py:317
  216.8 26.3 %collective-permute-start.29 = (f32[2,512,128]{2,1,0:T(8,128)}, f32[2,512,128]{2,1,0:T(8,128)}, u32[]{:S(2)}, u32[]{:S(2)}) collective-permute-start(f32[2,512,128]{2,1,0:T(8,128)} %select_select_fusion.3), channel_id=1, source_target_pairs={{0,8},{8,16},{16,24},{1,9},{9,17},{17,25},{2,10},{10,18},{18,26},{... | collective-permute-start | bytes 1572872 | tf_op jit(solution)/shard_map/ppermute | solution.py:338
  219.1 3.8 %collective-permute-start.25 = (f32[512,128]{1,0:T(8,128)S(1)}, f32[512,128]{1,0:T(8,128)S(1)}, u32[]{:S(2)}, u32[]{:S(2)}) collective-permute-start(f32[512,128]{1,0:T(8,128)S(1)} %pad_maximum_fusion.3), channel_id=1, source_target_pairs={{0,1},{1,0},{2,3},{3,2},{4,5},{5,4},{6,7},{7,6},{8,9},{9,8},{10,11... | collective-permute-start | bytes 786440 | tf_op jit(solution)/shard_map/ppermute | solution.py:195
  221.4 21.7 %collective-permute-start.30 = (f32[2,512,128]{2,1,0:T(8,128)}, f32[2,512,128]{2,1,0:T(8,128)S(1)}, u32[]{:S(2)}, u32[]{:S(2)}) collective-permute-start(f32[2,512,128]{2,1,0:T(8,128)} %select_select_fusion.2), channel_id=1, source_target_pairs={{0,8},{8,16},{16,24},{1,9},{9,17},{17,25},{2,10},{10,18},{18,26},{... | collective-permute-start | bytes 1572872 | tf_op jit(solution)/shard_map/ppermute | solution.py:338
  224.8 18.3 %collective-permute-start.26 = (f32[128,128]{1,0:T(8,128)S(1)}, f32[128,128]{1,0:T(8,128)S(1)}, u32[]{:S(2)}, u32[]{:S(2)}) collective-permute-start(f32[128,128]{1,0:T(8,128)S(1)} %get-tuple-element.225), channel_id=1, source_target_pairs={{0,8},{8,0},{16,24},{24,16},{1,9},{9,1},{17,25},{25,17},{2,10},{10... | collective-permute-start | bytes 196616 | tf_op jit(solution)/shard_map/ppermute | solution.py:330
  230.8 12.3 %collective-permute-start.27 = (f32[128,128]{1,0:T(8,128)S(1)}, f32[128,128]{1,0:T(8,128)S(1)}, u32[]{:S(2)}, u32[]{:S(2)}) collective-permute-start(f32[128,128]{1,0:T(8,128)S(1)} %get-tuple-element.227), channel_id=1, source_target_pairs={{0,16},{8,24},{16,0},{24,8},{1,17},{9,25},{17,1},{25,9},{2,18},{10... | collective-permute-start | bytes 196616 | tf_op jit(solution)/shard_map/ppermute | solution.py:330
  230.8 12.3 %collective-permute-start.28 = (f32[128,128]{1,0:T(8,128)S(1)}, f32[128,128]{1,0:T(8,128)S(1)}, u32[]{:S(2)}, u32[]{:S(2)}) collective-permute-start(f32[128,128]{1,0:T(8,128)S(1)} %get-tuple-element.226), channel_id=1, source_target_pairs={{0,24},{8,16},{16,8},{24,0},{1,25},{9,17},{17,9},{25,1},{2,26},{10... | collective-permute-start | bytes 196616 | tf_op jit(solution)/shard_map/ppermute | solution.py:330
  243.2 9.8 %collective-permute-start.35 = (f32[2,512,128]{2,1,0:T(8,128)}, f32[2,512,128]{2,1,0:T(8,128)}, u32[]{:S(2)}, u32[]{:S(2)}) collective-permute-start(f32[2,512,128]{2,1,0:T(8,128)} %collective-permute-done.29.near), channel_id=1, source_target_pairs={{0,1},{1,0},{2,3},{3,2},{4,5},{5,4},{6,7},{7,6},{8,9},{9,8},{10,11... | collective-permute-start | bytes 1572872 | tf_op jit(solution)/shard_map/ppermute | solution.py:195
  243.2 13.4 %collective-permute-start.34 = (f32[2,512,128]{2,1,0:T(8,128)S(1)}, f32[2,512,128]{2,1,0:T(8,128)S(1)}, u32[]{:S(2)}, u32[]{:S(2)}) collective-permute-start(f32[2,512,128]{2,1,0:T(8,128)S(1)} %collective-permute-done.30.near), channel_id=1, source_target_pairs={{0,1},{1,0},{2,3},{3,2},{4,5},{5,4},{6,7},{7,6},{8,9},{9,8},{10,11... | collective-permute-start | bytes 1572872 | tf_op jit(solution)/shard_map/ppermute | solution.py:195
  243.7 5.3 %collective-permute-start.31 = (f32[128,128]{1,0:T(8,128)S(1)}, f32[128,128]{1,0:T(8,128)S(1)}, u32[]{:S(2)}, u32[]{:S(2)}) collective-permute-start(f32[128,128]{1,0:T(8,128)S(1)} %add_add_fusion.1), channel_id=1, source_target_pairs={{0,2},{1,3},{2,0},{3,1},{4,6},{5,7},{6,4},{7,5},{8,10},{9,11},{10,... | collective-permute-start | bytes 196616 | tf_op jit(solution)/shard_map/ppermute | solution.py:317
  243.7 7.8 %collective-permute-start.32 = (f32[128,128]{1,0:T(8,128)S(1)}, f32[128,128]{1,0:T(8,128)S(1)}, u32[]{:S(2)}, u32[]{:S(2)}) collective-permute-start(f32[128,128]{1,0:T(8,128)S(1)} %add_add_fusion.1), channel_id=1, source_target_pairs={{0,4},{1,5},{2,6},{3,7},{4,0},{5,1},{6,2},{7,3},{8,12},{9,13},{10,... | collective-permute-start | bytes 196616 | tf_op jit(solution)/shard_map/ppermute | solution.py:317
  246.7 6.2 %collective-permute-start.33 = (f32[128,128]{1,0:T(8,128)S(1)}, f32[128,128]{1,0:T(8,128)S(1)}, u32[]{:S(2)}, u32[]{:S(2)}) collective-permute-start(f32[128,128]{1,0:T(8,128)S(1)} %add_add_fusion.1), channel_id=1, source_target_pairs={{0,6},{1,7},{2,4},{3,5},{4,2},{5,3},{6,0},{7,1},{8,14},{9,15},{10,... | collective-permute-start | bytes 196616 | tf_op jit(solution)/shard_map/ppermute | solution.py:317
  266.1 10.1 %collective-permute-start.37 = (f32[128,128]{1,0:T(8,128)S(1)}, f32[128,128]{1,0:T(8,128)S(1)}, u32[]{:S(2)}, u32[]{:S(2)}) collective-permute-start(f32[128,128]{1,0:T(8,128)S(1)} %get-tuple-element.222), channel_id=1, source_target_pairs={{0,8},{8,0},{16,24},{24,16},{1,9},{9,1},{17,25},{25,17},{2,10},{10... | collective-permute-start | bytes 196616 | tf_op jit(solution)/shard_map/ppermute | solution.py:330
  273.8 5.5 %collective-permute-start.38 = (f32[128,128]{1,0:T(8,128)S(1)}, f32[128,128]{1,0:T(8,128)S(1)}, u32[]{:S(2)}, u32[]{:S(2)}) collective-permute-start(f32[128,128]{1,0:T(8,128)S(1)} %get-tuple-element.224), channel_id=1, source_target_pairs={{0,16},{8,24},{16,0},{24,8},{1,17},{9,25},{17,1},{25,9},{2,18},{10... | collective-permute-start | bytes 196616 | tf_op jit(solution)/shard_map/ppermute | solution.py:330
  273.8 5.5 %collective-permute-start.39 = (f32[128,128]{1,0:T(8,128)S(1)}, f32[128,128]{1,0:T(8,128)S(1)}, u32[]{:S(2)}, u32[]{:S(2)}) collective-permute-start(f32[128,128]{1,0:T(8,128)S(1)} %get-tuple-element.223), channel_id=1, source_target_pairs={{0,24},{8,16},{16,8},{24,0},{1,25},{9,17},{17,9},{25,1},{2,26},{10... | collective-permute-start | bytes 196616 | tf_op jit(solution)/shard_map/ppermute | solution.py:330
  280.1 14.5 %collective-permute-start.43 = (f32[512,128]{1,0:T(8,128)S(1)}, f32[512,128]{1,0:T(8,128)S(1)}, u32[]{:S(2)}, u32[]{:S(2)}) collective-permute-start(f32[512,128]{1,0:T(8,128)S(1)} %pad_maximum_fusion.4.refs_0_), channel_id=1, source_target_pairs={{8,0},{9,1},{10,2},{11,3},{12,4},{13,5},{14,6},{15,7}} | collective-permute-start | bytes 786440 | tf_op jit(solution)/shard_map/ppermute | solution.py:399
  281.4 14.2 %collective-permute-start.44 = (f32[512,128]{1,0:T(8,128)S(1)}, f32[512,128]{1,0:T(8,128)S(1)}, u32[]{:S(2)}, u32[]{:S(2)}) collective-permute-start(f32[512,128]{1,0:T(8,128)S(1)} %pad_maximum_fusion.4.refs_0_), channel_id=1, source_target_pairs={{16,0},{17,1},{18,2},{19,3},{20,4},{21,5},{22,6},{23,7}} | collective-permute-start | bytes 786440 | tf_op jit(solution)/shard_map/ppermute | solution.py:399
  282.7 12.9 %collective-permute-start.45 = (f32[512,128]{1,0:T(8,128)S(1)}, f32[512,128]{1,0:T(8,128)S(1)}, u32[]{:S(2)}, u32[]{:S(2)}) collective-permute-start(f32[512,128]{1,0:T(8,128)S(1)} %pad_maximum_fusion.4.refs_0_), channel_id=1, source_target_pairs={{24,0},{25,1},{26,2},{27,3},{28,4},{29,5},{30,6},{31,7}} | collective-permute-start | bytes 786440 | tf_op jit(solution)/shard_map/ppermute | solution.py:399
  284.2 4.3 %collective-permute-start.40 = (f32[128,128]{1,0:T(8,128)S(1)}, f32[128,128]{1,0:T(8,128)S(1)}, u32[]{:S(2)}, u32[]{:S(2)}) collective-permute-start(f32[128,128]{1,0:T(8,128)S(1)} %bitcast_subtract_fusion.1), channel_id=1, source_target_pairs={{0,2},{1,3},{2,0},{3,1},{4,6},{5,7},{6,4},{7,5},{8,10},{9,11},{10,... | collective-permute-start | bytes 196616 | tf_op jit(solution)/shard_map/ppermute | solution.py:317
  285.2 6.7 %collective-permute-start.41 = (f32[128,128]{1,0:T(8,128)S(1)}, f32[128,128]{1,0:T(8,128)S(1)}, u32[]{:S(2)}, u32[]{:S(2)}) collective-permute-start(f32[128,128]{1,0:T(8,128)S(1)} %bitcast_subtract_fusion.1), channel_id=1, source_target_pairs={{0,4},{1,5},{2,6},{3,7},{4,0},{5,1},{6,2},{7,3},{8,12},{9,13},{10,... | collective-permute-start | bytes 196616 | tf_op jit(solution)/shard_map/ppermute | solution.py:317
  288.6 6.1 %collective-permute-start.42 = (f32[128,128]{1,0:T(8,128)S(1)}, f32[128,128]{1,0:T(8,128)S(1)}, u32[]{:S(2)}, u32[]{:S(2)}) collective-permute-start(f32[128,128]{1,0:T(8,128)S(1)} %bitcast_subtract_fusion.1), channel_id=1, source_target_pairs={{0,6},{1,7},{2,4},{3,5},{4,2},{5,3},{6,0},{7,1},{8,14},{9,15},{10,... | collective-permute-start | bytes 196616 | tf_op jit(solution)/shard_map/ppermute | solution.py:317
  301.7 11.1 %collective-permute-start.48 = (f32[128,128]{1,0:T(8,128)S(1)}, f32[128,128]{1,0:T(8,128)S(1)}, u32[]{:S(2)}, u32[]{:S(2)}) collective-permute-start(f32[128,128]{1,0:T(8,128)S(1)} %get-tuple-element.219), channel_id=1, source_target_pairs={{0,8},{8,0},{16,24},{24,16},{1,9},{9,1},{17,25},{25,17},{2,10},{10... | collective-permute-start | bytes 196616 | tf_op jit(solution)/shard_map/ppermute | solution.py:330
  302.3 10.5 %collective-permute-start.49 = (f32[128,128]{1,0:T(8,128)S(1)}, f32[128,128]{1,0:T(8,128)S(1)}, u32[]{:S(2)}, u32[]{:S(2)}) collective-permute-start(f32[128,128]{1,0:T(8,128)S(1)} %get-tuple-element.221), channel_id=1, source_target_pairs={{0,16},{8,24},{16,0},{24,8},{1,17},{9,25},{17,1},{25,9},{2,18},{10... | collective-permute-start | bytes 196616 | tf_op jit(solution)/shard_map/ppermute | solution.py:330
  305.0 7.8 %collective-permute-start.50 = (f32[128,128]{1,0:T(8,128)S(1)}, f32[128,128]{1,0:T(8,128)S(1)}, u32[]{:S(2)}, u32[]{:S(2)}) collective-permute-start(f32[128,128]{1,0:T(8,128)S(1)} %get-tuple-element.220), channel_id=1, source_target_pairs={{0,24},{8,16},{16,8},{24,0},{1,25},{9,17},{17,9},{25,1},{2,26},{10... | collective-permute-start | bytes 196616 | tf_op jit(solution)/shard_map/ppermute | solution.py:330
  312.9 4.8 %collective-permute-start.51 = (f32[128,128]{1,0:T(8,128)S(1)}, f32[128,128]{1,0:T(8,128)S(1)}, u32[]{:S(2)}, u32[]{:S(2)}) collective-permute-start(f32[128,128]{1,0:T(8,128)S(1)} %add_add_fusion), channel_id=1, source_target_pairs={{0,2},{1,3},{2,0},{3,1},{4,6},{5,7},{6,4},{7,5},{8,10},{9,11},{10,... | collective-permute-start | bytes 196616 | tf_op jit(solution)/shard_map/ppermute | solution.py:317
  313.8 6.7 %collective-permute-start.52 = (f32[128,128]{1,0:T(8,128)S(1)}, f32[128,128]{1,0:T(8,128)S(1)}, u32[]{:S(2)}, u32[]{:S(2)}) collective-permute-start(f32[128,128]{1,0:T(8,128)S(1)} %add_add_fusion), channel_id=1, source_target_pairs={{0,4},{1,5},{2,6},{3,7},{4,0},{5,1},{6,2},{7,3},{8,12},{9,13},{10,... | collective-permute-start | bytes 196616 | tf_op jit(solution)/shard_map/ppermute | solution.py:317
  315.4 6.1 %collective-permute-start.53 = (f32[128,128]{1,0:T(8,128)S(1)}, f32[128,128]{1,0:T(8,128)S(1)}, u32[]{:S(2)}, u32[]{:S(2)}) collective-permute-start(f32[128,128]{1,0:T(8,128)S(1)} %add_add_fusion), channel_id=1, source_target_pairs={{0,6},{1,7},{2,4},{3,5},{4,2},{5,3},{6,0},{7,1},{8,14},{9,15},{10,... | collective-permute-start | bytes 196616 | tf_op jit(solution)/shard_map/ppermute | solution.py:317
  326.6 4.6 %collective-permute-start.55 = (f32[128,128]{1,0:T(8,128)S(1)}, f32[128,128]{1,0:T(8,128)S(1)}, u32[]{:S(2)}, u32[]{:S(2)}) collective-permute-start(f32[128,128]{1,0:T(8,128)S(1)} %get-tuple-element.216), channel_id=1, source_target_pairs={{0,8},{8,0},{16,24},{24,16},{1,9},{9,1},{17,25},{25,17},{2,10},{10... | collective-permute-start | bytes 196616 | tf_op jit(solution)/shard_map/ppermute | solution.py:330
  326.7 5.7 %collective-permute-start.56 = (f32[128,128]{1,0:T(8,128)S(1)}, f32[128,128]{1,0:T(8,128)S(1)}, u32[]{:S(2)}, u32[]{:S(2)}) collective-permute-start(f32[128,128]{1,0:T(8,128)S(1)} %get-tuple-element.218), channel_id=1, source_target_pairs={{0,16},{8,24},{16,0},{24,8},{1,17},{9,25},{17,1},{25,9},{2,18},{10... | collective-permute-start | bytes 196616 | tf_op jit(solution)/shard_map/ppermute | solution.py:330
  327.2 5.2 %collective-permute-start.57 = (f32[128,128]{1,0:T(8,128)S(1)}, f32[128,128]{1,0:T(8,128)S(1)}, u32[]{:S(2)}, u32[]{:S(2)}) collective-permute-start(f32[128,128]{1,0:T(8,128)S(1)} %get-tuple-element.217), channel_id=1, source_target_pairs={{0,24},{8,16},{16,8},{24,0},{1,25},{9,17},{17,9},{25,1},{2,26},{10... | collective-permute-start | bytes 196616 | tf_op jit(solution)/shard_map/ppermute | solution.py:330
  333.3 8.0 %collective-permute-start.58 = (f32[128,128]{1,0:T(8,128)S(1)}, f32[128,128]{1,0:T(8,128)S(1)}, u32[]{:S(2)}, u32[]{:S(2)}) collective-permute-start(f32[128,128]{1,0:T(8,128)S(1)} %bitcast_subtract_fusion.2), channel_id=1, source_target_pairs={{0,2},{1,3},{2,0},{3,1},{4,6},{5,7},{6,4},{7,5},{8,10},{9,11},{10,... | collective-permute-start | bytes 196616 | tf_op jit(solution)/shard_map/ppermute | solution.py:317
  334.3 6.9 %collective-permute-start.59 = (f32[128,128]{1,0:T(8,128)S(1)}, f32[128,128]{1,0:T(8,128)S(1)}, u32[]{:S(2)}, u32[]{:S(2)}) collective-permute-start(f32[128,128]{1,0:T(8,128)S(1)} %bitcast_subtract_fusion.2), channel_id=1, source_target_pairs={{0,4},{1,5},{2,6},{3,7},{4,0},{5,1},{6,2},{7,3},{8,12},{9,13},{10,... | collective-permute-start | bytes 196616 | tf_op jit(solution)/shard_map/ppermute | solution.py:317
  335.9 6.2 %collective-permute-start.60 = (f32[128,128]{1,0:T(8,128)S(1)}, f32[128,128]{1,0:T(8,128)S(1)}, u32[]{:S(2)}, u32[]{:S(2)}) collective-permute-start(f32[128,128]{1,0:T(8,128)S(1)} %bitcast_subtract_fusion.2), channel_id=1, source_target_pairs={{0,6},{1,7},{2,4},{3,5},{4,2},{5,3},{6,0},{7,1},{8,14},{9,15},{10,... | collective-permute-start | bytes 196616 | tf_op jit(solution)/shard_map/ppermute | solution.py:317
  337.7 5.7 %collective-permute-start.61 = (f32[2,128,128]{2,1,0:T(8,128)S(1)}, f32[2,128,128]{2,1,0:T(8,128)S(1)}, u32[]{:S(2)}, u32[]{:S(2)}) collective-permute-start(f32[2,128,128]{2,1,0:T(8,128)S(1)} %pad_maximum_fusion.8), channel_id=1, source_target_pairs={{0,8},{8,0},{16,24},{24,16},{1,9},{9,1},{17,25},{25,17},{2,10},{10... | collective-permute-start | bytes 393224 | tf_op jit(solution)/shard_map/ppermute | solution.py:334
  339.5 5.5 %collective-permute-start.62 = (f32[2,128,128]{2,1,0:T(8,128)S(1)}, f32[2,128,128]{2,1,0:T(8,128)S(1)}, u32[]{:S(2)}, u32[]{:S(2)}) collective-permute-start(f32[2,128,128]{2,1,0:T(8,128)S(1)} %pad_maximum_fusion.8), channel_id=1, source_target_pairs={{0,16},{8,24},{16,0},{24,8},{1,17},{9,25},{17,1},{25,9},{2,18},{10... | collective-permute-start | bytes 393224 | tf_op jit(solution)/shard_map/ppermute | solution.py:334
  341.3 5.9 %collective-permute-start.63 = (f32[2,128,128]{2,1,0:T(8,128)S(1)}, f32[2,128,128]{2,1,0:T(8,128)S(1)}, u32[]{:S(2)}, u32[]{:S(2)}) collective-permute-start(f32[2,128,128]{2,1,0:T(8,128)S(1)} %pad_maximum_fusion.8), channel_id=1, source_target_pairs={{0,24},{8,16},{16,8},{24,0},{1,25},{9,17},{17,9},{25,1},{2,26},{10... | collective-permute-start | bytes 393224 | tf_op jit(solution)/shard_map/ppermute | solution.py:334
  350.7 4.6 %collective-permute-start.65 = (f32[128,128]{1,0:T(8,128)S(1)}, f32[128,128]{1,0:T(8,128)S(1)}, u32[]{:S(2)}, u32[]{:S(2)}) collective-permute-start(f32[128,128]{1,0:T(8,128)S(1)} %get-tuple-element.213), channel_id=1, source_target_pairs={{0,8},{8,0},{16,24},{24,16},{1,9},{9,1},{17,25},{25,17},{2,10},{10... | collective-permute-start | bytes 196616 | tf_op jit(solution)/shard_map/ppermute | solution.py:330
  350.8 5.0 %collective-permute-start.66 = (f32[128,128]{1,0:T(8,128)S(1)}, f32[128,128]{1,0:T(8,128)S(1)}, u32[]{:S(2)}, u32[]{:S(2)}) collective-permute-start(f32[128,128]{1,0:T(8,128)S(1)} %get-tuple-element.215), channel_id=1, source_target_pairs={{0,16},{8,24},{16,0},{24,8},{1,17},{9,25},{17,1},{25,9},{2,18},{10... | collective-permute-start | bytes 196616 | tf_op jit(solution)/shard_map/ppermute | solution.py:330
  351.3 5.2 %collective-permute-start.67 = (f32[128,128]{1,0:T(8,128)S(1)}, f32[128,128]{1,0:T(8,128)S(1)}, u32[]{:S(2)}, u32[]{:S(2)}) collective-permute-start(f32[128,128]{1,0:T(8,128)S(1)} %get-tuple-element.214), channel_id=1, source_target_pairs={{0,24},{8,16},{16,8},{24,0},{1,25},{9,17},{17,9},{25,1},{2,26},{10... | collective-permute-start | bytes 196616 | tf_op jit(solution)/shard_map/ppermute | solution.py:330
  356.5 4.6 %collective-permute-start.68 = (f32[1,128,128]{2,1,0:T(8,128)S(1)}, f32[1,128,128]{2,1,0:T(8,128)S(1)}, u32[]{:S(2)}, u32[]{:S(2)}) collective-permute-start(f32[1,128,128]{2,1,0:T(8,128)S(1)} %add_bitcast_fusion), channel_id=1, source_target_pairs={{0,8},{8,0},{16,24},{24,16},{1,9},{9,1},{17,25},{25,17},{2,10},{10... | collective-permute-start | bytes 196616 | tf_op jit(solution)/shard_map/ppermute | solution.py:334
  358.5 4.6 %collective-permute-start.69 = (f32[1,128,128]{2,1,0:T(8,128)S(1)}, f32[1,128,128]{2,1,0:T(8,128)S(1)}, u32[]{:S(2)}, u32[]{:S(2)}) collective-permute-start(f32[1,128,128]{2,1,0:T(8,128)S(1)} %add_bitcast_fusion), channel_id=1, source_target_pairs={{0,16},{8,24},{16,0},{24,8},{1,17},{9,25},{17,1},{25,9},{2,18},{10... | collective-permute-start | bytes 196616 | tf_op jit(solution)/shard_map/ppermute | solution.py:334
  360.1 5.2 %collective-permute-start.70 = (f32[1,128,128]{2,1,0:T(8,128)S(1)}, f32[1,128,128]{2,1,0:T(8,128)S(1)}, u32[]{:S(2)}, u32[]{:S(2)}) collective-permute-start(f32[1,128,128]{2,1,0:T(8,128)S(1)} %add_bitcast_fusion), channel_id=1, source_target_pairs={{0,24},{8,16},{16,8},{24,0},{1,25},{9,17},{17,9},{25,1},{2,26},{10... | collective-permute-start | bytes 196616 | tf_op jit(solution)/shard_map/ppermute | solution.py:334
  (27 other events, 346.1 us)
where the time goes:
time: 370 us; the launch traced here: 366 us
  waiting for transfers between devices  144 us (39%)
  starting transfers between devices  104 us (28%)
  Pallas kernels  84 us (23%)
  other arithmetic  13 us (4%)
  matrix products  12.1 us (3%)
  local copies, waits for them, and re-layouts  8.35 us (2%)
    pallas_call x10, Pallas kernels, call(): pl.pallas_call(kernel, out_shape=[jax.ShapeDtypeStruct(shape, F32)] * cou...  67.1 us
    ppermute x18, waiting for transfers between devices, sum_parts(): result = result + lax.ppermute(sent, 'lag', pairs(groups, mask))  62.2 us
    ppermute x18, starting transfers between devices, sum_parts(): result = result + lax.ppermute(sent, 'lag', pairs(groups, mask))  27.5 us
    ppermute x15, waiting for transfers between devices, gather_near(): lax.ppermute(value, 'row', pairs(devices, 2 * k))  24.6 us
    ppermute x6, waiting for transfers between devices, along(): lax.ppermute(value, 'row', [(2 * i + c, 2 * (i + step) + c) for i in sour...  23.4 us
    ppermute x15, starting transfers between devices, gather_near(): lax.ppermute(value, 'row', pairs(devices, 2 * k))  19.3 us
    pallas_call x2, Pallas kernels, columns(): pl.pallas_call(columns_kernel, out_shape=[shape(meet)] * (groups - 1) + [...  12.9 us
    ppermute x6, starting transfers between devices, along(): lax.ppermute(value, 'row', [(2 * i + c, 2 * (i + step) + c) for i in sour...  12.7 us
  transfers between devices with their start and end apart: 71, of which 42 were waited for; matrix products, arithmetic and copies ran while one was open for 4% of the time, Pallas kernels for 19%

commit v1 on v0

--- a/solution.py
+++ b/solution.py
@@ -7,7 +7,6 @@
 
 
 STEPS = 3
-HIGHEST = lax.Precision.HIGHEST
 F32 = jnp.float32
 BF16 = jnp.bfloat16
 
@@ -34,22 +33,28 @@
     return jnp.concatenate([jnp.where(core == 0, near, far), jnp.where(core == 0, far, near)], axis=0)
 
 
-def chip_kernel(where, weights, near, far, *refs):
+def chip_kernel(where, weights, *refs):
     outs, high, low = refs[-STEPS - 2 : -2], *refs[-2:]
-    totals = refs[:-STEPS - 2]
-    at = pl.program_id(0)
-    lags, rows, width = near.shape
+    pieces = refs[: len(refs) - STEPS - 2]
+    totals = pieces[len(pieces) - STEPS :] if len(pieces) % 2 else []
+    number, at = pl.program_id(0), pl.program_id(1)
+    lags, rows, width = pieces[0].shape
     core = where[0]
 
-    @pl.when(at == 0)
+    @pl.when(jnp.logical_and(number == 0, at == 0))
     def _():
         for n, out in enumerate(outs):
             out[...] = totals[n][...] if totals else jnp.zeros_like(out)
-        for k in range(lags):
-            columns = slice((lags - 1 - k) * width, (lags - k) * width)
-            for piece, side in ((near, core), (far, 1 - core)):
-                here = pl.ds(pl.multiple_of(side * rows, rows), rows)
-                high[here, columns], low[here, columns] = split(piece[k])
+
+    for i in range(len(pieces) // 2 - (1 if totals else 0)):
+
+        @pl.when(jnp.logical_and(number == i, at == 0))
+        def _():
+            for k in range(lags):
+                columns = slice((lags - 1 - k) * width, (lags - k) * width)
+                for piece, side in ((pieces[2 * i], core), (pieces[2 * i + 1], 1 - core)):
+                    here = pl.ds(pl.multiple_of(side * rows, rows), rows)
+                    high[here, columns], low[here, columns] = split(piece[k])
 
     for k in range(STEPS):
 
@@ -65,11 +70,12 @@
                 outs[n][...] += result[:, n * width : (n + 1) * width]
 
 
-def first_kernel(where, weights, near, far, total, out):
+def first_kernel(where, weights, near, far, total, out, tail):
     @pl.when(pl.program_id(0) == 0)
     def _():
         out[...] = total[...]
 
+    tail[...] = near[...]
     out[...] += product(weights[0], [ordered(where[0], near[0], far[0])])
 
 
@@ -90,25 +96,43 @@
         two_out[...] += result[:, width:]
 
 
-def entered_kernel(where, weights, near, far, one, two, one_out, two_out):
-    at = pl.program_id(0)
-    width = near.shape[-1]
-    last = ordered(where[0], near[1], far[1])
-
-    @pl.when(at == 0)
+def entered_kernel(where, weights, *refs):
+    pieces, (one, two, one_out, two_out, high, low) = refs[:-6], refs[-6:]
+    number, at = pl.program_id(0), pl.program_id(1)
+    before, rows, width = pieces[0].shape
+
+    @pl.when(jnp.logical_and(number == 0, at == 0))
     def _():
         one_out[...] = one[...]
         two_out[...] = two[...]
 
-    @pl.when(jnp.logical_and(where[1] > 0, at == 0))
-    def _():
-        result = product(weights[0], [last, ordered(where[0], near[0], far[0])])
-        one_out[...] += result[:, :width]
-        two_out[...] += result[:, width:]
-
-    @pl.when(jnp.logical_and(where[1] > 0, at == 1))
-    def _():
-        two_out[...] += product(weights[0], [last])
+    for i in range(len(pieces) // 2):
+
+        @pl.when(jnp.logical_and(number == i, at == 0))
+        def _():
+            for k in range(before):
+                columns = slice((before - 1 - k) * width, (before - k) * width)
+                for piece, side in ((pieces[2 * i], where[0]), (pieces[2 * i + 1], 1 - where[0])):
+                    here = pl.ds(pl.multiple_of(side * rows, rows), rows)
+                    high[here, columns], low[here, columns] = split(piece[k])
+
+    for k in range(before):
+
+        @pl.when(jnp.logical_and(where[1] > 0, at == k))
+        def _():
+            size = (before - k) * width
+            wh, wl = split(weights[0])
+            h = high[:, :size]
+            main = dot(wh, jnp.concatenate([h, low[:, :size]], axis=1))
+            result = main[:, :size] + main[:, size:] + dot(wl, h)
+            if k == 0:
+                one_out[...] += result[:, :width]
+            two_out[...] += result[:, size - width :]
+
+
+def multiply_kernel(where, matrix, near, far, total, out):
+    vector = jnp.concatenate([near[...], far[...]], axis=0)
+    out[...] = total[...] + product(matrix[...], [vector])
 
 
 def second_kernel(where, weights, *refs):
@@ -233,20 +257,32 @@
     def lag_spec(shift):
         return pl.BlockSpec((1, rows, width), lambda k, w: (jnp.maximum(k + shift, 0), 0, 0))
 
-    def add_chip(totals, near, far, stage):
+    def add_chip(totals, pieces, stage):
+        count = len(pieces) // 2
         return call(
-            chip_kernel, where, (lags,), (lag_weights, near, far, *totals),
-            [weight_spec(stage)] + [all_of(v.shape) for v in (near, far, *totals)], STEPS, square,
-            (18 * lags * tile * width, 4 * lags * tile), {4 + n: n for n in range(len(totals))},
+            chip_kernel, where, (count, lags), (lag_weights, *pieces, *totals),
+            [pl.BlockSpec((1, rows, 2 * rows), lambda i, k, w: (k, 0, w[2 + stage + i]))]
+            + [all_of(v.shape) for v in (*pieces, *totals)], STEPS, square,
+            (18 * count * lags * tile * width, 4 * count * lags * tile), {2 + len(pieces) + n: n for n in range(len(totals))},
             [pltpu.VMEM((2 * rows, lags * width), BF16)] * 2,
         )
 
     def add_first(total, near, far, stage):
-        return call(
-            first_kernel, where, (lags,), (lag_weights, near, far, total),
-            [weight_spec(stage), lag_spec(0), lag_spec(0), all_of(square)], 1, square,
-            (6 * lags * tile * width, 4 * lags * tile), {4: 0},
-        )[0]
+        before = STEPS - 1
+        return pl.pallas_call(
+            first_kernel,
+            out_shape=[jax.ShapeDtypeStruct(square, F32), jax.ShapeDtypeStruct((before, *square), F32)],
+            grid_spec=pltpu.PrefetchScalarGridSpec(
+                num_scalar_prefetch=1,
+                grid=(lags,),
+                in_specs=[weight_spec(stage), lag_spec(0), lag_spec(0), all_of(square)],
+                out_specs=[all_of(square), pl.BlockSpec((1, *square), lambda k, w: (jnp.maximum(k + before - lags, 0), 0, 0))],
+            ),
+            input_output_aliases={4: 0},
+            cost_estimate=pl.CostEstimate(flops=6 * lags * tile * width, bytes_accessed=4 * lags * tile, transcendentals=0),
+            compiler_params=pltpu.CompilerParams(dimension_semantics=("arbitrary",)),
+            name="first",
+        )(where, lag_weights, near, far, total)
 
     def add_rest(one, two, near, far, stage):
         return call(
@@ -255,13 +291,14 @@
             2, square, (12 * lags * tile * width, 4 * lags * tile), {6: 0, 7: 1},
         )
 
-    def add_entered(one, two, near, stage):
-        far = other_core(near)
-        spec = pl.BlockSpec((1, rows, 2 * rows), lambda k, w: (jnp.where(w[1] > 0, k, 0), 0, w[2 + stage]))
+    def add_entered(one, two, nears, stage):
+        pieces = [v for near in nears for v in (near, other_core(near))]
+        spec = pl.BlockSpec((1, rows, 2 * rows), lambda i, k, w: (jnp.where(w[1] > 0, k, 0), 0, jnp.where(w[1] > 0, w[2 + stage + i], 0)))
         return call(
-            entered_kernel, where, (STEPS - 1,), (lag_weights, near, far, one, two),
-            [spec, all_of(near.shape), all_of(near.shape), all_of(square), all_of(square)],
-            2, square, (18 * tile * width, 8 * tile), {4: 0, 5: 1},
+            entered_kernel, where, (len(nears), STEPS - 1), (lag_weights, *pieces, one, two),
+            [spec] + [all_of(v.shape) for v in (*pieces, one, two)],
+            2, square, (18 * len(nears) * tile * width, 8 * len(nears) * tile), {2 + len(pieces): 0, 3 + len(pieces): 1},
+            [pltpu.VMEM((2 * rows, (STEPS - 1) * width), BF16)] * 2,
         )
 
     def add_second(total, nears, fars):
@@ -317,9 +354,6 @@
         pieces = [value] + [lax.ppermute(value, "row", pairs(devices, 2 * k)) for k in range(1, chips)]
         return jnp.concatenate(pieces, axis=0)
 
-    def gather_far(mine):
-        return jnp.concatenate([mine, other_core(mine)], axis=0)
-
     def own_part(value):
         return lax.dynamic_slice(value, (group * part, 0), (part, value.shape[1]))
 
@@ -340,8 +374,12 @@
     def tails(arrays):
         return {hop: value[lags - (STEPS - 1) :] for hop, value in arrays.items()}
 
-    def multiply(matrix, vector):
-        return jnp.dot(matrix, vector, precision=HIGHEST)
+    def multiply(matrix, mine, total):
+        operands = (matrix, mine, other_core(mine), total)
+        return call(
+            multiply_kernel, where, (1,), operands, [all_of(v.shape) for v in operands],
+            1, square, (6 * rows * meet * width, 4 * rows * meet),
+        )[0]
 
     ups, downs = {1: go_up(history, 1)}, {1: go_down(history, 1)}
     tail = history[lags - (STEPS - 1) :]
@@ -360,60 +398,57 @@
         if stage == 1:
             last_near, entered[0] = tie((last_near, entered[0]))
             sent.append(lax.ppermute(last_near, "lag", [(0, groups - 1)]))
-            totals = add_chip([], history, own_far, 0)
         if stage == chips - 2:
             relayed, near = tie((relayed, near))
             sent.append(lax.ppermute(relayed, "lag", [(groups // 2, groups - 1)]))
-        totals = add_chip(totals, near, other_core(near), stage)
+        pieces = [near, other_core(near)]
+        totals = add_chip([], [history, own_far, *pieces], 0) if stage == 1 else add_chip(totals, pieces, stage)
         if stage == chips - 2:
-            for early in range(chips - 2):
-                entered[early], totals = tie((entered[early], totals))
-                totals = [totals[0], *add_entered(totals[1], totals[2], entered[early], early)]
+            totals = [totals[0], *add_entered(totals[1], totals[2], entered[:1], 0)]
         ups[stage + 1], downs[stage + 1] = next_up, next_down
         ups, downs, totals = tie((ups, downs, totals))
     first, one, two = totals
 
     near = choose(chips - 1, ups, downs)
     far = other_core(near)
-    first = add_first(first, near, far, chips - 1)
+    first, tail = add_first(first, near, far, chips - 1)
+    nothing = jnp.zeros(square, F32)
 
     right_side = own_part(excitation[0]) - sum_parts(first)
-    right_side, ups, downs, near, far, one, two = tie((right_side, ups, downs, near, far, one, two))
+    right_side, tail, near, far, one, two = tie((right_side, tail, near, far, one, two))
     mine = gather_near(right_side)
-    entered.append(enter(choose(chips - 1, tails(ups), tails(downs))))
+    entered.append(enter(tail))
     one, two = add_rest(one, two, near, far, chips - 1)
     mine, one, two, sent = tie((mine, one, two, sent))
-    density = sum_parts(multiply(head_columns, gather_far(mine)))
+    density = sum_parts(multiply(head_columns, mine, nothing))
     first_columns = pick([chunks[0], *sent])
     results = [density]
 
     density, first_columns, entered, one, two = tie((density, first_columns, entered, one, two))
     mine = gather_near(density)
-    for stage in (chips - 2, chips - 1):
-        one, two = add_entered(one, two, entered[stage], stage)
+    one, two = add_entered(one, two, entered[1:], 1)
     mine, one, two = tie((mine, one, two))
-    right_side = own_part(excitation[1]) - sum_parts(one + multiply(first_columns, gather_far(mine)))
+    right_side = own_part(excitation[1]) - sum_parts(multiply(first_columns, mine, one))
 
     right_side, two, old = tie((right_side, two, mine))
     mine = gather_near(right_side)
     nears = [old] + [lax.ppermute(old, "lag", [(j, 0)]) for j in range(1, groups)]
     mine, two, nears = tie((mine, two, nears))
-    spread = gather_far(mine)
+    density = sum_parts(multiply(head_columns, mine, nothing))
     fars = other_core(jnp.stack(nears))
-    spread, fars = tie((spread, fars))
-    density = sum_parts(multiply(head_columns, spread))
+    results.append(density)
+
+    density, two, nears, fars = tie((density, two, nears, fars))
+    mine = gather_near(density)
     two = add_second(two, nears, [fars[j] for j in range(groups)])
-    results.append(density)
-
-    density, two = tie((density, two))
-    mine = gather_near(density)
-    right_side = own_part(excitation[2]) - sum_parts(two + multiply(first_columns, gather_far(mine)))
+    mine, two = tie((mine, two))
+    right_side = own_part(excitation[2]) - sum_parts(multiply(first_columns, mine, two))
 
     right_side, results = tie((right_side, results))
     mine = gather_near(right_side)
     early = whole_rows(jnp.stack(results))
     mine, early = tie((mine, early))
-    density = sum_parts(multiply(head_columns, gather_far(mine)))
+    density = sum_parts(multiply(head_columns, mine, nothing))
     return jnp.concatenate([early, whole_rows(density[None])], axis=0)
 
 

time: 370 us -> 385 us (1.041)
  matrix products: 12.1 us -> 0 us
  Pallas kernels: 84 us -> 94.3 us
  local copies, waits for them, and re-layouts: 8.35 us -> 17 us
  other arithmetic: 13 us -> 17.1 us
    ppermute x18, waiting for transfers between devices: 62.2 us -> 76.3 us  [sum_parts(): result = result + lax.ppermute(sent, 'lag', pairs(groups, mask))]
    dot_general x5 -> x0, matrix products: 12.1 us -> none  [multiply(): return jnp.dot(matrix, vector, precision=HIGHEST)]
    pallas_call x0 -> x1, Pallas kernels: none -> 7.51 us  [add_first(): pl.pallas_call(first_kernel, out_shape=[jax.ShapeDtypeStruct(square, F32)...]
    ppermute x4, starting transfers between devices: 9.23 us -> 15.6 us  [enter(): return lax.ppermute(tail, 'lag', [(i, i + 1) for i in range(groups - 1)])]
    ppermute x4, waiting for transfers between devices: 9.44 us -> 4.4 us  [enter(): return lax.ppermute(tail, 'lag', [(i, i + 1) for i in range(groups - 1)])]
    ppermute x15, waiting for transfers between devices: 24.6 us -> 19.9 us  [gather_near(): lax.ppermute(value, 'row', pairs(devices, 2 * k))]
    ppermute x14, waiting for transfers between devices: 12.1 us -> 7.47 us  [other_core(): return lax.ppermute(value, 'row', pairs(devices, 1))]
    dynamic_slice x6, local copies, waits for them, and re-layouts: 1.19 us -> 5.5 us  [sum_parts(): sent = lax.dynamic_slice(value, ((group ^ mask) * part, 0), (part, width))]
  transfers between devices with their start and end apart: 71 -> 71, of which waited for: 42 -> 39; matrix products, arithmetic and copies ran while one was open for 4% -> 5% of each run, Pallas kernels for 19% -> 20%
where the time goes in v1:
time: 385 us; the launch traced here: 383 us
  waiting for transfers between devices  147 us (38%)
  starting transfers between devices  107 us (28%)
  Pallas kernels  94.3 us (24%)
  other arithmetic  17.1 us (4%)
  local copies, waits for them, and re-layouts  17 us (4%)
    ppermute x18, waiting for transfers between devices, sum_parts(): result = result + lax.ppermute(sent, 'lag', pairs(groups, mask))  76.3 us
    pallas_call x11, Pallas kernels, call(): pl.pallas_call(kernel, out_shape=[jax.ShapeDtypeStruct(shape, F32)] * cou...  69.9 us
    ppermute x18, starting transfers between devices, sum_parts(): result = result + lax.ppermute(sent, 'lag', pairs(groups, mask))  24.4 us
    ppermute x6, waiting for transfers between devices, along(): lax.ppermute(value, 'row', [(2 * i + c, 2 * (i + step) + c) for i in sour...  23.8 us
    ppermute x15, starting transfers between devices, gather_near(): lax.ppermute(value, 'row', pairs(devices, 2 * k))  21.4 us
    ppermute x15, waiting for transfers between devices, gather_near(): lax.ppermute(value, 'row', pairs(devices, 2 * k))  19.9 us
    ppermute x4, starting transfers between devices, enter(): return lax.ppermute(tail, 'lag', [(i, i + 1) for i in range(groups - 1)])  15.6 us
    pallas_call x2, Pallas kernels, columns(): pl.pallas_call(columns_kernel, out_shape=[shape(meet)] * (groups - 1) + [...  13 us
  transfers between devices with their start and end apart: 71, of which 39 were waited for; matrix products, arithmetic and copies ran while one was open for 5% of the time, Pallas kernels for 20%

profile of v1, /device:TPU:0, one launch (start us, length us, event | category | flops | bytes accessed | tf_op | source)
XLA Modules:
  0.0 382.6 jit_solution(1122662954863953576)
XLA Ops:
  0.0 5.9 %collective-permute-start = (f32[4,512,128]{2,1,0:T(8,128)}, f32[4,512,128]{2,1,0:T(8,128)}, u32[]{:S(2)}, u32[]{:S(2)}) collective-permute-start(f32[4,512,128]{2,1,0:T(8,128)} %refs_0_.2), channel_id=1, source_target_pairs={{0,2},{1,3},{2,4},{3,5},{4,6},{5,7},{8,10},{9,11},{10,12},{11,13},... | collective-permute-start | bytes 3145736 | tf_op jit(solution)/shard_map/ppermute | solution.py:222
  8.4 4.2 %collective-permute-start.2 = (f32[2,512,128]{2,1,0:T(8,128)S(1)}, f32[2,512,128]{2,1,0:T(8,128)}, u32[]{:S(2)}, u32[]{:S(2)}) collective-permute-start(f32[2,512,128]{2,1,0:T(8,128)S(1)} %slice_select_fusion.1), channel_id=1, source_target_pairs={{0,8},{8,16},{16,24},{1,9},{9,17},{17,25},{2,10},{10,18},{18,26},{... | collective-permute-start | bytes 1572872 | tf_op jit(solution)/shard_map/ppermute | solution.py:372
  13.5 5.8 %columns.2.matrix = f32[512,1024]{1,0:T(8,128)} custom-call(s32[2,5,4]{2,1,0:T(8,128)} %concatenate.28.where, f32[1,512,4096]{2,1,0:T(8,128)} %bitcast.40, f32[1,512,4096]{2,1,0:T(8,128)} %bitcast.41, f32[1,512,4096]{2,1,0:T(8,128)} %bitcast.42, f32[1,512,4096]{2,1,0:T(8,128)} %bitcast.43), custom_call_target="tpu_custom_call" | custom-call | bytes 16777216 | tf_op jit(solution)/shard_map/columns/pallas_call | solution.py:323
  19.2 4.4 %collective-permute-done.2.refs_0_ = f32[2,512,128]{2,1,0:T(8,128)} collective-permute-done((f32[2,512,128]{2,1,0:T(8,128)S(1)}, f32[2,512,128]{2,1,0:T(8,128)}, u32[]{:S(2)}, u32[]{:S(2)}) %collective-permute-start.2) | collective-permute-done | bytes 524320 | tf_op jit(solution)/shard_map/ppermute | solution.py:372
  23.6 4.1 %collective-permute-done = f32[4,512,128]{2,1,0:T(8,128)} collective-permute-done((f32[4,512,128]{2,1,0:T(8,128)}, f32[4,512,128]{2,1,0:T(8,128)}, u32[]{:S(2)}, u32[]{:S(2)}) %collective-permute-start) | collective-permute-done | bytes 1048608 | tf_op jit(solution)/shard_map/ppermute | solution.py:222
  27.7 5.0 %collective-permute-done.1 = f32[4,512,128]{2,1,0:T(8,128)S(1)} collective-permute-done((f32[4,512,128]{2,1,0:T(8,128)}, f32[4,512,128]{2,1,0:T(8,128)S(1)}, u32[]{:S(2)}, u32[]{:S(2)}) %collective-permute-start.1) | collective-permute-done | bytes 1048608 | tf_op jit(solution)/shard_map/ppermute | solution.py:222
  36.1 7.2 %columns.3 = (f32[512,1024]{1,0:T(8,128)}, f32[512,1024]{1,0:T(8,128)}, f32[512,1024]{1,0:T(8,128)}, f32[512,512]{1,0:T(8,128)}, f32[512,512]{1,0:T(8,128)}) custom-call(s32[2,5,4]{2,1,0:T(8,128)} %concatenate.28.where, f32[4,512,4096]{2,1,0:T(8,128)} %weights.13, f32[4,512,4096]{2,1,0:T(8,128)} %weights.13, f32[4,512,4096]{2,1,0:T(8,128)} %weights.13, ...), custom_call_target="tpu_custom_call" | custom-call | bytes 16777216 | tf_op jit(solution)/shard_map/columns/pallas_call | solution.py:323
  43.3 4.4 %collective-permute-start.9 = (f32[512,512]{1,0:T(8,128)}, f32[512,512]{1,0:T(8,128)}, u32[]{:S(2)}, u32[]{:S(2)}) collective-permute-start(f32[512,512]{1,0:T(8,128)} %get-tuple-element.102), channel_id=1, source_target_pairs={{0,16},{1,17},{2,18},{3,19},{4,20},{5,21},{6,22},{7,23}} | collective-permute-start | bytes 3145736 | tf_op jit(solution)/shard_map/ppermute | solution.py:389
  48.3 16.5 %shard_map.46 = (f32[512,128]{1,0:T(8,128)}, f32[512,128]{1,0:T(8,128)}, f32[512,128]{1,0:T(8,128)}) custom-call(s32[10]{0:T(128)} %stack.91.where, f32[4,512,4096]{2,1,0:T(8,128)} %weights.13, f32[4,512,128]{2,1,0:T(8,128)} %refs_0_.2, f32[4,512,128]{2,1,0:T(8,128)} %copy-done.9, f32[4,512,128]{2,1,0:T(8,128)} %broadcast_select_fusion.refs_2_, ...), custom_call_target="tpu_custom_call" | custom-call | flops 9663676416 | bytes 16777216 | tf_op jit(solution)/shard_map/pallas_call | solution.py:187
  66.4 3.7 collective-permute-done.9
  70.1 1.6 collective-permute-start.7
  73.8 9.9 %shard_map.47 = (f32[512,128]{1,0:T(8,128)}, f32[512,128]{1,0:T(8,128)}, f32[512,128]{1,0:T(8,128)}) custom-call(s32[10]{0:T(128)} %stack.91.where, f32[4,512,4096]{2,1,0:T(8,128)} %weights.13, f32[4,512,128]{2,1,0:T(8,128)} %select_select_fusion.1.refs_0_, ...), custom_call_target="tpu_custom_call", output_to_operand_aliasing={{0}: (4, {}), {1}: (5, {}), {2}: (6, {})} | custom-call | flops 4831838208 | bytes 8388608 | tf_op jit(solution)/shard_map/pallas_call | solution.py:187
  83.7 3.8 shard_map.48
  87.6 14.5 %collective-permute-done.8 = f32[4,512,128]{2,1,0:T(8,128)} collective-permute-done((f32[4,512,128]{2,1,0:T(8,128)S(1)}, f32[4,512,128]{2,1,0:T(8,128)}, u32[]{:S(2)}, u32[]{:S(2)}) %collective-permute-start.8) | collective-permute-done | bytes 1048608 | tf_op jit(solution)/shard_map/ppermute | solution.py:222
  103.6 2.6 collective-permute-start.19
  106.2 5.1 %collective-permute-start.20 = (f32[512,1024]{1,0:T(8,128)}, f32[512,1024]{1,0:T(8,128)}, u32[]{:S(2)}, u32[]{:S(2)}) collective-permute-start(f32[512,1024]{1,0:T(8,128)} %get-tuple-element.132), channel_id=1, source_target_pairs={{0,16},{1,17},{2,18},{3,19},{4,20},{5,21},{6,22},{7,23}} | collective-permute-start | bytes 6291464 | tf_op jit(solution)/shard_map/ppermute | solution.py:390
  112.3 7.5 %first.1 = (f32[512,128]{1,0:T(8,128)}, f32[2,512,128]{2,1,0:T(8,128)}) custom-call(s32[10]{0:T(128)} %stack.91.where, f32[4,512,4096]{2,1,0:T(8,128)} %weights.13, f32[4,512,128]{2,1,0:T(8,128)} %copy-done, f32[4,512,128]{2,1,0:T(8,128)} %copy-done.1, f32[512,128]{1,0:T(8,128)} %get-tuple-element.119.total), custom_call_target="tpu_custom_call", output_to_operand_aliasing={{0}: (4, {})} | custom-call | flops 1610612736 | bytes 8388608 | tf_op jit(solution)/shard_map/first/pallas_call | solution.py:272
  120.9 6.3 %collective-permute-start.21 = (f32[512,512]{1,0:T(8,128)}, f32[512,512]{1,0:T(8,128)}, u32[]{:S(2)}, u32[]{:S(2)}) collective-permute-start(f32[512,512]{1,0:T(8,128)} %get-tuple-element.133), channel_id=1, source_target_pairs={{0,24},{1,25},{2,26},{3,27},{4,28},{5,29},{6,30},{7,31}} | collective-permute-start | bytes 3145736 | tf_op jit(solution)/shard_map/ppermute | solution.py:400
  127.2 25.3 %collective-permute-done.13 = f32[128,128]{1,0:T(8,128)S(1)} collective-permute-done((f32[128,128]{1,0:T(8,128)S(1)}, f32[128,128]{1,0:T(8,128)S(1)}, u32[]{:S(2)}, u32[]{:S(2)}) %collective-permute-start.13) | collective-permute-done | bytes 65568 | tf_op jit(solution)/shard_map/ppermute | solution.py:364
  152.5 1.6 collective-permute-start.22
  154.2 2.9 collective-permute-done.14
  157.1 2.0 fusion
  159.1 17.1 %collective-permute-done.15 = f32[128,128]{1,0:T(8,128)S(1)} collective-permute-done((f32[128,128]{1,0:T(8,128)S(1)}, f32[128,128]{1,0:T(8,128)S(1)}, u32[]{:S(2)}, u32[]{:S(2)}) %collective-permute-start.15) | collective-permute-done | bytes 65568 | tf_op jit(solution)/shard_map/ppermute | solution.py:364
  177.1 4.3 %collective-permute-done.16 = f32[128,128]{1,0:T(8,128)S(1)} collective-permute-done((f32[128,128]{1,0:T(8,128)S(1)}, f32[128,128]{1,0:T(8,128)S(1)}, u32[]{:S(2)}, u32[]{:S(2)}) %collective-permute-start.16) | collective-permute-done | bytes 65568 | tf_op jit(solution)/shard_map/ppermute | solution.py:354
  181.4 1.9 slice_select_fusion
  183.3 3.6 collective-permute-done.17
  188.2 7.6 %shard_map.49 = (f32[512,128]{1,0:T(8,128)}, f32[512,128]{1,0:T(8,128)}) custom-call(s32[10]{0:T(128)} %stack.91.where, f32[4,512,4096]{2,1,0:T(8,128)} %weights.13, f32[4,512,128]{2,1,0:T(8,128)} %copy-done, f32[4,512,128]{2,1,0:T(8,128)} %copy-done, f32[4,512,128]{2,1,0:T(8,128)} %copy-done.1, ...), custom_call_target="tpu_custom_call", output_to_operand_aliasing={{0}: (6, {}), {1}: (7, {})} | custom-call | flops 3221225472 | bytes 8388608 | tf_op jit(solution)/shard_map/pallas_call | solution.py:187
  196.4 2.1 collective-permute-start.27
  201.8 8.0 %collective-permute-start.29 = (f32[2,512,128]{2,1,0:T(8,128)}, f32[2,512,128]{2,1,0:T(8,128)S(1)}, u32[]{:S(2)}, u32[]{:S(2)}) collective-permute-start(f32[2,512,128]{2,1,0:T(8,128)} %get-tuple-element.141), channel_id=1, source_target_pairs={{0,8},{8,16},{16,24},{1,9},{9,17},{17,25},{2,10},{10,18},{18,26},{... | collective-permute-start | bytes 1572872 | tf_op jit(solution)/shard_map/ppermute | solution.py:372
  211.2 3.8 %shard_map.50 = f32[512,128]{1,0:T(8,128)} custom-call(s32[10]{0:T(128)} %stack.91.where, f32[512,1024]{1,0:T(8,128)} %columns.2.matrix, f32[512,128]{1,0:T(8,128)} %copy-done.10, f32[512,128]{1,0:T(8,128)} %copy-done.19, f32[512,128]{1,0:T(8,128)} %broadcast_in_dim.17.total), custom_call_target="tpu_custom_call" | custom-call | flops 402653184 | bytes 2097152 | tf_op jit(solution)/shard_map/pallas_call | solution.py:187
  216.2 16.6 %collective-permute-done.24 = f32[128,128]{1,0:T(8,128)S(1)} collective-permute-done((f32[128,128]{1,0:T(8,128)S(1)}, f32[128,128]{1,0:T(8,128)S(1)}, u32[]{:S(2)}, u32[]{:S(2)}) %collective-permute-start.24) | collective-permute-done | bytes 65568 | tf_op jit(solution)/shard_map/ppermute | solution.py:364
  232.8 5.0 %collective-permute-start.26 = (f32[128,128]{1,0:T(8,128)S(1)}, f32[128,128]{1,0:T(8,128)S(1)}, u32[]{:S(2)}, u32[]{:S(2)}) collective-permute-start(f32[128,128]{1,0:T(8,128)S(1)} %get-tuple-element.206), channel_id=1, source_target_pairs={{0,24},{8,16},{16,8},{24,0},{1,25},{9,17},{17,9},{25,1},{2,26},{10... | collective-permute-start | bytes 196616 | tf_op jit(solution)/shard_map/ppermute | solution.py:364
  237.8 3.9 %pick.1.matrix = f32[512,1024]{1,0:T(8,128)} custom-call(s32[1]{0:T(128)} %bitcast.2.which, f32[512,1024]{1,0:T(8,128)} %get-tuple-element.136.refs_0_, f32[512,1024]{1,0:T(8,128)} %collective-permute-done.19.refs_1_, f32[512,1024]{1,0:T(8,128)} %collective-permute-done.20.refs_2_, f32[512,512]{1,0:T(8,128)} %collective-permute-done.21.refs_3_, ...), custom_call_target="tpu_custom_call" | custom-call | bytes 8388608 | tf_op jit(solution)/shard_map/pick/pallas_call | solution.py:339
  243.3 3.0 collective-permute-start.31
  246.3 2.6 collective-permute-done.30
  248.9 2.5 collective-permute-start.32
  251.4 3.5 collective-permute-done.32
  257.5 5.3 %shard_map.51 = (f32[512,128]{1,0:T(8,128)}, f32[512,128]{1,0:T(8,128)}) custom-call(s32[10]{0:T(128)} %stack.91.where, f32[4,512,4096]{2,1,0:T(8,128)} %weights.13, f32[2,512,128]{2,1,0:T(8,128)} %collective-permute-done.27.refs_0_, f32[2,512,128]{2,1,0:T(8,128)} %copy-done.16, ...), custom_call_target="tpu_custom_call", output_to_operand_aliasing={{0}: (8, {}), {1}: (9, {})} | custom-call | flops 3623878656 | bytes 12582912 | tf_op jit(solution)/shard_map/pallas_call | solution.py:187
  262.8 1.7 collective-permute-done.36.far
  265.3 3.9 %shard_map.52 = f32[512,128]{1,0:T(8,128)} custom-call(s32[10]{0:T(128)} %stack.91.where, f32[512,1024]{1,0:T(8,128)} %pick.1.matrix, f32[512,128]{1,0:T(8,128)} %pad_maximum_fusion.3.near.refs_0_, f32[512,128]{1,0:T(8,128)} %copy-done.22, f32[512,128]{1,0:T(8,128)} %get-tuple-element.154.total), custom_call_target="tpu_custom_call" | custom-call | flops 402653184 | bytes 2097152 | tf_op jit(solution)/shard_map/pallas_call | solution.py:187
  270.1 6.5 %collective-permute-start.37 = (f32[128,128]{1,0:T(8,128)S(1)}, f32[128,128]{1,0:T(8,128)S(1)}, u32[]{:S(2)}, u32[]{:S(2)}) collective-permute-start(f32[128,128]{1,0:T(8,128)S(1)} %get-tuple-element.202), channel_id=1, source_target_pairs={{0,8},{8,0},{16,24},{24,16},{1,9},{9,1},{17,25},{25,17},{2,10},{10... | collective-permute-start | bytes 196616 | tf_op jit(solution)/shard_map/ppermute | solution.py:364
  276.5 1.9 collective-permute-start.38
  278.9 1.9 collective-permute-done.38
  280.8 2.8 collective-permute-done.39
  288.5 3.1 collective-permute-start.41
  292.8 2.5 collective-permute-start.42
  295.3 3.6 collective-permute-done.42
  302.0 2.7 collective-permute-done.46.far
  304.6 3.8 shard_map.53
  309.6 2.7 collective-permute-start.48
  315.3 2.2 collective-permute-done.49
  318.4 3.1 collective-permute-start.52
  323.8 7.6 %shard_map.54.total = f32[512,128]{1,0:T(8,128)} custom-call(s32[10]{0:T(128)} %stack.91.where, f32[4,512,4096]{2,1,0:T(8,128)} %weights.13, f32[512,128]{1,0:T(8,128)} %pad_maximum_fusion.3.near.refs_0_, f32[512,128]{1,0:T(8,128)} %copy-done.6, f32[512,128]{1,0:T(8,128)} %copy-done.7, f32[512,128]{1,0:T(8,128)} %copy-done.8, ...), custom_call_target="tpu_custom_call", output_to_operand_aliasing={{}: (10, {})} | custom-call | flops 1610612736 | bytes 8388608 | tf_op jit(solution)/shard_map/pallas_call | solution.py:187
  333.8 3.8 %shard_map.55 = f32[512,128]{1,0:T(8,128)} custom-call(s32[10]{0:T(128)} %stack.91.where, f32[512,1024]{1,0:T(8,128)} %pick.1.matrix, f32[512,128]{1,0:T(8,128)} %copy-done.13, f32[512,128]{1,0:T(8,128)} %copy-done.21, f32[512,128]{1,0:T(8,128)} %shard_map.54.total), custom_call_target="tpu_custom_call" | custom-call | flops 402653184 | bytes 2097152 | tf_op jit(solution)/shard_map/pallas_call | solution.py:187
  338.7 3.4 collective-permute-start.57
  345.3 3.1 collective-permute-start.59
  349.7 1.8 collective-permute-start.61
  351.5 1.7 collective-permute-start.62
  357.0 2.1 collective-permute-done.63
  361.6 3.8 shard_map.56
  366.9 2.9 collective-permute-start.67
  373.0 2.0 collective-permute-start.68
  377.6 2.0 collective-permute-done.69
  379.6 2.1 collective-permute-done.70
  (181 shorter events, 68.1 us)
Async XLA Ops:
  0.0 27.7 %collective-permute-start = (f32[4,512,128]{2,1,0:T(8,128)}, f32[4,512,128]{2,1,0:T(8,128)}, u32[]{:S(2)}, u32[]{:S(2)}) collective-permute-start(f32[4,512,128]{2,1,0:T(8,128)} %refs_0_.2), channel_id=1, source_target_pairs={{0,2},{1,3},{2,4},{3,5},{4,6},{5,7},{8,10},{9,11},{10,12},{11,13},... | collective-permute-start | bytes 3145736 | tf_op jit(solution)/shard_map/ppermute | solution.py:222
  5.9 26.7 %collective-permute-start.1 = (f32[4,512,128]{2,1,0:T(8,128)}, f32[4,512,128]{2,1,0:T(8,128)S(1)}, u32[]{:S(2)}, u32[]{:S(2)}) collective-permute-start(f32[4,512,128]{2,1,0:T(8,128)} %refs_0_.2), channel_id=1, source_target_pairs={{2,0},{3,1},{4,2},{5,3},{6,4},{7,5},{10,8},{11,9},{12,10},{13,11},... | collective-permute-start | bytes 3145736 | tf_op jit(solution)/shard_map/ppermute | solution.py:222
  7.2 25.4 %collective-permute-start.3 = (f32[4,512,128]{2,1,0:T(8,128)}, f32[4,512,128]{2,1,0:T(8,128)S(1)}, u32[]{:S(2)}, u32[]{:S(2)}) collective-permute-start(f32[4,512,128]{2,1,0:T(8,128)} %refs_0_.2), channel_id=1, source_target_pairs={{0,1},{1,0},{2,3},{3,2},{4,5},{5,4},{6,7},{7,6},{8,9},{9,8},{10,11... | collective-permute-start | bytes 3145736 | tf_op jit(solution)/shard_map/ppermute | solution.py:219
  8.4 15.2 %collective-permute-start.2 = (f32[2,512,128]{2,1,0:T(8,128)S(1)}, f32[2,512,128]{2,1,0:T(8,128)}, u32[]{:S(2)}, u32[]{:S(2)}) collective-permute-start(f32[2,512,128]{2,1,0:T(8,128)S(1)} %slice_select_fusion.1), channel_id=1, source_target_pairs={{0,8},{8,16},{16,24},{1,9},{9,17},{17,25},{2,10},{10,18},{18,26},{... | collective-permute-start | bytes 1572872 | tf_op jit(solution)/shard_map/ppermute | solution.py:372
  34.1 14.2 %collective-permute-start.6 = (f32[4,512,128]{2,1,0:T(8,128)}, f32[4,512,128]{2,1,0:T(8,128)}, u32[]{:S(2)}, u32[]{:S(2)}) collective-permute-start(f32[4,512,128]{2,1,0:T(8,128)} %broadcast_select_fusion.refs_2_), channel_id=1, source_target_pairs={{0,1},{1,0},{2,3},{3,2},{4,5},{5,4},{6,7},{7,6},{8,9},{9,8},{10,11... | collective-permute-start | bytes 3145736 | tf_op jit(solution)/shard_map/ppermute | solution.py:219
  34.1 30.7 %collective-permute-start.4 = (f32[4,512,128]{2,1,0:T(8,128)}, f32[4,512,128]{2,1,0:T(8,128)S(1)}, u32[]{:S(2)}, u32[]{:S(2)}) collective-permute-start(f32[4,512,128]{2,1,0:T(8,128)} %collective-permute-done), channel_id=1, source_target_pairs={{2,4},{3,5},{4,6},{5,7},{10,12},{11,13},{12,14},{13,15},{18,20},{1... | collective-permute-start | bytes 3145736 | tf_op jit(solution)/shard_map/ppermute | solution.py:222
  34.8 30.2 %collective-permute-start.5 = (f32[4,512,128]{2,1,0:T(8,128)S(1)}, f32[4,512,128]{2,1,0:T(8,128)S(1)}, u32[]{:S(2)}, u32[]{:S(2)}) collective-permute-start(f32[4,512,128]{2,1,0:T(8,128)S(1)} %collective-permute-done.1), channel_id=1, source_target_pairs={{2,0},{3,1},{4,2},{5,3},{10,8},{11,9},{12,10},{13,11},{18,16},{19,... | collective-permute-start | bytes 3145736 | tf_op jit(solution)/shard_map/ppermute | solution.py:222
  43.3 26.8 %collective-permute-start.9 = (f32[512,512]{1,0:T(8,128)}, f32[512,512]{1,0:T(8,128)}, u32[]{:S(2)}, u32[]{:S(2)}) collective-permute-start(f32[512,512]{1,0:T(8,128)} %get-tuple-element.102), channel_id=1, source_target_pairs={{0,16},{1,17},{2,18},{3,19},{4,20},{5,21},{6,22},{7,23}} | collective-permute-start | bytes 3145736 | tf_op jit(solution)/shard_map/ppermute | solution.py:389
  70.1 17.4 %collective-permute-start.7 = (f32[4,512,128]{2,1,0:T(8,128)S(1)}, f32[4,512,128]{2,1,0:T(8,128)}, u32[]{:S(2)}, u32[]{:S(2)}) collective-permute-start(f32[4,512,128]{2,1,0:T(8,128)S(1)} %collective-permute-done.4), channel_id=1, source_target_pairs={{4,6},{5,7},{12,14},{13,15},{20,22},{21,23},{28,30},{29,31}} | collective-permute-start | bytes 3145736 | tf_op jit(solution)/shard_map/ppermute | solution.py:222
  71.8 30.3 %collective-permute-start.8 = (f32[4,512,128]{2,1,0:T(8,128)S(1)}, f32[4,512,128]{2,1,0:T(8,128)}, u32[]{:S(2)}, u32[]{:S(2)}) collective-permute-start(f32[4,512,128]{2,1,0:T(8,128)S(1)} %collective-permute-done.5), channel_id=1, source_target_pairs={{2,0},{3,1},{10,8},{11,9},{18,16},{19,17},{26,24},{27,25}} | collective-permute-start | bytes 3145736 | tf_op jit(solution)/shard_map/ppermute | solution.py:222
  73.2 10.5 %collective-permute-start.11 = (f32[2,512,128]{2,1,0:T(8,128)}, f32[2,512,128]{2,1,0:T(8,128)}, u32[]{:S(2)}, u32[]{:S(2)}) collective-permute-start(f32[2,512,128]{2,1,0:T(8,128)} %collective-permute-done.2.refs_0_), channel_id=1, source_target_pairs={{0,1},{1,0},{2,3},{3,2},{4,5},{5,4},{6,7},{7,6},{8,9},{9,8},{10,11... | collective-permute-start | bytes 1572872 | tf_op jit(solution)/shard_map/ppermute | solution.py:219
  103.5 7.8 %collective-permute-start.12 = (f32[4,512,128]{2,1,0:T(8,128)S(1)}, f32[4,512,128]{2,1,0:T(8,128)S(1)}, u32[]{:S(2)}, u32[]{:S(2)}) collective-permute-start(f32[4,512,128]{2,1,0:T(8,128)S(1)} %select_select_fusion.near.near_before), channel_id=1, source_target_pairs={{0,1},{1,0},{2,3},{3,2},{4,5},{5,4},{6,7},{7,6},{8,9},{9,8},{10,11... | collective-permute-start | bytes 3145736 | tf_op jit(solution)/shard_map/ppermute | solution.py:219
  103.6 95.8 %collective-permute-start.19 = (f32[512,1024]{1,0:T(8,128)}, f32[512,1024]{1,0:T(8,128)}, u32[]{:S(2)}, u32[]{:S(2)}) collective-permute-start(f32[512,1024]{1,0:T(8,128)} %get-tuple-element.131), channel_id=1, source_target_pairs={{0,8},{1,9},{2,10},{3,11},{4,12},{5,13},{6,14},{7,15}} | collective-permute-start | bytes 6291464 | tf_op jit(solution)/shard_map/ppermute | solution.py:390
  106.2 93.2 %collective-permute-start.20 = (f32[512,1024]{1,0:T(8,128)}, f32[512,1024]{1,0:T(8,128)}, u32[]{:S(2)}, u32[]{:S(2)}) collective-permute-start(f32[512,1024]{1,0:T(8,128)} %get-tuple-element.132), channel_id=1, source_target_pairs={{0,16},{1,17},{2,18},{3,19},{4,20},{5,21},{6,22},{7,23}} | collective-permute-start | bytes 6291464 | tf_op jit(solution)/shard_map/ppermute | solution.py:390
  120.7 31.8 %collective-permute-start.13 = (f32[128,128]{1,0:T(8,128)S(1)}, f32[128,128]{1,0:T(8,128)S(1)}, u32[]{:S(2)}, u32[]{:S(2)}) collective-permute-start(f32[128,128]{1,0:T(8,128)S(1)} %get-tuple-element.208), channel_id=1, source_target_pairs={{0,8},{8,0},{16,24},{24,16},{1,9},{9,1},{17,25},{25,17},{2,10},{10... | collective-permute-start | bytes 196616 | tf_op jit(solution)/shard_map/ppermute | solution.py:364
  120.8 36.3 %collective-permute-start.14 = (f32[128,128]{1,0:T(8,128)S(1)}, f32[128,128]{1,0:T(8,128)S(1)}, u32[]{:S(2)}, u32[]{:S(2)}) collective-permute-start(f32[128,128]{1,0:T(8,128)S(1)} %get-tuple-element.210), channel_id=1, source_target_pairs={{0,16},{8,24},{16,0},{24,8},{1,17},{9,25},{17,1},{25,9},{2,18},{10... | collective-permute-start | bytes 196616 | tf_op jit(solution)/shard_map/ppermute | solution.py:364
  120.9 78.5 %collective-permute-start.21 = (f32[512,512]{1,0:T(8,128)}, f32[512,512]{1,0:T(8,128)}, u32[]{:S(2)}, u32[]{:S(2)}) collective-permute-start(f32[512,512]{1,0:T(8,128)} %get-tuple-element.133), channel_id=1, source_target_pairs={{0,24},{1,25},{2,26},{3,27},{4,28},{5,29},{6,30},{7,31}} | collective-permute-start | bytes 3145736 | tf_op jit(solution)/shard_map/ppermute | solution.py:400
  152.5 46.9 %collective-permute-start.22 = (f32[512,512]{1,0:T(8,128)}, f32[512,512]{1,0:T(8,128)}, u32[]{:S(2)}, u32[]{:S(2)}) collective-permute-start(f32[512,512]{1,0:T(8,128)} %collective-permute-done.9), channel_id=1, source_target_pairs={{16,24},{17,25},{18,26},{19,27},{20,28},{21,29},{22,30},{23,31}} | collective-permute-start | bytes 3145736 | tf_op jit(solution)/shard_map/ppermute | solution.py:403
  157.1 19.1 %collective-permute-start.15 = (f32[128,128]{1,0:T(8,128)S(1)}, f32[128,128]{1,0:T(8,128)S(1)}, u32[]{:S(2)}, u32[]{:S(2)}) collective-permute-start(f32[128,128]{1,0:T(8,128)S(1)} %get-tuple-element.209), channel_id=1, source_target_pairs={{0,24},{8,16},{16,8},{24,0},{1,25},{9,17},{17,9},{25,1},{2,26},{10... | collective-permute-start | bytes 196616 | tf_op jit(solution)/shard_map/ppermute | solution.py:364
  177.1 4.3 %collective-permute-start.16 = (f32[128,128]{1,0:T(8,128)S(1)}, f32[128,128]{1,0:T(8,128)S(1)}, u32[]{:S(2)}, u32[]{:S(2)}) collective-permute-start(f32[128,128]{1,0:T(8,128)S(1)} %bitcast_subtract_fusion.1), channel_id=1, source_target_pairs={{0,2},{1,3},{2,0},{3,1},{4,6},{5,7},{6,4},{7,5},{8,10},{9,11},{10,... | collective-permute-start | bytes 196616 | tf_op jit(solution)/shard_map/ppermute | solution.py:354
  181.4 5.5 %collective-permute-start.17 = (f32[128,128]{1,0:T(8,128)S(1)}, f32[128,128]{1,0:T(8,128)S(1)}, u32[]{:S(2)}, u32[]{:S(2)}) collective-permute-start(f32[128,128]{1,0:T(8,128)S(1)} %bitcast_subtract_fusion.1), channel_id=1, source_target_pairs={{0,4},{1,5},{2,6},{3,7},{4,0},{5,1},{6,2},{7,3},{8,12},{9,13},{10,... | collective-permute-start | bytes 196616 | tf_op jit(solution)/shard_map/ppermute | solution.py:354
  186.9 8.9 %collective-permute-start.18 = (f32[128,128]{1,0:T(8,128)S(1)}, f32[128,128]{1,0:T(8,128)S(1)}, u32[]{:S(2)}, u32[]{:S(2)}) collective-permute-start(f32[128,128]{1,0:T(8,128)S(1)} %bitcast_subtract_fusion.1), channel_id=1, source_target_pairs={{0,6},{1,7},{2,4},{3,5},{4,2},{5,3},{6,0},{7,1},{8,14},{9,15},{10,... | collective-permute-start | bytes 196616 | tf_op jit(solution)/shard_map/ppermute | solution.py:354
  196.4 46.2 %collective-permute-start.27 = (f32[2,512,128]{2,1,0:T(8,128)}, f32[2,512,128]{2,1,0:T(8,128)}, u32[]{:S(2)}, u32[]{:S(2)}) collective-permute-start(f32[2,512,128]{2,1,0:T(8,128)} %slice_select_fusion), channel_id=1, source_target_pairs={{0,8},{8,16},{16,24},{1,9},{9,17},{17,25},{2,10},{10,18},{18,26},{... | collective-permute-start | bytes 1572872 | tf_op jit(solution)/shard_map/ppermute | solution.py:372
  199.4 10.3 %collective-permute-start.23 = (f32[512,128]{1,0:T(8,128)S(1)}, f32[512,128]{1,0:T(8,128)S(1)}, u32[]{:S(2)}, u32[]{:S(2)}) collective-permute-start(f32[512,128]{1,0:T(8,128)S(1)} %pad_maximum_fusion.2.near), channel_id=1, source_target_pairs={{0,1},{1,0},{2,3},{3,2},{4,5},{5,4},{6,7},{7,6},{8,9},{9,8},{10,11... | collective-permute-start | bytes 786440 | tf_op jit(solution)/shard_map/ppermute | solution.py:219
  200.5 42.1 %collective-permute-start.28 = (f32[2,512,128]{2,1,0:T(8,128)}, f32[2,512,128]{2,1,0:T(8,128)S(1)}, u32[]{:S(2)}, u32[]{:S(2)}) collective-permute-start(f32[2,512,128]{2,1,0:T(8,128)} %select_select_fusion.2), channel_id=1, source_target_pairs={{0,8},{8,16},{16,24},{1,9},{9,17},{17,25},{2,10},{10,18},{18,26},{... | collective-permute-start | bytes 1572872 | tf_op jit(solution)/shard_map/ppermute | solution.py:372
  201.8 40.8 %collective-permute-start.29 = (f32[2,512,128]{2,1,0:T(8,128)}, f32[2,512,128]{2,1,0:T(8,128)S(1)}, u32[]{:S(2)}, u32[]{:S(2)}) collective-permute-start(f32[2,512,128]{2,1,0:T(8,128)} %get-tuple-element.141), channel_id=1, source_target_pairs={{0,8},{8,16},{16,24},{1,9},{9,17},{17,25},{2,10},{10,18},{18,26},{... | collective-permute-start | bytes 1572872 | tf_op jit(solution)/shard_map/ppermute | solution.py:372
  216.0 16.8 %collective-permute-start.24 = (f32[128,128]{1,0:T(8,128)S(1)}, f32[128,128]{1,0:T(8,128)S(1)}, u32[]{:S(2)}, u32[]{:S(2)}) collective-permute-start(f32[128,128]{1,0:T(8,128)S(1)} %get-tuple-element.205), channel_id=1, source_target_pairs={{0,8},{8,0},{16,24},{24,16},{1,9},{9,1},{17,25},{25,17},{2,10},{10... | collective-permute-start | bytes 196616 | tf_op jit(solution)/shard_map/ppermute | solution.py:364
  216.1 25.6 %collective-permute-start.25 = (f32[128,128]{1,0:T(8,128)S(1)}, f32[128,128]{1,0:T(8,128)S(1)}, u32[]{:S(2)}, u32[]{:S(2)}) collective-permute-start(f32[128,128]{1,0:T(8,128)S(1)} %get-tuple-element.207), channel_id=1, source_target_pairs={{0,16},{8,24},{16,0},{24,8},{1,17},{9,25},{17,1},{25,9},{2,18},{10... | collective-permute-start | bytes 196616 | tf_op jit(solution)/shard_map/ppermute | solution.py:364
  232.8 9.0 %collective-permute-start.26 = (f32[128,128]{1,0:T(8,128)S(1)}, f32[128,128]{1,0:T(8,128)S(1)}, u32[]{:S(2)}, u32[]{:S(2)}) collective-permute-start(f32[128,128]{1,0:T(8,128)S(1)} %get-tuple-element.206), channel_id=1, source_target_pairs={{0,24},{8,16},{16,8},{24,0},{1,25},{9,17},{17,9},{25,1},{2,26},{10... | collective-permute-start | bytes 196616 | tf_op jit(solution)/shard_map/ppermute | solution.py:364
  242.7 13.1 %collective-permute-start.33 = (f32[2,512,128]{2,1,0:T(8,128)}, f32[2,512,128]{2,1,0:T(8,128)S(1)}, u32[]{:S(2)}, u32[]{:S(2)}) collective-permute-start(f32[2,512,128]{2,1,0:T(8,128)} %collective-permute-done.27.refs_0_), channel_id=1, source_target_pairs={{0,1},{1,0},{2,3},{3,2},{4,5},{5,4},{6,7},{7,6},{8,9},{9,8},{10,11... | collective-permute-start | bytes 1572872 | tf_op jit(solution)/shard_map/ppermute | solution.py:219
  242.7 13.0 %collective-permute-start.34 = (f32[2,512,128]{2,1,0:T(8,128)S(1)}, f32[2,512,128]{2,1,0:T(8,128)S(1)}, u32[]{:S(2)}, u32[]{:S(2)}) collective-permute-start(f32[2,512,128]{2,1,0:T(8,128)S(1)} %collective-permute-done.28.refs_2_), channel_id=1, source_target_pairs={{0,1},{1,0},{2,3},{3,2},{4,5},{5,4},{6,7},{7,6},{8,9},{9,8},{10,11... | collective-permute-start | bytes 1572872 | tf_op jit(solution)/shard_map/ppermute | solution.py:219
  243.2 12.5 %collective-permute-start.35 = (f32[2,512,128]{2,1,0:T(8,128)S(1)}, f32[2,512,128]{2,1,0:T(8,128)S(1)}, u32[]{:S(2)}, u32[]{:S(2)}) collective-permute-start(f32[2,512,128]{2,1,0:T(8,128)S(1)} %collective-permute-done.29.refs_4_), channel_id=1, source_target_pairs={{0,1},{1,0},{2,3},{3,2},{4,5},{5,4},{6,7},{7,6},{8,9},{9,8},{10,11... | collective-permute-start | bytes 1572872 | tf_op jit(solution)/shard_map/ppermute | solution.py:219
  243.3 5.6 %collective-permute-start.30 = (f32[128,128]{1,0:T(8,128)S(1)}, f32[128,128]{1,0:T(8,128)S(1)}, u32[]{:S(2)}, u32[]{:S(2)}) collective-permute-start(f32[128,128]{1,0:T(8,128)S(1)} %add_add_fusion.1), channel_id=1, source_target_pairs={{0,2},{1,3},{2,0},{3,1},{4,6},{5,7},{6,4},{7,5},{8,10},{9,11},{10,... | collective-permute-start | bytes 196616 | tf_op jit(solution)/shard_map/ppermute | solution.py:354
  243.3 8.1 %collective-permute-start.31 = (f32[128,128]{1,0:T(8,128)S(1)}, f32[128,128]{1,0:T(8,128)S(1)}, u32[]{:S(2)}, u32[]{:S(2)}) collective-permute-start(f32[128,128]{1,0:T(8,128)S(1)} %add_add_fusion.1), channel_id=1, source_target_pairs={{0,4},{1,5},{2,6},{3,7},{4,0},{5,1},{6,2},{7,3},{8,12},{9,13},{10,... | collective-permute-start | bytes 196616 | tf_op jit(solution)/shard_map/ppermute | solution.py:354
  248.9 6.1 %collective-permute-start.32 = (f32[128,128]{1,0:T(8,128)S(1)}, f32[128,128]{1,0:T(8,128)S(1)}, u32[]{:S(2)}, u32[]{:S(2)}) collective-permute-start(f32[128,128]{1,0:T(8,128)S(1)} %add_add_fusion.1), channel_id=1, source_target_pairs={{0,6},{1,7},{2,4},{3,5},{4,2},{5,3},{6,0},{7,1},{8,14},{9,15},{10,... | collective-permute-start | bytes 196616 | tf_op jit(solution)/shard_map/ppermute | solution.py:354
  270.1 8.9 %collective-permute-start.37 = (f32[128,128]{1,0:T(8,128)S(1)}, f32[128,128]{1,0:T(8,128)S(1)}, u32[]{:S(2)}, u32[]{:S(2)}) collective-permute-start(f32[128,128]{1,0:T(8,128)S(1)} %get-tuple-element.202), channel_id=1, source_target_pairs={{0,8},{8,0},{16,24},{24,16},{1,9},{9,1},{17,25},{25,17},{2,10},{10... | collective-permute-start | bytes 196616 | tf_op jit(solution)/shard_map/ppermute | solution.py:364
  278.5 5.2 %collective-permute-start.39 = (f32[128,128]{1,0:T(8,128)S(1)}, f32[128,128]{1,0:T(8,128)S(1)}, u32[]{:S(2)}, u32[]{:S(2)}) collective-permute-start(f32[128,128]{1,0:T(8,128)S(1)} %get-tuple-element.203), channel_id=1, source_target_pairs={{0,24},{8,16},{16,8},{24,0},{1,25},{9,17},{17,9},{25,1},{2,26},{10... | collective-permute-start | bytes 196616 | tf_op jit(solution)/shard_map/ppermute | solution.py:364
  284.5 14.3 %collective-permute-start.43 = (f32[512,128]{1,0:T(8,128)}, f32[512,128]{1,0:T(8,128)S(1)}, u32[]{:S(2)}, u32[]{:S(2)}) collective-permute-start(f32[512,128]{1,0:T(8,128)} %pad_maximum_fusion.3.near.refs_0_), channel_id=1, source_target_pairs={{8,0},{9,1},{10,2},{11,3},{12,4},{13,5},{14,6},{15,7}} | collective-permute-start | bytes 786440 | tf_op jit(solution)/shard_map/ppermute | solution.py:435
  285.8 14.4 %collective-permute-start.44 = (f32[512,128]{1,0:T(8,128)}, f32[512,128]{1,0:T(8,128)S(1)}, u32[]{:S(2)}, u32[]{:S(2)}) collective-permute-start(f32[512,128]{1,0:T(8,128)} %pad_maximum_fusion.3.near.refs_0_), channel_id=1, source_target_pairs={{16,0},{17,1},{18,2},{19,3},{20,4},{21,5},{22,6},{23,7}} | collective-permute-start | bytes 786440 | tf_op jit(solution)/shard_map/ppermute | solution.py:435
  287.1 13.1 %collective-permute-start.45 = (f32[512,128]{1,0:T(8,128)}, f32[512,128]{1,0:T(8,128)S(1)}, u32[]{:S(2)}, u32[]{:S(2)}) collective-permute-start(f32[512,128]{1,0:T(8,128)} %pad_maximum_fusion.3.near.refs_0_), channel_id=1, source_target_pairs={{24,0},{25,1},{26,2},{27,3},{28,4},{29,5},{30,6},{31,7}} | collective-permute-start | bytes 786440 | tf_op jit(solution)/shard_map/ppermute | solution.py:435
  288.5 6.8 %collective-permute-start.41 = (f32[128,128]{1,0:T(8,128)S(1)}, f32[128,128]{1,0:T(8,128)S(1)}, u32[]{:S(2)}, u32[]{:S(2)}) collective-permute-start(f32[128,128]{1,0:T(8,128)S(1)} %bitcast_subtract_fusion), channel_id=1, source_target_pairs={{0,4},{1,5},{2,6},{3,7},{4,0},{5,1},{6,2},{7,3},{8,12},{9,13},{10,... | collective-permute-start | bytes 196616 | tf_op jit(solution)/shard_map/ppermute | solution.py:354
  292.8 6.1 %collective-permute-start.42 = (f32[128,128]{1,0:T(8,128)S(1)}, f32[128,128]{1,0:T(8,128)S(1)}, u32[]{:S(2)}, u32[]{:S(2)}) collective-permute-start(f32[128,128]{1,0:T(8,128)S(1)} %bitcast_subtract_fusion), channel_id=1, source_target_pairs={{0,6},{1,7},{2,4},{3,5},{4,2},{5,3},{6,0},{7,1},{8,14},{9,15},{10,... | collective-permute-start | bytes 196616 | tf_op jit(solution)/shard_map/ppermute | solution.py:354
  301.4 17.0 %collective-permute-start.50 = (f32[4,512,128]{2,1,0:T(8,128)S(1)}, f32[4,512,128]{2,1,0:T(8,128)S(1)}, u32[]{:S(2)}, u32[]{:S(2)}) collective-permute-start(f32[4,512,128]{2,1,0:T(8,128)S(1)} %pad_maximum_fusion), channel_id=1, source_target_pairs={{0,1},{1,0},{2,3},{3,2},{4,5},{5,4},{6,7},{7,6},{8,9},{9,8},{10,11... | collective-permute-start | bytes 3145736 | tf_op jit(solution)/shard_map/ppermute | solution.py:219
  309.4 4.3 %collective-permute-start.47 = (f32[128,128]{1,0:T(8,128)S(1)}, f32[128,128]{1,0:T(8,128)S(1)}, u32[]{:S(2)}, u32[]{:S(2)}) collective-permute-start(f32[128,128]{1,0:T(8,128)S(1)} %get-tuple-element.199), channel_id=1, source_target_pairs={{0,8},{8,0},{16,24},{24,16},{1,9},{9,1},{17,25},{25,17},{2,10},{10... | collective-permute-start | bytes 196616 | tf_op jit(solution)/shard_map/ppermute | solution.py:364
  309.6 5.7 %collective-permute-start.48 = (f32[128,128]{1,0:T(8,128)S(1)}, f32[128,128]{1,0:T(8,128)S(1)}, u32[]{:S(2)}, u32[]{:S(2)}) collective-permute-start(f32[128,128]{1,0:T(8,128)S(1)} %get-tuple-element.201), channel_id=1, source_target_pairs={{0,16},{8,24},{16,0},{24,8},{1,17},{9,25},{17,1},{25,9},{2,18},{10... | collective-permute-start | bytes 196616 | tf_op jit(solution)/shard_map/ppermute | solution.py:364
  312.3 5.2 %collective-permute-start.49 = (f32[128,128]{1,0:T(8,128)S(1)}, f32[128,128]{1,0:T(8,128)S(1)}, u32[]{:S(2)}, u32[]{:S(2)}) collective-permute-start(f32[128,128]{1,0:T(8,128)S(1)} %get-tuple-element.200), channel_id=1, source_target_pairs={{0,24},{8,16},{16,8},{24,0},{1,25},{9,17},{17,9},{25,1},{2,26},{10... | collective-permute-start | bytes 196616 | tf_op jit(solution)/shard_map/ppermute | solution.py:364
  318.4 13.0 %collective-permute-start.51 = (f32[128,128]{1,0:T(8,128)S(1)}, f32[128,128]{1,0:T(8,128)S(1)}, u32[]{:S(2)}, u32[]{:S(2)}) collective-permute-start(f32[128,128]{1,0:T(8,128)S(1)} %add_add_fusion), channel_id=1, source_target_pairs={{0,2},{1,3},{2,0},{3,1},{4,6},{5,7},{6,4},{7,5},{8,10},{9,11},{10,... | collective-permute-start | bytes 196616 | tf_op jit(solution)/shard_map/ppermute | solution.py:354
  318.4 12.9 %collective-permute-start.52 = (f32[128,128]{1,0:T(8,128)S(1)}, f32[128,128]{1,0:T(8,128)S(1)}, u32[]{:S(2)}, u32[]{:S(2)}) collective-permute-start(f32[128,128]{1,0:T(8,128)S(1)} %add_add_fusion), channel_id=1, source_target_pairs={{0,4},{1,5},{2,6},{3,7},{4,0},{5,1},{6,2},{7,3},{8,12},{9,13},{10,... | collective-permute-start | bytes 196616 | tf_op jit(solution)/shard_map/ppermute | solution.py:354
  321.5 9.9 %collective-permute-start.53 = (f32[128,128]{1,0:T(8,128)S(1)}, f32[128,128]{1,0:T(8,128)S(1)}, u32[]{:S(2)}, u32[]{:S(2)}) collective-permute-start(f32[128,128]{1,0:T(8,128)S(1)} %add_add_fusion), channel_id=1, source_target_pairs={{0,6},{1,7},{2,4},{3,5},{4,2},{5,3},{6,0},{7,1},{8,14},{9,15},{10,... | collective-permute-start | bytes 196616 | tf_op jit(solution)/shard_map/ppermute | solution.py:354
  338.5 4.6 %collective-permute-start.55 = (f32[128,128]{1,0:T(8,128)S(1)}, f32[128,128]{1,0:T(8,128)S(1)}, u32[]{:S(2)}, u32[]{:S(2)}) collective-permute-start(f32[128,128]{1,0:T(8,128)S(1)} %get-tuple-element.196), channel_id=1, source_target_pairs={{0,8},{8,0},{16,24},{24,16},{1,9},{9,1},{17,25},{25,17},{2,10},{10... | collective-permute-start | bytes 196616 | tf_op jit(solution)/shard_map/ppermute | solution.py:364
  338.6 5.7 %collective-permute-start.56 = (f32[128,128]{1,0:T(8,128)S(1)}, f32[128,128]{1,0:T(8,128)S(1)}, u32[]{:S(2)}, u32[]{:S(2)}) collective-permute-start(f32[128,128]{1,0:T(8,128)S(1)} %get-tuple-element.198), channel_id=1, source_target_pairs={{0,16},{8,24},{16,0},{24,8},{1,17},{9,25},{17,1},{25,9},{2,18},{10... | collective-permute-start | bytes 196616 | tf_op jit(solution)/shard_map/ppermute | solution.py:364
  338.7 5.7 %collective-permute-start.57 = (f32[128,128]{1,0:T(8,128)S(1)}, f32[128,128]{1,0:T(8,128)S(1)}, u32[]{:S(2)}, u32[]{:S(2)}) collective-permute-start(f32[128,128]{1,0:T(8,128)S(1)} %get-tuple-element.197), channel_id=1, source_target_pairs={{0,24},{8,16},{16,8},{24,0},{1,25},{9,17},{17,9},{25,1},{2,26},{10... | collective-permute-start | bytes 196616 | tf_op jit(solution)/shard_map/ppermute | solution.py:364
  345.2 8.0 %collective-permute-start.58 = (f32[128,128]{1,0:T(8,128)S(1)}, f32[128,128]{1,0:T(8,128)S(1)}, u32[]{:S(2)}, u32[]{:S(2)}) collective-permute-start(f32[128,128]{1,0:T(8,128)S(1)} %bitcast_subtract_fusion.2), channel_id=1, source_target_pairs={{0,2},{1,3},{2,0},{3,1},{4,6},{5,7},{6,4},{7,5},{8,10},{9,11},{10,... | collective-permute-start | bytes 196616 | tf_op jit(solution)/shard_map/ppermute | solution.py:354
  345.3 7.9 %collective-permute-start.59 = (f32[128,128]{1,0:T(8,128)S(1)}, f32[128,128]{1,0:T(8,128)S(1)}, u32[]{:S(2)}, u32[]{:S(2)}) collective-permute-start(f32[128,128]{1,0:T(8,128)S(1)} %bitcast_subtract_fusion.2), channel_id=1, source_target_pairs={{0,4},{1,5},{2,6},{3,7},{4,0},{5,1},{6,2},{7,3},{8,12},{9,13},{10,... | collective-permute-start | bytes 196616 | tf_op jit(solution)/shard_map/ppermute | solution.py:354
  348.4 6.1 %collective-permute-start.60 = (f32[128,128]{1,0:T(8,128)S(1)}, f32[128,128]{1,0:T(8,128)S(1)}, u32[]{:S(2)}, u32[]{:S(2)}) collective-permute-start(f32[128,128]{1,0:T(8,128)S(1)} %bitcast_subtract_fusion.2), channel_id=1, source_target_pairs={{0,6},{1,7},{2,4},{3,5},{4,2},{5,3},{6,0},{7,1},{8,14},{9,15},{10,... | collective-permute-start | bytes 196616 | tf_op jit(solution)/shard_map/ppermute | solution.py:354
  349.7 5.7 %collective-permute-start.61 = (f32[2,128,128]{2,1,0:T(8,128)S(1)}, f32[2,128,128]{2,1,0:T(8,128)S(1)}, u32[]{:S(2)}, u32[]{:S(2)}) collective-permute-start(f32[2,128,128]{2,1,0:T(8,128)S(1)} %pad_maximum_fusion.7), channel_id=1, source_target_pairs={{0,8},{8,0},{16,24},{24,16},{1,9},{9,1},{17,25},{25,17},{2,10},{10... | collective-permute-start | bytes 393224 | tf_op jit(solution)/shard_map/ppermute | solution.py:368
  351.5 5.5 %collective-permute-start.62 = (f32[2,128,128]{2,1,0:T(8,128)S(1)}, f32[2,128,128]{2,1,0:T(8,128)S(1)}, u32[]{:S(2)}, u32[]{:S(2)}) collective-permute-start(f32[2,128,128]{2,1,0:T(8,128)S(1)} %pad_maximum_fusion.7), channel_id=1, source_target_pairs={{0,16},{8,24},{16,0},{24,8},{1,17},{9,25},{17,1},{25,9},{2,18},{10... | collective-permute-start | bytes 393224 | tf_op jit(solution)/shard_map/ppermute | solution.py:368
  353.2 5.9 %collective-permute-start.63 = (f32[2,128,128]{2,1,0:T(8,128)S(1)}, f32[2,128,128]{2,1,0:T(8,128)S(1)}, u32[]{:S(2)}, u32[]{:S(2)}) collective-permute-start(f32[2,128,128]{2,1,0:T(8,128)S(1)} %pad_maximum_fusion.7), channel_id=1, source_target_pairs={{0,24},{8,16},{16,8},{24,0},{1,25},{9,17},{17,9},{25,1},{2,26},{10... | collective-permute-start | bytes 393224 | tf_op jit(solution)/shard_map/ppermute | solution.py:368
  366.3 4.6 %collective-permute-start.65 = (f32[128,128]{1,0:T(8,128)S(1)}, f32[128,128]{1,0:T(8,128)S(1)}, u32[]{:S(2)}, u32[]{:S(2)}) collective-permute-start(f32[128,128]{1,0:T(8,128)S(1)} %get-tuple-element.193), channel_id=1, source_target_pairs={{0,8},{8,0},{16,24},{24,16},{1,9},{9,1},{17,25},{25,17},{2,10},{10... | collective-permute-start | bytes 196616 | tf_op jit(solution)/shard_map/ppermute | solution.py:364
  366.4 5.0 %collective-permute-start.66 = (f32[128,128]{1,0:T(8,128)S(1)}, f32[128,128]{1,0:T(8,128)S(1)}, u32[]{:S(2)}, u32[]{:S(2)}) collective-permute-start(f32[128,128]{1,0:T(8,128)S(1)} %get-tuple-element.195), channel_id=1, source_target_pairs={{0,16},{8,24},{16,0},{24,8},{1,17},{9,25},{17,1},{25,9},{2,18},{10... | collective-permute-start | bytes 196616 | tf_op jit(solution)/shard_map/ppermute | solution.py:364
  366.9 5.2 %collective-permute-start.67 = (f32[128,128]{1,0:T(8,128)S(1)}, f32[128,128]{1,0:T(8,128)S(1)}, u32[]{:S(2)}, u32[]{:S(2)}) collective-permute-start(f32[128,128]{1,0:T(8,128)S(1)} %get-tuple-element.194), channel_id=1, source_target_pairs={{0,24},{8,16},{16,8},{24,0},{1,25},{9,17},{17,9},{25,1},{2,26},{10... | collective-permute-start | bytes 196616 | tf_op jit(solution)/shard_map/ppermute | solution.py:364
  373.0 4.6 %collective-permute-start.68 = (f32[1,128,128]{2,1,0:T(8,128)S(1)}, f32[1,128,128]{2,1,0:T(8,128)S(1)}, u32[]{:S(2)}, u32[]{:S(2)}) collective-permute-start(f32[1,128,128]{2,1,0:T(8,128)S(1)} %add_bitcast_fusion), channel_id=1, source_target_pairs={{0,8},{8,0},{16,24},{24,16},{1,9},{9,1},{17,25},{25,17},{2,10},{10... | collective-permute-start | bytes 196616 | tf_op jit(solution)/shard_map/ppermute | solution.py:368
  375.0 4.6 %collective-permute-start.69 = (f32[1,128,128]{2,1,0:T(8,128)S(1)}, f32[1,128,128]{2,1,0:T(8,128)S(1)}, u32[]{:S(2)}, u32[]{:S(2)}) collective-permute-start(f32[1,128,128]{2,1,0:T(8,128)S(1)} %add_bitcast_fusion), channel_id=1, source_target_pairs={{0,16},{8,24},{16,0},{24,8},{1,17},{9,25},{17,1},{25,9},{2,18},{10... | collective-permute-start | bytes 196616 | tf_op jit(solution)/shard_map/ppermute | solution.py:368
  376.5 5.2 %collective-permute-start.70 = (f32[1,128,128]{2,1,0:T(8,128)S(1)}, f32[1,128,128]{2,1,0:T(8,128)S(1)}, u32[]{:S(2)}, u32[]{:S(2)}) collective-permute-start(f32[1,128,128]{2,1,0:T(8,128)S(1)} %add_bitcast_fusion), channel_id=1, source_target_pairs={{0,24},{8,16},{16,8},{24,0},{1,25},{9,17},{17,9},{25,1},{2,26},{10... | collective-permute-start | bytes 196616 | tf_op jit(solution)/shard_map/ppermute | solution.py:368
  (32 other events, 200.2 us)

commit v2 on v1

--- a/solution.py
+++ b/solution.py
@@ -34,8 +34,8 @@
 
 
 def chip_kernel(where, weights, *refs):
-    outs, high, low = refs[-STEPS - 2 : -2], *refs[-2:]
-    pieces = refs[: len(refs) - STEPS - 2]
+    outs, tail, high, low = refs[-STEPS - 3 : -3], *refs[-3:]
+    pieces = refs[: len(refs) - STEPS - 3]
     totals = pieces[len(pieces) - STEPS :] if len(pieces) % 2 else []
     number, at = pl.program_id(0), pl.program_id(1)
     lags, rows, width = pieces[0].shape
@@ -46,7 +46,13 @@
         for n, out in enumerate(outs):
             out[...] = totals[n][...] if totals else jnp.zeros_like(out)
 
-    for i in range(len(pieces) // 2 - (1 if totals else 0)):
+    count = len(pieces) // 2 - (1 if totals else 0)
+
+    @pl.when(jnp.logical_and(number == count - 1, at == 0))
+    def _():
+        tail[...] = pieces[2 * count - 2][lags - tail.shape[0] :]
+
+    for i in range(count):
 
         @pl.when(jnp.logical_and(number == i, at == 0))
         def _():
@@ -128,11 +134,6 @@
             if k == 0:
                 one_out[...] += result[:, :width]
             two_out[...] += result[:, size - width :]
-
-
-def multiply_kernel(where, matrix, near, far, total, out):
-    vector = jnp.concatenate([near[...], far[...]], axis=0)
-    out[...] = total[...] + product(matrix[...], [vector])
 
 
 def second_kernel(where, weights, *refs):
@@ -259,13 +260,24 @@
 
     def add_chip(totals, pieces, stage):
         count = len(pieces) // 2
-        return call(
-            chip_kernel, where, (count, lags), (lag_weights, *pieces, *totals),
-            [pl.BlockSpec((1, rows, 2 * rows), lambda i, k, w: (k, 0, w[2 + stage + i]))]
-            + [all_of(v.shape) for v in (*pieces, *totals)], STEPS, square,
-            (18 * count * lags * tile * width, 4 * count * lags * tile), {2 + len(pieces) + n: n for n in range(len(totals))},
-            [pltpu.VMEM((2 * rows, lags * width), BF16)] * 2,
-        )
+        before = (STEPS - 1, *square)
+        *totals, tail = pl.pallas_call(
+            chip_kernel,
+            out_shape=[jax.ShapeDtypeStruct(square, F32)] * STEPS + [jax.ShapeDtypeStruct(before, F32)],
+            grid_spec=pltpu.PrefetchScalarGridSpec(
+                num_scalar_prefetch=1,
+                grid=(count, lags),
+                in_specs=[pl.BlockSpec((1, rows, 2 * rows), lambda i, k, w: (k, 0, w[2 + stage + i]))]
+                + [all_of(v.shape) for v in (*pieces, *totals)],
+                out_specs=[all_of(square)] * STEPS + [all_of(before)],
+                scratch_shapes=[pltpu.VMEM((2 * rows, lags * width), BF16)] * 2,
+            ),
+            input_output_aliases={2 + len(pieces) + n: n for n in range(len(totals))},
+            cost_estimate=pl.CostEstimate(flops=18 * count * lags * tile * width, bytes_accessed=4 * count * lags * tile, transcendentals=0),
+            compiler_params=pltpu.CompilerParams(dimension_semantics=("arbitrary", "arbitrary")),
+            name="chip",
+        )(where, lag_weights, *pieces, *totals)
+        return totals, tail
 
     def add_first(total, near, far, stage):
         before = STEPS - 1
@@ -371,15 +383,9 @@
     def enter(tail):
         return lax.ppermute(tail, "lag", [(i, i + 1) for i in range(groups - 1)])
 
-    def tails(arrays):
-        return {hop: value[lags - (STEPS - 1) :] for hop, value in arrays.items()}
-
-    def multiply(matrix, mine, total):
-        operands = (matrix, mine, other_core(mine), total)
-        return call(
-            multiply_kernel, where, (1,), operands, [all_of(v.shape) for v in operands],
-            1, square, (6 * rows * meet * width, 4 * rows * meet),
-        )[0]
+    def multiply(matrix, mine):
+        vector = jnp.concatenate([mine, other_core(mine)], axis=0)
+        return jnp.dot(matrix, vector, precision=lax.Precision.HIGH)
 
     ups, downs = {1: go_up(history, 1)}, {1: go_down(history, 1)}
     tail = history[lags - (STEPS - 1) :]
@@ -390,20 +396,25 @@
     sent = [lax.ppermute(chunks[j], "lag", [(0, j)]) for j in range(1, groups - 1)]
     (head_columns,) = columns(inverse_head[None], False)
     ups[1], downs[1], entered, own_far, head_columns = tie((ups[1], downs[1], entered, own_far, head_columns))
-    totals = []
+    totals, waiting = [], []
     for stage in range(1, chips - 1):
         next_up, next_down = go_up(ups[stage], stage + 1), go_down(downs[stage], stage + 1)
         near = choose(stage, ups, downs)
-        entered.append(enter(choose(stage, tails(ups), tails(downs))))
-        if stage == 1:
-            last_near, entered[0] = tie((last_near, entered[0]))
-            sent.append(lax.ppermute(last_near, "lag", [(0, groups - 1)]))
         if stage == chips - 2:
             relayed, near = tie((relayed, near))
             sent.append(lax.ppermute(relayed, "lag", [(groups // 2, groups - 1)]))
         pieces = [near, other_core(near)]
-        totals = add_chip([], [history, own_far, *pieces], 0) if stage == 1 else add_chip(totals, pieces, stage)
-        if stage == chips - 2:
+        if stage == 1:
+            pieces = [history, own_far, *pieces]
+        totals, tail = add_chip(totals, pieces, stage if stage > 1 else 0)
+        if stage < chips - 2:
+            entered.append(enter(tail))
+            if stage == 1:
+                last_near, tail = tie((last_near, tail))
+                late = lax.ppermute(last_near, "lag", [(0, groups - 1)])
+                sent.append(late)
+        else:
+            waiting.append(tail)
             totals = [totals[0], *add_entered(totals[1], totals[2], entered[:1], 0)]
         ups[stage + 1], downs[stage + 1] = next_up, next_down
         ups, downs, totals = tie((ups, downs, totals))
@@ -412,15 +423,14 @@
     near = choose(chips - 1, ups, downs)
     far = other_core(near)
     first, tail = add_first(first, near, far, chips - 1)
-    nothing = jnp.zeros(square, F32)
 
     right_side = own_part(excitation[0]) - sum_parts(first)
-    right_side, tail, near, far, one, two = tie((right_side, tail, near, far, one, two))
+    right_side, waiting, tail, near, far, one, two = tie((right_side, waiting, tail, near, far, one, two))
     mine = gather_near(right_side)
-    entered.append(enter(tail))
+    entered += [enter(value) for value in (*waiting, tail)]
     one, two = add_rest(one, two, near, far, chips - 1)
     mine, one, two, sent = tie((mine, one, two, sent))
-    density = sum_parts(multiply(head_columns, mine, nothing))
+    density = sum_parts(multiply(head_columns, mine))
     first_columns = pick([chunks[0], *sent])
     results = [density]
 
@@ -428,13 +438,13 @@
     mine = gather_near(density)
     one, two = add_entered(one, two, entered[1:], 1)
     mine, one, two = tie((mine, one, two))
-    right_side = own_part(excitation[1]) - sum_parts(multiply(first_columns, mine, one))
+    right_side = own_part(excitation[1]) - sum_parts(one + multiply(first_columns, mine))
 
     right_side, two, old = tie((right_side, two, mine))
     mine = gather_near(right_side)
     nears = [old] + [lax.ppermute(old, "lag", [(j, 0)]) for j in range(1, groups)]
     mine, two, nears = tie((mine, two, nears))
-    density = sum_parts(multiply(head_columns, mine, nothing))
+    density = sum_parts(multiply(head_columns, mine))
     fars = other_core(jnp.stack(nears))
     results.append(density)
 
@@ -442,13 +452,13 @@
     mine = gather_near(density)
     two = add_second(two, nears, [fars[j] for j in range(groups)])
     mine, two = tie((mine, two))
-    right_side = own_part(excitation[2]) - sum_parts(multiply(first_columns, mine, two))
+    right_side = own_part(excitation[2]) - sum_parts(two + multiply(first_columns, mine))
 
     right_side, results = tie((right_side, results))
     mine = gather_near(right_side)
     early = whole_rows(jnp.stack(results))
     mine, early = tie((mine, early))
-    density = sum_parts(multiply(head_columns, mine, nothing))
+    density = sum_parts(multiply(head_columns, mine))
     return jnp.concatenate([early, whole_rows(density[None])], axis=0)
 
 

time: 385 us -> 368 us (0.956)
  Pallas kernels: 94.3 us -> 75.4 us
  waiting for transfers between devices: 147 us -> 163 us
  matrix products: 0 us -> 8.11 us
  other arithmetic: 17.1 us -> 9.14 us
  local copies, waits for them, and re-layouts: 17 us -> 9.13 us
  starting transfers between devices: 107 us -> 102 us
    pallas_call x11 -> x4, Pallas kernels: 69.9 us -> 24.3 us  [call(): pl.pallas_call(kernel, out_shape=[jax.ShapeDtypeStruct(shape, F32)] * cou...]
    pallas_call x0 -> x2, Pallas kernels: none -> 26.7 us  [add_chip(): pl.pallas_call(chip_kernel, out_shape=[jax.ShapeDtypeStruct(square, F32)]...]
    ppermute x18, waiting for transfers between devices: 76.3 us -> 90.8 us  [sum_parts(): result = result + lax.ppermute(sent, 'lag', pairs(groups, mask))]
    dot_general x0 -> x5, matrix products: none -> 8.11 us  [multiply(): return jnp.dot(matrix, vector, precision=lax.Precision.HIGH)]
    ppermute x1, starting transfers between devices: 6.27 us -> 2.26 us  [on_device(): late = lax.ppermute(last_near, 'lag', [(0, groups - 1)])]
  transfers between devices with their start and end apart: 71 -> 71, of which waited for: 39 -> 38; matrix products, arithmetic and copies ran while one was open for 5% -> 3% of each run, Pallas kernels for 20% -> 19%
where the time goes in v2:
time: 368 us; the launch traced here: 367 us
  waiting for transfers between devices  163 us (44%)
  starting transfers between devices  102 us (28%)
  Pallas kernels  75.4 us (20%)
  other arithmetic  9.14 us (2%)
  local copies, waits for them, and re-layouts  9.13 us (2%)
  matrix products  8.11 us (2%)
    ppermute x18, waiting for transfers between devices, sum_parts(): result = result + lax.ppermute(sent, 'lag', pairs(groups, mask))  90.8 us
    pallas_call x2, Pallas kernels, add_chip(): pl.pallas_call(chip_kernel, out_shape=[jax.ShapeDtypeStruct(square, F32)]...  26.7 us
    ppermute x18, starting transfers between devices, sum_parts(): result = result + lax.ppermute(sent, 'lag', pairs(groups, mask))  25.6 us
    pallas_call x4, Pallas kernels, call(): pl.pallas_call(kernel, out_shape=[jax.ShapeDtypeStruct(shape, F32)] * cou...  24.3 us
    ppermute x15, waiting for transfers between devices, gather_near(): lax.ppermute(value, 'row', pairs(devices, 2 * k))  23.7 us
    ppermute x6, waiting for transfers between devices, along(): lax.ppermute(value, 'row', [(2 * i + c, 2 * (i + step) + c) for i in sour...  22.1 us
    ppermute x15, starting transfers between devices, gather_near(): lax.ppermute(value, 'row', pairs(devices, 2 * k))  20 us
    ppermute x4, starting transfers between devices, enter(): return lax.ppermute(tail, 'lag', [(i, i + 1) for i in range(groups - 1)])  16.1 us
  transfers between devices with their start and end apart: 71, of which 38 were waited for; matrix products, arithmetic and copies ran while one was open for 3% of the time, Pallas kernels for 19%

profile of v2, /device:TPU:0, one launch (start us, length us, event | category | flops | bytes accessed | tf_op | source)
XLA Modules:
  0.0 366.8 jit_solution(2406288222113956937)
XLA Ops:
  0.0 5.0 %collective-permute-start = (f32[4,512,128]{2,1,0:T(8,128)}, f32[4,512,128]{2,1,0:T(8,128)S(1)}, u32[]{:S(2)}, u32[]{:S(2)}) collective-permute-start(f32[4,512,128]{2,1,0:T(8,128)} %refs_0_.2), channel_id=1, source_target_pairs={{0,2},{1,3},{2,4},{3,5},{4,6},{5,7},{8,10},{9,11},{10,12},{11,13},... | collective-permute-start | bytes 3145736 | tf_op jit(solution)/shard_map/ppermute | solution.py:223
  7.5 4.2 %collective-permute-start.2 = (f32[2,512,128]{2,1,0:T(8,128)S(1)}, f32[2,512,128]{2,1,0:T(8,128)}, u32[]{:S(2)}, u32[]{:S(2)}) collective-permute-start(f32[2,512,128]{2,1,0:T(8,128)S(1)} %slice_select_fusion), channel_id=1, source_target_pairs={{0,8},{8,16},{16,24},{1,9},{9,17},{17,25},{2,10},{10,18},{18,26},{... | collective-permute-start | bytes 1572872 | tf_op jit(solution)/shard_map/ppermute | solution.py:384
  12.5 5.8 %columns.2 = f32[512,1024]{1,0:T(8,128)} custom-call(s32[2,5,4]{2,1,0:T(8,128)} %concatenate.43.where, f32[1,512,4096]{2,1,0:T(8,128)} %bitcast.45, f32[1,512,4096]{2,1,0:T(8,128)} %bitcast.46, f32[1,512,4096]{2,1,0:T(8,128)} %bitcast.47, f32[1,512,4096]{2,1,0:T(8,128)} %bitcast.48), custom_call_target="tpu_custom_call" | custom-call | bytes 16777216 | tf_op jit(solution)/shard_map/columns/pallas_call | solution.py:335
  18.3 4.4 %collective-permute-done.2.refs_0_ = f32[2,512,128]{2,1,0:T(8,128)} collective-permute-done((f32[2,512,128]{2,1,0:T(8,128)S(1)}, f32[2,512,128]{2,1,0:T(8,128)}, u32[]{:S(2)}, u32[]{:S(2)}) %collective-permute-start.2) | collective-permute-done | bytes 524320 | tf_op jit(solution)/shard_map/ppermute | solution.py:384
  22.7 5.0 %collective-permute-done = f32[4,512,128]{2,1,0:T(8,128)S(1)} collective-permute-done((f32[4,512,128]{2,1,0:T(8,128)}, f32[4,512,128]{2,1,0:T(8,128)S(1)}, u32[]{:S(2)}, u32[]{:S(2)}) %collective-permute-start) | collective-permute-done | bytes 1048608 | tf_op jit(solution)/shard_map/ppermute | solution.py:223
  27.7 4.1 %collective-permute-done.1 = f32[4,512,128]{2,1,0:T(8,128)S(1)} collective-permute-done((f32[4,512,128]{2,1,0:T(8,128)}, f32[4,512,128]{2,1,0:T(8,128)S(1)}, u32[]{:S(2)}, u32[]{:S(2)}) %collective-permute-start.1) | collective-permute-done | bytes 1048608 | tf_op jit(solution)/shard_map/ppermute | solution.py:223
  34.0 7.1 %columns.3 = (f32[512,1024]{1,0:T(8,128)}, f32[512,1024]{1,0:T(8,128)}, f32[512,1024]{1,0:T(8,128)}, f32[512,512]{1,0:T(8,128)}, f32[512,512]{1,0:T(8,128)}) custom-call(s32[2,5,4]{2,1,0:T(8,128)} %concatenate.43.where, f32[4,512,4096]{2,1,0:T(8,128)} %weights.13, f32[4,512,4096]{2,1,0:T(8,128)} %weights.13, f32[4,512,4096]{2,1,0:T(8,128)} %weights.13, ...), custom_call_target="tpu_custom_call" | custom-call | bytes 16777216 | tf_op jit(solution)/shard_map/columns/pallas_call | solution.py:335
  41.1 4.4 %collective-permute-start.9 = (f32[512,512]{1,0:T(8,128)}, f32[512,512]{1,0:T(8,128)}, u32[]{:S(2)}, u32[]{:S(2)}) collective-permute-start(f32[512,512]{1,0:T(8,128)} %get-tuple-element.104), channel_id=1, source_target_pairs={{0,16},{1,17},{2,18},{3,19},{4,20},{5,21},{6,22},{7,23}} | collective-permute-start | bytes 3145736 | tf_op jit(solution)/shard_map/ppermute | solution.py:395
  46.2 16.6 %chip.2 = (f32[512,128]{1,0:T(8,128)}, f32[512,128]{1,0:T(8,128)}, f32[512,128]{1,0:T(8,128)}, f32[2,512,128]{2,1,0:T(8,128)}) custom-call(s32[10]{0:T(128)} %stack.100.where, f32[4,512,4096]{2,1,0:T(8,128)} %weights.13, f32[4,512,128]{2,1,0:T(8,128)} %refs_0_.2, f32[4,512,128]{2,1,0:T(8,128)} %collective-permute-done.3.refs_1_, f32[4,512,128]{2,1,0:T(8,128)} %copy-done.7, ...), custom_call_target="tpu_custom_call" | custom-call | flops 9663676416 | bytes 16777216 | tf_op jit(solution)/shard_map/chip/pallas_call | solution.py:264
  62.8 1.7 select_select_fusion.1.refs_0_
  64.6 3.3 collective-permute-done.9
  72.6 10.1 %chip.3 = (f32[512,128]{1,0:T(8,128)}, f32[512,128]{1,0:T(8,128)}, f32[512,128]{1,0:T(8,128)}, f32[2,512,128]{2,1,0:T(8,128)}) custom-call(s32[10]{0:T(128)} %stack.100.where, f32[4,512,4096]{2,1,0:T(8,128)} %weights.13, f32[4,512,128]{2,1,0:T(8,128)} %copy-done.6, ...), custom_call_target="tpu_custom_call", output_to_operand_aliasing={{0}: (4, {}), {1}: (5, {}), {2}: (6, {})} | custom-call | flops 4831838208 | bytes 8388608 | tf_op jit(solution)/shard_map/chip/pallas_call | solution.py:264
  82.7 3.9 %shard_map.46 = (f32[512,128]{1,0:T(8,128)}, f32[512,128]{1,0:T(8,128)}) custom-call(s32[10]{0:T(128)} %stack.100.where, f32[4,512,4096]{2,1,0:T(8,128)} %weights.13, f32[2,512,128]{2,1,0:T(8,128)} %collective-permute-done.2.refs_0_, f32[2,512,128]{2,1,0:T(8,128)} %collective-permute-done.11.refs_1_, ...), custom_call_target="tpu_custom_call", output_to_operand_aliasing={{0}: (4, {}), {1}: (5, {})} | custom-call | flops 1207959552 | bytes 4194304 | tf_op jit(solution)/shard_map/pallas_call | solution.py:188
  86.6 13.0 %collective-permute-done.8 = f32[4,512,128]{2,1,0:T(8,128)} collective-permute-done((f32[4,512,128]{2,1,0:T(8,128)}, f32[4,512,128]{2,1,0:T(8,128)}, u32[]{:S(2)}, u32[]{:S(2)}) %collective-permute-start.8) | collective-permute-done | bytes 1048608 | tf_op jit(solution)/shard_map/ppermute | solution.py:223
  101.1 2.6 collective-permute-start.19
  103.8 5.1 %collective-permute-start.20 = (f32[512,1024]{1,0:T(8,128)}, f32[512,1024]{1,0:T(8,128)}, u32[]{:S(2)}, u32[]{:S(2)}) collective-permute-start(f32[512,1024]{1,0:T(8,128)} %get-tuple-element.133), channel_id=1, source_target_pairs={{0,16},{1,17},{2,18},{3,19},{4,20},{5,21},{6,22},{7,23}} | collective-permute-start | bytes 6291464 | tf_op jit(solution)/shard_map/ppermute | solution.py:396
  109.8 7.5 %first.1 = (f32[512,128]{1,0:T(8,128)}, f32[2,512,128]{2,1,0:T(8,128)}) custom-call(s32[10]{0:T(128)} %stack.100.where, f32[4,512,4096]{2,1,0:T(8,128)} %weights.13, f32[4,512,128]{2,1,0:T(8,128)} %copy-done.1, f32[4,512,128]{2,1,0:T(8,128)} %copy-done.3, f32[512,128]{1,0:T(8,128)} %get-tuple-element.119.total), custom_call_target="tpu_custom_call", output_to_operand_aliasing={{0}: (4, {})} | custom-call | flops 1610612736 | bytes 8388608 | tf_op jit(solution)/shard_map/first/pallas_call | solution.py:284
  119.1 30.7 %collective-permute-done.13 = f32[128,128]{1,0:T(8,128)S(1)} collective-permute-done((f32[128,128]{1,0:T(8,128)S(1)}, f32[128,128]{1,0:T(8,128)S(1)}, u32[]{:S(2)}, u32[]{:S(2)}) %collective-permute-start.13) | collective-permute-done | bytes 65568 | tf_op jit(solution)/shard_map/ppermute | solution.py:376
  149.9 2.3 collective-permute-start.21
  152.1 2.5 collective-permute-done.14
  154.6 1.9 fusion.25
  156.6 18.9 %collective-permute-done.15 = f32[128,128]{1,0:T(8,128)S(1)} collective-permute-done((f32[128,128]{1,0:T(8,128)S(1)}, f32[128,128]{1,0:T(8,128)S(1)}, u32[]{:S(2)}, u32[]{:S(2)}) %collective-permute-start.15) | collective-permute-done | bytes 65568 | tf_op jit(solution)/shard_map/ppermute | solution.py:376
  176.5 4.3 %collective-permute-done.16 = f32[128,128]{1,0:T(8,128)S(1)} collective-permute-done((f32[128,128]{1,0:T(8,128)S(1)}, f32[128,128]{1,0:T(8,128)S(1)}, u32[]{:S(2)}, u32[]{:S(2)}) %collective-permute-start.16) | collective-permute-done | bytes 65568 | tf_op jit(solution)/shard_map/ppermute | solution.py:366
  181.0 5.7 %collective-permute-done.17 = f32[128,128]{1,0:T(8,128)S(1)} collective-permute-done((f32[128,128]{1,0:T(8,128)S(1)}, f32[128,128]{1,0:T(8,128)S(1)}, u32[]{:S(2)}, u32[]{:S(2)}) %collective-permute-start.17) | collective-permute-done | bytes 65568 | tf_op jit(solution)/shard_map/ppermute | solution.py:366
  186.7 1.8 collective-permute-start.18
  188.5 7.6 %shard_map.47 = (f32[512,128]{1,0:T(8,128)}, f32[512,128]{1,0:T(8,128)}) custom-call(s32[10]{0:T(128)} %stack.100.where, f32[4,512,4096]{2,1,0:T(8,128)} %weights.13, f32[4,512,128]{2,1,0:T(8,128)} %copy-done.1, f32[4,512,128]{2,1,0:T(8,128)} %copy-done.1, f32[4,512,128]{2,1,0:T(8,128)} %copy-done.3, ...), custom_call_target="tpu_custom_call", output_to_operand_aliasing={{0}: (6, {}), {1}: (7, {})} | custom-call | flops 3221225472 | bytes 8388608 | tf_op jit(solution)/shard_map/pallas_call | solution.py:188
  196.3 2.1 collective-permute-start.27
  198.4 2.1 collective-permute-start.28
  200.5 7.7 %collective-permute-start.29 = (f32[2,512,128]{2,1,0:T(8,128)}, f32[2,512,128]{2,1,0:T(8,128)}, u32[]{:S(2)}, u32[]{:S(2)}) collective-permute-start(f32[2,512,128]{2,1,0:T(8,128)} %get-tuple-element.145), channel_id=1, source_target_pairs={{0,8},{8,16},{16,24},{1,9},{9,17},{17,25},{2,10},{10,18},{18,26},{... | collective-permute-start | bytes 1572872 | tf_op jit(solution)/shard_map/ppermute | solution.py:384
  209.9 23.9 %collective-permute-done.24 = f32[128,128]{1,0:T(8,128)S(1)} collective-permute-done((f32[128,128]{1,0:T(8,128)S(1)}, f32[128,128]{1,0:T(8,128)S(1)}, u32[]{:S(2)}, u32[]{:S(2)}) %collective-permute-start.24) | collective-permute-done | bytes 65568 | tf_op jit(solution)/shard_map/ppermute | solution.py:376
  233.8 6.1 %collective-permute-start.26 = (f32[128,128]{1,0:T(8,128)}, f32[128,128]{1,0:T(8,128)}, u32[]{:S(2)}, u32[]{:S(2)}) collective-permute-start(f32[128,128]{1,0:T(8,128)} %get-tuple-element.210), channel_id=1, source_target_pairs={{0,24},{8,16},{16,8},{24,0},{1,25},{9,17},{17,9},{25,1},{2,26},{10... | collective-permute-start | bytes 196616 | tf_op jit(solution)/shard_map/ppermute | solution.py:376
  239.9 4.0 %pick.1 = f32[512,1024]{1,0:T(8,128)} custom-call(s32[1]{0:T(128)} %bitcast.13.which, f32[512,1024]{1,0:T(8,128)} %get-tuple-element.139.refs_0_, f32[512,1024]{1,0:T(8,128)} %collective-permute-done.19.refs_1_, f32[512,1024]{1,0:T(8,128)} %collective-permute-done.20.refs_2_, f32[512,512]{1,0:T(8,128)} %collective-permute-done.21.refs_3_, f32[512,512]{1,0:T(8,128)} %copy-done.15), custom_call_target="tpu_custom_call" | custom-call | bytes 8388608 | tf_op jit(solution)/shard_map/pick/pallas_call | solution.py:351
  245.5 2.5 collective-permute-start.31
  247.9 3.2 collective-permute-done.30
  251.1 1.9 collective-permute-start.32
  253.1 4.1 %collective-permute-done.32 = f32[128,128]{1,0:T(8,128)S(1)} collective-permute-done((f32[128,128]{1,0:T(8,128)S(1)}, f32[128,128]{1,0:T(8,128)S(1)}, u32[]{:S(2)}, u32[]{:S(2)}) %collective-permute-start.32) | collective-permute-done | bytes 65568 | tf_op jit(solution)/shard_map/ppermute | solution.py:366
  258.2 5.3 %shard_map.48 = (f32[512,128]{1,0:T(8,128)}, f32[512,128]{1,0:T(8,128)}) custom-call(s32[10]{0:T(128)} %stack.100.where, f32[4,512,4096]{2,1,0:T(8,128)} %weights.13, f32[2,512,128]{2,1,0:T(8,128)} %collective-permute-done.27.refs_0_, f32[2,512,128]{2,1,0:T(8,128)} %copy-done.16, ...), custom_call_target="tpu_custom_call", output_to_operand_aliasing={{0}: (8, {}), {1}: (9, {})} | custom-call | flops 3623878656 | bytes 12582912 | tf_op jit(solution)/shard_map/pallas_call | solution.py:188
  265.0 2.6 fusion.4
  267.7 6.5 %collective-permute-start.37 = (f32[128,128]{1,0:T(8,128)S(1)}, f32[128,128]{1,0:T(8,128)S(1)}, u32[]{:S(2)}, u32[]{:S(2)}) collective-permute-start(f32[128,128]{1,0:T(8,128)S(1)} %get-tuple-element.206), channel_id=1, source_target_pairs={{0,8},{8,0},{16,24},{24,16},{1,9},{9,1},{17,25},{25,17},{2,10},{10... | collective-permute-start | bytes 196616 | tf_op jit(solution)/shard_map/ppermute | solution.py:376
  274.2 2.2 collective-permute-start.38
  276.6 2.8 collective-permute-done.38
  279.4 2.2 collective-permute-done.39
  286.7 2.5 collective-permute-start.41
  289.1 1.8 collective-permute-done.40
  290.9 1.9 collective-permute-start.42
  292.8 4.1 %collective-permute-done.42 = f32[128,128]{1,0:T(8,128)S(1)} collective-permute-done((f32[128,128]{1,0:T(8,128)S(1)}, f32[128,128]{1,0:T(8,128)S(1)}, u32[]{:S(2)}, u32[]{:S(2)}) %collective-permute-start.42) | collective-permute-done | bytes 65568 | tf_op jit(solution)/shard_map/ppermute | solution.py:366
  298.5 2.5 collective-permute-done.46
  302.8 2.7 collective-permute-start.48
  306.4 2.1 collective-permute-done.48
  308.5 2.2 collective-permute-done.49
  310.8 2.5 collective-permute-start.52
  313.2 1.9 collective-permute-start.53
  316.1 7.5 %shard_map.49 = f32[512,128]{1,0:T(8,128)} custom-call(s32[10]{0:T(128)} %stack.100.where, f32[4,512,4096]{2,1,0:T(8,128)} %weights.13, f32[512,128]{1,0:T(8,128)} %copy-done.5, f32[512,128]{1,0:T(8,128)} %copy-done.10, f32[512,128]{1,0:T(8,128)} %copy-done.11, f32[512,128]{1,0:T(8,128)} %copy-done.12, ...), custom_call_target="tpu_custom_call", output_to_operand_aliasing={{}: (10, {})} | custom-call | flops 1610612736 | bytes 8388608 | tf_op jit(solution)/shard_map/pallas_call | solution.py:188
  325.3 2.6 fusion.12
  328.1 3.4 collective-permute-start.57
  334.7 2.5 collective-permute-start.59
  337.2 1.9 collective-permute-start.60
  339.1 1.8 collective-permute-start.61
  340.9 1.7 collective-permute-start.62
  346.4 2.1 collective-permute-done.63
  351.9 2.9 collective-permute-start.67
  357.1 2.0 collective-permute-start.68
  361.8 2.0 collective-permute-done.69
  363.8 2.1 collective-permute-done.70
  (166 shorter events, 50.7 us)
Async XLA Ops:
  0.0 27.7 %collective-permute-start = (f32[4,512,128]{2,1,0:T(8,128)}, f32[4,512,128]{2,1,0:T(8,128)S(1)}, u32[]{:S(2)}, u32[]{:S(2)}) collective-permute-start(f32[4,512,128]{2,1,0:T(8,128)} %refs_0_.2), channel_id=1, source_target_pairs={{0,2},{1,3},{2,4},{3,5},{4,6},{5,7},{8,10},{9,11},{10,12},{11,13},... | collective-permute-start | bytes 3145736 | tf_op jit(solution)/shard_map/ppermute | solution.py:223
  5.0 26.7 %collective-permute-start.1 = (f32[4,512,128]{2,1,0:T(8,128)}, f32[4,512,128]{2,1,0:T(8,128)S(1)}, u32[]{:S(2)}, u32[]{:S(2)}) collective-permute-start(f32[4,512,128]{2,1,0:T(8,128)} %refs_0_.2), channel_id=1, source_target_pairs={{2,0},{3,1},{4,2},{5,3},{6,4},{7,5},{10,8},{11,9},{12,10},{13,11},... | collective-permute-start | bytes 3145736 | tf_op jit(solution)/shard_map/ppermute | solution.py:223
  6.3 25.4 %collective-permute-start.3 = (f32[4,512,128]{2,1,0:T(8,128)}, f32[4,512,128]{2,1,0:T(8,128)}, u32[]{:S(2)}, u32[]{:S(2)}) collective-permute-start(f32[4,512,128]{2,1,0:T(8,128)} %refs_0_.2), channel_id=1, source_target_pairs={{0,1},{1,0},{2,3},{3,2},{4,5},{5,4},{6,7},{7,6},{8,9},{9,8},{10,11... | collective-permute-start | bytes 3145736 | tf_op jit(solution)/shard_map/ppermute | solution.py:220
  7.5 15.2 %collective-permute-start.2 = (f32[2,512,128]{2,1,0:T(8,128)S(1)}, f32[2,512,128]{2,1,0:T(8,128)}, u32[]{:S(2)}, u32[]{:S(2)}) collective-permute-start(f32[2,512,128]{2,1,0:T(8,128)S(1)} %slice_select_fusion), channel_id=1, source_target_pairs={{0,8},{8,16},{16,24},{1,9},{9,17},{17,25},{2,10},{10,18},{18,26},{... | collective-permute-start | bytes 1572872 | tf_op jit(solution)/shard_map/ppermute | solution.py:384
  31.9 14.3 %collective-permute-start.6 = (f32[4,512,128]{2,1,0:T(8,128)S(1)}, f32[4,512,128]{2,1,0:T(8,128)}, u32[]{:S(2)}, u32[]{:S(2)}) collective-permute-start(f32[4,512,128]{2,1,0:T(8,128)S(1)} %broadcast_select_fusion.refs_2_), channel_id=1, source_target_pairs={{0,1},{1,0},{2,3},{3,2},{4,5},{5,4},{6,7},{7,6},{8,9},{9,8},{10,11... | collective-permute-start | bytes 3145736 | tf_op jit(solution)/shard_map/ppermute | solution.py:220
  32.0 30.9 %collective-permute-start.4 = (f32[4,512,128]{2,1,0:T(8,128)}, f32[4,512,128]{2,1,0:T(8,128)S(1)}, u32[]{:S(2)}, u32[]{:S(2)}) collective-permute-start(f32[4,512,128]{2,1,0:T(8,128)} %copy-done.14), channel_id=1, source_target_pairs={{2,4},{3,5},{4,6},{5,7},{10,12},{11,13},{12,14},{13,15},{18,20},{1... | collective-permute-start | bytes 3145736 | tf_op jit(solution)/shard_map/ppermute | solution.py:223
  32.7 30.1 %collective-permute-start.5 = (f32[4,512,128]{2,1,0:T(8,128)S(1)}, f32[4,512,128]{2,1,0:T(8,128)}, u32[]{:S(2)}, u32[]{:S(2)}) collective-permute-start(f32[4,512,128]{2,1,0:T(8,128)S(1)} %collective-permute-done.1), channel_id=1, source_target_pairs={{2,0},{3,1},{4,2},{5,3},{10,8},{11,9},{12,10},{13,11},{18,16},{19,... | collective-permute-start | bytes 3145736 | tf_op jit(solution)/shard_map/ppermute | solution.py:223
  41.1 26.8 %collective-permute-start.9 = (f32[512,512]{1,0:T(8,128)}, f32[512,512]{1,0:T(8,128)}, u32[]{:S(2)}, u32[]{:S(2)}) collective-permute-start(f32[512,512]{1,0:T(8,128)} %get-tuple-element.104), channel_id=1, source_target_pairs={{0,16},{1,17},{2,18},{3,19},{4,20},{5,21},{6,22},{7,23}} | collective-permute-start | bytes 3145736 | tf_op jit(solution)/shard_map/ppermute | solution.py:395
  67.9 18.7 %collective-permute-start.7 = (f32[4,512,128]{2,1,0:T(8,128)S(1)}, f32[4,512,128]{2,1,0:T(8,128)}, u32[]{:S(2)}, u32[]{:S(2)}) collective-permute-start(f32[4,512,128]{2,1,0:T(8,128)S(1)} %collective-permute-done.4), channel_id=1, source_target_pairs={{4,6},{5,7},{12,14},{13,15},{20,22},{21,23},{28,30},{29,31}} | collective-permute-start | bytes 3145736 | tf_op jit(solution)/shard_map/ppermute | solution.py:223
  69.5 30.1 %collective-permute-start.8 = (f32[4,512,128]{2,1,0:T(8,128)}, f32[4,512,128]{2,1,0:T(8,128)}, u32[]{:S(2)}, u32[]{:S(2)}) collective-permute-start(f32[4,512,128]{2,1,0:T(8,128)} %collective-permute-done.5), channel_id=1, source_target_pairs={{2,0},{3,1},{10,8},{11,9},{18,16},{19,17},{26,24},{27,25}} | collective-permute-start | bytes 3145736 | tf_op jit(solution)/shard_map/ppermute | solution.py:223
  71.0 11.7 %collective-permute-start.11 = (f32[2,512,128]{2,1,0:T(8,128)}, f32[2,512,128]{2,1,0:T(8,128)}, u32[]{:S(2)}, u32[]{:S(2)}) collective-permute-start(f32[2,512,128]{2,1,0:T(8,128)} %collective-permute-done.2.refs_0_), channel_id=1, source_target_pairs={{0,1},{1,0},{2,3},{3,2},{4,5},{5,4},{6,7},{7,6},{8,9},{9,8},{10,11... | collective-permute-start | bytes 1572872 | tf_op jit(solution)/shard_map/ppermute | solution.py:220
  101.1 7.8 %collective-permute-start.12 = (f32[4,512,128]{2,1,0:T(8,128)S(1)}, f32[4,512,128]{2,1,0:T(8,128)S(1)}, u32[]{:S(2)}, u32[]{:S(2)}) collective-permute-start(f32[4,512,128]{2,1,0:T(8,128)S(1)} %select_select_fusion.near.near_before), channel_id=1, source_target_pairs={{0,1},{1,0},{2,3},{3,2},{4,5},{5,4},{6,7},{7,6},{8,9},{9,8},{10,11... | collective-permute-start | bytes 3145736 | tf_op jit(solution)/shard_map/ppermute | solution.py:220
  101.1 95.0 %collective-permute-start.19 = (f32[512,1024]{1,0:T(8,128)}, f32[512,1024]{1,0:T(8,128)}, u32[]{:S(2)}, u32[]{:S(2)}) collective-permute-start(f32[512,1024]{1,0:T(8,128)} %get-tuple-element.132), channel_id=1, source_target_pairs={{0,8},{1,9},{2,10},{3,11},{4,12},{5,13},{6,14},{7,15}} | collective-permute-start | bytes 6291464 | tf_op jit(solution)/shard_map/ppermute | solution.py:396
  103.8 92.4 %collective-permute-start.20 = (f32[512,1024]{1,0:T(8,128)}, f32[512,1024]{1,0:T(8,128)}, u32[]{:S(2)}, u32[]{:S(2)}) collective-permute-start(f32[512,1024]{1,0:T(8,128)} %get-tuple-element.133), channel_id=1, source_target_pairs={{0,16},{1,17},{2,18},{3,19},{4,20},{5,21},{6,22},{7,23}} | collective-permute-start | bytes 6291464 | tf_op jit(solution)/shard_map/ppermute | solution.py:396
  118.3 31.6 %collective-permute-start.13 = (f32[128,128]{1,0:T(8,128)S(1)}, f32[128,128]{1,0:T(8,128)S(1)}, u32[]{:S(2)}, u32[]{:S(2)}) collective-permute-start(f32[128,128]{1,0:T(8,128)S(1)} %get-tuple-element.212), channel_id=1, source_target_pairs={{0,8},{8,0},{16,24},{24,16},{1,9},{9,1},{17,25},{25,17},{2,10},{10... | collective-permute-start | bytes 196616 | tf_op jit(solution)/shard_map/ppermute | solution.py:376
  118.3 36.3 %collective-permute-start.14 = (f32[128,128]{1,0:T(8,128)S(1)}, f32[128,128]{1,0:T(8,128)S(1)}, u32[]{:S(2)}, u32[]{:S(2)}) collective-permute-start(f32[128,128]{1,0:T(8,128)S(1)} %get-tuple-element.214), channel_id=1, source_target_pairs={{0,16},{8,24},{16,0},{24,8},{1,17},{9,25},{17,1},{25,9},{2,18},{10... | collective-permute-start | bytes 196616 | tf_op jit(solution)/shard_map/ppermute | solution.py:376
  118.4 77.8 %collective-permute-start.22 = (f32[512,512]{1,0:T(8,128)}, f32[512,512]{1,0:T(8,128)S(1)}, u32[]{:S(2)}, u32[]{:S(2)}) collective-permute-start(f32[512,512]{1,0:T(8,128)} %collective-permute-done.9), channel_id=1, source_target_pairs={{16,24},{17,25},{18,26},{19,27},{20,28},{21,29},{22,30},{23,31}} | collective-permute-start | bytes 3145736 | tf_op jit(solution)/shard_map/ppermute | solution.py:405
  149.9 46.4 %collective-permute-start.21 = (f32[512,512]{1,0:T(8,128)}, f32[512,512]{1,0:T(8,128)}, u32[]{:S(2)}, u32[]{:S(2)}) collective-permute-start(f32[512,512]{1,0:T(8,128)} %get-tuple-element.136), channel_id=1, source_target_pairs={{0,24},{1,25},{2,26},{3,27},{4,28},{5,29},{6,30},{7,31}} | collective-permute-start | bytes 3145736 | tf_op jit(solution)/shard_map/ppermute | solution.py:414
  154.6 20.9 %collective-permute-start.15 = (f32[128,128]{1,0:T(8,128)S(1)}, f32[128,128]{1,0:T(8,128)S(1)}, u32[]{:S(2)}, u32[]{:S(2)}) collective-permute-start(f32[128,128]{1,0:T(8,128)S(1)} %get-tuple-element.213), channel_id=1, source_target_pairs={{0,24},{8,16},{16,8},{24,0},{1,25},{9,17},{17,9},{25,1},{2,26},{10... | collective-permute-start | bytes 196616 | tf_op jit(solution)/shard_map/ppermute | solution.py:376
  180.7 6.0 %collective-permute-start.17 = (f32[128,128]{1,0:T(8,128)S(1)}, f32[128,128]{1,0:T(8,128)S(1)}, u32[]{:S(2)}, u32[]{:S(2)}) collective-permute-start(f32[128,128]{1,0:T(8,128)S(1)} %bitcast_subtract_fusion), channel_id=1, source_target_pairs={{0,4},{1,5},{2,6},{3,7},{4,0},{5,1},{6,2},{7,3},{8,12},{9,13},{10,... | collective-permute-start | bytes 196616 | tf_op jit(solution)/shard_map/ppermute | solution.py:366
  186.7 9.4 %collective-permute-start.18 = (f32[128,128]{1,0:T(8,128)S(1)}, f32[128,128]{1,0:T(8,128)S(1)}, u32[]{:S(2)}, u32[]{:S(2)}) collective-permute-start(f32[128,128]{1,0:T(8,128)S(1)} %bitcast_subtract_fusion), channel_id=1, source_target_pairs={{0,6},{1,7},{2,4},{3,5},{4,2},{5,3},{6,0},{7,1},{8,14},{9,15},{10,... | collective-permute-start | bytes 196616 | tf_op jit(solution)/shard_map/ppermute | solution.py:366
  196.2 12.0 %collective-permute-start.23 = (f32[512,128]{1,0:T(8,128)S(1)}, f32[512,128]{1,0:T(8,128)S(1)}, u32[]{:S(2)}, u32[]{:S(2)}) collective-permute-start(f32[512,128]{1,0:T(8,128)S(1)} %pad_maximum_fusion.2), channel_id=1, source_target_pairs={{0,1},{1,0},{2,3},{3,2},{4,5},{5,4},{6,7},{7,6},{8,9},{9,8},{10,11... | collective-permute-start | bytes 786440 | tf_op jit(solution)/shard_map/ppermute | solution.py:220
  196.3 48.5 %collective-permute-start.27 = (f32[2,512,128]{2,1,0:T(8,128)}, f32[2,512,128]{2,1,0:T(8,128)}, u32[]{:S(2)}, u32[]{:S(2)}) collective-permute-start(f32[2,512,128]{2,1,0:T(8,128)} %get-tuple-element.135), channel_id=1, source_target_pairs={{0,8},{8,16},{16,24},{1,9},{9,17},{17,25},{2,10},{10,18},{18,26},{... | collective-permute-start | bytes 1572872 | tf_op jit(solution)/shard_map/ppermute | solution.py:384
  198.4 46.4 %collective-permute-start.28 = (f32[2,512,128]{2,1,0:T(8,128)}, f32[2,512,128]{2,1,0:T(8,128)}, u32[]{:S(2)}, u32[]{:S(2)}) collective-permute-start(f32[2,512,128]{2,1,0:T(8,128)} %get-tuple-element.144), channel_id=1, source_target_pairs={{0,8},{8,16},{16,24},{1,9},{9,17},{17,25},{2,10},{10,18},{18,26},{... | collective-permute-start | bytes 1572872 | tf_op jit(solution)/shard_map/ppermute | solution.py:384
  200.5 44.3 %collective-permute-start.29 = (f32[2,512,128]{2,1,0:T(8,128)}, f32[2,512,128]{2,1,0:T(8,128)}, u32[]{:S(2)}, u32[]{:S(2)}) collective-permute-start(f32[2,512,128]{2,1,0:T(8,128)} %get-tuple-element.145), channel_id=1, source_target_pairs={{0,8},{8,16},{16,24},{1,9},{9,17},{17,25},{2,10},{10,18},{18,26},{... | collective-permute-start | bytes 1572872 | tf_op jit(solution)/shard_map/ppermute | solution.py:384
  209.9 23.9 %collective-permute-start.24 = (f32[128,128]{1,0:T(8,128)S(1)}, f32[128,128]{1,0:T(8,128)S(1)}, u32[]{:S(2)}, u32[]{:S(2)}) collective-permute-start(f32[128,128]{1,0:T(8,128)S(1)} %get-tuple-element.209), channel_id=1, source_target_pairs={{0,8},{8,0},{16,24},{24,16},{1,9},{9,1},{17,25},{25,17},{2,10},{10... | collective-permute-start | bytes 196616 | tf_op jit(solution)/shard_map/ppermute | solution.py:376
  209.9 34.0 %collective-permute-start.25 = (f32[128,128]{1,0:T(8,128)}, f32[128,128]{1,0:T(8,128)S(1)}, u32[]{:S(2)}, u32[]{:S(2)}) collective-permute-start(f32[128,128]{1,0:T(8,128)} %get-tuple-element.211), channel_id=1, source_target_pairs={{0,16},{8,24},{16,0},{24,8},{1,17},{9,25},{17,1},{25,9},{2,18},{10... | collective-permute-start | bytes 196616 | tf_op jit(solution)/shard_map/ppermute | solution.py:376
  233.8 10.1 %collective-permute-start.26 = (f32[128,128]{1,0:T(8,128)}, f32[128,128]{1,0:T(8,128)}, u32[]{:S(2)}, u32[]{:S(2)}) collective-permute-start(f32[128,128]{1,0:T(8,128)} %get-tuple-element.210), channel_id=1, source_target_pairs={{0,24},{8,16},{16,8},{24,0},{1,25},{9,17},{17,9},{25,1},{2,26},{10... | collective-permute-start | bytes 196616 | tf_op jit(solution)/shard_map/ppermute | solution.py:376
  244.8 12.4 %collective-permute-start.33 = (f32[2,512,128]{2,1,0:T(8,128)}, f32[2,512,128]{2,1,0:T(8,128)S(1)}, u32[]{:S(2)}, u32[]{:S(2)}) collective-permute-start(f32[2,512,128]{2,1,0:T(8,128)} %collective-permute-done.27.refs_0_), channel_id=1, source_target_pairs={{0,1},{1,0},{2,3},{3,2},{4,5},{5,4},{6,7},{7,6},{8,9},{9,8},{10,11... | collective-permute-start | bytes 1572872 | tf_op jit(solution)/shard_map/ppermute | solution.py:220
  244.9 12.4 %collective-permute-start.34 = (f32[2,512,128]{2,1,0:T(8,128)}, f32[2,512,128]{2,1,0:T(8,128)S(1)}, u32[]{:S(2)}, u32[]{:S(2)}) collective-permute-start(f32[2,512,128]{2,1,0:T(8,128)} %collective-permute-done.28.refs_2_), channel_id=1, source_target_pairs={{0,1},{1,0},{2,3},{3,2},{4,5},{5,4},{6,7},{7,6},{8,9},{9,8},{10,11... | collective-permute-start | bytes 1572872 | tf_op jit(solution)/shard_map/ppermute | solution.py:220
  245.4 11.9 %collective-permute-start.35 = (f32[2,512,128]{2,1,0:T(8,128)}, f32[2,512,128]{2,1,0:T(8,128)}, u32[]{:S(2)}, u32[]{:S(2)}) collective-permute-start(f32[2,512,128]{2,1,0:T(8,128)} %collective-permute-done.29.refs_4_), channel_id=1, source_target_pairs={{0,1},{1,0},{2,3},{3,2},{4,5},{5,4},{6,7},{7,6},{8,9},{9,8},{10,11... | collective-permute-start | bytes 1572872 | tf_op jit(solution)/shard_map/ppermute | solution.py:220
  245.4 5.7 %collective-permute-start.30 = (f32[128,128]{1,0:T(8,128)S(1)}, f32[128,128]{1,0:T(8,128)S(1)}, u32[]{:S(2)}, u32[]{:S(2)}) collective-permute-start(f32[128,128]{1,0:T(8,128)S(1)} %add_add_fusion.1), channel_id=1, source_target_pairs={{0,2},{1,3},{2,0},{3,1},{4,6},{5,7},{6,4},{7,5},{8,10},{9,11},{10,... | collective-permute-start | bytes 196616 | tf_op jit(solution)/shard_map/ppermute | solution.py:366
  245.5 7.6 %collective-permute-start.31 = (f32[128,128]{1,0:T(8,128)S(1)}, f32[128,128]{1,0:T(8,128)S(1)}, u32[]{:S(2)}, u32[]{:S(2)}) collective-permute-start(f32[128,128]{1,0:T(8,128)S(1)} %add_add_fusion.1), channel_id=1, source_target_pairs={{0,4},{1,5},{2,6},{3,7},{4,0},{5,1},{6,2},{7,3},{8,12},{9,13},{10,... | collective-permute-start | bytes 196616 | tf_op jit(solution)/shard_map/ppermute | solution.py:366
  251.1 6.1 %collective-permute-start.32 = (f32[128,128]{1,0:T(8,128)S(1)}, f32[128,128]{1,0:T(8,128)S(1)}, u32[]{:S(2)}, u32[]{:S(2)}) collective-permute-start(f32[128,128]{1,0:T(8,128)S(1)} %add_add_fusion.1), channel_id=1, source_target_pairs={{0,6},{1,7},{2,4},{3,5},{4,2},{5,3},{6,0},{7,1},{8,14},{9,15},{10,... | collective-permute-start | bytes 196616 | tf_op jit(solution)/shard_map/ppermute | solution.py:366
  267.7 8.9 %collective-permute-start.37 = (f32[128,128]{1,0:T(8,128)S(1)}, f32[128,128]{1,0:T(8,128)S(1)}, u32[]{:S(2)}, u32[]{:S(2)}) collective-permute-start(f32[128,128]{1,0:T(8,128)S(1)} %get-tuple-element.206), channel_id=1, source_target_pairs={{0,8},{8,0},{16,24},{24,16},{1,9},{9,1},{17,25},{25,17},{2,10},{10... | collective-permute-start | bytes 196616 | tf_op jit(solution)/shard_map/ppermute | solution.py:376
  274.2 5.2 %collective-permute-start.38 = (f32[128,128]{1,0:T(8,128)S(1)}, f32[128,128]{1,0:T(8,128)S(1)}, u32[]{:S(2)}, u32[]{:S(2)}) collective-permute-start(f32[128,128]{1,0:T(8,128)S(1)} %get-tuple-element.208), channel_id=1, source_target_pairs={{0,16},{8,24},{16,0},{24,8},{1,17},{9,25},{17,1},{25,9},{2,18},{10... | collective-permute-start | bytes 196616 | tf_op jit(solution)/shard_map/ppermute | solution.py:376
  276.4 5.2 %collective-permute-start.39 = (f32[128,128]{1,0:T(8,128)S(1)}, f32[128,128]{1,0:T(8,128)S(1)}, u32[]{:S(2)}, u32[]{:S(2)}) collective-permute-start(f32[128,128]{1,0:T(8,128)S(1)} %get-tuple-element.207), channel_id=1, source_target_pairs={{0,24},{8,16},{16,8},{24,0},{1,25},{9,17},{17,9},{25,1},{2,26},{10... | collective-permute-start | bytes 196616 | tf_op jit(solution)/shard_map/ppermute | solution.py:376
  282.4 14.6 %collective-permute-start.43 = (f32[512,128]{1,0:T(8,128)S(1)}, f32[512,128]{1,0:T(8,128)S(1)}, u32[]{:S(2)}, u32[]{:S(2)}) collective-permute-start(f32[512,128]{1,0:T(8,128)S(1)} %pad_maximum_fusion.3.refs_0_), channel_id=1, source_target_pairs={{8,0},{9,1},{10,2},{11,3},{12,4},{13,5},{14,6},{15,7}} | collective-permute-start | bytes 786440 | tf_op jit(solution)/shard_map/ppermute | solution.py:445
  283.7 14.1 %collective-permute-start.44 = (f32[512,128]{1,0:T(8,128)S(1)}, f32[512,128]{1,0:T(8,128)S(1)}, u32[]{:S(2)}, u32[]{:S(2)}) collective-permute-start(f32[512,128]{1,0:T(8,128)S(1)} %pad_maximum_fusion.3.refs_0_), channel_id=1, source_target_pairs={{16,0},{17,1},{18,2},{19,3},{20,4},{21,5},{22,6},{23,7}} | collective-permute-start | bytes 786440 | tf_op jit(solution)/shard_map/ppermute | solution.py:445
  285.0 12.9 %collective-permute-start.45 = (f32[512,128]{1,0:T(8,128)S(1)}, f32[512,128]{1,0:T(8,128)S(1)}, u32[]{:S(2)}, u32[]{:S(2)}) collective-permute-start(f32[512,128]{1,0:T(8,128)S(1)} %pad_maximum_fusion.3.refs_0_), channel_id=1, source_target_pairs={{24,0},{25,1},{26,2},{27,3},{28,4},{29,5},{30,6},{31,7}} | collective-permute-start | bytes 786440 | tf_op jit(solution)/shard_map/ppermute | solution.py:445
  286.7 6.2 %collective-permute-start.41 = (f32[128,128]{1,0:T(8,128)S(1)}, f32[128,128]{1,0:T(8,128)S(1)}, u32[]{:S(2)}, u32[]{:S(2)}) collective-permute-start(f32[128,128]{1,0:T(8,128)S(1)} %bitcast_subtract_fusion.1), channel_id=1, source_target_pairs={{0,4},{1,5},{2,6},{3,7},{4,0},{5,1},{6,2},{7,3},{8,12},{9,13},{10,... | collective-permute-start | bytes 196616 | tf_op jit(solution)/shard_map/ppermute | solution.py:366
  290.9 6.1 %collective-permute-start.42 = (f32[128,128]{1,0:T(8,128)S(1)}, f32[128,128]{1,0:T(8,128)S(1)}, u32[]{:S(2)}, u32[]{:S(2)}) collective-permute-start(f32[128,128]{1,0:T(8,128)S(1)} %bitcast_subtract_fusion.1), channel_id=1, source_target_pairs={{0,6},{1,7},{2,4},{3,5},{4,2},{5,3},{6,0},{7,1},{8,14},{9,15},{10,... | collective-permute-start | bytes 196616 | tf_op jit(solution)/shard_map/ppermute | solution.py:366
  298.0 12.7 %collective-permute-start.50 = (f32[4,512,128]{2,1,0:T(8,128)S(1)}, f32[4,512,128]{2,1,0:T(8,128)S(1)}, u32[]{:S(2)}, u32[]{:S(2)}) collective-permute-start(f32[4,512,128]{2,1,0:T(8,128)S(1)} %pad_maximum_fusion), channel_id=1, source_target_pairs={{0,1},{1,0},{2,3},{3,2},{4,5},{5,4},{6,7},{7,6},{8,9},{9,8},{10,11... | collective-permute-start | bytes 3145736 | tf_op jit(solution)/shard_map/ppermute | solution.py:220
  302.1 4.3 %collective-permute-start.47 = (f32[128,128]{1,0:T(8,128)S(1)}, f32[128,128]{1,0:T(8,128)S(1)}, u32[]{:S(2)}, u32[]{:S(2)}) collective-permute-start(f32[128,128]{1,0:T(8,128)S(1)} %get-tuple-element.203), channel_id=1, source_target_pairs={{0,8},{8,0},{16,24},{24,16},{1,9},{9,1},{17,25},{25,17},{2,10},{10... | collective-permute-start | bytes 196616 | tf_op jit(solution)/shard_map/ppermute | solution.py:376
  302.8 5.7 %collective-permute-start.48 = (f32[128,128]{1,0:T(8,128)S(1)}, f32[128,128]{1,0:T(8,128)S(1)}, u32[]{:S(2)}, u32[]{:S(2)}) collective-permute-start(f32[128,128]{1,0:T(8,128)S(1)} %get-tuple-element.205), channel_id=1, source_target_pairs={{0,16},{8,24},{16,0},{24,8},{1,17},{9,25},{17,1},{25,9},{2,18},{10... | collective-permute-start | bytes 196616 | tf_op jit(solution)/shard_map/ppermute | solution.py:376
  305.5 5.2 %collective-permute-start.49 = (f32[128,128]{1,0:T(8,128)S(1)}, f32[128,128]{1,0:T(8,128)S(1)}, u32[]{:S(2)}, u32[]{:S(2)}) collective-permute-start(f32[128,128]{1,0:T(8,128)S(1)} %get-tuple-element.204), channel_id=1, source_target_pairs={{0,24},{8,16},{16,8},{24,0},{1,25},{9,17},{17,9},{25,1},{2,26},{10... | collective-permute-start | bytes 196616 | tf_op jit(solution)/shard_map/ppermute | solution.py:376
  310.7 13.0 %collective-permute-start.51 = (f32[128,128]{1,0:T(8,128)S(1)}, f32[128,128]{1,0:T(8,128)S(1)}, u32[]{:S(2)}, u32[]{:S(2)}) collective-permute-start(f32[128,128]{1,0:T(8,128)S(1)} %add_add_fusion), channel_id=1, source_target_pairs={{0,2},{1,3},{2,0},{3,1},{4,6},{5,7},{6,4},{7,5},{8,10},{9,11},{10,... | collective-permute-start | bytes 196616 | tf_op jit(solution)/shard_map/ppermute | solution.py:366
  310.8 12.9 %collective-permute-start.52 = (f32[128,128]{1,0:T(8,128)S(1)}, f32[128,128]{1,0:T(8,128)S(1)}, u32[]{:S(2)}, u32[]{:S(2)}) collective-permute-start(f32[128,128]{1,0:T(8,128)S(1)} %add_add_fusion), channel_id=1, source_target_pairs={{0,4},{1,5},{2,6},{3,7},{4,0},{5,1},{6,2},{7,3},{8,12},{9,13},{10,... | collective-permute-start | bytes 196616 | tf_op jit(solution)/shard_map/ppermute | solution.py:366
  313.2 10.4 %collective-permute-start.53 = (f32[128,128]{1,0:T(8,128)S(1)}, f32[128,128]{1,0:T(8,128)S(1)}, u32[]{:S(2)}, u32[]{:S(2)}) collective-permute-start(f32[128,128]{1,0:T(8,128)S(1)} %add_add_fusion), channel_id=1, source_target_pairs={{0,6},{1,7},{2,4},{3,5},{4,2},{5,3},{6,0},{7,1},{8,14},{9,15},{10,... | collective-permute-start | bytes 196616 | tf_op jit(solution)/shard_map/ppermute | solution.py:366
  328.0 4.6 %collective-permute-start.55 = (f32[128,128]{1,0:T(8,128)S(1)}, f32[128,128]{1,0:T(8,128)S(1)}, u32[]{:S(2)}, u32[]{:S(2)}) collective-permute-start(f32[128,128]{1,0:T(8,128)S(1)} %get-tuple-element.200), channel_id=1, source_target_pairs={{0,8},{8,0},{16,24},{24,16},{1,9},{9,1},{17,25},{25,17},{2,10},{10... | collective-permute-start | bytes 196616 | tf_op jit(solution)/shard_map/ppermute | solution.py:376
  328.1 5.7 %collective-permute-start.56 = (f32[128,128]{1,0:T(8,128)S(1)}, f32[128,128]{1,0:T(8,128)S(1)}, u32[]{:S(2)}, u32[]{:S(2)}) collective-permute-start(f32[128,128]{1,0:T(8,128)S(1)} %get-tuple-element.202), channel_id=1, source_target_pairs={{0,16},{8,24},{16,0},{24,8},{1,17},{9,25},{17,1},{25,9},{2,18},{10... | collective-permute-start | bytes 196616 | tf_op jit(solution)/shard_map/ppermute | solution.py:376
  328.1 5.7 %collective-permute-start.57 = (f32[128,128]{1,0:T(8,128)S(1)}, f32[128,128]{1,0:T(8,128)S(1)}, u32[]{:S(2)}, u32[]{:S(2)}) collective-permute-start(f32[128,128]{1,0:T(8,128)S(1)} %get-tuple-element.201), channel_id=1, source_target_pairs={{0,24},{8,16},{16,8},{24,0},{1,25},{9,17},{17,9},{25,1},{2,26},{10... | collective-permute-start | bytes 196616 | tf_op jit(solution)/shard_map/ppermute | solution.py:376
  334.7 8.0 %collective-permute-start.58 = (f32[128,128]{1,0:T(8,128)S(1)}, f32[128,128]{1,0:T(8,128)S(1)}, u32[]{:S(2)}, u32[]{:S(2)}) collective-permute-start(f32[128,128]{1,0:T(8,128)S(1)} %bitcast_subtract_fusion.2), channel_id=1, source_target_pairs={{0,2},{1,3},{2,0},{3,1},{4,6},{5,7},{6,4},{7,5},{8,10},{9,11},{10,... | collective-permute-start | bytes 196616 | tf_op jit(solution)/shard_map/ppermute | solution.py:366
  334.7 7.9 %collective-permute-start.59 = (f32[128,128]{1,0:T(8,128)S(1)}, f32[128,128]{1,0:T(8,128)S(1)}, u32[]{:S(2)}, u32[]{:S(2)}) collective-permute-start(f32[128,128]{1,0:T(8,128)S(1)} %bitcast_subtract_fusion.2), channel_id=1, source_target_pairs={{0,4},{1,5},{2,6},{3,7},{4,0},{5,1},{6,2},{7,3},{8,12},{9,13},{10,... | collective-permute-start | bytes 196616 | tf_op jit(solution)/shard_map/ppermute | solution.py:366
  337.2 6.1 %collective-permute-start.60 = (f32[128,128]{1,0:T(8,128)S(1)}, f32[128,128]{1,0:T(8,128)S(1)}, u32[]{:S(2)}, u32[]{:S(2)}) collective-permute-start(f32[128,128]{1,0:T(8,128)S(1)} %bitcast_subtract_fusion.2), channel_id=1, source_target_pairs={{0,6},{1,7},{2,4},{3,5},{4,2},{5,3},{6,0},{7,1},{8,14},{9,15},{10,... | collective-permute-start | bytes 196616 | tf_op jit(solution)/shard_map/ppermute | solution.py:366
  339.1 5.7 %collective-permute-start.61 = (f32[2,128,128]{2,1,0:T(8,128)S(1)}, f32[2,128,128]{2,1,0:T(8,128)S(1)}, u32[]{:S(2)}, u32[]{:S(2)}) collective-permute-start(f32[2,128,128]{2,1,0:T(8,128)S(1)} %pad_maximum_fusion.7), channel_id=1, source_target_pairs={{0,8},{8,0},{16,24},{24,16},{1,9},{9,1},{17,25},{25,17},{2,10},{10... | collective-permute-start | bytes 393224 | tf_op jit(solution)/shard_map/ppermute | solution.py:380
  340.9 5.5 %collective-permute-start.62 = (f32[2,128,128]{2,1,0:T(8,128)S(1)}, f32[2,128,128]{2,1,0:T(8,128)S(1)}, u32[]{:S(2)}, u32[]{:S(2)}) collective-permute-start(f32[2,128,128]{2,1,0:T(8,128)S(1)} %pad_maximum_fusion.7), channel_id=1, source_target_pairs={{0,16},{8,24},{16,0},{24,8},{1,17},{9,25},{17,1},{25,9},{2,18},{10... | collective-permute-start | bytes 393224 | tf_op jit(solution)/shard_map/ppermute | solution.py:380
  342.7 5.9 %collective-permute-start.63 = (f32[2,128,128]{2,1,0:T(8,128)S(1)}, f32[2,128,128]{2,1,0:T(8,128)S(1)}, u32[]{:S(2)}, u32[]{:S(2)}) collective-permute-start(f32[2,128,128]{2,1,0:T(8,128)S(1)} %pad_maximum_fusion.7), channel_id=1, source_target_pairs={{0,24},{8,16},{16,8},{24,0},{1,25},{9,17},{17,9},{25,1},{2,26},{10... | collective-permute-start | bytes 393224 | tf_op jit(solution)/shard_map/ppermute | solution.py:380
  351.3 4.6 %collective-permute-start.65 = (f32[128,128]{1,0:T(8,128)S(1)}, f32[128,128]{1,0:T(8,128)S(1)}, u32[]{:S(2)}, u32[]{:S(2)}) collective-permute-start(f32[128,128]{1,0:T(8,128)S(1)} %get-tuple-element.197), channel_id=1, source_target_pairs={{0,8},{8,0},{16,24},{24,16},{1,9},{9,1},{17,25},{25,17},{2,10},{10... | collective-permute-start | bytes 196616 | tf_op jit(solution)/shard_map/ppermute | solution.py:376
  351.4 5.0 %collective-permute-start.66 = (f32[128,128]{1,0:T(8,128)S(1)}, f32[128,128]{1,0:T(8,128)S(1)}, u32[]{:S(2)}, u32[]{:S(2)}) collective-permute-start(f32[128,128]{1,0:T(8,128)S(1)} %get-tuple-element.199), channel_id=1, source_target_pairs={{0,16},{8,24},{16,0},{24,8},{1,17},{9,25},{17,1},{25,9},{2,18},{10... | collective-permute-start | bytes 196616 | tf_op jit(solution)/shard_map/ppermute | solution.py:376
  351.9 5.2 %collective-permute-start.67 = (f32[128,128]{1,0:T(8,128)S(1)}, f32[128,128]{1,0:T(8,128)S(1)}, u32[]{:S(2)}, u32[]{:S(2)}) collective-permute-start(f32[128,128]{1,0:T(8,128)S(1)} %get-tuple-element.198), channel_id=1, source_target_pairs={{0,24},{8,16},{16,8},{24,0},{1,25},{9,17},{17,9},{25,1},{2,26},{10... | collective-permute-start | bytes 196616 | tf_op jit(solution)/shard_map/ppermute | solution.py:376
  357.1 4.6 %collective-permute-start.68 = (f32[1,128,128]{2,1,0:T(8,128)S(1)}, f32[1,128,128]{2,1,0:T(8,128)S(1)}, u32[]{:S(2)}, u32[]{:S(2)}) collective-permute-start(f32[1,128,128]{2,1,0:T(8,128)S(1)} %add_bitcast_fusion), channel_id=1, source_target_pairs={{0,8},{8,0},{16,24},{24,16},{1,9},{9,1},{17,25},{25,17},{2,10},{10... | collective-permute-start | bytes 196616 | tf_op jit(solution)/shard_map/ppermute | solution.py:380
  359.1 4.6 %collective-permute-start.69 = (f32[1,128,128]{2,1,0:T(8,128)S(1)}, f32[1,128,128]{2,1,0:T(8,128)S(1)}, u32[]{:S(2)}, u32[]{:S(2)}) collective-permute-start(f32[1,128,128]{2,1,0:T(8,128)S(1)} %add_bitcast_fusion), channel_id=1, source_target_pairs={{0,16},{8,24},{16,0},{24,8},{1,17},{9,25},{17,1},{25,9},{2,18},{10... | collective-permute-start | bytes 196616 | tf_op jit(solution)/shard_map/ppermute | solution.py:380
  360.7 5.2 %collective-permute-start.70 = (f32[1,128,128]{2,1,0:T(8,128)S(1)}, f32[1,128,128]{2,1,0:T(8,128)S(1)}, u32[]{:S(2)}, u32[]{:S(2)}) collective-permute-start(f32[1,128,128]{2,1,0:T(8,128)S(1)} %add_bitcast_fusion), channel_id=1, source_target_pairs={{0,24},{8,16},{16,8},{24,0},{1,25},{9,17},{17,9},{25,1},{2,26},{10... | collective-permute-start | bytes 196616 | tf_op jit(solution)/shard_map/ppermute | solution.py:380
  (25 other events, 212.2 us)

commit v3 on v2

--- a/solution.py
+++ b/solution.py
@@ -103,50 +103,51 @@
 
 
 def entered_kernel(where, weights, *refs):
-    pieces, (one, two, one_out, two_out, high, low) = refs[:-6], refs[-6:]
-    number, at = pl.program_id(0), pl.program_id(1)
-    before, rows, width = pieces[0].shape
-
-    @pl.when(jnp.logical_and(number == 0, at == 0))
+    pieces, (one, two, one_out, two_out) = refs[:-4], refs[-4:]
+    number = pl.program_id(0)
+    width = pieces[0].shape[2]
+
+    @pl.when(number == 0)
     def _():
         one_out[...] = one[...]
         two_out[...] = two[...]
 
     for i in range(len(pieces) // 2):
 
-        @pl.when(jnp.logical_and(number == i, at == 0))
-        def _():
-            for k in range(before):
-                columns = slice((before - 1 - k) * width, (before - k) * width)
-                for piece, side in ((pieces[2 * i], where[0]), (pieces[2 * i + 1], 1 - where[0])):
-                    here = pl.ds(pl.multiple_of(side * rows, rows), rows)
-                    high[here, columns], low[here, columns] = split(piece[k])
-
-    for k in range(before):
-
-        @pl.when(jnp.logical_and(where[1] > 0, at == k))
-        def _():
-            size = (before - k) * width
-            wh, wl = split(weights[0])
-            h = high[:, :size]
-            main = dot(wh, jnp.concatenate([h, low[:, :size]], axis=1))
-            result = main[:, :size] + main[:, size:] + dot(wl, h)
-            if k == 0:
-                one_out[...] += result[:, :width]
-            two_out[...] += result[:, size - width :]
+        @pl.when(jnp.logical_and(where[1] > 0, number == i))
+        def _():
+            near, far = pieces[2 * i : 2 * i + 2]
+            result = product(weights[0], [ordered(where[0], near[k], far[k]) for k in (1, 0)])
+            one_out[...] += result[:, :width]
+            two_out[...] += result[:, width:]
 
 
 def second_kernel(where, weights, *refs):
-    nears, fars, total, out = refs[: len(refs) // 2 - 1], refs[len(refs) // 2 - 1 : -2], refs[-2], refs[-1]
-
-    @pl.when(pl.program_id(0) == 0)
+    (fars, total, out, vector), operands = refs[-4:], refs[:-4]
+    groups = fars.shape[0]
+    chips = (len(operands) - groups) // 2
+    nears, pieces = operands[:groups], operands[groups:]
+    rows, number = vector.shape[0] // 2, pl.program_id(0)
+    part = rows // groups
+
+    @pl.when(number == 0)
     def _():
         out[...] = total[...]
 
     @pl.when(where[1] == 0)
     def _():
-        near, far = (jnp.concatenate([p[...] for p in parts], axis=0) for parts in (nears, fars))
-        out[...] += product(weights[0], [ordered(where[0], near, far)])
+        here = pl.ds(pl.multiple_of(number * part, part), part)
+        near = jnp.concatenate([p[here, :] for p in nears], axis=0)
+        far = jnp.concatenate([fars[j, here, :] for j in range(groups)], axis=0)
+        vector[...] = ordered(where[0], near, far)
+
+    for i in range(chips):
+
+        @pl.when(jnp.logical_and(where[1] > 0, number == i))
+        def _():
+            vector[...] = ordered(where[0], pieces[2 * i][0], pieces[2 * i + 1][0])
+
+    out[...] += product(weights[0], [vector[...]])
 
 
 def columns_kernel(where, *refs):
@@ -303,23 +304,23 @@
             2, square, (12 * lags * tile * width, 4 * lags * tile), {6: 0, 7: 1},
         )
 
-    def add_entered(one, two, nears, stage):
-        pieces = [v for near in nears for v in (near, other_core(near))]
-        spec = pl.BlockSpec((1, rows, 2 * rows), lambda i, k, w: (jnp.where(w[1] > 0, k, 0), 0, jnp.where(w[1] > 0, w[2 + stage + i], 0)))
+    def add_entered(one, two, pieces, stage):
+        count = len(pieces) // 2
+        spec = pl.BlockSpec((1, rows, 2 * rows), lambda i, w: (0, 0, jnp.where(w[1] > 0, w[2 + stage + i], 0)))
         return call(
-            entered_kernel, where, (len(nears), STEPS - 1), (lag_weights, *pieces, one, two),
+            entered_kernel, where, (count,), (lag_weights, *pieces, one, two),
             [spec] + [all_of(v.shape) for v in (*pieces, one, two)],
-            2, square, (18 * len(nears) * tile * width, 8 * len(nears) * tile), {2 + len(pieces): 0, 3 + len(pieces): 1},
-            [pltpu.VMEM((2 * rows, (STEPS - 1) * width), BF16)] * 2,
+            2, square, (12 * count * tile * width, 4 * count * tile), {2 + len(pieces): 0, 3 + len(pieces): 1},
         )
 
-    def add_second(total, nears, fars):
-        block = pl.BlockSpec((part, width), lambda k, w: (k, 0))
+    def add_second(total, nears, pieces, fars):
+        spec = pl.BlockSpec((1, rows, 2 * rows), lambda i, w: (1, 0, w[2 + i + jnp.where(w[1] == 0, chips, 0)]))
+        last = pl.BlockSpec((1, rows, width), lambda i, w: (STEPS - 2, 0, 0))
         return call(
-            second_kernel, where, (chips,), (lag_weights, *nears, *fars, total),
-            [pl.BlockSpec((1, rows, 2 * rows), lambda k, w: (1, 0, jnp.where(w[1] == 0, w[2 + chips + k], 0)))]
-            + [block] * 2 * groups + [all_of(square)],
-            1, square, (6 * rows * order * width, 4 * rows * order), {2 + 2 * groups: 0},
+            second_kernel, where, (chips,), (lag_weights, *nears, *pieces, fars, total),
+            [spec] + [all_of(v.shape) for v in nears] + [last] * len(pieces) + [all_of(fars.shape), all_of(square)],
+            1, square, (6 * rows * order * width, 4 * rows * order), {3 + len(nears) + len(pieces): 0},
+            [pltpu.VMEM((2 * rows, width), F32)],
         )[0]
 
     slots = jnp.stack([(chip ^ k) * 2 + (core ^ h) for h in (0, 1) for k in range(chips)]).astype(jnp.int32)
@@ -396,7 +397,7 @@
     sent = [lax.ppermute(chunks[j], "lag", [(0, j)]) for j in range(1, groups - 1)]
     (head_columns,) = columns(inverse_head[None], False)
     ups[1], downs[1], entered, own_far, head_columns = tie((ups[1], downs[1], entered, own_far, head_columns))
-    totals, waiting = [], []
+    totals = []
     for stage in range(1, chips - 1):
         next_up, next_down = go_up(ups[stage], stage + 1), go_down(downs[stage], stage + 1)
         near = choose(stage, ups, downs)
@@ -407,15 +408,13 @@
         if stage == 1:
             pieces = [history, own_far, *pieces]
         totals, tail = add_chip(totals, pieces, stage if stage > 1 else 0)
-        if stage < chips - 2:
-            entered.append(enter(tail))
-            if stage == 1:
-                last_near, tail = tie((last_near, tail))
-                late = lax.ppermute(last_near, "lag", [(0, groups - 1)])
-                sent.append(late)
-        else:
-            waiting.append(tail)
-            totals = [totals[0], *add_entered(totals[1], totals[2], entered[:1], 0)]
+        entered.append(enter(tail))
+        if stage == 1:
+            last_near, tail = tie((last_near, tail))
+            sent.append(lax.ppermute(last_near, "lag", [(0, groups - 1)]))
+        if stage == chips - 2:
+            both = [entered[0], other_core(entered[0])]
+            totals = [totals[0], *add_entered(totals[1], totals[2], both, 0)]
         ups[stage + 1], downs[stage + 1] = next_up, next_down
         ups, downs, totals = tie((ups, downs, totals))
     first, one, two = totals
@@ -425,9 +424,9 @@
     first, tail = add_first(first, near, far, chips - 1)
 
     right_side = own_part(excitation[0]) - sum_parts(first)
-    right_side, waiting, tail, near, far, one, two = tie((right_side, waiting, tail, near, far, one, two))
+    right_side, tail, near, far, one, two = tie((right_side, tail, near, far, one, two))
     mine = gather_near(right_side)
-    entered += [enter(value) for value in (*waiting, tail)]
+    entered.append(enter(tail))
     one, two = add_rest(one, two, near, far, chips - 1)
     mine, one, two, sent = tie((mine, one, two, sent))
     density = sum_parts(multiply(head_columns, mine))
@@ -436,21 +435,22 @@
 
     density, first_columns, entered, one, two = tie((density, first_columns, entered, one, two))
     mine = gather_near(density)
-    one, two = add_entered(one, two, entered[1:], 1)
-    mine, one, two = tie((mine, one, two))
+    both += [v for piece in entered[1:] for v in (piece, other_core(piece))]
+    one, two = add_entered(one, two, both[2:], 1)
+    mine, one, two, both = tie((mine, one, two, both))
     right_side = own_part(excitation[1]) - sum_parts(one + multiply(first_columns, mine))
 
-    right_side, two, old = tie((right_side, two, mine))
+    right_side, two, old, both = tie((right_side, two, mine, both))
     mine = gather_near(right_side)
     nears = [old] + [lax.ppermute(old, "lag", [(j, 0)]) for j in range(1, groups)]
-    mine, two, nears = tie((mine, two, nears))
+    mine, two = tie((mine, two))
     density = sum_parts(multiply(head_columns, mine))
     fars = other_core(jnp.stack(nears))
     results.append(density)
 
     density, two, nears, fars = tie((density, two, nears, fars))
     mine = gather_near(density)
-    two = add_second(two, nears, [fars[j] for j in range(groups)])
+    two = add_second(two, nears, both, fars)
     mine, two = tie((mine, two))
     right_side = own_part(excitation[2]) - sum_parts(two + multiply(first_columns, mine))
 

time: 368 us -> 363 us (0.986)
  starting transfers between devices: 102 us -> 97.8 us
    ppermute x15, waiting for transfers between devices: 23.7 us -> 17.7 us  [gather_near(): lax.ppermute(value, 'row', pairs(devices, 2 * k))]
    ppermute x6, waiting for transfers between devices: 10.3 us -> 4.47 us  [whole_rows(): lax.ppermute(value, 'lag', pairs(groups, mask))]
    ppermute x3, waiting for transfers between devices: 0.85 us -> 6.47 us  [on_device(): lax.ppermute(old, 'lag', [(j, 0)])]
    ppermute x18, starting transfers between devices: 25.6 us -> 21.9 us  [sum_parts(): result = result + lax.ppermute(sent, 'lag', pairs(groups, mask))]
  transfers between devices with their start and end apart: 71 -> 71, of which waited for: 38 -> 37; matrix products, arithmetic and copies ran while one was open for 3% -> 3% of each run, Pallas kernels for 19% -> 20%
where the time goes in v3:
time: 363 us; the launch traced here: 362 us
  waiting for transfers between devices  160 us (44%)
  starting transfers between devices  97.8 us (27%)
  Pallas kernels  75 us (21%)
  local copies, waits for them, and re-layouts  11.2 us (3%)
  other arithmetic  9.16 us (3%)
  matrix products  8.11 us (2%)
    ppermute x18, waiting for transfers between devices, sum_parts(): result = result + lax.ppermute(sent, 'lag', pairs(groups, mask))  93.5 us
    pallas_call x2, Pallas kernels, add_chip(): pl.pallas_call(chip_kernel, out_shape=[jax.ShapeDtypeStruct(square, F32)]...  26.7 us
    pallas_call x4, Pallas kernels, call(): pl.pallas_call(kernel, out_shape=[jax.ShapeDtypeStruct(shape, F32)] * cou...  24 us
    ppermute x6, waiting for transfers between devices, along(): lax.ppermute(value, 'row', [(2 * i + c, 2 * (i + step) + c) for i in sour...  22.7 us
    ppermute x18, starting transfers between devices, sum_parts(): result = result + lax.ppermute(sent, 'lag', pairs(groups, mask))  21.9 us
    ppermute x15, starting transfers between devices, gather_near(): lax.ppermute(value, 'row', pairs(devices, 2 * k))  19.8 us
    ppermute x15, waiting for transfers between devices, gather_near(): lax.ppermute(value, 'row', pairs(devices, 2 * k))  17.7 us
    ppermute x4, starting transfers between devices, enter(): return lax.ppermute(tail, 'lag', [(i, i + 1) for i in range(groups - 1)])  16.1 us
  transfers between devices with their start and end apart: 71, of which 37 were waited for; matrix products, arithmetic and copies ran while one was open for 3% of the time, Pallas kernels for 20%

profile of v3, /device:TPU:0, one launch (start us, length us, event | category | flops | bytes accessed | tf_op | source)
XLA Modules:
  0.0 361.6 jit_solution(3080303233290949128)
XLA Ops:
  0.0 5.0 %collective-permute-start = (f32[4,512,128]{2,1,0:T(8,128)}, f32[4,512,128]{2,1,0:T(8,128)S(1)}, u32[]{:S(2)}, u32[]{:S(2)}) collective-permute-start(f32[4,512,128]{2,1,0:T(8,128)} %refs_0_.2), channel_id=1, source_target_pairs={{0,2},{1,3},{2,4},{3,5},{4,6},{5,7},{8,10},{9,11},{10,12},{11,13},... | collective-permute-start | bytes 3145736 | tf_op jit(solution)/shard_map/ppermute | solution.py:224
  7.5 4.2 %collective-permute-start.2 = (f32[2,512,128]{2,1,0:T(8,128)S(1)}, f32[2,512,128]{2,1,0:T(8,128)}, u32[]{:S(2)}, u32[]{:S(2)}) collective-permute-start(f32[2,512,128]{2,1,0:T(8,128)S(1)} %slice_select_fusion), channel_id=1, source_target_pairs={{0,8},{8,16},{16,24},{1,9},{9,17},{17,25},{2,10},{10,18},{18,26},{... | collective-permute-start | bytes 1572872 | tf_op jit(solution)/shard_map/ppermute | solution.py:385
  12.6 5.8 %columns.2 = f32[512,1024]{1,0:T(8,128)} custom-call(s32[2,5,4]{2,1,0:T(8,128)} %concatenate.43.where, f32[1,512,4096]{2,1,0:T(8,128)} %bitcast.37, f32[1,512,4096]{2,1,0:T(8,128)} %bitcast.38, f32[1,512,4096]{2,1,0:T(8,128)} %bitcast.39, f32[1,512,4096]{2,1,0:T(8,128)} %bitcast.40), custom_call_target="tpu_custom_call" | custom-call | bytes 16777216 | tf_op jit(solution)/shard_map/columns/pallas_call | solution.py:336
  18.3 4.4 %collective-permute-done.2.refs_0_.refs_4_ = f32[2,512,128]{2,1,0:T(8,128)} collective-permute-done((f32[2,512,128]{2,1,0:T(8,128)S(1)}, f32[2,512,128]{2,1,0:T(8,128)}, u32[]{:S(2)}, u32[]{:S(2)}) %collective-permute-start.2) | collective-permute-done | bytes 524320 | tf_op jit(solution)/shard_map/ppermute | solution.py:385
  22.7 5.0 %collective-permute-done = f32[4,512,128]{2,1,0:T(8,128)S(1)} collective-permute-done((f32[4,512,128]{2,1,0:T(8,128)}, f32[4,512,128]{2,1,0:T(8,128)S(1)}, u32[]{:S(2)}, u32[]{:S(2)}) %collective-permute-start) | collective-permute-done | bytes 1048608 | tf_op jit(solution)/shard_map/ppermute | solution.py:224
  27.7 4.1 %collective-permute-done.1 = f32[4,512,128]{2,1,0:T(8,128)S(1)} collective-permute-done((f32[4,512,128]{2,1,0:T(8,128)}, f32[4,512,128]{2,1,0:T(8,128)S(1)}, u32[]{:S(2)}, u32[]{:S(2)}) %collective-permute-start.1) | collective-permute-done | bytes 1048608 | tf_op jit(solution)/shard_map/ppermute | solution.py:224
  34.0 7.1 %columns.3 = (f32[512,1024]{1,0:T(8,128)}, f32[512,1024]{1,0:T(8,128)}, f32[512,1024]{1,0:T(8,128)}, f32[512,512]{1,0:T(8,128)}, f32[512,512]{1,0:T(8,128)}) custom-call(s32[2,5,4]{2,1,0:T(8,128)} %concatenate.43.where, f32[4,512,4096]{2,1,0:T(8,128)} %weights.13, f32[4,512,4096]{2,1,0:T(8,128)} %weights.13, f32[4,512,4096]{2,1,0:T(8,128)} %weights.13, ...), custom_call_target="tpu_custom_call" | custom-call | bytes 16777216 | tf_op jit(solution)/shard_map/columns/pallas_call | solution.py:336
  41.1 4.5 %collective-permute-start.9 = (f32[512,512]{1,0:T(8,128)}, f32[512,512]{1,0:T(8,128)}, u32[]{:S(2)}, u32[]{:S(2)}) collective-permute-start(f32[512,512]{1,0:T(8,128)} %get-tuple-element.115), channel_id=1, source_target_pairs={{0,16},{1,17},{2,18},{3,19},{4,20},{5,21},{6,22},{7,23}} | collective-permute-start | bytes 3145736 | tf_op jit(solution)/shard_map/ppermute | solution.py:396
  46.2 16.6 %chip.2 = (f32[512,128]{1,0:T(8,128)}, f32[512,128]{1,0:T(8,128)}, f32[512,128]{1,0:T(8,128)}, f32[2,512,128]{2,1,0:T(8,128)}) custom-call(s32[10]{0:T(128)} %stack.100.where, f32[4,512,4096]{2,1,0:T(8,128)} %weights.13, f32[4,512,128]{2,1,0:T(8,128)} %refs_0_.2, f32[4,512,128]{2,1,0:T(8,128)} %collective-permute-done.3.refs_1_, f32[4,512,128]{2,1,0:T(8,128)} %copy-done.7, ...), custom_call_target="tpu_custom_call" | custom-call | flops 9663676416 | bytes 16777216 | tf_op jit(solution)/shard_map/chip/pallas_call | solution.py:265
  62.9 1.7 select_select_fusion.1.refs_0_
  64.6 3.3 collective-permute-done.9
  67.9 1.6 collective-permute-start.7
  71.4 10.1 %chip.3 = (f32[512,128]{1,0:T(8,128)}, f32[512,128]{1,0:T(8,128)}, f32[512,128]{1,0:T(8,128)}, f32[2,512,128]{2,1,0:T(8,128)}) custom-call(s32[10]{0:T(128)} %stack.100.where, f32[4,512,4096]{2,1,0:T(8,128)} %weights.13, f32[4,512,128]{2,1,0:T(8,128)} %copy-done.6, ...), custom_call_target="tpu_custom_call", output_to_operand_aliasing={{0}: (4, {}), {1}: (5, {}), {2}: (6, {})} | custom-call | flops 4831838208 | bytes 8388608 | tf_op jit(solution)/shard_map/chip/pallas_call | solution.py:265
  82.3 3.6 %shard_map.46 = (f32[512,128]{1,0:T(8,128)}, f32[512,128]{1,0:T(8,128)}) custom-call(s32[10]{0:T(128)} %stack.100.where, f32[4,512,4096]{2,1,0:T(8,128)} %weights.13, f32[2,512,128]{2,1,0:T(8,128)} %collective-permute-done.2.refs_0_.refs_4_, f32[2,512,128]{2,1,0:T(8,128)} %copy-done.10, ...), custom_call_target="tpu_custom_call", output_to_operand_aliasing={{0}: (4, {}), {1}: (5, {})} | custom-call | flops 805306368 | bytes 2097152 | tf_op jit(solution)/shard_map/pallas_call | solution.py:189
  85.9 13.7 %collective-permute-done.8 = f32[4,512,128]{2,1,0:T(8,128)} collective-permute-done((f32[4,512,128]{2,1,0:T(8,128)}, f32[4,512,128]{2,1,0:T(8,128)}, u32[]{:S(2)}, u32[]{:S(2)}) %collective-permute-start.8) | collective-permute-done | bytes 1048608 | tf_op jit(solution)/shard_map/ppermute | solution.py:224
  101.1 2.8 collective-permute-start.19
  103.9 5.1 %collective-permute-start.20 = (f32[512,1024]{1,0:T(8,128)}, f32[512,1024]{1,0:T(8,128)}, u32[]{:S(2)}, u32[]{:S(2)}) collective-permute-start(f32[512,1024]{1,0:T(8,128)} %get-tuple-element.143), channel_id=1, source_target_pairs={{0,16},{1,17},{2,18},{3,19},{4,20},{5,21},{6,22},{7,23}} | collective-permute-start | bytes 6291464 | tf_op jit(solution)/shard_map/ppermute | solution.py:397
  110.0 7.5 %first.1 = (f32[512,128]{1,0:T(8,128)}, f32[2,512,128]{2,1,0:T(8,128)}) custom-call(s32[10]{0:T(128)} %stack.100.where, f32[4,512,4096]{2,1,0:T(8,128)} %weights.13, f32[4,512,128]{2,1,0:T(8,128)} %copy-done.1, f32[4,512,128]{2,1,0:T(8,128)} %copy-done.3, f32[512,128]{1,0:T(8,128)} %get-tuple-element.130.total), custom_call_target="tpu_custom_call", output_to_operand_aliasing={{0}: (4, {})} | custom-call | flops 1610612736 | bytes 8388608 | tf_op jit(solution)/shard_map/first/pallas_call | solution.py:285
  119.4 30.5 %collective-permute-done.13 = f32[128,128]{1,0:T(8,128)S(1)} collective-permute-done((f32[128,128]{1,0:T(8,128)S(1)}, f32[128,128]{1,0:T(8,128)S(1)}, u32[]{:S(2)}, u32[]{:S(2)}) %collective-permute-start.13) | collective-permute-done | bytes 65568 | tf_op jit(solution)/shard_map/ppermute | solution.py:377
  149.8 2.3 collective-permute-start.21
  152.1 2.7 collective-permute-done.14
  154.8 2.0 fusion.25
  156.8 18.7 %collective-permute-done.15 = f32[128,128]{1,0:T(8,128)S(1)} collective-permute-done((f32[128,128]{1,0:T(8,128)S(1)}, f32[128,128]{1,0:T(8,128)S(1)}, u32[]{:S(2)}, u32[]{:S(2)}) %collective-permute-start.15) | collective-permute-done | bytes 65568 | tf_op jit(solution)/shard_map/ppermute | solution.py:377
  176.5 4.3 %collective-permute-done.16 = f32[128,128]{1,0:T(8,128)S(1)} collective-permute-done((f32[128,128]{1,0:T(8,128)S(1)}, f32[128,128]{1,0:T(8,128)S(1)}, u32[]{:S(2)}, u32[]{:S(2)}) %collective-permute-start.16) | collective-permute-done | bytes 65568 | tf_op jit(solution)/shard_map/ppermute | solution.py:367
  181.0 5.7 %collective-permute-done.17 = f32[128,128]{1,0:T(8,128)S(1)} collective-permute-done((f32[128,128]{1,0:T(8,128)S(1)}, f32[128,128]{1,0:T(8,128)S(1)}, u32[]{:S(2)}, u32[]{:S(2)}) %collective-permute-start.17) | collective-permute-done | bytes 65568 | tf_op jit(solution)/shard_map/ppermute | solution.py:367
  186.7 1.8 collective-permute-start.18
  188.5 7.6 %shard_map.47 = (f32[512,128]{1,0:T(8,128)}, f32[512,128]{1,0:T(8,128)}) custom-call(s32[10]{0:T(128)} %stack.100.where, f32[4,512,4096]{2,1,0:T(8,128)} %weights.13, f32[4,512,128]{2,1,0:T(8,128)} %copy-done.1, f32[4,512,128]{2,1,0:T(8,128)} %copy-done.1, f32[4,512,128]{2,1,0:T(8,128)} %copy-done.3, ...), custom_call_target="tpu_custom_call", output_to_operand_aliasing={{0}: (6, {}), {1}: (7, {})} | custom-call | flops 3221225472 | bytes 8388608 | tf_op jit(solution)/shard_map/pallas_call | solution.py:189
  199.8 9.2 %collective-permute-start.29 = (f32[2,512,128]{2,1,0:T(8,128)}, f32[2,512,128]{2,1,0:T(8,128)}, u32[]{:S(2)}, u32[]{:S(2)}) collective-permute-start(f32[2,512,128]{2,1,0:T(8,128)} %get-tuple-element.155), channel_id=1, source_target_pairs={{0,8},{8,16},{16,24},{1,9},{9,17},{17,25},{2,10},{10,18},{18,26},{... | collective-permute-start | bytes 1572872 | tf_op jit(solution)/shard_map/ppermute | solution.py:385
  210.7 23.9 %collective-permute-done.24 = f32[128,128]{1,0:T(8,128)S(1)} collective-permute-done((f32[128,128]{1,0:T(8,128)S(1)}, f32[128,128]{1,0:T(8,128)S(1)}, u32[]{:S(2)}, u32[]{:S(2)}) %collective-permute-start.24) | collective-permute-done | bytes 65568 | tf_op jit(solution)/shard_map/ppermute | solution.py:377
  234.6 6.1 %collective-permute-start.26 = (f32[128,128]{1,0:T(8,128)}, f32[128,128]{1,0:T(8,128)}, u32[]{:S(2)}, u32[]{:S(2)}) collective-permute-start(f32[128,128]{1,0:T(8,128)} %get-tuple-element.228), channel_id=1, source_target_pairs={{0,24},{8,16},{16,8},{24,0},{1,25},{9,17},{17,9},{25,1},{2,26},{10... | collective-permute-start | bytes 196616 | tf_op jit(solution)/shard_map/ppermute | solution.py:377
  240.8 3.9 %pick.1 = f32[512,1024]{1,0:T(8,128)} custom-call(s32[1]{0:T(128)} %bitcast.13.which, f32[512,1024]{1,0:T(8,128)} %get-tuple-element.149.refs_0_, f32[512,1024]{1,0:T(8,128)} %collective-permute-done.19.refs_1_, f32[512,1024]{1,0:T(8,128)} %collective-permute-done.20.refs_2_, f32[512,512]{1,0:T(8,128)} %collective-permute-done.21.refs_3_, f32[512,512]{1,0:T(8,128)} %copy-done.20), custom_call_target="tpu_custom_call" | custom-call | bytes 8388608 | tf_op jit(solution)/shard_map/pick/pallas_call | solution.py:352
  246.9 2.7 collective-permute-start.31
  249.6 3.0 collective-permute-done.30
  252.6 2.1 collective-permute-start.32
  254.7 3.9 %collective-permute-done.32 = f32[128,128]{1,0:T(8,128)S(1)} collective-permute-done((f32[128,128]{1,0:T(8,128)S(1)}, f32[128,128]{1,0:T(8,128)S(1)}, u32[]{:S(2)}, u32[]{:S(2)}) %collective-permute-start.32) | collective-permute-done | bytes 65568 | tf_op jit(solution)/shard_map/ppermute | solution.py:367
  260.4 4.3 %shard_map.48 = (f32[512,128]{1,0:T(8,128)}, f32[512,128]{1,0:T(8,128)}) custom-call(s32[10]{0:T(128)} %stack.100.where, f32[4,512,4096]{2,1,0:T(8,128)} %weights.13, f32[2,512,128]{2,1,0:T(8,128)} %copy-done.11, f32[2,512,128]{2,1,0:T(8,128)} %copy-done.13, f32[2,512,128]{2,1,0:T(8,128)} %copy-done.12, ...), custom_call_target="tpu_custom_call", output_to_operand_aliasing={{0}: (8, {}), {1}: (9, {})} | custom-call | flops 2415919104 | bytes 6291456 | tf_op jit(solution)/shard_map/pallas_call | solution.py:189
  264.7 1.5 collective-permute-done.36
  266.2 2.6 fusion.4
  268.9 3.4 collective-permute-start.37
  272.3 1.6 collective-permute-start.38
  274.7 1.9 collective-permute-done.38
  276.6 2.5 collective-permute-done.39
  284.1 2.7 collective-permute-start.41
  286.8 1.7 collective-permute-done.47.refs_1_
  288.5 2.1 collective-permute-start.42
  290.6 4.8 %collective-permute-done.48.refs_2_ = f32[512,128]{1,0:T(8,128)S(1)} collective-permute-done((f32[512,128]{1,0:T(8,128)S(1)}, f32[512,128]{1,0:T(8,128)S(1)}, u32[]{:S(2)}, u32[]{:S(2)}) %collective-permute-start.48) | collective-permute-done | bytes 262176 | tf_op jit(solution)/shard_map/ppermute | solution.py:445
  296.2 2.4 collective-permute-done.43
  299.8 3.4 collective-permute-start.46
  306.5 1.8 collective-permute-start.52
  308.3 1.7 collective-permute-start.53
  310.0 8.5 %shard_map.49 = f32[512,128]{1,0:T(8,128)} custom-call(s32[10]{0:T(128)} %stack.100.where, f32[4,512,4096]{2,1,0:T(8,128)} %weights.13, f32[512,128]{1,0:T(8,128)} %copy-done.5, f32[512,128]{1,0:T(8,128)} %copy-done.15, f32[512,128]{1,0:T(8,128)} %copy-done.16, f32[512,128]{1,0:T(8,128)} %copy-done.17, ...), custom_call_target="tpu_custom_call", output_to_operand_aliasing={{}: (15, {})} | custom-call | flops 1610612736 | bytes 8388608 | tf_op jit(solution)/shard_map/pallas_call | solution.py:189
  320.1 2.6 fusion.12
  322.8 1.8 collective-permute-start.55
  324.5 1.7 collective-permute-start.56
  327.1 1.7 collective-permute-done.56
  328.8 2.6 collective-permute-done.57
  332.4 2.7 collective-permute-start.59
  335.0 1.7 collective-permute-start.60
  337.4 2.9 collective-permute-start.63
  346.1 2.0 collective-permute-start.65
  348.0 1.5 collective-permute-start.66
  350.5 1.9 collective-permute-done.66
  352.3 2.4 collective-permute-done.67
  355.4 2.9 collective-permute-start.70
  (173 shorter events, 49.2 us)
Async XLA Ops:
  0.0 27.7 %collective-permute-start = (f32[4,512,128]{2,1,0:T(8,128)}, f32[4,512,128]{2,1,0:T(8,128)S(1)}, u32[]{:S(2)}, u32[]{:S(2)}) collective-permute-start(f32[4,512,128]{2,1,0:T(8,128)} %refs_0_.2), channel_id=1, source_target_pairs={{0,2},{1,3},{2,4},{3,5},{4,6},{5,7},{8,10},{9,11},{10,12},{11,13},... | collective-permute-start | bytes 3145736 | tf_op jit(solution)/shard_map/ppermute | solution.py:224
  5.0 26.7 %collective-permute-start.1 = (f32[4,512,128]{2,1,0:T(8,128)}, f32[4,512,128]{2,1,0:T(8,128)S(1)}, u32[]{:S(2)}, u32[]{:S(2)}) collective-permute-start(f32[4,512,128]{2,1,0:T(8,128)} %refs_0_.2), channel_id=1, source_target_pairs={{2,0},{3,1},{4,2},{5,3},{6,4},{7,5},{10,8},{11,9},{12,10},{13,11},... | collective-permute-start | bytes 3145736 | tf_op jit(solution)/shard_map/ppermute | solution.py:224
  6.3 25.4 %collective-permute-start.3 = (f32[4,512,128]{2,1,0:T(8,128)}, f32[4,512,128]{2,1,0:T(8,128)}, u32[]{:S(2)}, u32[]{:S(2)}) collective-permute-start(f32[4,512,128]{2,1,0:T(8,128)} %refs_0_.2), channel_id=1, source_target_pairs={{0,1},{1,0},{2,3},{3,2},{4,5},{5,4},{6,7},{7,6},{8,9},{9,8},{10,11... | collective-permute-start | bytes 3145736 | tf_op jit(solution)/shard_map/ppermute | solution.py:221
  7.5 15.2 %collective-permute-start.2 = (f32[2,512,128]{2,1,0:T(8,128)S(1)}, f32[2,512,128]{2,1,0:T(8,128)}, u32[]{:S(2)}, u32[]{:S(2)}) collective-permute-start(f32[2,512,128]{2,1,0:T(8,128)S(1)} %slice_select_fusion), channel_id=1, source_target_pairs={{0,8},{8,16},{16,24},{1,9},{9,17},{17,25},{2,10},{10,18},{18,26},{... | collective-permute-start | bytes 1572872 | tf_op jit(solution)/shard_map/ppermute | solution.py:385
  31.9 14.3 %collective-permute-start.6 = (f32[4,512,128]{2,1,0:T(8,128)S(1)}, f32[4,512,128]{2,1,0:T(8,128)}, u32[]{:S(2)}, u32[]{:S(2)}) collective-permute-start(f32[4,512,128]{2,1,0:T(8,128)S(1)} %broadcast_select_fusion.refs_2_), channel_id=1, source_target_pairs={{0,1},{1,0},{2,3},{3,2},{4,5},{5,4},{6,7},{7,6},{8,9},{9,8},{10,11... | collective-permute-start | bytes 3145736 | tf_op jit(solution)/shard_map/ppermute | solution.py:221
  32.0 30.9 %collective-permute-start.4 = (f32[4,512,128]{2,1,0:T(8,128)}, f32[4,512,128]{2,1,0:T(8,128)S(1)}, u32[]{:S(2)}, u32[]{:S(2)}) collective-permute-start(f32[4,512,128]{2,1,0:T(8,128)} %copy-done.19), channel_id=1, source_target_pairs={{2,4},{3,5},{4,6},{5,7},{10,12},{11,13},{12,14},{13,15},{18,20},{1... | collective-permute-start | bytes 3145736 | tf_op jit(solution)/shard_map/ppermute | solution.py:224
  32.7 30.2 %collective-permute-start.5 = (f32[4,512,128]{2,1,0:T(8,128)S(1)}, f32[4,512,128]{2,1,0:T(8,128)}, u32[]{:S(2)}, u32[]{:S(2)}) collective-permute-start(f32[4,512,128]{2,1,0:T(8,128)S(1)} %collective-permute-done.1), channel_id=1, source_target_pairs={{2,0},{3,1},{4,2},{5,3},{10,8},{11,9},{12,10},{13,11},{18,16},{19,... | collective-permute-start | bytes 3145736 | tf_op jit(solution)/shard_map/ppermute | solution.py:224
  41.1 26.8 %collective-permute-start.9 = (f32[512,512]{1,0:T(8,128)}, f32[512,512]{1,0:T(8,128)}, u32[]{:S(2)}, u32[]{:S(2)}) collective-permute-start(f32[512,512]{1,0:T(8,128)} %get-tuple-element.115), channel_id=1, source_target_pairs={{0,16},{1,17},{2,18},{3,19},{4,20},{5,21},{6,22},{7,23}} | collective-permute-start | bytes 3145736 | tf_op jit(solution)/shard_map/ppermute | solution.py:396
  67.9 18.0 %collective-permute-start.7 = (f32[4,512,128]{2,1,0:T(8,128)S(1)}, f32[4,512,128]{2,1,0:T(8,128)}, u32[]{:S(2)}, u32[]{:S(2)}) collective-permute-start(f32[4,512,128]{2,1,0:T(8,128)S(1)} %collective-permute-done.4), channel_id=1, source_target_pairs={{4,6},{5,7},{12,14},{13,15},{20,22},{21,23},{28,30},{29,31}} | collective-permute-start | bytes 3145736 | tf_op jit(solution)/shard_map/ppermute | solution.py:224
  69.5 30.1 %collective-permute-start.8 = (f32[4,512,128]{2,1,0:T(8,128)}, f32[4,512,128]{2,1,0:T(8,128)}, u32[]{:S(2)}, u32[]{:S(2)}) collective-permute-start(f32[4,512,128]{2,1,0:T(8,128)} %collective-permute-done.5), channel_id=1, source_target_pairs={{2,0},{3,1},{10,8},{11,9},{18,16},{19,17},{26,24},{27,25}} | collective-permute-start | bytes 3145736 | tf_op jit(solution)/shard_map/ppermute | solution.py:224
  70.8 10.7 %collective-permute-start.11 = (f32[2,512,128]{2,1,0:T(8,128)}, f32[2,512,128]{2,1,0:T(8,128)S(1)}, u32[]{:S(2)}, u32[]{:S(2)}) collective-permute-start(f32[2,512,128]{2,1,0:T(8,128)} %collective-permute-done.2.refs_0_.refs_4_), channel_id=1, source_target_pairs={{0,1},{1,0},{2,3},{3,2},{4,5},{5,4},{6,7},{7,6},{8,9},{9,8},{10,11... | collective-permute-start | bytes 1572872 | tf_op jit(solution)/shard_map/ppermute | solution.py:221
  101.1 8.0 %collective-permute-start.12 = (f32[4,512,128]{2,1,0:T(8,128)S(1)}, f32[4,512,128]{2,1,0:T(8,128)S(1)}, u32[]{:S(2)}, u32[]{:S(2)}) collective-permute-start(f32[4,512,128]{2,1,0:T(8,128)S(1)} %select_select_fusion.near.near_before), channel_id=1, source_target_pairs={{0,1},{1,0},{2,3},{3,2},{4,5},{5,4},{6,7},{7,6},{8,9},{9,8},{10,11... | collective-permute-start | bytes 3145736 | tf_op jit(solution)/shard_map/ppermute | solution.py:221
  101.1 94.9 %collective-permute-start.19 = (f32[512,1024]{1,0:T(8,128)}, f32[512,1024]{1,0:T(8,128)}, u32[]{:S(2)}, u32[]{:S(2)}) collective-permute-start(f32[512,1024]{1,0:T(8,128)} %get-tuple-element.142), channel_id=1, source_target_pairs={{0,8},{1,9},{2,10},{3,11},{4,12},{5,13},{6,14},{7,15}} | collective-permute-start | bytes 6291464 | tf_op jit(solution)/shard_map/ppermute | solution.py:397
  103.9 92.2 %collective-permute-start.20 = (f32[512,1024]{1,0:T(8,128)}, f32[512,1024]{1,0:T(8,128)}, u32[]{:S(2)}, u32[]{:S(2)}) collective-permute-start(f32[512,1024]{1,0:T(8,128)} %get-tuple-element.143), channel_id=1, source_target_pairs={{0,16},{1,17},{2,18},{3,19},{4,20},{5,21},{6,22},{7,23}} | collective-permute-start | bytes 6291464 | tf_op jit(solution)/shard_map/ppermute | solution.py:397
  118.5 31.4 %collective-permute-start.13 = (f32[128,128]{1,0:T(8,128)S(1)}, f32[128,128]{1,0:T(8,128)S(1)}, u32[]{:S(2)}, u32[]{:S(2)}) collective-permute-start(f32[128,128]{1,0:T(8,128)S(1)} %get-tuple-element.230), channel_id=1, source_target_pairs={{0,8},{8,0},{16,24},{24,16},{1,9},{9,1},{17,25},{25,17},{2,10},{10... | collective-permute-start | bytes 196616 | tf_op jit(solution)/shard_map/ppermute | solution.py:377
  118.6 36.3 %collective-permute-start.14 = (f32[128,128]{1,0:T(8,128)S(1)}, f32[128,128]{1,0:T(8,128)S(1)}, u32[]{:S(2)}, u32[]{:S(2)}) collective-permute-start(f32[128,128]{1,0:T(8,128)S(1)} %get-tuple-element.232), channel_id=1, source_target_pairs={{0,16},{8,24},{16,0},{24,8},{1,17},{9,25},{17,1},{25,9},{2,18},{10... | collective-permute-start | bytes 196616 | tf_op jit(solution)/shard_map/ppermute | solution.py:377
  118.6 77.5 %collective-permute-start.22 = (f32[512,512]{1,0:T(8,128)}, f32[512,512]{1,0:T(8,128)S(1)}, u32[]{:S(2)}, u32[]{:S(2)}) collective-permute-start(f32[512,512]{1,0:T(8,128)} %collective-permute-done.9), channel_id=1, source_target_pairs={{16,24},{17,25},{18,26},{19,27},{20,28},{21,29},{22,30},{23,31}} | collective-permute-start | bytes 3145736 | tf_op jit(solution)/shard_map/ppermute | solution.py:406
  149.8 46.3 %collective-permute-start.21 = (f32[512,512]{1,0:T(8,128)}, f32[512,512]{1,0:T(8,128)}, u32[]{:S(2)}, u32[]{:S(2)}) collective-permute-start(f32[512,512]{1,0:T(8,128)} %get-tuple-element.146), channel_id=1, source_target_pairs={{0,24},{1,25},{2,26},{3,27},{4,28},{5,29},{6,30},{7,31}} | collective-permute-start | bytes 3145736 | tf_op jit(solution)/shard_map/ppermute | solution.py:414
  154.8 20.7 %collective-permute-start.15 = (f32[128,128]{1,0:T(8,128)S(1)}, f32[128,128]{1,0:T(8,128)S(1)}, u32[]{:S(2)}, u32[]{:S(2)}) collective-permute-start(f32[128,128]{1,0:T(8,128)S(1)} %get-tuple-element.231), channel_id=1, source_target_pairs={{0,24},{8,16},{16,8},{24,0},{1,25},{9,17},{17,9},{25,1},{2,26},{10... | collective-permute-start | bytes 196616 | tf_op jit(solution)/shard_map/ppermute | solution.py:377
  176.4 4.3 %collective-permute-start.16 = (f32[128,128]{1,0:T(8,128)S(1)}, f32[128,128]{1,0:T(8,128)S(1)}, u32[]{:S(2)}, u32[]{:S(2)}) collective-permute-start(f32[128,128]{1,0:T(8,128)S(1)} %bitcast_subtract_fusion), channel_id=1, source_target_pairs={{0,2},{1,3},{2,0},{3,1},{4,6},{5,7},{6,4},{7,5},{8,10},{9,11},{10,... | collective-permute-start | bytes 196616 | tf_op jit(solution)/shard_map/ppermute | solution.py:367
  180.7 6.0 %collective-permute-start.17 = (f32[128,128]{1,0:T(8,128)S(1)}, f32[128,128]{1,0:T(8,128)S(1)}, u32[]{:S(2)}, u32[]{:S(2)}) collective-permute-start(f32[128,128]{1,0:T(8,128)S(1)} %bitcast_subtract_fusion), channel_id=1, source_target_pairs={{0,4},{1,5},{2,6},{3,7},{4,0},{5,1},{6,2},{7,3},{8,12},{9,13},{10,... | collective-permute-start | bytes 196616 | tf_op jit(solution)/shard_map/ppermute | solution.py:367
  186.7 9.3 %collective-permute-start.18 = (f32[128,128]{1,0:T(8,128)S(1)}, f32[128,128]{1,0:T(8,128)S(1)}, u32[]{:S(2)}, u32[]{:S(2)}) collective-permute-start(f32[128,128]{1,0:T(8,128)S(1)} %bitcast_subtract_fusion), channel_id=1, source_target_pairs={{0,6},{1,7},{2,4},{3,5},{4,2},{5,3},{6,0},{7,1},{8,14},{9,15},{10,... | collective-permute-start | bytes 196616 | tf_op jit(solution)/shard_map/ppermute | solution.py:367
  197.1 11.9 %collective-permute-start.23 = (f32[512,128]{1,0:T(8,128)S(1)}, f32[512,128]{1,0:T(8,128)S(1)}, u32[]{:S(2)}, u32[]{:S(2)}) collective-permute-start(f32[512,128]{1,0:T(8,128)S(1)} %pad_maximum_fusion.2), channel_id=1, source_target_pairs={{0,1},{1,0},{2,3},{3,2},{4,5},{5,4},{6,7},{7,6},{8,9},{9,8},{10,11... | collective-permute-start | bytes 786440 | tf_op jit(solution)/shard_map/ppermute | solution.py:221
  197.1 49.1 %collective-permute-start.27 = (f32[2,512,128]{2,1,0:T(8,128)}, f32[2,512,128]{2,1,0:T(8,128)S(1)}, u32[]{:S(2)}, u32[]{:S(2)}) collective-permute-start(f32[2,512,128]{2,1,0:T(8,128)} %get-tuple-element.145), channel_id=1, source_target_pairs={{0,8},{8,16},{16,24},{1,9},{9,17},{17,25},{2,10},{10,18},{18,26},{... | collective-permute-start | bytes 1572872 | tf_op jit(solution)/shard_map/ppermute | solution.py:385
  198.5 47.8 %collective-permute-start.28 = (f32[2,512,128]{2,1,0:T(8,128)}, f32[2,512,128]{2,1,0:T(8,128)S(1)}, u32[]{:S(2)}, u32[]{:S(2)}) collective-permute-start(f32[2,512,128]{2,1,0:T(8,128)} %get-tuple-element.154), channel_id=1, source_target_pairs={{0,8},{8,16},{16,24},{1,9},{9,17},{17,25},{2,10},{10,18},{18,26},{... | collective-permute-start | bytes 1572872 | tf_op jit(solution)/shard_map/ppermute | solution.py:385
  199.8 46.5 %collective-permute-start.29 = (f32[2,512,128]{2,1,0:T(8,128)}, f32[2,512,128]{2,1,0:T(8,128)}, u32[]{:S(2)}, u32[]{:S(2)}) collective-permute-start(f32[2,512,128]{2,1,0:T(8,128)} %get-tuple-element.155), channel_id=1, source_target_pairs={{0,8},{8,16},{16,24},{1,9},{9,17},{17,25},{2,10},{10,18},{18,26},{... | collective-permute-start | bytes 1572872 | tf_op jit(solution)/shard_map/ppermute | solution.py:385
  210.7 23.9 %collective-permute-start.24 = (f32[128,128]{1,0:T(8,128)S(1)}, f32[128,128]{1,0:T(8,128)S(1)}, u32[]{:S(2)}, u32[]{:S(2)}) collective-permute-start(f32[128,128]{1,0:T(8,128)S(1)} %get-tuple-element.227), channel_id=1, source_target_pairs={{0,8},{8,0},{16,24},{24,16},{1,9},{9,1},{17,25},{25,17},{2,10},{10... | collective-permute-start | bytes 196616 | tf_op jit(solution)/shard_map/ppermute | solution.py:377
  210.7 34.0 %collective-permute-start.25 = (f32[128,128]{1,0:T(8,128)}, f32[128,128]{1,0:T(8,128)S(1)}, u32[]{:S(2)}, u32[]{:S(2)}) collective-permute-start(f32[128,128]{1,0:T(8,128)} %get-tuple-element.229), channel_id=1, source_target_pairs={{0,16},{8,24},{16,0},{24,8},{1,17},{9,25},{17,1},{25,9},{2,18},{10... | collective-permute-start | bytes 196616 | tf_op jit(solution)/shard_map/ppermute | solution.py:377
  234.6 10.7 %collective-permute-start.26 = (f32[128,128]{1,0:T(8,128)}, f32[128,128]{1,0:T(8,128)}, u32[]{:S(2)}, u32[]{:S(2)}) collective-permute-start(f32[128,128]{1,0:T(8,128)} %get-tuple-element.228), channel_id=1, source_target_pairs={{0,24},{8,16},{16,8},{24,0},{1,25},{9,17},{17,9},{25,1},{2,26},{10... | collective-permute-start | bytes 196616 | tf_op jit(solution)/shard_map/ppermute | solution.py:377
  246.3 12.4 %collective-permute-start.33 = (f32[2,512,128]{2,1,0:T(8,128)S(1)}, f32[2,512,128]{2,1,0:T(8,128)S(1)}, u32[]{:S(2)}, u32[]{:S(2)}) collective-permute-start(f32[2,512,128]{2,1,0:T(8,128)S(1)} %collective-permute-done.27.refs_0_.refs_6_), channel_id=1, source_target_pairs={{0,1},{1,0},{2,3},{3,2},{4,5},{5,4},{6,7},{7,6},{8,9},{9,8},{10,11... | collective-permute-start | bytes 1572872 | tf_op jit(solution)/shard_map/ppermute | solution.py:221
  246.4 12.4 %collective-permute-start.34 = (f32[2,512,128]{2,1,0:T(8,128)S(1)}, f32[2,512,128]{2,1,0:T(8,128)S(1)}, u32[]{:S(2)}, u32[]{:S(2)}) collective-permute-start(f32[2,512,128]{2,1,0:T(8,128)S(1)} %collective-permute-done.28.refs_2_.refs_8_), channel_id=1, source_target_pairs={{0,1},{1,0},{2,3},{3,2},{4,5},{5,4},{6,7},{7,6},{8,9},{9,8},{10,11... | collective-permute-start | bytes 1572872 | tf_op jit(solution)/shard_map/ppermute | solution.py:221
  246.9 13.5 %collective-permute-start.35 = (f32[2,512,128]{2,1,0:T(8,128)}, f32[2,512,128]{2,1,0:T(8,128)}, u32[]{:S(2)}, u32[]{:S(2)}) collective-permute-start(f32[2,512,128]{2,1,0:T(8,128)} %collective-permute-done.29.refs_4_.refs_10_), channel_id=1, source_target_pairs={{0,1},{1,0},{2,3},{3,2},{4,5},{5,4},{6,7},{7,6},{8,9},{9,8},{10,11... | collective-permute-start | bytes 1572872 | tf_op jit(solution)/shard_map/ppermute | solution.py:221
  246.9 5.7 %collective-permute-start.30 = (f32[128,128]{1,0:T(8,128)S(1)}, f32[128,128]{1,0:T(8,128)S(1)}, u32[]{:S(2)}, u32[]{:S(2)}) collective-permute-start(f32[128,128]{1,0:T(8,128)S(1)} %add_add_fusion.1), channel_id=1, source_target_pairs={{0,2},{1,3},{2,0},{3,1},{4,6},{5,7},{6,4},{7,5},{8,10},{9,11},{10,... | collective-permute-start | bytes 196616 | tf_op jit(solution)/shard_map/ppermute | solution.py:367
  246.9 7.8 %collective-permute-start.31 = (f32[128,128]{1,0:T(8,128)S(1)}, f32[128,128]{1,0:T(8,128)S(1)}, u32[]{:S(2)}, u32[]{:S(2)}) collective-permute-start(f32[128,128]{1,0:T(8,128)S(1)} %add_add_fusion.1), channel_id=1, source_target_pairs={{0,4},{1,5},{2,6},{3,7},{4,0},{5,1},{6,2},{7,3},{8,12},{9,13},{10,... | collective-permute-start | bytes 196616 | tf_op jit(solution)/shard_map/ppermute | solution.py:367
  252.6 6.1 %collective-permute-start.32 = (f32[128,128]{1,0:T(8,128)S(1)}, f32[128,128]{1,0:T(8,128)S(1)}, u32[]{:S(2)}, u32[]{:S(2)}) collective-permute-start(f32[128,128]{1,0:T(8,128)S(1)} %add_add_fusion.1), channel_id=1, source_target_pairs={{0,6},{1,7},{2,4},{3,5},{4,2},{5,3},{6,0},{7,1},{8,14},{9,15},{10,... | collective-permute-start | bytes 196616 | tf_op jit(solution)/shard_map/ppermute | solution.py:367
  268.9 5.8 %collective-permute-start.37 = (f32[128,128]{1,0:T(8,128)S(1)}, f32[128,128]{1,0:T(8,128)S(1)}, u32[]{:S(2)}, u32[]{:S(2)}) collective-permute-start(f32[128,128]{1,0:T(8,128)S(1)} %get-tuple-element.224), channel_id=1, source_target_pairs={{0,8},{8,0},{16,24},{24,16},{1,9},{9,1},{17,25},{25,17},{2,10},{10... | collective-permute-start | bytes 196616 | tf_op jit(solution)/shard_map/ppermute | solution.py:377
  272.3 4.3 %collective-permute-start.38 = (f32[128,128]{1,0:T(8,128)S(1)}, f32[128,128]{1,0:T(8,128)S(1)}, u32[]{:S(2)}, u32[]{:S(2)}) collective-permute-start(f32[128,128]{1,0:T(8,128)S(1)} %get-tuple-element.226), channel_id=1, source_target_pairs={{0,16},{8,24},{16,0},{24,8},{1,17},{9,25},{17,1},{25,9},{2,18},{10... | collective-permute-start | bytes 196616 | tf_op jit(solution)/shard_map/ppermute | solution.py:377
  273.9 5.2 %collective-permute-start.39 = (f32[128,128]{1,0:T(8,128)S(1)}, f32[128,128]{1,0:T(8,128)S(1)}, u32[]{:S(2)}, u32[]{:S(2)}) collective-permute-start(f32[128,128]{1,0:T(8,128)S(1)} %get-tuple-element.225), channel_id=1, source_target_pairs={{0,24},{8,16},{16,8},{24,0},{1,25},{9,17},{17,9},{25,1},{2,26},{10... | collective-permute-start | bytes 196616 | tf_op jit(solution)/shard_map/ppermute | solution.py:377
  279.9 8.5 %collective-permute-start.47 = (f32[512,128]{1,0:T(8,128)S(1)}, f32[512,128]{1,0:T(8,128)S(1)}, u32[]{:S(2)}, u32[]{:S(2)}) collective-permute-start(f32[512,128]{1,0:T(8,128)S(1)} %pad_maximum_fusion.3.refs_0_), channel_id=1, source_target_pairs={{8,0},{9,1},{10,2},{11,3},{12,4},{13,5},{14,6},{15,7}} | collective-permute-start | bytes 786440 | tf_op jit(solution)/shard_map/ppermute | solution.py:445
  281.2 14.2 %collective-permute-start.48 = (f32[512,128]{1,0:T(8,128)S(1)}, f32[512,128]{1,0:T(8,128)S(1)}, u32[]{:S(2)}, u32[]{:S(2)}) collective-permute-start(f32[512,128]{1,0:T(8,128)S(1)} %pad_maximum_fusion.3.refs_0_), channel_id=1, source_target_pairs={{16,0},{17,1},{18,2},{19,3},{20,4},{21,5},{22,6},{23,7}} | collective-permute-start | bytes 786440 | tf_op jit(solution)/shard_map/ppermute | solution.py:445
  282.5 12.9 %collective-permute-start.49 = (f32[512,128]{1,0:T(8,128)S(1)}, f32[512,128]{1,0:T(8,128)S(1)}, u32[]{:S(2)}, u32[]{:S(2)}) collective-permute-start(f32[512,128]{1,0:T(8,128)S(1)} %pad_maximum_fusion.3.refs_0_), channel_id=1, source_target_pairs={{24,0},{25,1},{26,2},{27,3},{28,4},{29,5},{30,6},{31,7}} | collective-permute-start | bytes 786440 | tf_op jit(solution)/shard_map/ppermute | solution.py:445
  284.1 11.5 %collective-permute-start.40 = (f32[128,128]{1,0:T(8,128)S(1)}, f32[128,128]{1,0:T(8,128)S(1)}, u32[]{:S(2)}, u32[]{:S(2)}) collective-permute-start(f32[128,128]{1,0:T(8,128)S(1)} %bitcast_subtract_fusion.1), channel_id=1, source_target_pairs={{0,2},{1,3},{2,0},{3,1},{4,6},{5,7},{6,4},{7,5},{8,10},{9,11},{10,... | collective-permute-start | bytes 196616 | tf_op jit(solution)/shard_map/ppermute | solution.py:367
  284.1 11.4 %collective-permute-start.41 = (f32[128,128]{1,0:T(8,128)S(1)}, f32[128,128]{1,0:T(8,128)S(1)}, u32[]{:S(2)}, u32[]{:S(2)}) collective-permute-start(f32[128,128]{1,0:T(8,128)S(1)} %bitcast_subtract_fusion.1), channel_id=1, source_target_pairs={{0,4},{1,5},{2,6},{3,7},{4,0},{5,1},{6,2},{7,3},{8,12},{9,13},{10,... | collective-permute-start | bytes 196616 | tf_op jit(solution)/shard_map/ppermute | solution.py:367
  288.5 7.1 %collective-permute-start.42 = (f32[128,128]{1,0:T(8,128)S(1)}, f32[128,128]{1,0:T(8,128)S(1)}, u32[]{:S(2)}, u32[]{:S(2)}) collective-permute-start(f32[128,128]{1,0:T(8,128)S(1)} %bitcast_subtract_fusion.1), channel_id=1, source_target_pairs={{0,6},{1,7},{2,4},{3,5},{4,2},{5,3},{6,0},{7,1},{8,14},{9,15},{10,... | collective-permute-start | bytes 196616 | tf_op jit(solution)/shard_map/ppermute | solution.py:367
  295.5 10.0 %collective-permute-start.50 = (f32[4,512,128]{2,1,0:T(8,128)S(1)}, f32[4,512,128]{2,1,0:T(8,128)S(1)}, u32[]{:S(2)}, u32[]{:S(2)}) collective-permute-start(f32[4,512,128]{2,1,0:T(8,128)S(1)} %pad_maximum_fusion), channel_id=1, source_target_pairs={{0,1},{1,0},{2,3},{3,2},{4,5},{5,4},{6,7},{7,6},{8,9},{9,8},{10,11... | collective-permute-start | bytes 3145736 | tf_op jit(solution)/shard_map/ppermute | solution.py:221
  299.6 4.6 %collective-permute-start.44 = (f32[128,128]{1,0:T(8,128)S(1)}, f32[128,128]{1,0:T(8,128)S(1)}, u32[]{:S(2)}, u32[]{:S(2)}) collective-permute-start(f32[128,128]{1,0:T(8,128)S(1)} %get-tuple-element.221), channel_id=1, source_target_pairs={{0,8},{8,0},{16,24},{24,16},{1,9},{9,1},{17,25},{25,17},{2,10},{10... | collective-permute-start | bytes 196616 | tf_op jit(solution)/shard_map/ppermute | solution.py:377
  299.7 5.7 %collective-permute-start.45 = (f32[128,128]{1,0:T(8,128)S(1)}, f32[128,128]{1,0:T(8,128)S(1)}, u32[]{:S(2)}, u32[]{:S(2)}) collective-permute-start(f32[128,128]{1,0:T(8,128)S(1)} %get-tuple-element.223), channel_id=1, source_target_pairs={{0,16},{8,24},{16,0},{24,8},{1,17},{9,25},{17,1},{25,9},{2,18},{10... | collective-permute-start | bytes 196616 | tf_op jit(solution)/shard_map/ppermute | solution.py:377
  299.8 5.7 %collective-permute-start.46 = (f32[128,128]{1,0:T(8,128)S(1)}, f32[128,128]{1,0:T(8,128)S(1)}, u32[]{:S(2)}, u32[]{:S(2)}) collective-permute-start(f32[128,128]{1,0:T(8,128)S(1)} %get-tuple-element.222), channel_id=1, source_target_pairs={{0,24},{8,16},{16,8},{24,0},{1,25},{9,17},{17,9},{25,1},{2,26},{10... | collective-permute-start | bytes 196616 | tf_op jit(solution)/shard_map/ppermute | solution.py:377
  305.5 12.9 %collective-permute-start.51 = (f32[128,128]{1,0:T(8,128)S(1)}, f32[128,128]{1,0:T(8,128)S(1)}, u32[]{:S(2)}, u32[]{:S(2)}) collective-permute-start(f32[128,128]{1,0:T(8,128)S(1)} %add_add_fusion), channel_id=1, source_target_pairs={{0,2},{1,3},{2,0},{3,1},{4,6},{5,7},{6,4},{7,5},{8,10},{9,11},{10,... | collective-permute-start | bytes 196616 | tf_op jit(solution)/shard_map/ppermute | solution.py:367
  306.5 12.0 %collective-permute-start.52 = (f32[128,128]{1,0:T(8,128)S(1)}, f32[128,128]{1,0:T(8,128)S(1)}, u32[]{:S(2)}, u32[]{:S(2)}) collective-permute-start(f32[128,128]{1,0:T(8,128)S(1)} %add_add_fusion), channel_id=1, source_target_pairs={{0,4},{1,5},{2,6},{3,7},{4,0},{5,1},{6,2},{7,3},{8,12},{9,13},{10,... | collective-permute-start | bytes 196616 | tf_op jit(solution)/shard_map/ppermute | solution.py:367
  308.3 10.2 %collective-permute-start.53 = (f32[128,128]{1,0:T(8,128)S(1)}, f32[128,128]{1,0:T(8,128)S(1)}, u32[]{:S(2)}, u32[]{:S(2)}) collective-permute-start(f32[128,128]{1,0:T(8,128)S(1)} %add_add_fusion), channel_id=1, source_target_pairs={{0,6},{1,7},{2,4},{3,5},{4,2},{5,3},{6,0},{7,1},{8,14},{9,15},{10,... | collective-permute-start | bytes 196616 | tf_op jit(solution)/shard_map/ppermute | solution.py:367
  322.8 4.3 %collective-permute-start.55 = (f32[128,128]{1,0:T(8,128)S(1)}, f32[128,128]{1,0:T(8,128)S(1)}, u32[]{:S(2)}, u32[]{:S(2)}) collective-permute-start(f32[128,128]{1,0:T(8,128)S(1)} %get-tuple-element.218), channel_id=1, source_target_pairs={{0,8},{8,0},{16,24},{24,16},{1,9},{9,1},{17,25},{25,17},{2,10},{10... | collective-permute-start | bytes 196616 | tf_op jit(solution)/shard_map/ppermute | solution.py:377
  326.3 5.2 %collective-permute-start.57 = (f32[128,128]{1,0:T(8,128)S(1)}, f32[128,128]{1,0:T(8,128)S(1)}, u32[]{:S(2)}, u32[]{:S(2)}) collective-permute-start(f32[128,128]{1,0:T(8,128)S(1)} %get-tuple-element.219), channel_id=1, source_target_pairs={{0,24},{8,16},{16,8},{24,0},{1,25},{9,17},{17,9},{25,1},{2,26},{10... | collective-permute-start | bytes 196616 | tf_op jit(solution)/shard_map/ppermute | solution.py:377
  332.3 5.1 %collective-permute-start.58 = (f32[128,128]{1,0:T(8,128)S(1)}, f32[128,128]{1,0:T(8,128)S(1)}, u32[]{:S(2)}, u32[]{:S(2)}) collective-permute-start(f32[128,128]{1,0:T(8,128)S(1)} %bitcast_subtract_fusion.2), channel_id=1, source_target_pairs={{0,2},{1,3},{2,0},{3,1},{4,6},{5,7},{6,4},{7,5},{8,10},{9,11},{10,... | collective-permute-start | bytes 196616 | tf_op jit(solution)/shard_map/ppermute | solution.py:367
  332.4 7.9 %collective-permute-start.59 = (f32[128,128]{1,0:T(8,128)S(1)}, f32[128,128]{1,0:T(8,128)S(1)}, u32[]{:S(2)}, u32[]{:S(2)}) collective-permute-start(f32[128,128]{1,0:T(8,128)S(1)} %bitcast_subtract_fusion.2), channel_id=1, source_target_pairs={{0,4},{1,5},{2,6},{3,7},{4,0},{5,1},{6,2},{7,3},{8,12},{9,13},{10,... | collective-permute-start | bytes 196616 | tf_op jit(solution)/shard_map/ppermute | solution.py:367
  335.0 6.1 %collective-permute-start.60 = (f32[128,128]{1,0:T(8,128)S(1)}, f32[128,128]{1,0:T(8,128)S(1)}, u32[]{:S(2)}, u32[]{:S(2)}) collective-permute-start(f32[128,128]{1,0:T(8,128)S(1)} %bitcast_subtract_fusion.2), channel_id=1, source_target_pairs={{0,6},{1,7},{2,4},{3,5},{4,2},{5,3},{6,0},{7,1},{8,14},{9,15},{10,... | collective-permute-start | bytes 196616 | tf_op jit(solution)/shard_map/ppermute | solution.py:367
  336.8 5.0 %collective-permute-start.61 = (f32[2,128,128]{2,1,0:T(8,128)S(1)}, f32[2,128,128]{2,1,0:T(8,128)S(1)}, u32[]{:S(2)}, u32[]{:S(2)}) collective-permute-start(f32[2,128,128]{2,1,0:T(8,128)S(1)} %pad_maximum_fusion.7), channel_id=1, source_target_pairs={{0,8},{8,0},{16,24},{24,16},{1,9},{9,1},{17,25},{25,17},{2,10},{10... | collective-permute-start | bytes 393224 | tf_op jit(solution)/shard_map/ppermute | solution.py:381
  336.9 5.0 %collective-permute-start.62 = (f32[2,128,128]{2,1,0:T(8,128)S(1)}, f32[2,128,128]{2,1,0:T(8,128)S(1)}, u32[]{:S(2)}, u32[]{:S(2)}) collective-permute-start(f32[2,128,128]{2,1,0:T(8,128)S(1)} %pad_maximum_fusion.7), channel_id=1, source_target_pairs={{0,16},{8,24},{16,0},{24,8},{1,17},{9,25},{17,1},{25,9},{2,18},{10... | collective-permute-start | bytes 393224 | tf_op jit(solution)/shard_map/ppermute | solution.py:381
  337.4 5.9 %collective-permute-start.63 = (f32[2,128,128]{2,1,0:T(8,128)S(1)}, f32[2,128,128]{2,1,0:T(8,128)S(1)}, u32[]{:S(2)}, u32[]{:S(2)}) collective-permute-start(f32[2,128,128]{2,1,0:T(8,128)S(1)} %pad_maximum_fusion.7), channel_id=1, source_target_pairs={{0,24},{8,16},{16,8},{24,0},{1,25},{9,17},{17,9},{25,1},{2,26},{10... | collective-permute-start | bytes 393224 | tf_op jit(solution)/shard_map/ppermute | solution.py:381
  346.1 4.4 %collective-permute-start.65 = (f32[128,128]{1,0:T(8,128)S(1)}, f32[128,128]{1,0:T(8,128)S(1)}, u32[]{:S(2)}, u32[]{:S(2)}) collective-permute-start(f32[128,128]{1,0:T(8,128)S(1)} %get-tuple-element.215), channel_id=1, source_target_pairs={{0,8},{8,0},{16,24},{24,16},{1,9},{9,1},{17,25},{25,17},{2,10},{10... | collective-permute-start | bytes 196616 | tf_op jit(solution)/shard_map/ppermute | solution.py:377
  348.0 4.3 %collective-permute-start.66 = (f32[128,128]{1,0:T(8,128)S(1)}, f32[128,128]{1,0:T(8,128)S(1)}, u32[]{:S(2)}, u32[]{:S(2)}) collective-permute-start(f32[128,128]{1,0:T(8,128)S(1)} %get-tuple-element.217), channel_id=1, source_target_pairs={{0,16},{8,24},{16,0},{24,8},{1,17},{9,25},{17,1},{25,9},{2,18},{10... | collective-permute-start | bytes 196616 | tf_op jit(solution)/shard_map/ppermute | solution.py:377
  349.6 5.2 %collective-permute-start.67 = (f32[128,128]{1,0:T(8,128)S(1)}, f32[128,128]{1,0:T(8,128)S(1)}, u32[]{:S(2)}, u32[]{:S(2)}) collective-permute-start(f32[128,128]{1,0:T(8,128)S(1)} %get-tuple-element.216), channel_id=1, source_target_pairs={{0,24},{8,16},{16,8},{24,0},{1,25},{9,17},{17,9},{25,1},{2,26},{10... | collective-permute-start | bytes 196616 | tf_op jit(solution)/shard_map/ppermute | solution.py:377
  354.8 4.3 %collective-permute-start.68 = (f32[1,128,128]{2,1,0:T(8,128)S(1)}, f32[1,128,128]{2,1,0:T(8,128)S(1)}, u32[]{:S(2)}, u32[]{:S(2)}) collective-permute-start(f32[1,128,128]{2,1,0:T(8,128)S(1)} %add_bitcast_fusion), channel_id=1, source_target_pairs={{0,8},{8,0},{16,24},{24,16},{1,9},{9,1},{17,25},{25,17},{2,10},{10... | collective-permute-start | bytes 196616 | tf_op jit(solution)/shard_map/ppermute | solution.py:381
  355.4 5.2 %collective-permute-start.70 = (f32[1,128,128]{2,1,0:T(8,128)S(1)}, f32[1,128,128]{2,1,0:T(8,128)S(1)}, u32[]{:S(2)}, u32[]{:S(2)}) collective-permute-start(f32[1,128,128]{2,1,0:T(8,128)S(1)} %add_bitcast_fusion), channel_id=1, source_target_pairs={{0,24},{8,16},{16,8},{24,0},{1,25},{9,17},{17,9},{25,1},{2,26},{10... | collective-permute-start | bytes 196616 | tf_op jit(solution)/shard_map/ppermute | solution.py:381
  (29 other events, 201.9 us)

commit v4 on v3

--- a/solution.py
+++ b/solution.py
@@ -34,8 +34,8 @@
 
 
 def chip_kernel(where, weights, *refs):
-    outs, tail, high, low = refs[-STEPS - 3 : -3], *refs[-3:]
-    pieces = refs[: len(refs) - STEPS - 3]
+    outs, nearest, farther, high, low = refs[-STEPS - 4 : -4], *refs[-4:]
+    pieces = refs[: len(refs) - STEPS - 4]
     totals = pieces[len(pieces) - STEPS :] if len(pieces) % 2 else []
     number, at = pl.program_id(0), pl.program_id(1)
     lags, rows, width = pieces[0].shape
@@ -50,7 +50,8 @@
 
     @pl.when(jnp.logical_and(number == count - 1, at == 0))
     def _():
-        tail[...] = pieces[2 * count - 2][lags - tail.shape[0] :]
+        nearest[0] = pieces[2 * count - 2][lags - 1]
+        farther[0] = pieces[2 * count - 2][lags - 2]
 
     for i in range(count):
 
@@ -76,12 +77,21 @@
                 outs[n][...] += result[:, n * width : (n + 1) * width]
 
 
-def first_kernel(where, weights, near, far, total, out, tail):
+def first_kernel(where, weights, near, far, total, out, nearest, farther):
+    at, lags = pl.program_id(0), pl.num_programs(0)
+
+    @pl.when(at == lags - 2)
+    def _():
+        farther[...] = near[...]
+
+    @pl.when(at == lags - 1)
+    def _():
+        nearest[...] = near[...]
+
     @pl.when(pl.program_id(0) == 0)
     def _():
         out[...] = total[...]
 
-    tail[...] = near[...]
     out[...] += product(weights[0], [ordered(where[0], near[0], far[0])])
 
 
@@ -103,23 +113,18 @@
 
 
 def entered_kernel(where, weights, *refs):
-    pieces, (one, two, one_out, two_out) = refs[:-4], refs[-4:]
+    pieces, (total, out) = refs[:-2], refs[-2:]
     number = pl.program_id(0)
-    width = pieces[0].shape[2]
 
     @pl.when(number == 0)
     def _():
-        one_out[...] = one[...]
-        two_out[...] = two[...]
+        out[...] = total[...]
 
     for i in range(len(pieces) // 2):
 
         @pl.when(jnp.logical_and(where[1] > 0, number == i))
         def _():
-            near, far = pieces[2 * i : 2 * i + 2]
-            result = product(weights[0], [ordered(where[0], near[k], far[k]) for k in (1, 0)])
-            one_out[...] += result[:, :width]
-            two_out[...] += result[:, width:]
+            out[...] += product(weights[0], [ordered(where[0], pieces[2 * i][0], pieces[2 * i + 1][0])])
 
 
 def second_kernel(where, weights, *refs):
@@ -261,16 +266,16 @@
 
     def add_chip(totals, pieces, stage):
         count = len(pieces) // 2
-        before = (STEPS - 1, *square)
-        *totals, tail = pl.pallas_call(
+        single = (1, *square)
+        *totals, nearest, farther = pl.pallas_call(
             chip_kernel,
-            out_shape=[jax.ShapeDtypeStruct(square, F32)] * STEPS + [jax.ShapeDtypeStruct(before, F32)],
+            out_shape=[jax.ShapeDtypeStruct(square, F32)] * STEPS + [jax.ShapeDtypeStruct(single, F32)] * 2,
             grid_spec=pltpu.PrefetchScalarGridSpec(
                 num_scalar_prefetch=1,
                 grid=(count, lags),
                 in_specs=[pl.BlockSpec((1, rows, 2 * rows), lambda i, k, w: (k, 0, w[2 + stage + i]))]
                 + [all_of(v.shape) for v in (*pieces, *totals)],
-                out_specs=[all_of(square)] * STEPS + [all_of(before)],
+                out_specs=[all_of(square)] * STEPS + [all_of(single)] * 2,
                 scratch_shapes=[pltpu.VMEM((2 * rows, lags * width), BF16)] * 2,
             ),
             input_output_aliases={2 + len(pieces) + n: n for n in range(len(totals))},
@@ -278,18 +283,18 @@
             compiler_params=pltpu.CompilerParams(dimension_semantics=("arbitrary", "arbitrary")),
             name="chip",
         )(where, lag_weights, *pieces, *totals)
-        return totals, tail
+        return totals, nearest, farther
 
     def add_first(total, near, far, stage):
-        before = STEPS - 1
+        single = (1, *square)
         return pl.pallas_call(
             first_kernel,
-            out_shape=[jax.ShapeDtypeStruct(square, F32), jax.ShapeDtypeStruct((before, *square), F32)],
+            out_shape=[jax.ShapeDtypeStruct(square, F32)] + [jax.ShapeDtypeStruct(single, F32)] * 2,
             grid_spec=pltpu.PrefetchScalarGridSpec(
                 num_scalar_prefetch=1,
                 grid=(lags,),
                 in_specs=[weight_spec(stage), lag_spec(0), lag_spec(0), all_of(square)],
-                out_specs=[all_of(square), pl.BlockSpec((1, *square), lambda k, w: (jnp.maximum(k + before - lags, 0), 0, 0))],
+                out_specs=[all_of(square)] + [all_of(single)] * 2,
             ),
             input_output_aliases={4: 0},
             cost_estimate=pl.CostEstimate(flops=6 * lags * tile * width, bytes_accessed=4 * lags * tile, transcendentals=0),
@@ -304,18 +309,18 @@
             2, square, (12 * lags * tile * width, 4 * lags * tile), {6: 0, 7: 1},
         )
 
-    def add_entered(one, two, pieces, stage):
+    def add_entered(total, pieces, stage):
         count = len(pieces) // 2
         spec = pl.BlockSpec((1, rows, 2 * rows), lambda i, w: (0, 0, jnp.where(w[1] > 0, w[2 + stage + i], 0)))
         return call(
-            entered_kernel, where, (count,), (lag_weights, *pieces, one, two),
-            [spec] + [all_of(v.shape) for v in (*pieces, one, two)],
-            2, square, (12 * count * tile * width, 4 * count * tile), {2 + len(pieces): 0, 3 + len(pieces): 1},
-        )
+            entered_kernel, where, (count,), (lag_weights, *[v for v, _ in pieces], total),
+            [spec] + [pl.BlockSpec((1, rows, width), lambda i, w, at=at: (at, 0, 0)) for _, at in pieces] + [all_of(square)],
+            1, square, (6 * count * tile * width, 4 * count * tile), {2 + len(pieces): 0},
+        )[0]
 
     def add_second(total, nears, pieces, fars):
         spec = pl.BlockSpec((1, rows, 2 * rows), lambda i, w: (1, 0, w[2 + i + jnp.where(w[1] == 0, chips, 0)]))
-        last = pl.BlockSpec((1, rows, width), lambda i, w: (STEPS - 2, 0, 0))
+        last = all_of((1, rows, width))
         return call(
             second_kernel, where, (chips,), (lag_weights, *nears, *pieces, fars, total),
             [spec] + [all_of(v.shape) for v in nears] + [last] * len(pieces) + [all_of(fars.shape), all_of(square)],
@@ -389,8 +394,8 @@
         return jnp.dot(matrix, vector, precision=lax.Precision.HIGH)
 
     ups, downs = {1: go_up(history, 1)}, {1: go_down(history, 1)}
-    tail = history[lags - (STEPS - 1) :]
-    entered = [enter(jnp.where(group >= 0, tail, 0.0))]
+    entered = [enter(jnp.where(group >= 0, history[lags - 1 :], 0.0))]
+    farthers = [history[lags - 2 : lags - 1]]
     own_far = other_core(history)
     *chunks, last_near, last_far = columns(lag_weights, True)
     relayed = lax.ppermute(last_far, "lag", [(0, groups // 2)])
@@ -407,48 +412,56 @@
         pieces = [near, other_core(near)]
         if stage == 1:
             pieces = [history, own_far, *pieces]
-        totals, tail = add_chip(totals, pieces, stage if stage > 1 else 0)
+        totals, tail, farther = add_chip(totals, pieces, stage if stage > 1 else 0)
+        farthers.append(farther)
         entered.append(enter(tail))
         if stage == 1:
             last_near, tail = tie((last_near, tail))
             sent.append(lax.ppermute(last_near, "lag", [(0, groups - 1)]))
         if stage == chips - 2:
             both = [entered[0], other_core(entered[0])]
-            totals = [totals[0], *add_entered(totals[1], totals[2], both, 0)]
+            totals[1] = add_entered(totals[1], [(v, 0) for v in both], 0)
         ups[stage + 1], downs[stage + 1] = next_up, next_down
         ups, downs, totals = tie((ups, downs, totals))
     first, one, two = totals
 
     near = choose(chips - 1, ups, downs)
     far = other_core(near)
-    first, tail = add_first(first, near, far, chips - 1)
+    first, tail, farther = add_first(first, near, far, chips - 1)
 
     right_side = own_part(excitation[0]) - sum_parts(first)
-    right_side, tail, near, far, one, two = tie((right_side, tail, near, far, one, two))
+    farthers.append(farther)
+    right_side, tail, farthers, near, far, one, two = tie((right_side, tail, farthers, near, far, one, two))
     mine = gather_near(right_side)
     entered.append(enter(tail))
+    packs = [enter(jnp.concatenate(farthers[: chips // 2], axis=0))]
     one, two = add_rest(one, two, near, far, chips - 1)
     mine, one, two, sent = tie((mine, one, two, sent))
     density = sum_parts(multiply(head_columns, mine))
     first_columns = pick([chunks[0], *sent])
     results = [density]
 
-    density, first_columns, entered, one, two = tie((density, first_columns, entered, one, two))
+    density, first_columns, entered, farthers, one, two = tie((density, first_columns, entered, farthers, one, two))
     mine = gather_near(density)
+    packs.append(enter(jnp.concatenate(farthers[chips // 2 :], axis=0)))
     both += [v for piece in entered[1:] for v in (piece, other_core(piece))]
-    one, two = add_entered(one, two, both[2:], 1)
+    one = add_entered(one, [(v, 0) for v in both[2:]], 1)
     mine, one, two, both = tie((mine, one, two, both))
     right_side = own_part(excitation[1]) - sum_parts(one + multiply(first_columns, mine))
 
-    right_side, two, old, both = tie((right_side, two, mine, both))
+    right_side, two, old, both, packs = tie((right_side, two, mine, both, packs))
     mine = gather_near(right_side)
     nears = [old] + [lax.ppermute(old, "lag", [(j, 0)]) for j in range(1, groups)]
+    pack_fars = [other_core(pack) for pack in packs]
+    last = [(pack, far, i) for pack, far in zip(packs, pack_fars) for i in range(chips // 2)]
+    two = add_entered(two, [v for pack, far, i in last for v in ((pack, i), (far, i))], 0)
     mine, two = tie((mine, two))
-    density = sum_parts(multiply(head_columns, mine))
+    carried = multiply(head_columns, mine)
+    density = sum_parts(carried)
     fars = other_core(jnp.stack(nears))
     results.append(density)
 
-    density, two, nears, fars = tie((density, two, nears, fars))
+    density, two = tie((density, two))
     mine = gather_near(density)
     two = add_second(two, nears, both, fars)
     mine, two = tie((mine, two))

time: 363 us -> 373 us (1.028)
  starting transfers between devices: 97.8 us -> 104 us
  other arithmetic: 9.16 us -> 12.9 us
    ppermute x18, waiting for transfers between devices: 93.5 us -> 78.9 us  [sum_parts(): result = result + lax.ppermute(sent, 'lag', pairs(groups, mask))]
    ppermute x4 -> x6, starting transfers between devices: 16.1 us -> 25.8 us  [enter(): return lax.ppermute(tail, 'lag', [(i, i + 1) for i in range(groups - 1)])]
    ppermute x15, waiting for transfers between devices: 17.7 us -> 24.2 us  [gather_near(): lax.ppermute(value, 'row', pairs(devices, 2 * k))]
    ppermute x6, waiting for transfers between devices: 4.47 us -> 10.2 us  [whole_rows(): lax.ppermute(value, 'lag', pairs(groups, mask))]
    ppermute x6, waiting for transfers between devices: 22.7 us -> 27.6 us  [along(): lax.ppermute(value, 'row', [(2 * i + c, 2 * (i + step) + c) for i in sour...]
    pallas_call x4 -> x5, Pallas kernels: 24 us -> 26.9 us  [call(): pl.pallas_call(kernel, out_shape=[jax.ShapeDtypeStruct(shape, F32)] * cou...]
  transfers between devices with their start and end apart: 71 -> 75, of which waited for: 37 -> 37; matrix products, arithmetic and copies ran while one was open for 3% -> 5% of each run, Pallas kernels for 20% -> 18%
where the time goes in v4:
time: 373 us; the launch traced here: 372 us
  waiting for transfers between devices  158 us (42%)
  starting transfers between devices  104 us (28%)
  Pallas kernels  77.9 us (21%)
  other arithmetic  12.9 us (3%)
  local copies, waits for them, and re-layouts  9.8 us (3%)
  matrix products  8.11 us (2%)
    ppermute x18, waiting for transfers between devices, sum_parts(): result = result + lax.ppermute(sent, 'lag', pairs(groups, mask))  78.9 us
    ppermute x6, waiting for transfers between devices, along(): lax.ppermute(value, 'row', [(2 * i + c, 2 * (i + step) + c) for i in sour...  27.6 us
    pallas_call x5, Pallas kernels, call(): pl.pallas_call(kernel, out_shape=[jax.ShapeDtypeStruct(shape, F32)] * cou...  26.9 us
    pallas_call x2, Pallas kernels, add_chip(): pl.pallas_call(chip_kernel, out_shape=[jax.ShapeDtypeStruct(square, F32)]...  26.7 us
    ppermute x6, starting transfers between devices, enter(): return lax.ppermute(tail, 'lag', [(i, i + 1) for i in range(groups - 1)])  25.8 us
    ppermute x15, waiting for transfers between devices, gather_near(): lax.ppermute(value, 'row', pairs(devices, 2 * k))  24.2 us
    ppermute x15, starting transfers between devices, gather_near(): lax.ppermute(value, 'row', pairs(devices, 2 * k))  20 us
    ppermute x18, starting transfers between devices, sum_parts(): result = result + lax.ppermute(sent, 'lag', pairs(groups, mask))  18.9 us
  transfers between devices with their start and end apart: 75, of which 37 were waited for; matrix products, arithmetic and copies ran while one was open for 5% of the time, Pallas kernels for 18%

profile of v4, /device:TPU:0, one launch (start us, length us, event | category | flops | bytes accessed | tf_op | source)
XLA Modules:
  0.0 372.0 jit_solution(752748002931253746)
XLA Ops:
  0.0 5.0 %collective-permute-start = (f32[4,512,128]{2,1,0:T(8,128)}, f32[4,512,128]{2,1,0:T(8,128)S(1)}, u32[]{:S(2)}, u32[]{:S(2)}) collective-permute-start(f32[4,512,128]{2,1,0:T(8,128)} %refs_0_.2), channel_id=1, source_target_pairs={{0,2},{1,3},{2,4},{3,5},{4,6},{5,7},{8,10},{9,11},{10,12},{11,13},... | collective-permute-start | bytes 3145736 | tf_op jit(solution)/shard_map/ppermute | solution.py:229
  6.4 1.8 fusion.25
  8.2 3.4 collective-permute-start.2
  12.5 5.8 %columns.2 = f32[512,1024]{1,0:T(8,128)} custom-call(s32[2,5,4]{2,1,0:T(8,128)} %concatenate.49.where, f32[1,512,4096]{2,1,0:T(8,128)} %bitcast.37, f32[1,512,4096]{2,1,0:T(8,128)} %bitcast.38, f32[1,512,4096]{2,1,0:T(8,128)} %bitcast.39, f32[1,512,4096]{2,1,0:T(8,128)} %bitcast.40), custom_call_target="tpu_custom_call" | custom-call | bytes 16777216 | tf_op jit(solution)/shard_map/columns/pallas_call | solution.py:341
  18.3 9.4 %collective-permute-done = f32[4,512,128]{2,1,0:T(8,128)S(1)} collective-permute-done((f32[4,512,128]{2,1,0:T(8,128)}, f32[4,512,128]{2,1,0:T(8,128)S(1)}, u32[]{:S(2)}, u32[]{:S(2)}) %collective-permute-start) | collective-permute-done | bytes 1048608 | tf_op jit(solution)/shard_map/ppermute | solution.py:229
  27.7 4.1 %collective-permute-done.1 = f32[4,512,128]{2,1,0:T(8,128)S(1)} collective-permute-done((f32[4,512,128]{2,1,0:T(8,128)}, f32[4,512,128]{2,1,0:T(8,128)S(1)}, u32[]{:S(2)}, u32[]{:S(2)}) %collective-permute-start.1) | collective-permute-done | bytes 1048608 | tf_op jit(solution)/shard_map/ppermute | solution.py:229
  34.0 7.1 %columns.3 = (f32[512,1024]{1,0:T(8,128)}, f32[512,1024]{1,0:T(8,128)}, f32[512,1024]{1,0:T(8,128)}, f32[512,512]{1,0:T(8,128)}, f32[512,512]{1,0:T(8,128)}) custom-call(s32[2,5,4]{2,1,0:T(8,128)} %concatenate.49.where, f32[4,512,4096]{2,1,0:T(8,128)} %weights.15, f32[4,512,4096]{2,1,0:T(8,128)} %weights.15, f32[4,512,4096]{2,1,0:T(8,128)} %weights.15, ...), custom_call_target="tpu_custom_call" | custom-call | bytes 16777216 | tf_op jit(solution)/shard_map/columns/pallas_call | solution.py:341
  41.1 4.4 %collective-permute-start.9 = (f32[512,512]{1,0:T(8,128)}, f32[512,512]{1,0:T(8,128)}, u32[]{:S(2)}, u32[]{:S(2)}) collective-permute-start(f32[512,512]{1,0:T(8,128)} %get-tuple-element.117), channel_id=1, source_target_pairs={{0,16},{1,17},{2,18},{3,19},{4,20},{5,21},{6,22},{7,23}} | collective-permute-start | bytes 3145736 | tf_op jit(solution)/shard_map/ppermute | solution.py:401
  46.2 16.6 %chip.2 = (f32[512,128]{1,0:T(8,128)}, f32[512,128]{1,0:T(8,128)}, f32[512,128]{1,0:T(8,128)}, f32[1,512,128]{2,1,0:T(8,128)}, f32[1,512,128]{2,1,0:T(8,128)}) custom-call(s32[10]{0:T(128)} %stack.100.where, f32[4,512,4096]{2,1,0:T(8,128)} %weights.15, f32[4,512,128]{2,1,0:T(8,128)} %refs_0_.2, f32[4,512,128]{2,1,0:T(8,128)} %collective-permute-done.3.refs_1_, ...), custom_call_target="tpu_custom_call" | custom-call | flops 9663676416 | bytes 16777216 | tf_op jit(solution)/shard_map/chip/pallas_call | solution.py:270
  62.9 1.7 select_select_fusion.1.refs_0_
  64.7 3.3 collective-permute-done.9
  67.9 1.6 collective-permute-start.7
  71.5 10.1 %chip.3 = (f32[512,128]{1,0:T(8,128)}, f32[512,128]{1,0:T(8,128)}, f32[512,128]{1,0:T(8,128)}, f32[1,512,128]{2,1,0:T(8,128)}, f32[1,512,128]{2,1,0:T(8,128)}) custom-call(s32[10]{0:T(128)} %stack.100.where, f32[4,512,4096]{2,1,0:T(8,128)} %weights.15, f32[4,512,128]{2,1,0:T(8,128)} %copy-done.6, ...), custom_call_target="tpu_custom_call", output_to_operand_aliasing={{0}: (4, {}), {1}: (5, {}), {2}: (6, {})} | custom-call | flops 4831838208 | bytes 8388608 | tf_op jit(solution)/shard_map/chip/pallas_call | solution.py:270
  82.2 3.3 shard_map.46.one
  85.5 14.1 %collective-permute-done.8 = f32[4,512,128]{2,1,0:T(8,128)} collective-permute-done((f32[4,512,128]{2,1,0:T(8,128)}, f32[4,512,128]{2,1,0:T(8,128)}, u32[]{:S(2)}, u32[]{:S(2)}) %collective-permute-start.8) | collective-permute-done | bytes 1048608 | tf_op jit(solution)/shard_map/ppermute | solution.py:229
  101.2 2.6 collective-permute-start.19
  103.8 5.1 %collective-permute-start.20 = (f32[512,1024]{1,0:T(8,128)}, f32[512,1024]{1,0:T(8,128)}, u32[]{:S(2)}, u32[]{:S(2)}) collective-permute-start(f32[512,1024]{1,0:T(8,128)} %get-tuple-element.146), channel_id=1, source_target_pairs={{0,16},{1,17},{2,18},{3,19},{4,20},{5,21},{6,22},{7,23}} | collective-permute-start | bytes 6291464 | tf_op jit(solution)/shard_map/ppermute | solution.py:402
  109.9 7.4 %first.1 = (f32[512,128]{1,0:T(8,128)}, f32[1,512,128]{2,1,0:T(8,128)}, f32[1,512,128]{2,1,0:T(8,128)}) custom-call(s32[10]{0:T(128)} %stack.100.where, f32[4,512,4096]{2,1,0:T(8,128)} %weights.15, f32[4,512,128]{2,1,0:T(8,128)} %copy-done.1, f32[4,512,128]{2,1,0:T(8,128)} %copy-done.2, ...), custom_call_target="tpu_custom_call", output_to_operand_aliasing={{0}: (4, {})} | custom-call | flops 1610612736 | bytes 8388608 | tf_op jit(solution)/shard_map/first/pallas_call | solution.py:290
  119.1 30.8 %collective-permute-done.13 = f32[128,128]{1,0:T(8,128)S(1)} collective-permute-done((f32[128,128]{1,0:T(8,128)S(1)}, f32[128,128]{1,0:T(8,128)S(1)}, u32[]{:S(2)}, u32[]{:S(2)}) %collective-permute-start.13) | collective-permute-done | bytes 65568 | tf_op jit(solution)/shard_map/ppermute | solution.py:382
  149.9 2.3 collective-permute-start.21
  152.1 2.5 collective-permute-done.14
  154.7 2.0 fusion.26
  156.6 18.9 %collective-permute-done.15 = f32[128,128]{1,0:T(8,128)S(1)} collective-permute-done((f32[128,128]{1,0:T(8,128)S(1)}, f32[128,128]{1,0:T(8,128)S(1)}, u32[]{:S(2)}, u32[]{:S(2)}) %collective-permute-start.15) | collective-permute-done | bytes 65568 | tf_op jit(solution)/shard_map/ppermute | solution.py:382
  176.5 4.3 %collective-permute-done.16 = f32[128,128]{1,0:T(8,128)S(1)} collective-permute-done((f32[128,128]{1,0:T(8,128)S(1)}, f32[128,128]{1,0:T(8,128)S(1)}, u32[]{:S(2)}, u32[]{:S(2)}) %collective-permute-start.16) | collective-permute-done | bytes 65568 | tf_op jit(solution)/shard_map/ppermute | solution.py:372
  181.0 5.7 %collective-permute-done.17 = f32[128,128]{1,0:T(8,128)S(1)} collective-permute-done((f32[128,128]{1,0:T(8,128)S(1)}, f32[128,128]{1,0:T(8,128)S(1)}, u32[]{:S(2)}, u32[]{:S(2)}) %collective-permute-start.17) | collective-permute-done | bytes 65568 | tf_op jit(solution)/shard_map/ppermute | solution.py:372
  186.7 1.7 collective-permute-start.18
  188.5 7.6 %shard_map.47 = (f32[512,128]{1,0:T(8,128)}, f32[512,128]{1,0:T(8,128)}) custom-call(s32[10]{0:T(128)} %stack.100.where, f32[4,512,4096]{2,1,0:T(8,128)} %weights.15, f32[4,512,128]{2,1,0:T(8,128)} %copy-done.1, f32[4,512,128]{2,1,0:T(8,128)} %copy-done.1, f32[4,512,128]{2,1,0:T(8,128)} %copy-done.2, ...), custom_call_target="tpu_custom_call", output_to_operand_aliasing={{0}: (6, {}), {1}: (7, {})} | custom-call | flops 3221225472 | bytes 8388608 | tf_op jit(solution)/shard_map/pallas_call | solution.py:194
  198.8 3.9 %collective-permute-start.25 = (f32[128,128]{1,0:T(8,128)S(1)}, f32[128,128]{1,0:T(8,128)S(1)}, u32[]{:S(2)}, u32[]{:S(2)}) collective-permute-start(f32[128,128]{1,0:T(8,128)S(1)} %get-tuple-element.235), channel_id=1, source_target_pairs={{0,16},{8,24},{16,0},{24,8},{1,17},{9,25},{17,1},{25,9},{2,18},{10... | collective-permute-start | bytes 196616 | tf_op jit(solution)/shard_map/ppermute | solution.py:382
  202.7 3.4 collective-permute-start.27
  206.1 3.4 collective-permute-start.28
  209.6 3.9 %collective-permute-start.29 = (f32[1,512,128]{2,1,0:T(8,128)}, f32[1,512,128]{2,1,0:T(8,128)S(1)}, u32[]{:S(2)}, u32[]{:S(2)}) collective-permute-start(f32[1,512,128]{2,1,0:T(8,128)} %get-tuple-element.158), channel_id=1, source_target_pairs={{0,8},{8,16},{16,24},{1,9},{9,17},{17,25},{2,10},{10,18},{18,26},{... | collective-permute-start | bytes 786440 | tf_op jit(solution)/shard_map/ppermute | solution.py:390
  213.4 4.0 %pick.1 = f32[512,1024]{1,0:T(8,128)} custom-call(s32[1]{0:T(128)} %bitcast.13.which, f32[512,1024]{1,0:T(8,128)} %get-tuple-element.152.refs_0_, f32[512,1024]{1,0:T(8,128)} %collective-permute-done.19.refs_1_, f32[512,1024]{1,0:T(8,128)} %collective-permute-done.20.refs_2_, f32[512,512]{1,0:T(8,128)} %collective-permute-done.21.refs_3_, f32[512,512]{1,0:T(8,128)} %copy-done.23), custom_call_target="tpu_custom_call" | custom-call | bytes 8388608 | tf_op jit(solution)/shard_map/pick/pallas_call | solution.py:357
  218.7 4.2 %collective-permute-done.29.refs_4_.refs_10_ = f32[1,512,128]{2,1,0:T(8,128)S(1)} collective-permute-done((f32[1,512,128]{2,1,0:T(8,128)}, f32[1,512,128]{2,1,0:T(8,128)S(1)}, u32[]{:S(2)}, u32[]{:S(2)}) %collective-permute-start.29) | collective-permute-done | bytes 262176 | tf_op jit(solution)/shard_map/ppermute | solution.py:390
  223.5 2.6 collective-permute-start.31
  226.1 3.1 collective-permute-done.30
  229.2 2.0 collective-permute-start.32
  231.2 4.0 %collective-permute-done.32 = f32[128,128]{1,0:T(8,128)S(1)} collective-permute-done((f32[128,128]{1,0:T(8,128)S(1)}, f32[128,128]{1,0:T(8,128)S(1)}, u32[]{:S(2)}, u32[]{:S(2)}) %collective-permute-start.32) | collective-permute-done | bytes 65568 | tf_op jit(solution)/shard_map/ppermute | solution.py:372
  236.2 3.6 shard_map.48
  240.9 7.4 %collective-permute-start.40 = (f32[2,512,128]{2,1,0:T(8,128)S(1)}, f32[2,512,128]{2,1,0:T(8,128)S(1)}, u32[]{:S(2)}, u32[]{:S(2)}) collective-permute-start(f32[2,512,128]{2,1,0:T(8,128)S(1)} %pad_maximum_fusion.1), channel_id=1, source_target_pairs={{0,8},{8,16},{16,24},{1,9},{9,17},{17,25},{2,10},{10,18},{18,26},{... | collective-permute-start | bytes 1572872 | tf_op jit(solution)/shard_map/ppermute | solution.py:390
  249.3 4.3 %collective-permute-start.41 = (f32[2,512,128]{2,1,0:T(8,128)S(1)}, f32[2,512,128]{2,1,0:T(8,128)S(1)}, u32[]{:S(2)}, u32[]{:S(2)}) collective-permute-start(f32[2,512,128]{2,1,0:T(8,128)S(1)} %pad_maximum_fusion.2), channel_id=1, source_target_pairs={{0,8},{8,16},{16,24},{1,9},{9,17},{17,25},{2,10},{10,18},{18,26},{... | collective-permute-start | bytes 1572872 | tf_op jit(solution)/shard_map/ppermute | solution.py:390
  253.7 2.6 fusion.4
  257.2 2.7 collective-permute-start.39
  259.9 16.2 %collective-permute-done.37 = f32[128,128]{1,0:T(8,128)S(1)} collective-permute-done((f32[128,128]{1,0:T(8,128)S(1)}, f32[128,128]{1,0:T(8,128)S(1)}, u32[]{:S(2)}, u32[]{:S(2)}) %collective-permute-start.37) | collective-permute-done | bytes 65568 | tf_op jit(solution)/shard_map/ppermute | solution.py:382
  277.6 2.6 collective-permute-start.43
  280.2 1.8 collective-permute-start.44
  289.9 3.9 %shard_map.49.refs_13_ = f32[512,128]{1,0:T(8,128)} custom-call(s32[10]{0:T(128)} %stack.100.where, f32[4,512,4096]{2,1,0:T(8,128)} %weights.15, f32[2,512,128]{2,1,0:T(8,128)} %copy-done.10, f32[2,512,128]{2,1,0:T(8,128)} %copy-done.12, f32[2,512,128]{2,1,0:T(8,128)} %copy-done.10, f32[2,512,128]{2,1,0:T(8,128)} %copy-done.12, ...), custom_call_target="tpu_custom_call", output_to_operand_aliasing={{}: (10, {})} | custom-call | flops 1610612736 | bytes 8388608 | tf_op jit(solution)/shard_map/pallas_call | solution.py:194
  293.8 4.8 %collective-permute-done.55.refs_2_ = f32[512,128]{1,0:T(8,128)} collective-permute-done((f32[512,128]{1,0:T(8,128)S(1)}, f32[512,128]{1,0:T(8,128)}, u32[]{:S(2)}, u32[]{:S(2)}) %collective-permute-start.55) | collective-permute-done | bytes 262176 | tf_op jit(solution)/shard_map/ppermute | solution.py:454
  302.2 2.8 collective-permute-start.49
  305.5 2.5 collective-permute-done.49
  308.1 2.2 collective-permute-done.50
  311.0 2.5 collective-permute-start.52
  314.7 2.8 collective-permute-done.52
  317.6 2.0 collective-permute-done.53
  320.6 8.5 %shard_map.50 = f32[512,128]{1,0:T(8,128)} custom-call(s32[10]{0:T(128)} %stack.100.where, f32[4,512,4096]{2,1,0:T(8,128)} %weights.15, f32[512,128]{1,0:T(8,128)} %copy-done.5, f32[512,128]{1,0:T(8,128)} %collective-permute-done.54.refs_1_, f32[512,128]{1,0:T(8,128)} %collective-permute-done.55.refs_2_, ...), custom_call_target="tpu_custom_call", output_to_operand_aliasing={{}: (15, {})} | custom-call | flops 1610612736 | bytes 8388608 | tf_op jit(solution)/shard_map/pallas_call | solution.py:194
  329.0 1.5 collective-permute-done.58
  330.6 2.6 fusion.12
  334.1 2.6 collective-permute-start.61
  340.3 1.9 collective-permute-start.63
  342.1 2.5 collective-permute-start.64
  346.2 1.7 collective-permute-start.66
  348.3 1.9 collective-permute-done.65
  351.4 2.4 collective-permute-done.67
  357.7 2.4 collective-permute-start.71
  368.9 2.2 collective-permute-done.74
  (188 shorter events, 59.0 us)
Async XLA Ops:
  0.0 27.7 %collective-permute-start = (f32[4,512,128]{2,1,0:T(8,128)}, f32[4,512,128]{2,1,0:T(8,128)S(1)}, u32[]{:S(2)}, u32[]{:S(2)}) collective-permute-start(f32[4,512,128]{2,1,0:T(8,128)} %refs_0_.2), channel_id=1, source_target_pairs={{0,2},{1,3},{2,4},{3,5},{4,6},{5,7},{8,10},{9,11},{10,12},{11,13},... | collective-permute-start | bytes 3145736 | tf_op jit(solution)/shard_map/ppermute | solution.py:229
  5.0 26.7 %collective-permute-start.1 = (f32[4,512,128]{2,1,0:T(8,128)}, f32[4,512,128]{2,1,0:T(8,128)S(1)}, u32[]{:S(2)}, u32[]{:S(2)}) collective-permute-start(f32[4,512,128]{2,1,0:T(8,128)} %refs_0_.2), channel_id=1, source_target_pairs={{2,0},{3,1},{4,2},{5,3},{6,4},{7,5},{10,8},{11,9},{12,10},{13,11},... | collective-permute-start | bytes 3145736 | tf_op jit(solution)/shard_map/ppermute | solution.py:229
  6.3 25.4 %collective-permute-start.3 = (f32[4,512,128]{2,1,0:T(8,128)}, f32[4,512,128]{2,1,0:T(8,128)}, u32[]{:S(2)}, u32[]{:S(2)}) collective-permute-start(f32[4,512,128]{2,1,0:T(8,128)} %refs_0_.2), channel_id=1, source_target_pairs={{0,1},{1,0},{2,3},{3,2},{4,5},{5,4},{6,7},{7,6},{8,9},{9,8},{10,11... | collective-permute-start | bytes 3145736 | tf_op jit(solution)/shard_map/ppermute | solution.py:226
  8.2 10.1 %collective-permute-start.2 = (f32[1,512,128]{2,1,0:T(8,128)S(1)}, f32[1,512,128]{2,1,0:T(8,128)S(1)}, u32[]{:S(2)}, u32[]{:S(2)}) collective-permute-start(f32[1,512,128]{2,1,0:T(8,128)S(1)} %get-tuple-element.210), channel_id=1, source_target_pairs={{0,8},{8,16},{16,24},{1,9},{9,17},{17,25},{2,10},{10,18},{18,26},{... | collective-permute-start | bytes 786440 | tf_op jit(solution)/shard_map/ppermute | solution.py:390
  31.9 14.4 %collective-permute-start.6 = (f32[4,512,128]{2,1,0:T(8,128)S(1)}, f32[4,512,128]{2,1,0:T(8,128)}, u32[]{:S(2)}, u32[]{:S(2)}) collective-permute-start(f32[4,512,128]{2,1,0:T(8,128)S(1)} %broadcast_select_fusion.refs_2_), channel_id=1, source_target_pairs={{0,1},{1,0},{2,3},{3,2},{4,5},{5,4},{6,7},{7,6},{8,9},{9,8},{10,11... | collective-permute-start | bytes 3145736 | tf_op jit(solution)/shard_map/ppermute | solution.py:226
  32.0 30.9 %collective-permute-start.4 = (f32[4,512,128]{2,1,0:T(8,128)}, f32[4,512,128]{2,1,0:T(8,128)S(1)}, u32[]{:S(2)}, u32[]{:S(2)}) collective-permute-start(f32[4,512,128]{2,1,0:T(8,128)} %copy-done.21), channel_id=1, source_target_pairs={{2,4},{3,5},{4,6},{5,7},{10,12},{11,13},{12,14},{13,15},{18,20},{1... | collective-permute-start | bytes 3145736 | tf_op jit(solution)/shard_map/ppermute | solution.py:229
  32.7 30.2 %collective-permute-start.5 = (f32[4,512,128]{2,1,0:T(8,128)S(1)}, f32[4,512,128]{2,1,0:T(8,128)}, u32[]{:S(2)}, u32[]{:S(2)}) collective-permute-start(f32[4,512,128]{2,1,0:T(8,128)S(1)} %collective-permute-done.1), channel_id=1, source_target_pairs={{2,0},{3,1},{4,2},{5,3},{10,8},{11,9},{12,10},{13,11},{18,16},{19,... | collective-permute-start | bytes 3145736 | tf_op jit(solution)/shard_map/ppermute | solution.py:229
  41.1 26.8 %collective-permute-start.9 = (f32[512,512]{1,0:T(8,128)}, f32[512,512]{1,0:T(8,128)}, u32[]{:S(2)}, u32[]{:S(2)}) collective-permute-start(f32[512,512]{1,0:T(8,128)} %get-tuple-element.117), channel_id=1, source_target_pairs={{0,16},{1,17},{2,18},{3,19},{4,20},{5,21},{6,22},{7,23}} | collective-permute-start | bytes 3145736 | tf_op jit(solution)/shard_map/ppermute | solution.py:401
  67.9 17.6 %collective-permute-start.7 = (f32[4,512,128]{2,1,0:T(8,128)S(1)}, f32[4,512,128]{2,1,0:T(8,128)}, u32[]{:S(2)}, u32[]{:S(2)}) collective-permute-start(f32[4,512,128]{2,1,0:T(8,128)S(1)} %collective-permute-done.4), channel_id=1, source_target_pairs={{4,6},{5,7},{12,14},{13,15},{20,22},{21,23},{28,30},{29,31}} | collective-permute-start | bytes 3145736 | tf_op jit(solution)/shard_map/ppermute | solution.py:229
  69.6 30.1 %collective-permute-start.8 = (f32[4,512,128]{2,1,0:T(8,128)}, f32[4,512,128]{2,1,0:T(8,128)}, u32[]{:S(2)}, u32[]{:S(2)}) collective-permute-start(f32[4,512,128]{2,1,0:T(8,128)} %collective-permute-done.5), channel_id=1, source_target_pairs={{2,0},{3,1},{10,8},{11,9},{18,16},{19,17},{26,24},{27,25}} | collective-permute-start | bytes 3145736 | tf_op jit(solution)/shard_map/ppermute | solution.py:229
  70.9 10.6 %collective-permute-start.11 = (f32[1,512,128]{2,1,0:T(8,128)S(1)}, f32[1,512,128]{2,1,0:T(8,128)S(1)}, u32[]{:S(2)}, u32[]{:S(2)}) collective-permute-start(f32[1,512,128]{2,1,0:T(8,128)S(1)} %collective-permute-done.2.refs_0_.refs_4_), channel_id=1, source_target_pairs={{0,1},{1,0},{2,3},{3,2},{4,5},{5,4},{6,7},{7,6},{8,9},{9,8},{10,11... | collective-permute-start | bytes 786440 | tf_op jit(solution)/shard_map/ppermute | solution.py:226
  101.1 7.8 %collective-permute-start.12 = (f32[4,512,128]{2,1,0:T(8,128)S(1)}, f32[4,512,128]{2,1,0:T(8,128)S(1)}, u32[]{:S(2)}, u32[]{:S(2)}) collective-permute-start(f32[4,512,128]{2,1,0:T(8,128)S(1)} %select_select_fusion.near.near_before), channel_id=1, source_target_pairs={{0,1},{1,0},{2,3},{3,2},{4,5},{5,4},{6,7},{7,6},{8,9},{9,8},{10,11... | collective-permute-start | bytes 3145736 | tf_op jit(solution)/shard_map/ppermute | solution.py:226
  101.2 94.9 %collective-permute-start.19 = (f32[512,1024]{1,0:T(8,128)}, f32[512,1024]{1,0:T(8,128)}, u32[]{:S(2)}, u32[]{:S(2)}) collective-permute-start(f32[512,1024]{1,0:T(8,128)} %get-tuple-element.145), channel_id=1, source_target_pairs={{0,8},{1,9},{2,10},{3,11},{4,12},{5,13},{6,14},{7,15}} | collective-permute-start | bytes 6291464 | tf_op jit(solution)/shard_map/ppermute | solution.py:402
  103.8 92.3 %collective-permute-start.20 = (f32[512,1024]{1,0:T(8,128)}, f32[512,1024]{1,0:T(8,128)}, u32[]{:S(2)}, u32[]{:S(2)}) collective-permute-start(f32[512,1024]{1,0:T(8,128)} %get-tuple-element.146), channel_id=1, source_target_pairs={{0,16},{1,17},{2,18},{3,19},{4,20},{5,21},{6,22},{7,23}} | collective-permute-start | bytes 6291464 | tf_op jit(solution)/shard_map/ppermute | solution.py:402
  118.2 31.7 %collective-permute-start.13 = (f32[128,128]{1,0:T(8,128)S(1)}, f32[128,128]{1,0:T(8,128)S(1)}, u32[]{:S(2)}, u32[]{:S(2)}) collective-permute-start(f32[128,128]{1,0:T(8,128)S(1)} %get-tuple-element.236), channel_id=1, source_target_pairs={{0,8},{8,0},{16,24},{24,16},{1,9},{9,1},{17,25},{25,17},{2,10},{10... | collective-permute-start | bytes 196616 | tf_op jit(solution)/shard_map/ppermute | solution.py:382
  118.3 36.4 %collective-permute-start.14 = (f32[128,128]{1,0:T(8,128)S(1)}, f32[128,128]{1,0:T(8,128)S(1)}, u32[]{:S(2)}, u32[]{:S(2)}) collective-permute-start(f32[128,128]{1,0:T(8,128)S(1)} %get-tuple-element.238), channel_id=1, source_target_pairs={{0,16},{8,24},{16,0},{24,8},{1,17},{9,25},{17,1},{25,9},{2,18},{10... | collective-permute-start | bytes 196616 | tf_op jit(solution)/shard_map/ppermute | solution.py:382
  118.4 77.8 %collective-permute-start.22 = (f32[512,512]{1,0:T(8,128)}, f32[512,512]{1,0:T(8,128)S(1)}, u32[]{:S(2)}, u32[]{:S(2)}) collective-permute-start(f32[512,512]{1,0:T(8,128)} %collective-permute-done.9), channel_id=1, source_target_pairs={{16,24},{17,25},{18,26},{19,27},{20,28},{21,29},{22,30},{23,31}} | collective-permute-start | bytes 3145736 | tf_op jit(solution)/shard_map/ppermute | solution.py:411
  149.9 46.3 %collective-permute-start.21 = (f32[512,512]{1,0:T(8,128)}, f32[512,512]{1,0:T(8,128)}, u32[]{:S(2)}, u32[]{:S(2)}) collective-permute-start(f32[512,512]{1,0:T(8,128)} %get-tuple-element.149), channel_id=1, source_target_pairs={{0,24},{1,25},{2,26},{3,27},{4,28},{5,29},{6,30},{7,31}} | collective-permute-start | bytes 3145736 | tf_op jit(solution)/shard_map/ppermute | solution.py:420
  154.7 20.9 %collective-permute-start.15 = (f32[128,128]{1,0:T(8,128)S(1)}, f32[128,128]{1,0:T(8,128)S(1)}, u32[]{:S(2)}, u32[]{:S(2)}) collective-permute-start(f32[128,128]{1,0:T(8,128)S(1)} %get-tuple-element.237), channel_id=1, source_target_pairs={{0,24},{8,16},{16,8},{24,0},{1,25},{9,17},{17,9},{25,1},{2,26},{10... | collective-permute-start | bytes 196616 | tf_op jit(solution)/shard_map/ppermute | solution.py:382
  180.7 6.0 %collective-permute-start.17 = (f32[128,128]{1,0:T(8,128)S(1)}, f32[128,128]{1,0:T(8,128)S(1)}, u32[]{:S(2)}, u32[]{:S(2)}) collective-permute-start(f32[128,128]{1,0:T(8,128)S(1)} %bitcast_subtract_fusion), channel_id=1, source_target_pairs={{0,4},{1,5},{2,6},{3,7},{4,0},{5,1},{6,2},{7,3},{8,12},{9,13},{10,... | collective-permute-start | bytes 196616 | tf_op jit(solution)/shard_map/ppermute | solution.py:372
  186.7 9.3 %collective-permute-start.18 = (f32[128,128]{1,0:T(8,128)S(1)}, f32[128,128]{1,0:T(8,128)S(1)}, u32[]{:S(2)}, u32[]{:S(2)}) collective-permute-start(f32[128,128]{1,0:T(8,128)S(1)} %bitcast_subtract_fusion), channel_id=1, source_target_pairs={{0,6},{1,7},{2,4},{3,5},{4,2},{5,3},{6,0},{7,1},{8,14},{9,15},{10,... | collective-permute-start | bytes 196616 | tf_op jit(solution)/shard_map/ppermute | solution.py:372
  198.8 10.8 %collective-permute-start.24 = (f32[128,128]{1,0:T(8,128)S(1)}, f32[128,128]{1,0:T(8,128)S(1)}, u32[]{:S(2)}, u32[]{:S(2)}) collective-permute-start(f32[128,128]{1,0:T(8,128)S(1)} %get-tuple-element.233), channel_id=1, source_target_pairs={{0,8},{8,0},{16,24},{24,16},{1,9},{9,1},{17,25},{25,17},{2,10},{10... | collective-permute-start | bytes 196616 | tf_op jit(solution)/shard_map/ppermute | solution.py:382
  198.8 18.6 %collective-permute-start.25 = (f32[128,128]{1,0:T(8,128)S(1)}, f32[128,128]{1,0:T(8,128)S(1)}, u32[]{:S(2)}, u32[]{:S(2)}) collective-permute-start(f32[128,128]{1,0:T(8,128)S(1)} %get-tuple-element.235), channel_id=1, source_target_pairs={{0,16},{8,24},{16,0},{24,8},{1,17},{9,25},{17,1},{25,9},{2,18},{10... | collective-permute-start | bytes 196616 | tf_op jit(solution)/shard_map/ppermute | solution.py:382
  202.7 14.7 %collective-permute-start.26 = (f32[128,128]{1,0:T(8,128)S(1)}, f32[128,128]{1,0:T(8,128)S(1)}, u32[]{:S(2)}, u32[]{:S(2)}) collective-permute-start(f32[128,128]{1,0:T(8,128)S(1)} %get-tuple-element.234), channel_id=1, source_target_pairs={{0,24},{8,16},{16,8},{24,0},{1,25},{9,17},{17,9},{25,1},{2,26},{10... | collective-permute-start | bytes 196616 | tf_op jit(solution)/shard_map/ppermute | solution.py:382
  202.7 14.7 %collective-permute-start.27 = (f32[1,512,128]{2,1,0:T(8,128)}, f32[1,512,128]{2,1,0:T(8,128)S(1)}, u32[]{:S(2)}, u32[]{:S(2)}) collective-permute-start(f32[1,512,128]{2,1,0:T(8,128)} %get-tuple-element.148), channel_id=1, source_target_pairs={{0,8},{8,16},{16,24},{1,9},{9,17},{17,25},{2,10},{10,18},{18,26},{... | collective-permute-start | bytes 786440 | tf_op jit(solution)/shard_map/ppermute | solution.py:390
  206.1 12.6 %collective-permute-start.28 = (f32[1,512,128]{2,1,0:T(8,128)}, f32[1,512,128]{2,1,0:T(8,128)S(1)}, u32[]{:S(2)}, u32[]{:S(2)}) collective-permute-start(f32[1,512,128]{2,1,0:T(8,128)} %get-tuple-element.157), channel_id=1, source_target_pairs={{0,8},{8,16},{16,24},{1,9},{9,17},{17,25},{2,10},{10,18},{18,26},{... | collective-permute-start | bytes 786440 | tf_op jit(solution)/shard_map/ppermute | solution.py:390
  209.6 13.4 %collective-permute-start.29 = (f32[1,512,128]{2,1,0:T(8,128)}, f32[1,512,128]{2,1,0:T(8,128)S(1)}, u32[]{:S(2)}, u32[]{:S(2)}) collective-permute-start(f32[1,512,128]{2,1,0:T(8,128)} %get-tuple-element.158), channel_id=1, source_target_pairs={{0,8},{8,16},{16,24},{1,9},{9,17},{17,25},{2,10},{10,18},{18,26},{... | collective-permute-start | bytes 786440 | tf_op jit(solution)/shard_map/ppermute | solution.py:390
  222.9 12.4 %collective-permute-start.33 = (f32[1,512,128]{2,1,0:T(8,128)S(1)}, f32[1,512,128]{2,1,0:T(8,128)S(1)}, u32[]{:S(2)}, u32[]{:S(2)}) collective-permute-start(f32[1,512,128]{2,1,0:T(8,128)S(1)} %collective-permute-done.27.refs_0_.refs_6_), channel_id=1, source_target_pairs={{0,1},{1,0},{2,3},{3,2},{4,5},{5,4},{6,7},{7,6},{8,9},{9,8},{10,11... | collective-permute-start | bytes 786440 | tf_op jit(solution)/shard_map/ppermute | solution.py:226
  222.9 12.4 %collective-permute-start.34 = (f32[1,512,128]{2,1,0:T(8,128)S(1)}, f32[1,512,128]{2,1,0:T(8,128)S(1)}, u32[]{:S(2)}, u32[]{:S(2)}) collective-permute-start(f32[1,512,128]{2,1,0:T(8,128)S(1)} %collective-permute-done.28.refs_2_.refs_8_), channel_id=1, source_target_pairs={{0,1},{1,0},{2,3},{3,2},{4,5},{5,4},{6,7},{7,6},{8,9},{9,8},{10,11... | collective-permute-start | bytes 786440 | tf_op jit(solution)/shard_map/ppermute | solution.py:226
  223.4 12.7 %collective-permute-start.35 = (f32[1,512,128]{2,1,0:T(8,128)S(1)}, f32[1,512,128]{2,1,0:T(8,128)}, u32[]{:S(2)}, u32[]{:S(2)}) collective-permute-start(f32[1,512,128]{2,1,0:T(8,128)S(1)} %collective-permute-done.29.refs_4_.refs_10_), channel_id=1, source_target_pairs={{0,1},{1,0},{2,3},{3,2},{4,5},{5,4},{6,7},{7,6},{8,9},{9,8},{10,11... | collective-permute-start | bytes 786440 | tf_op jit(solution)/shard_map/ppermute | solution.py:226
  223.5 5.7 %collective-permute-start.30 = (f32[128,128]{1,0:T(8,128)S(1)}, f32[128,128]{1,0:T(8,128)S(1)}, u32[]{:S(2)}, u32[]{:S(2)}) collective-permute-start(f32[128,128]{1,0:T(8,128)S(1)} %add_add_fusion.1), channel_id=1, source_target_pairs={{0,2},{1,3},{2,0},{3,1},{4,6},{5,7},{6,4},{7,5},{8,10},{9,11},{10,... | collective-permute-start | bytes 196616 | tf_op jit(solution)/shard_map/ppermute | solution.py:372
  223.5 7.8 %collective-permute-start.31 = (f32[128,128]{1,0:T(8,128)S(1)}, f32[128,128]{1,0:T(8,128)S(1)}, u32[]{:S(2)}, u32[]{:S(2)}) collective-permute-start(f32[128,128]{1,0:T(8,128)S(1)} %add_add_fusion.1), channel_id=1, source_target_pairs={{0,4},{1,5},{2,6},{3,7},{4,0},{5,1},{6,2},{7,3},{8,12},{9,13},{10,... | collective-permute-start | bytes 196616 | tf_op jit(solution)/shard_map/ppermute | solution.py:372
  229.2 6.1 %collective-permute-start.32 = (f32[128,128]{1,0:T(8,128)S(1)}, f32[128,128]{1,0:T(8,128)S(1)}, u32[]{:S(2)}, u32[]{:S(2)}) collective-permute-start(f32[128,128]{1,0:T(8,128)S(1)} %add_add_fusion.1), channel_id=1, source_target_pairs={{0,6},{1,7},{2,4},{3,5},{4,2},{5,3},{6,0},{7,1},{8,14},{9,15},{10,... | collective-permute-start | bytes 196616 | tf_op jit(solution)/shard_map/ppermute | solution.py:372
  239.8 13.9 %collective-permute-start.36 = (f32[512,128]{1,0:T(8,128)S(1)}, f32[512,128]{1,0:T(8,128)S(1)}, u32[]{:S(2)}, u32[]{:S(2)}) collective-permute-start(f32[512,128]{1,0:T(8,128)S(1)} %pad_maximum_fusion.5.refs_0_), channel_id=1, source_target_pairs={{0,1},{1,0},{2,3},{3,2},{4,5},{5,4},{6,7},{7,6},{8,9},{9,8},{10,11... | collective-permute-start | bytes 786440 | tf_op jit(solution)/shard_map/ppermute | solution.py:226
  240.9 36.1 %collective-permute-start.40 = (f32[2,512,128]{2,1,0:T(8,128)S(1)}, f32[2,512,128]{2,1,0:T(8,128)S(1)}, u32[]{:S(2)}, u32[]{:S(2)}) collective-permute-start(f32[2,512,128]{2,1,0:T(8,128)S(1)} %pad_maximum_fusion.1), channel_id=1, source_target_pairs={{0,8},{8,16},{16,24},{1,9},{9,17},{17,25},{2,10},{10,18},{18,26},{... | collective-permute-start | bytes 1572872 | tf_op jit(solution)/shard_map/ppermute | solution.py:390
  249.3 27.7 %collective-permute-start.41 = (f32[2,512,128]{2,1,0:T(8,128)S(1)}, f32[2,512,128]{2,1,0:T(8,128)S(1)}, u32[]{:S(2)}, u32[]{:S(2)}) collective-permute-start(f32[2,512,128]{2,1,0:T(8,128)S(1)} %pad_maximum_fusion.2), channel_id=1, source_target_pairs={{0,8},{8,16},{16,24},{1,9},{9,17},{17,25},{2,10},{10,18},{18,26},{... | collective-permute-start | bytes 1572872 | tf_op jit(solution)/shard_map/ppermute | solution.py:390
  256.4 19.7 %collective-permute-start.37 = (f32[128,128]{1,0:T(8,128)S(1)}, f32[128,128]{1,0:T(8,128)S(1)}, u32[]{:S(2)}, u32[]{:S(2)}) collective-permute-start(f32[128,128]{1,0:T(8,128)S(1)} %get-tuple-element.230), channel_id=1, source_target_pairs={{0,8},{8,0},{16,24},{24,16},{1,9},{9,1},{17,25},{25,17},{2,10},{10... | collective-permute-start | bytes 196616 | tf_op jit(solution)/shard_map/ppermute | solution.py:382
  257.2 18.9 %collective-permute-start.38 = (f32[128,128]{1,0:T(8,128)S(1)}, f32[128,128]{1,0:T(8,128)S(1)}, u32[]{:S(2)}, u32[]{:S(2)}) collective-permute-start(f32[128,128]{1,0:T(8,128)S(1)} %get-tuple-element.232), channel_id=1, source_target_pairs={{0,16},{8,24},{16,0},{24,8},{1,17},{9,25},{17,1},{25,9},{2,18},{10... | collective-permute-start | bytes 196616 | tf_op jit(solution)/shard_map/ppermute | solution.py:382
  257.2 18.9 %collective-permute-start.39 = (f32[128,128]{1,0:T(8,128)S(1)}, f32[128,128]{1,0:T(8,128)S(1)}, u32[]{:S(2)}, u32[]{:S(2)}) collective-permute-start(f32[128,128]{1,0:T(8,128)S(1)} %get-tuple-element.231), channel_id=1, source_target_pairs={{0,24},{8,16},{16,8},{24,0},{1,25},{9,17},{17,9},{25,1},{2,26},{10... | collective-permute-start | bytes 196616 | tf_op jit(solution)/shard_map/ppermute | solution.py:382
  277.0 12.1 %collective-permute-start.45 = (f32[2,512,128]{2,1,0:T(8,128)S(1)}, f32[2,512,128]{2,1,0:T(8,128)S(1)}, u32[]{:S(2)}, u32[]{:S(2)}) collective-permute-start(f32[2,512,128]{2,1,0:T(8,128)S(1)} %collective-permute-done.40.refs_0_.refs_2_), channel_id=1, source_target_pairs={{0,1},{1,0},{2,3},{3,2},{4,5},{5,4},{6,7},{7,6},{8,9},{9,8},{10,11... | collective-permute-start | bytes 1572872 | tf_op jit(solution)/shard_map/ppermute | solution.py:226
  277.1 12.8 %collective-permute-start.46 = (f32[2,512,128]{2,1,0:T(8,128)S(1)}, f32[2,512,128]{2,1,0:T(8,128)}, u32[]{:S(2)}, u32[]{:S(2)}) collective-permute-start(f32[2,512,128]{2,1,0:T(8,128)S(1)} %collective-permute-done.41.refs_4_.refs_6_), channel_id=1, source_target_pairs={{0,1},{1,0},{2,3},{3,2},{4,5},{5,4},{6,7},{7,6},{8,9},{9,8},{10,11... | collective-permute-start | bytes 1572872 | tf_op jit(solution)/shard_map/ppermute | solution.py:226
  277.6 5.2 %collective-permute-start.42 = (f32[128,128]{1,0:T(8,128)S(1)}, f32[128,128]{1,0:T(8,128)S(1)}, u32[]{:S(2)}, u32[]{:S(2)}) collective-permute-start(f32[128,128]{1,0:T(8,128)S(1)} %bitcast_subtract_fusion.1), channel_id=1, source_target_pairs={{0,2},{1,3},{2,0},{3,1},{4,6},{5,7},{6,4},{7,5},{8,10},{9,11},{10,... | collective-permute-start | bytes 196616 | tf_op jit(solution)/shard_map/ppermute | solution.py:372
  277.6 7.9 %collective-permute-start.43 = (f32[128,128]{1,0:T(8,128)S(1)}, f32[128,128]{1,0:T(8,128)S(1)}, u32[]{:S(2)}, u32[]{:S(2)}) collective-permute-start(f32[128,128]{1,0:T(8,128)S(1)} %bitcast_subtract_fusion.1), channel_id=1, source_target_pairs={{0,4},{1,5},{2,6},{3,7},{4,0},{5,1},{6,2},{7,3},{8,12},{9,13},{10,... | collective-permute-start | bytes 196616 | tf_op jit(solution)/shard_map/ppermute | solution.py:372
  280.2 6.6 %collective-permute-start.44 = (f32[128,128]{1,0:T(8,128)S(1)}, f32[128,128]{1,0:T(8,128)S(1)}, u32[]{:S(2)}, u32[]{:S(2)}) collective-permute-start(f32[128,128]{1,0:T(8,128)S(1)} %bitcast_subtract_fusion.1), channel_id=1, source_target_pairs={{0,6},{1,7},{2,4},{3,5},{4,2},{5,3},{6,0},{7,1},{8,14},{9,15},{10,... | collective-permute-start | bytes 196616 | tf_op jit(solution)/shard_map/ppermute | solution.py:372
  282.8 11.1 %collective-permute-start.54 = (f32[512,128]{1,0:T(8,128)S(1)}, f32[512,128]{1,0:T(8,128)}, u32[]{:S(2)}, u32[]{:S(2)}) collective-permute-start(f32[512,128]{1,0:T(8,128)S(1)} %pad_maximum_fusion.5.refs_0_), channel_id=1, source_target_pairs={{8,0},{9,1},{10,2},{11,3},{12,4},{13,5},{14,6},{15,7}} | collective-permute-start | bytes 786440 | tf_op jit(solution)/shard_map/ppermute | solution.py:454
  285.5 13.1 %collective-permute-start.55 = (f32[512,128]{1,0:T(8,128)S(1)}, f32[512,128]{1,0:T(8,128)}, u32[]{:S(2)}, u32[]{:S(2)}) collective-permute-start(f32[512,128]{1,0:T(8,128)S(1)} %pad_maximum_fusion.5.refs_0_), channel_id=1, source_target_pairs={{16,0},{17,1},{18,2},{19,3},{20,4},{21,5},{22,6},{23,7}} | collective-permute-start | bytes 786440 | tf_op jit(solution)/shard_map/ppermute | solution.py:454
  286.8 11.8 %collective-permute-start.56 = (f32[512,128]{1,0:T(8,128)S(1)}, f32[512,128]{1,0:T(8,128)}, u32[]{:S(2)}, u32[]{:S(2)}) collective-permute-start(f32[512,128]{1,0:T(8,128)S(1)} %pad_maximum_fusion.5.refs_0_), channel_id=1, source_target_pairs={{24,0},{25,1},{26,2},{27,3},{28,4},{29,5},{30,6},{31,7}} | collective-permute-start | bytes 786440 | tf_op jit(solution)/shard_map/ppermute | solution.py:454
  293.8 6.1 %collective-permute-start.47 = (f32[512,128]{1,0:T(8,128)}, f32[512,128]{1,0:T(8,128)S(1)}, u32[]{:S(2)}, u32[]{:S(2)}) collective-permute-start(f32[512,128]{1,0:T(8,128)} %pad_maximum_fusion.6), channel_id=1, source_target_pairs={{0,1},{1,0},{2,3},{3,2},{4,5},{5,4},{6,7},{7,6},{8,9},{9,8},{10,11... | collective-permute-start | bytes 786440 | tf_op jit(solution)/shard_map/ppermute | solution.py:226
  299.9 19.7 %collective-permute-start.57 = (f32[4,512,128]{2,1,0:T(8,128)S(1)}, f32[4,512,128]{2,1,0:T(8,128)S(1)}, u32[]{:S(2)}, u32[]{:S(2)}) collective-permute-start(f32[4,512,128]{2,1,0:T(8,128)S(1)} %pad_maximum_fusion), channel_id=1, source_target_pairs={{0,1},{1,0},{2,3},{3,2},{4,5},{5,4},{6,7},{7,6},{8,9},{9,8},{10,11... | collective-permute-start | bytes 3145736 | tf_op jit(solution)/shard_map/ppermute | solution.py:226
  302.2 5.8 %collective-permute-start.49 = (f32[128,128]{1,0:T(8,128)S(1)}, f32[128,128]{1,0:T(8,128)S(1)}, u32[]{:S(2)}, u32[]{:S(2)}) collective-permute-start(f32[128,128]{1,0:T(8,128)S(1)} %get-tuple-element.229), channel_id=1, source_target_pairs={{0,16},{8,24},{16,0},{24,8},{1,17},{9,25},{17,1},{25,9},{2,18},{10... | collective-permute-start | bytes 196616 | tf_op jit(solution)/shard_map/ppermute | solution.py:382
  305.1 5.2 %collective-permute-start.50 = (f32[128,128]{1,0:T(8,128)S(1)}, f32[128,128]{1,0:T(8,128)S(1)}, u32[]{:S(2)}, u32[]{:S(2)}) collective-permute-start(f32[128,128]{1,0:T(8,128)S(1)} %get-tuple-element.228), channel_id=1, source_target_pairs={{0,24},{8,16},{16,8},{24,0},{1,25},{9,17},{17,9},{25,1},{2,26},{10... | collective-permute-start | bytes 196616 | tf_op jit(solution)/shard_map/ppermute | solution.py:382
  311.0 6.6 %collective-permute-start.52 = (f32[128,128]{1,0:T(8,128)S(1)}, f32[128,128]{1,0:T(8,128)S(1)}, u32[]{:S(2)}, u32[]{:S(2)}) collective-permute-start(f32[128,128]{1,0:T(8,128)S(1)} %add_add_fusion), channel_id=1, source_target_pairs={{0,4},{1,5},{2,6},{3,7},{4,0},{5,1},{6,2},{7,3},{8,12},{9,13},{10,... | collective-permute-start | bytes 196616 | tf_op jit(solution)/shard_map/ppermute | solution.py:372
  313.5 6.1 %collective-permute-start.53 = (f32[128,128]{1,0:T(8,128)S(1)}, f32[128,128]{1,0:T(8,128)S(1)}, u32[]{:S(2)}, u32[]{:S(2)}) collective-permute-start(f32[128,128]{1,0:T(8,128)S(1)} %add_add_fusion), channel_id=1, source_target_pairs={{0,6},{1,7},{2,4},{3,5},{4,2},{5,3},{6,0},{7,1},{8,14},{9,15},{10,... | collective-permute-start | bytes 196616 | tf_op jit(solution)/shard_map/ppermute | solution.py:372
  334.1 5.2 %collective-permute-start.61 = (f32[128,128]{1,0:T(8,128)S(1)}, f32[128,128]{1,0:T(8,128)S(1)}, u32[]{:S(2)}, u32[]{:S(2)}) collective-permute-start(f32[128,128]{1,0:T(8,128)S(1)} %get-tuple-element.225), channel_id=1, source_target_pairs={{0,24},{8,16},{16,8},{24,0},{1,25},{9,17},{17,9},{25,1},{2,26},{10... | collective-permute-start | bytes 196616 | tf_op jit(solution)/shard_map/ppermute | solution.py:382
  340.2 7.7 %collective-permute-start.62 = (f32[128,128]{1,0:T(8,128)S(1)}, f32[128,128]{1,0:T(8,128)S(1)}, u32[]{:S(2)}, u32[]{:S(2)}) collective-permute-start(f32[128,128]{1,0:T(8,128)S(1)} %bitcast_subtract_fusion.2), channel_id=1, source_target_pairs={{0,2},{1,3},{2,0},{3,1},{4,6},{5,7},{6,4},{7,5},{8,10},{9,11},{10,... | collective-permute-start | bytes 196616 | tf_op jit(solution)/shard_map/ppermute | solution.py:372
  340.3 7.9 %collective-permute-start.63 = (f32[128,128]{1,0:T(8,128)S(1)}, f32[128,128]{1,0:T(8,128)S(1)}, u32[]{:S(2)}, u32[]{:S(2)}) collective-permute-start(f32[128,128]{1,0:T(8,128)S(1)} %bitcast_subtract_fusion.2), channel_id=1, source_target_pairs={{0,4},{1,5},{2,6},{3,7},{4,0},{5,1},{6,2},{7,3},{8,12},{9,13},{10,... | collective-permute-start | bytes 196616 | tf_op jit(solution)/shard_map/ppermute | solution.py:372
  342.1 6.1 %collective-permute-start.64 = (f32[128,128]{1,0:T(8,128)S(1)}, f32[128,128]{1,0:T(8,128)S(1)}, u32[]{:S(2)}, u32[]{:S(2)}) collective-permute-start(f32[128,128]{1,0:T(8,128)S(1)} %bitcast_subtract_fusion.2), channel_id=1, source_target_pairs={{0,6},{1,7},{2,4},{3,5},{4,2},{5,3},{6,0},{7,1},{8,14},{9,15},{10,... | collective-permute-start | bytes 196616 | tf_op jit(solution)/shard_map/ppermute | solution.py:372
  344.7 5.5 %collective-permute-start.65 = (f32[2,128,128]{2,1,0:T(8,128)S(1)}, f32[2,128,128]{2,1,0:T(8,128)S(1)}, u32[]{:S(2)}, u32[]{:S(2)}) collective-permute-start(f32[2,128,128]{2,1,0:T(8,128)S(1)} %pad_maximum_fusion.9), channel_id=1, source_target_pairs={{0,8},{8,0},{16,24},{24,16},{1,9},{9,1},{17,25},{25,17},{2,10},{10... | collective-permute-start | bytes 393224 | tf_op jit(solution)/shard_map/ppermute | solution.py:386
  346.2 5.2 %collective-permute-start.66 = (f32[2,128,128]{2,1,0:T(8,128)S(1)}, f32[2,128,128]{2,1,0:T(8,128)S(1)}, u32[]{:S(2)}, u32[]{:S(2)}) collective-permute-start(f32[2,128,128]{2,1,0:T(8,128)S(1)} %pad_maximum_fusion.9), channel_id=1, source_target_pairs={{0,16},{8,24},{16,0},{24,8},{1,17},{9,25},{17,1},{25,9},{2,18},{10... | collective-permute-start | bytes 393224 | tf_op jit(solution)/shard_map/ppermute | solution.py:386
  347.9 5.9 %collective-permute-start.67 = (f32[2,128,128]{2,1,0:T(8,128)S(1)}, f32[2,128,128]{2,1,0:T(8,128)S(1)}, u32[]{:S(2)}, u32[]{:S(2)}) collective-permute-start(f32[2,128,128]{2,1,0:T(8,128)S(1)} %pad_maximum_fusion.9), channel_id=1, source_target_pairs={{0,24},{8,16},{16,8},{24,0},{1,25},{9,17},{17,9},{25,1},{2,26},{10... | collective-permute-start | bytes 393224 | tf_op jit(solution)/shard_map/ppermute | solution.py:386
  357.2 5.0 %collective-permute-start.70 = (f32[128,128]{1,0:T(8,128)S(1)}, f32[128,128]{1,0:T(8,128)S(1)}, u32[]{:S(2)}, u32[]{:S(2)}) collective-permute-start(f32[128,128]{1,0:T(8,128)S(1)} %get-tuple-element.223), channel_id=1, source_target_pairs={{0,16},{8,24},{16,0},{24,8},{1,17},{9,25},{17,1},{25,9},{2,18},{10... | collective-permute-start | bytes 196616 | tf_op jit(solution)/shard_map/ppermute | solution.py:382
  357.7 5.2 %collective-permute-start.71 = (f32[128,128]{1,0:T(8,128)S(1)}, f32[128,128]{1,0:T(8,128)S(1)}, u32[]{:S(2)}, u32[]{:S(2)}) collective-permute-start(f32[128,128]{1,0:T(8,128)S(1)} %get-tuple-element.222), channel_id=1, source_target_pairs={{0,24},{8,16},{16,8},{24,0},{1,25},{9,17},{17,9},{25,1},{2,26},{10... | collective-permute-start | bytes 196616 | tf_op jit(solution)/shard_map/ppermute | solution.py:382
  362.9 4.9 %collective-permute-start.72 = (f32[1,128,128]{2,1,0:T(8,128)S(1)}, f32[1,128,128]{2,1,0:T(8,128)S(1)}, u32[]{:S(2)}, u32[]{:S(2)}) collective-permute-start(f32[1,128,128]{2,1,0:T(8,128)S(1)} %add_bitcast_fusion), channel_id=1, source_target_pairs={{0,8},{8,0},{16,24},{24,16},{1,9},{9,1},{17,25},{25,17},{2,10},{10... | collective-permute-start | bytes 196616 | tf_op jit(solution)/shard_map/ppermute | solution.py:386
  365.9 5.2 %collective-permute-start.74 = (f32[1,128,128]{2,1,0:T(8,128)S(1)}, f32[1,128,128]{2,1,0:T(8,128)S(1)}, u32[]{:S(2)}, u32[]{:S(2)}) collective-permute-start(f32[1,128,128]{2,1,0:T(8,128)S(1)} %add_bitcast_fusion), channel_id=1, source_target_pairs={{0,24},{8,16},{16,8},{24,0},{1,25},{9,17},{17,9},{25,1},{2,26},{10... | collective-permute-start | bytes 196616 | tf_op jit(solution)/shard_map/ppermute | solution.py:386
  (35 other events, 334.4 us)

commit v5 on v3

--- a/solution.py
+++ b/solution.py
@@ -408,7 +408,10 @@
         if stage == 1:
             pieces = [history, own_far, *pieces]
         totals, tail = add_chip(totals, pieces, stage if stage > 1 else 0)
-        entered.append(enter(tail))
+        if stage == chips - 2:
+            waiting = tail
+        else:
+            entered.append(enter(tail))
         if stage == 1:
             last_near, tail = tie((last_near, tail))
             sent.append(lax.ppermute(last_near, "lag", [(0, groups - 1)]))
@@ -424,9 +427,9 @@
     first, tail = add_first(first, near, far, chips - 1)
 
     right_side = own_part(excitation[0]) - sum_parts(first)
-    right_side, tail, near, far, one, two = tie((right_side, tail, near, far, one, two))
+    right_side, waiting, tail, near, far, one, two = tie((right_side, waiting, tail, near, far, one, two))
     mine = gather_near(right_side)
-    entered.append(enter(tail))
+    entered += [enter(waiting), enter(tail)]
     one, two = add_rest(one, two, near, far, chips - 1)
     mine, one, two, sent = tie((mine, one, two, sent))
     density = sum_parts(multiply(head_columns, mine))
@@ -444,11 +447,12 @@
     mine = gather_near(right_side)
     nears = [old] + [lax.ppermute(old, "lag", [(j, 0)]) for j in range(1, groups)]
     mine, two = tie((mine, two))
-    density = sum_parts(multiply(head_columns, mine))
+    carried = multiply(head_columns, mine)
+    density = sum_parts(carried)
     fars = other_core(jnp.stack(nears))
     results.append(density)
 
-    density, two, nears, fars = tie((density, two, nears, fars))
+    density, two = tie((density, two))
     mine = gather_near(density)
     two = add_second(two, nears, both, fars)
     mine, two = tie((mine, two))

time: 363 us -> 368 us (1.014)
  waiting for transfers between devices: 160 us -> 165 us
    ppermute x15, waiting for transfers between devices: 17.7 us -> 27.4 us  [gather_near(): lax.ppermute(value, 'row', pairs(devices, 2 * k))]
    ppermute x6, waiting for transfers between devices: 4.47 us -> 10.5 us  [whole_rows(): lax.ppermute(value, 'lag', pairs(groups, mask))]
    ppermute x3, waiting for transfers between devices: 6.47 us -> 0.82 us  [on_device(): lax.ppermute(old, 'lag', [(j, 0)])]
  transfers between devices with their start and end apart: 71 -> 71, of which waited for: 37 -> 40; matrix products, arithmetic and copies ran while one was open for 3% -> 3% of each run, Pallas kernels for 20% -> 17%
where the time goes in v5:
time: 368 us; the launch traced here: 367 us
  waiting for transfers between devices  165 us (45%)
  starting transfers between devices  98.5 us (27%)
  Pallas kernels  75.1 us (20%)
  local copies, waits for them, and re-layouts  10.2 us (3%)
  other arithmetic  9.16 us (2%)
  matrix products  8.11 us (2%)
    ppermute x18, waiting for transfers between devices, sum_parts(): result = result + lax.ppermute(sent, 'lag', pairs(groups, mask))  90.7 us
    ppermute x15, waiting for transfers between devices, gather_near(): lax.ppermute(value, 'row', pairs(devices, 2 * k))  27.4 us
    pallas_call x2, Pallas kernels, add_chip(): pl.pallas_call(chip_kernel, out_shape=[jax.ShapeDtypeStruct(square, F32)]...  26.7 us
    pallas_call x4, Pallas kernels, call(): pl.pallas_call(kernel, out_shape=[jax.ShapeDtypeStruct(shape, F32)] * cou...  24 us
    ppermute x6, waiting for transfers between devices, along(): lax.ppermute(value, 'row', [(2 * i + c, 2 * (i + step) + c) for i in sour...  22.7 us
    ppermute x18, starting transfers between devices, sum_parts(): result = result + lax.ppermute(sent, 'lag', pairs(groups, mask))  22.6 us
    ppermute x15, starting transfers between devices, gather_near(): lax.ppermute(value, 'row', pairs(devices, 2 * k))  20.4 us
    ppermute x4, starting transfers between devices, enter(): return lax.ppermute(tail, 'lag', [(i, i + 1) for i in range(groups - 1)])  16.1 us
  transfers between devices with their start and end apart: 71, of which 40 were waited for; matrix products, arithmetic and copies ran while one was open for 3% of the time, Pallas kernels for 17%

profile of v5, /device:TPU:0, one launch (start us, length us, event | category | flops | bytes accessed | tf_op | source)
XLA Modules:
  0.0 366.8 jit_solution(2556899584156162531)
XLA Ops:
  0.0 5.0 %collective-permute-start = (f32[4,512,128]{2,1,0:T(8,128)}, f32[4,512,128]{2,1,0:T(8,128)S(1)}, u32[]{:S(2)}, u32[]{:S(2)}) collective-permute-start(f32[4,512,128]{2,1,0:T(8,128)} %refs_0_.2), channel_id=1, source_target_pairs={{0,2},{1,3},{2,4},{3,5},{4,6},{5,7},{8,10},{9,11},{10,12},{11,13},... | collective-permute-start | bytes 3145736 | tf_op jit(solution)/shard_map/ppermute | solution.py:224
  7.5 4.2 %collective-permute-start.2 = (f32[2,512,128]{2,1,0:T(8,128)S(1)}, f32[2,512,128]{2,1,0:T(8,128)}, u32[]{:S(2)}, u32[]{:S(2)}) collective-permute-start(f32[2,512,128]{2,1,0:T(8,128)S(1)} %slice_select_fusion), channel_id=1, source_target_pairs={{0,8},{8,16},{16,24},{1,9},{9,17},{17,25},{2,10},{10,18},{18,26},{... | collective-permute-start | bytes 1572872 | tf_op jit(solution)/shard_map/ppermute | solution.py:385
  12.6 5.8 %columns.2 = f32[512,1024]{1,0:T(8,128)} custom-call(s32[2,5,4]{2,1,0:T(8,128)} %concatenate.43.where, f32[1,512,4096]{2,1,0:T(8,128)} %bitcast.37, f32[1,512,4096]{2,1,0:T(8,128)} %bitcast.38, f32[1,512,4096]{2,1,0:T(8,128)} %bitcast.39, f32[1,512,4096]{2,1,0:T(8,128)} %bitcast.40), custom_call_target="tpu_custom_call" | custom-call | bytes 16777216 | tf_op jit(solution)/shard_map/columns/pallas_call | solution.py:336
  18.4 4.4 %collective-permute-done.2.refs_0_.refs_4_ = f32[2,512,128]{2,1,0:T(8,128)} collective-permute-done((f32[2,512,128]{2,1,0:T(8,128)S(1)}, f32[2,512,128]{2,1,0:T(8,128)}, u32[]{:S(2)}, u32[]{:S(2)}) %collective-permute-start.2) | collective-permute-done | bytes 524320 | tf_op jit(solution)/shard_map/ppermute | solution.py:385
  22.7 5.0 %collective-permute-done = f32[4,512,128]{2,1,0:T(8,128)S(1)} collective-permute-done((f32[4,512,128]{2,1,0:T(8,128)}, f32[4,512,128]{2,1,0:T(8,128)S(1)}, u32[]{:S(2)}, u32[]{:S(2)}) %collective-permute-start) | collective-permute-done | bytes 1048608 | tf_op jit(solution)/shard_map/ppermute | solution.py:224
  27.7 4.1 %collective-permute-done.1 = f32[4,512,128]{2,1,0:T(8,128)S(1)} collective-permute-done((f32[4,512,128]{2,1,0:T(8,128)}, f32[4,512,128]{2,1,0:T(8,128)S(1)}, u32[]{:S(2)}, u32[]{:S(2)}) %collective-permute-start.1) | collective-permute-done | bytes 1048608 | tf_op jit(solution)/shard_map/ppermute | solution.py:224
  34.0 7.1 %columns.3 = (f32[512,1024]{1,0:T(8,128)}, f32[512,1024]{1,0:T(8,128)}, f32[512,1024]{1,0:T(8,128)}, f32[512,512]{1,0:T(8,128)}, f32[512,512]{1,0:T(8,128)}) custom-call(s32[2,5,4]{2,1,0:T(8,128)} %concatenate.43.where, f32[4,512,4096]{2,1,0:T(8,128)} %weights.13, f32[4,512,4096]{2,1,0:T(8,128)} %weights.13, f32[4,512,4096]{2,1,0:T(8,128)} %weights.13, ...), custom_call_target="tpu_custom_call" | custom-call | bytes 16777216 | tf_op jit(solution)/shard_map/columns/pallas_call | solution.py:336
  41.1 4.4 %collective-permute-start.9 = (f32[512,512]{1,0:T(8,128)}, f32[512,512]{1,0:T(8,128)}, u32[]{:S(2)}, u32[]{:S(2)}) collective-permute-start(f32[512,512]{1,0:T(8,128)} %get-tuple-element.111), channel_id=1, source_target_pairs={{0,16},{1,17},{2,18},{3,19},{4,20},{5,21},{6,22},{7,23}} | collective-permute-start | bytes 3145736 | tf_op jit(solution)/shard_map/ppermute | solution.py:396
  46.2 16.6 %chip.2 = (f32[512,128]{1,0:T(8,128)}, f32[512,128]{1,0:T(8,128)}, f32[512,128]{1,0:T(8,128)}, f32[2,512,128]{2,1,0:T(8,128)}) custom-call(s32[10]{0:T(128)} %stack.100.where, f32[4,512,4096]{2,1,0:T(8,128)} %weights.13, f32[4,512,128]{2,1,0:T(8,128)} %refs_0_.2, f32[4,512,128]{2,1,0:T(8,128)} %collective-permute-done.3.refs_1_, f32[4,512,128]{2,1,0:T(8,128)} %copy-done.7, ...), custom_call_target="tpu_custom_call" | custom-call | flops 9663676416 | bytes 16777216 | tf_op jit(solution)/shard_map/chip/pallas_call | solution.py:265
  62.8 1.7 select_select_fusion.1.refs_0_
  64.6 3.3 collective-permute-done.9
  67.9 1.6 collective-permute-start.7
  71.4 10.1 %chip.3 = (f32[512,128]{1,0:T(8,128)}, f32[512,128]{1,0:T(8,128)}, f32[512,128]{1,0:T(8,128)}, f32[2,512,128]{2,1,0:T(8,128)}) custom-call(s32[10]{0:T(128)} %stack.100.where, f32[4,512,4096]{2,1,0:T(8,128)} %weights.13, f32[4,512,128]{2,1,0:T(8,128)} %copy-done.6, ...), custom_call_target="tpu_custom_call", output_to_operand_aliasing={{0}: (4, {}), {1}: (5, {}), {2}: (6, {})} | custom-call | flops 4831838208 | bytes 8388608 | tf_op jit(solution)/shard_map/chip/pallas_call | solution.py:265
  82.3 3.6 shard_map.46
  85.9 13.7 %collective-permute-done.8 = f32[4,512,128]{2,1,0:T(8,128)} collective-permute-done((f32[4,512,128]{2,1,0:T(8,128)}, f32[4,512,128]{2,1,0:T(8,128)}, u32[]{:S(2)}, u32[]{:S(2)}) %collective-permute-start.8) | collective-permute-done | bytes 1048608 | tf_op jit(solution)/shard_map/ppermute | solution.py:224
  101.2 2.8 collective-permute-start.19
  104.0 5.1 %collective-permute-start.20 = (f32[512,1024]{1,0:T(8,128)}, f32[512,1024]{1,0:T(8,128)}, u32[]{:S(2)}, u32[]{:S(2)}) collective-permute-start(f32[512,1024]{1,0:T(8,128)} %get-tuple-element.140), channel_id=1, source_target_pairs={{0,16},{1,17},{2,18},{3,19},{4,20},{5,21},{6,22},{7,23}} | collective-permute-start | bytes 6291464 | tf_op jit(solution)/shard_map/ppermute | solution.py:397
  110.0 7.5 %first.1 = (f32[512,128]{1,0:T(8,128)}, f32[2,512,128]{2,1,0:T(8,128)}) custom-call(s32[10]{0:T(128)} %stack.100.where, f32[4,512,4096]{2,1,0:T(8,128)} %weights.13, f32[4,512,128]{2,1,0:T(8,128)} %copy-done.1, f32[4,512,128]{2,1,0:T(8,128)} %copy-done.3, f32[512,128]{1,0:T(8,128)} %get-tuple-element.126.total), custom_call_target="tpu_custom_call", output_to_operand_aliasing={{0}: (4, {})} | custom-call | flops 1610612736 | bytes 8388608 | tf_op jit(solution)/shard_map/first/pallas_call | solution.py:285
  119.4 30.5 %collective-permute-done.13 = f32[128,128]{1,0:T(8,128)S(1)} collective-permute-done((f32[128,128]{1,0:T(8,128)S(1)}, f32[128,128]{1,0:T(8,128)S(1)}, u32[]{:S(2)}, u32[]{:S(2)}) %collective-permute-start.13) | collective-permute-done | bytes 65568 | tf_op jit(solution)/shard_map/ppermute | solution.py:377
  149.9 2.3 collective-permute-start.21
  152.1 2.7 collective-permute-done.14
  154.8 2.0 fusion.25
  156.8 18.7 %collective-permute-done.15 = f32[128,128]{1,0:T(8,128)S(1)} collective-permute-done((f32[128,128]{1,0:T(8,128)S(1)}, f32[128,128]{1,0:T(8,128)S(1)}, u32[]{:S(2)}, u32[]{:S(2)}) %collective-permute-start.15) | collective-permute-done | bytes 65568 | tf_op jit(solution)/shard_map/ppermute | solution.py:377
  176.5 4.3 %collective-permute-done.16 = f32[128,128]{1,0:T(8,128)S(1)} collective-permute-done((f32[128,128]{1,0:T(8,128)S(1)}, f32[128,128]{1,0:T(8,128)S(1)}, u32[]{:S(2)}, u32[]{:S(2)}) %collective-permute-start.16) | collective-permute-done | bytes 65568 | tf_op jit(solution)/shard_map/ppermute | solution.py:367
  181.0 5.7 %collective-permute-done.17 = f32[128,128]{1,0:T(8,128)S(1)} collective-permute-done((f32[128,128]{1,0:T(8,128)S(1)}, f32[128,128]{1,0:T(8,128)S(1)}, u32[]{:S(2)}, u32[]{:S(2)}) %collective-permute-start.17) | collective-permute-done | bytes 65568 | tf_op jit(solution)/shard_map/ppermute | solution.py:367
  186.7 1.8 collective-permute-start.18
  188.5 7.6 %shard_map.47 = (f32[512,128]{1,0:T(8,128)}, f32[512,128]{1,0:T(8,128)}) custom-call(s32[10]{0:T(128)} %stack.100.where, f32[4,512,4096]{2,1,0:T(8,128)} %weights.13, f32[4,512,128]{2,1,0:T(8,128)} %copy-done.1, f32[4,512,128]{2,1,0:T(8,128)} %copy-done.1, f32[4,512,128]{2,1,0:T(8,128)} %copy-done.3, ...), custom_call_target="tpu_custom_call", output_to_operand_aliasing={{0}: (6, {}), {1}: (7, {})} | custom-call | flops 3221225472 | bytes 8388608 | tf_op jit(solution)/shard_map/pallas_call | solution.py:189
  199.8 9.2 %collective-permute-start.29 = (f32[2,512,128]{2,1,0:T(8,128)}, f32[2,512,128]{2,1,0:T(8,128)}, u32[]{:S(2)}, u32[]{:S(2)}) collective-permute-start(f32[2,512,128]{2,1,0:T(8,128)} %get-tuple-element.152), channel_id=1, source_target_pairs={{0,8},{8,16},{16,24},{1,9},{9,17},{17,25},{2,10},{10,18},{18,26},{... | collective-permute-start | bytes 1572872 | tf_op jit(solution)/shard_map/ppermute | solution.py:385
  210.8 23.9 %collective-permute-done.24 = f32[128,128]{1,0:T(8,128)S(1)} collective-permute-done((f32[128,128]{1,0:T(8,128)S(1)}, f32[128,128]{1,0:T(8,128)S(1)}, u32[]{:S(2)}, u32[]{:S(2)}) %collective-permute-start.24) | collective-permute-done | bytes 65568 | tf_op jit(solution)/shard_map/ppermute | solution.py:377
  234.7 6.1 %collective-permute-start.26 = (f32[128,128]{1,0:T(8,128)}, f32[128,128]{1,0:T(8,128)}, u32[]{:S(2)}, u32[]{:S(2)}) collective-permute-start(f32[128,128]{1,0:T(8,128)} %get-tuple-element.220), channel_id=1, source_target_pairs={{0,24},{8,16},{16,8},{24,0},{1,25},{9,17},{17,9},{25,1},{2,26},{10... | collective-permute-start | bytes 196616 | tf_op jit(solution)/shard_map/ppermute | solution.py:377
  240.8 4.0 %pick.1 = f32[512,1024]{1,0:T(8,128)} custom-call(s32[1]{0:T(128)} %bitcast.13.which, f32[512,1024]{1,0:T(8,128)} %get-tuple-element.146.refs_0_, f32[512,1024]{1,0:T(8,128)} %collective-permute-done.19.refs_1_, f32[512,1024]{1,0:T(8,128)} %collective-permute-done.20.refs_2_, f32[512,512]{1,0:T(8,128)} %collective-permute-done.21.refs_3_, f32[512,512]{1,0:T(8,128)} %copy-done.19), custom_call_target="tpu_custom_call" | custom-call | bytes 8388608 | tf_op jit(solution)/shard_map/pick/pallas_call | solution.py:352
  247.0 2.6 collective-permute-start.31
  249.6 3.1 collective-permute-done.30
  252.7 2.0 collective-permute-start.32
  254.7 4.0 %collective-permute-done.32 = f32[128,128]{1,0:T(8,128)S(1)} collective-permute-done((f32[128,128]{1,0:T(8,128)S(1)}, f32[128,128]{1,0:T(8,128)S(1)}, u32[]{:S(2)}, u32[]{:S(2)}) %collective-permute-start.32) | collective-permute-done | bytes 65568 | tf_op jit(solution)/shard_map/ppermute | solution.py:367
  260.4 4.3 %shard_map.48 = (f32[512,128]{1,0:T(8,128)}, f32[512,128]{1,0:T(8,128)}) custom-call(s32[10]{0:T(128)} %stack.100.where, f32[4,512,4096]{2,1,0:T(8,128)} %weights.13, f32[2,512,128]{2,1,0:T(8,128)} %copy-done.11, f32[2,512,128]{2,1,0:T(8,128)} %copy-done.13, f32[2,512,128]{2,1,0:T(8,128)} %copy-done.12, ...), custom_call_target="tpu_custom_call", output_to_operand_aliasing={{0}: (8, {}), {1}: (9, {})} | custom-call | flops 2415919104 | bytes 6291456 | tf_op jit(solution)/shard_map/pallas_call | solution.py:189
  266.3 2.6 fusion.4
  268.9 3.4 collective-permute-start.37
  274.7 1.9 collective-permute-done.38
  276.6 2.5 collective-permute-done.39
  284.2 2.6 collective-permute-start.41
  286.8 1.7 collective-permute-done.40
  288.4 2.0 collective-permute-start.42
  290.5 4.0 %collective-permute-done.42 = f32[128,128]{1,0:T(8,128)S(1)} collective-permute-done((f32[128,128]{1,0:T(8,128)S(1)}, f32[128,128]{1,0:T(8,128)S(1)}, u32[]{:S(2)}, u32[]{:S(2)}) %collective-permute-start.42) | collective-permute-done | bytes 65568 | tf_op jit(solution)/shard_map/ppermute | solution.py:367
  298.7 2.7 collective-permute-start.45
  301.5 2.9 collective-permute-done.45
  304.4 2.1 collective-permute-done.46
  306.6 2.6 collective-permute-start.48
  309.2 1.8 collective-permute-start.49
  311.0 2.3 collective-permute-done.48
  313.2 2.0 collective-permute-done.49
  315.3 8.5 %shard_map.49 = f32[512,128]{1,0:T(8,128)} custom-call(s32[10]{0:T(128)} %stack.100.where, f32[4,512,4096]{2,1,0:T(8,128)} %weights.13, f32[512,128]{1,0:T(8,128)} %copy-done.5, f32[512,128]{1,0:T(8,128)} %copy-done.15, f32[512,128]{1,0:T(8,128)} %copy-done.16, f32[512,128]{1,0:T(8,128)} %copy-done.17, ...), custom_call_target="tpu_custom_call", output_to_operand_aliasing={{}: (15, {})} | custom-call | flops 1610612736 | bytes 8388608 | tf_op jit(solution)/shard_map/pallas_call | solution.py:189
  325.3 2.6 fusion.12
  328.6 2.9 collective-permute-start.57
  334.8 2.3 collective-permute-start.59
  337.1 2.0 collective-permute-start.60
  339.1 1.8 collective-permute-start.61
  340.9 1.7 collective-permute-start.62
  343.2 1.7 collective-permute-done.61
  346.4 2.1 collective-permute-done.63
  351.9 2.9 collective-permute-start.67
  357.1 2.0 collective-permute-start.68
  361.8 2.0 collective-permute-done.69
  363.8 2.1 collective-permute-done.70
  (171 shorter events, 53.4 us)
Async XLA Ops:
  0.0 27.7 %collective-permute-start = (f32[4,512,128]{2,1,0:T(8,128)}, f32[4,512,128]{2,1,0:T(8,128)S(1)}, u32[]{:S(2)}, u32[]{:S(2)}) collective-permute-start(f32[4,512,128]{2,1,0:T(8,128)} %refs_0_.2), channel_id=1, source_target_pairs={{0,2},{1,3},{2,4},{3,5},{4,6},{5,7},{8,10},{9,11},{10,12},{11,13},... | collective-permute-start | bytes 3145736 | tf_op jit(solution)/shard_map/ppermute | solution.py:224
  5.0 26.7 %collective-permute-start.1 = (f32[4,512,128]{2,1,0:T(8,128)}, f32[4,512,128]{2,1,0:T(8,128)S(1)}, u32[]{:S(2)}, u32[]{:S(2)}) collective-permute-start(f32[4,512,128]{2,1,0:T(8,128)} %refs_0_.2), channel_id=1, source_target_pairs={{2,0},{3,1},{4,2},{5,3},{6,4},{7,5},{10,8},{11,9},{12,10},{13,11},... | collective-permute-start | bytes 3145736 | tf_op jit(solution)/shard_map/ppermute | solution.py:224
  6.3 25.4 %collective-permute-start.3 = (f32[4,512,128]{2,1,0:T(8,128)}, f32[4,512,128]{2,1,0:T(8,128)}, u32[]{:S(2)}, u32[]{:S(2)}) collective-permute-start(f32[4,512,128]{2,1,0:T(8,128)} %refs_0_.2), channel_id=1, source_target_pairs={{0,1},{1,0},{2,3},{3,2},{4,5},{5,4},{6,7},{7,6},{8,9},{9,8},{10,11... | collective-permute-start | bytes 3145736 | tf_op jit(solution)/shard_map/ppermute | solution.py:221
  7.5 15.2 %collective-permute-start.2 = (f32[2,512,128]{2,1,0:T(8,128)S(1)}, f32[2,512,128]{2,1,0:T(8,128)}, u32[]{:S(2)}, u32[]{:S(2)}) collective-permute-start(f32[2,512,128]{2,1,0:T(8,128)S(1)} %slice_select_fusion), channel_id=1, source_target_pairs={{0,8},{8,16},{16,24},{1,9},{9,17},{17,25},{2,10},{10,18},{18,26},{... | collective-permute-start | bytes 1572872 | tf_op jit(solution)/shard_map/ppermute | solution.py:385
  31.9 14.3 %collective-permute-start.6 = (f32[4,512,128]{2,1,0:T(8,128)S(1)}, f32[4,512,128]{2,1,0:T(8,128)}, u32[]{:S(2)}, u32[]{:S(2)}) collective-permute-start(f32[4,512,128]{2,1,0:T(8,128)S(1)} %broadcast_select_fusion.refs_2_), channel_id=1, source_target_pairs={{0,1},{1,0},{2,3},{3,2},{4,5},{5,4},{6,7},{7,6},{8,9},{9,8},{10,11... | collective-permute-start | bytes 3145736 | tf_op jit(solution)/shard_map/ppermute | solution.py:221
  32.0 30.9 %collective-permute-start.4 = (f32[4,512,128]{2,1,0:T(8,128)}, f32[4,512,128]{2,1,0:T(8,128)S(1)}, u32[]{:S(2)}, u32[]{:S(2)}) collective-permute-start(f32[4,512,128]{2,1,0:T(8,128)} %copy-done.18), channel_id=1, source_target_pairs={{2,4},{3,5},{4,6},{5,7},{10,12},{11,13},{12,14},{13,15},{18,20},{1... | collective-permute-start | bytes 3145736 | tf_op jit(solution)/shard_map/ppermute | solution.py:224
  32.7 30.1 %collective-permute-start.5 = (f32[4,512,128]{2,1,0:T(8,128)S(1)}, f32[4,512,128]{2,1,0:T(8,128)}, u32[]{:S(2)}, u32[]{:S(2)}) collective-permute-start(f32[4,512,128]{2,1,0:T(8,128)S(1)} %collective-permute-done.1), channel_id=1, source_target_pairs={{2,0},{3,1},{4,2},{5,3},{10,8},{11,9},{12,10},{13,11},{18,16},{19,... | collective-permute-start | bytes 3145736 | tf_op jit(solution)/shard_map/ppermute | solution.py:224
  41.1 26.8 %collective-permute-start.9 = (f32[512,512]{1,0:T(8,128)}, f32[512,512]{1,0:T(8,128)}, u32[]{:S(2)}, u32[]{:S(2)}) collective-permute-start(f32[512,512]{1,0:T(8,128)} %get-tuple-element.111), channel_id=1, source_target_pairs={{0,16},{1,17},{2,18},{3,19},{4,20},{5,21},{6,22},{7,23}} | collective-permute-start | bytes 3145736 | tf_op jit(solution)/shard_map/ppermute | solution.py:396
  67.9 18.0 %collective-permute-start.7 = (f32[4,512,128]{2,1,0:T(8,128)S(1)}, f32[4,512,128]{2,1,0:T(8,128)}, u32[]{:S(2)}, u32[]{:S(2)}) collective-permute-start(f32[4,512,128]{2,1,0:T(8,128)S(1)} %collective-permute-done.4), channel_id=1, source_target_pairs={{4,6},{5,7},{12,14},{13,15},{20,22},{21,23},{28,30},{29,31}} | collective-permute-start | bytes 3145736 | tf_op jit(solution)/shard_map/ppermute | solution.py:224
  69.6 30.1 %collective-permute-start.8 = (f32[4,512,128]{2,1,0:T(8,128)}, f32[4,512,128]{2,1,0:T(8,128)}, u32[]{:S(2)}, u32[]{:S(2)}) collective-permute-start(f32[4,512,128]{2,1,0:T(8,128)} %collective-permute-done.5), channel_id=1, source_target_pairs={{2,0},{3,1},{10,8},{11,9},{18,16},{19,17},{26,24},{27,25}} | collective-permute-start | bytes 3145736 | tf_op jit(solution)/shard_map/ppermute | solution.py:224
  70.8 10.7 %collective-permute-start.11 = (f32[2,512,128]{2,1,0:T(8,128)}, f32[2,512,128]{2,1,0:T(8,128)S(1)}, u32[]{:S(2)}, u32[]{:S(2)}) collective-permute-start(f32[2,512,128]{2,1,0:T(8,128)} %collective-permute-done.2.refs_0_.refs_4_), channel_id=1, source_target_pairs={{0,1},{1,0},{2,3},{3,2},{4,5},{5,4},{6,7},{7,6},{8,9},{9,8},{10,11... | collective-permute-start | bytes 1572872 | tf_op jit(solution)/shard_map/ppermute | solution.py:221
  101.1 8.0 %collective-permute-start.12 = (f32[4,512,128]{2,1,0:T(8,128)S(1)}, f32[4,512,128]{2,1,0:T(8,128)S(1)}, u32[]{:S(2)}, u32[]{:S(2)}) collective-permute-start(f32[4,512,128]{2,1,0:T(8,128)S(1)} %select_select_fusion.near.near_before), channel_id=1, source_target_pairs={{0,1},{1,0},{2,3},{3,2},{4,5},{5,4},{6,7},{7,6},{8,9},{9,8},{10,11... | collective-permute-start | bytes 3145736 | tf_op jit(solution)/shard_map/ppermute | solution.py:221
  101.2 95.0 %collective-permute-start.19 = (f32[512,1024]{1,0:T(8,128)}, f32[512,1024]{1,0:T(8,128)}, u32[]{:S(2)}, u32[]{:S(2)}) collective-permute-start(f32[512,1024]{1,0:T(8,128)} %get-tuple-element.139), channel_id=1, source_target_pairs={{0,8},{1,9},{2,10},{3,11},{4,12},{5,13},{6,14},{7,15}} | collective-permute-start | bytes 6291464 | tf_op jit(solution)/shard_map/ppermute | solution.py:397
  104.0 92.2 %collective-permute-start.20 = (f32[512,1024]{1,0:T(8,128)}, f32[512,1024]{1,0:T(8,128)}, u32[]{:S(2)}, u32[]{:S(2)}) collective-permute-start(f32[512,1024]{1,0:T(8,128)} %get-tuple-element.140), channel_id=1, source_target_pairs={{0,16},{1,17},{2,18},{3,19},{4,20},{5,21},{6,22},{7,23}} | collective-permute-start | bytes 6291464 | tf_op jit(solution)/shard_map/ppermute | solution.py:397
  118.5 31.4 %collective-permute-start.13 = (f32[128,128]{1,0:T(8,128)S(1)}, f32[128,128]{1,0:T(8,128)S(1)}, u32[]{:S(2)}, u32[]{:S(2)}) collective-permute-start(f32[128,128]{1,0:T(8,128)S(1)} %get-tuple-element.222), channel_id=1, source_target_pairs={{0,8},{8,0},{16,24},{24,16},{1,9},{9,1},{17,25},{25,17},{2,10},{10... | collective-permute-start | bytes 196616 | tf_op jit(solution)/shard_map/ppermute | solution.py:377
  118.5 36.3 %collective-permute-start.14 = (f32[128,128]{1,0:T(8,128)S(1)}, f32[128,128]{1,0:T(8,128)S(1)}, u32[]{:S(2)}, u32[]{:S(2)}) collective-permute-start(f32[128,128]{1,0:T(8,128)S(1)} %get-tuple-element.224), channel_id=1, source_target_pairs={{0,16},{8,24},{16,0},{24,8},{1,17},{9,25},{17,1},{25,9},{2,18},{10... | collective-permute-start | bytes 196616 | tf_op jit(solution)/shard_map/ppermute | solution.py:377
  118.6 77.6 %collective-permute-start.22 = (f32[512,512]{1,0:T(8,128)}, f32[512,512]{1,0:T(8,128)S(1)}, u32[]{:S(2)}, u32[]{:S(2)}) collective-permute-start(f32[512,512]{1,0:T(8,128)} %collective-permute-done.9), channel_id=1, source_target_pairs={{16,24},{17,25},{18,26},{19,27},{20,28},{21,29},{22,30},{23,31}} | collective-permute-start | bytes 3145736 | tf_op jit(solution)/shard_map/ppermute | solution.py:406
  149.9 46.3 %collective-permute-start.21 = (f32[512,512]{1,0:T(8,128)}, f32[512,512]{1,0:T(8,128)}, u32[]{:S(2)}, u32[]{:S(2)}) collective-permute-start(f32[512,512]{1,0:T(8,128)} %get-tuple-element.143), channel_id=1, source_target_pairs={{0,24},{1,25},{2,26},{3,27},{4,28},{5,29},{6,30},{7,31}} | collective-permute-start | bytes 3145736 | tf_op jit(solution)/shard_map/ppermute | solution.py:417
  154.8 20.7 %collective-permute-start.15 = (f32[128,128]{1,0:T(8,128)S(1)}, f32[128,128]{1,0:T(8,128)S(1)}, u32[]{:S(2)}, u32[]{:S(2)}) collective-permute-start(f32[128,128]{1,0:T(8,128)S(1)} %get-tuple-element.223), channel_id=1, source_target_pairs={{0,24},{8,16},{16,8},{24,0},{1,25},{9,17},{17,9},{25,1},{2,26},{10... | collective-permute-start | bytes 196616 | tf_op jit(solution)/shard_map/ppermute | solution.py:377
  176.4 4.3 %collective-permute-start.16 = (f32[128,128]{1,0:T(8,128)S(1)}, f32[128,128]{1,0:T(8,128)S(1)}, u32[]{:S(2)}, u32[]{:S(2)}) collective-permute-start(f32[128,128]{1,0:T(8,128)S(1)} %bitcast_subtract_fusion), channel_id=1, source_target_pairs={{0,2},{1,3},{2,0},{3,1},{4,6},{5,7},{6,4},{7,5},{8,10},{9,11},{10,... | collective-permute-start | bytes 196616 | tf_op jit(solution)/shard_map/ppermute | solution.py:367
  180.7 6.0 %collective-permute-start.17 = (f32[128,128]{1,0:T(8,128)S(1)}, f32[128,128]{1,0:T(8,128)S(1)}, u32[]{:S(2)}, u32[]{:S(2)}) collective-permute-start(f32[128,128]{1,0:T(8,128)S(1)} %bitcast_subtract_fusion), channel_id=1, source_target_pairs={{0,4},{1,5},{2,6},{3,7},{4,0},{5,1},{6,2},{7,3},{8,12},{9,13},{10,... | collective-permute-start | bytes 196616 | tf_op jit(solution)/shard_map/ppermute | solution.py:367
  186.7 9.4 %collective-permute-start.18 = (f32[128,128]{1,0:T(8,128)S(1)}, f32[128,128]{1,0:T(8,128)S(1)}, u32[]{:S(2)}, u32[]{:S(2)}) collective-permute-start(f32[128,128]{1,0:T(8,128)S(1)} %bitcast_subtract_fusion), channel_id=1, source_target_pairs={{0,6},{1,7},{2,4},{3,5},{4,2},{5,3},{6,0},{7,1},{8,14},{9,15},{10,... | collective-permute-start | bytes 196616 | tf_op jit(solution)/shard_map/ppermute | solution.py:367
  197.2 11.9 %collective-permute-start.23 = (f32[512,128]{1,0:T(8,128)S(1)}, f32[512,128]{1,0:T(8,128)S(1)}, u32[]{:S(2)}, u32[]{:S(2)}) collective-permute-start(f32[512,128]{1,0:T(8,128)S(1)} %pad_maximum_fusion.2), channel_id=1, source_target_pairs={{0,1},{1,0},{2,3},{3,2},{4,5},{5,4},{6,7},{7,6},{8,9},{9,8},{10,11... | collective-permute-start | bytes 786440 | tf_op jit(solution)/shard_map/ppermute | solution.py:221
  197.2 49.1 %collective-permute-start.27 = (f32[2,512,128]{2,1,0:T(8,128)}, f32[2,512,128]{2,1,0:T(8,128)S(1)}, u32[]{:S(2)}, u32[]{:S(2)}) collective-permute-start(f32[2,512,128]{2,1,0:T(8,128)} %get-tuple-element.142), channel_id=1, source_target_pairs={{0,8},{8,16},{16,24},{1,9},{9,17},{17,25},{2,10},{10,18},{18,26},{... | collective-permute-start | bytes 1572872 | tf_op jit(solution)/shard_map/ppermute | solution.py:385
  198.5 47.8 %collective-permute-start.28 = (f32[2,512,128]{2,1,0:T(8,128)}, f32[2,512,128]{2,1,0:T(8,128)S(1)}, u32[]{:S(2)}, u32[]{:S(2)}) collective-permute-start(f32[2,512,128]{2,1,0:T(8,128)} %get-tuple-element.151), channel_id=1, source_target_pairs={{0,8},{8,16},{16,24},{1,9},{9,17},{17,25},{2,10},{10,18},{18,26},{... | collective-permute-start | bytes 1572872 | tf_op jit(solution)/shard_map/ppermute | solution.py:385
  199.8 46.5 %collective-permute-start.29 = (f32[2,512,128]{2,1,0:T(8,128)}, f32[2,512,128]{2,1,0:T(8,128)}, u32[]{:S(2)}, u32[]{:S(2)}) collective-permute-start(f32[2,512,128]{2,1,0:T(8,128)} %get-tuple-element.152), channel_id=1, source_target_pairs={{0,8},{8,16},{16,24},{1,9},{9,17},{17,25},{2,10},{10,18},{18,26},{... | collective-permute-start | bytes 1572872 | tf_op jit(solution)/shard_map/ppermute | solution.py:385
  210.7 23.9 %collective-permute-start.24 = (f32[128,128]{1,0:T(8,128)S(1)}, f32[128,128]{1,0:T(8,128)S(1)}, u32[]{:S(2)}, u32[]{:S(2)}) collective-permute-start(f32[128,128]{1,0:T(8,128)S(1)} %get-tuple-element.219), channel_id=1, source_target_pairs={{0,8},{8,0},{16,24},{24,16},{1,9},{9,1},{17,25},{25,17},{2,10},{10... | collective-permute-start | bytes 196616 | tf_op jit(solution)/shard_map/ppermute | solution.py:377
  210.8 34.0 %collective-permute-start.25 = (f32[128,128]{1,0:T(8,128)}, f32[128,128]{1,0:T(8,128)S(1)}, u32[]{:S(2)}, u32[]{:S(2)}) collective-permute-start(f32[128,128]{1,0:T(8,128)} %get-tuple-element.221), channel_id=1, source_target_pairs={{0,16},{8,24},{16,0},{24,8},{1,17},{9,25},{17,1},{25,9},{2,18},{10... | collective-permute-start | bytes 196616 | tf_op jit(solution)/shard_map/ppermute | solution.py:377
  234.7 10.7 %collective-permute-start.26 = (f32[128,128]{1,0:T(8,128)}, f32[128,128]{1,0:T(8,128)}, u32[]{:S(2)}, u32[]{:S(2)}) collective-permute-start(f32[128,128]{1,0:T(8,128)} %get-tuple-element.220), channel_id=1, source_target_pairs={{0,24},{8,16},{16,8},{24,0},{1,25},{9,17},{17,9},{25,1},{2,26},{10... | collective-permute-start | bytes 196616 | tf_op jit(solution)/shard_map/ppermute | solution.py:377
  246.4 12.4 %collective-permute-start.33 = (f32[2,512,128]{2,1,0:T(8,128)S(1)}, f32[2,512,128]{2,1,0:T(8,128)S(1)}, u32[]{:S(2)}, u32[]{:S(2)}) collective-permute-start(f32[2,512,128]{2,1,0:T(8,128)S(1)} %collective-permute-done.27.refs_0_.refs_6_), channel_id=1, source_target_pairs={{0,1},{1,0},{2,3},{3,2},{4,5},{5,4},{6,7},{7,6},{8,9},{9,8},{10,11... | collective-permute-start | bytes 1572872 | tf_op jit(solution)/shard_map/ppermute | solution.py:221
  246.4 12.4 %collective-permute-start.34 = (f32[2,512,128]{2,1,0:T(8,128)S(1)}, f32[2,512,128]{2,1,0:T(8,128)S(1)}, u32[]{:S(2)}, u32[]{:S(2)}) collective-permute-start(f32[2,512,128]{2,1,0:T(8,128)S(1)} %collective-permute-done.28.refs_2_.refs_8_), channel_id=1, source_target_pairs={{0,1},{1,0},{2,3},{3,2},{4,5},{5,4},{6,7},{7,6},{8,9},{9,8},{10,11... | collective-permute-start | bytes 1572872 | tf_op jit(solution)/shard_map/ppermute | solution.py:221
  246.9 13.5 %collective-permute-start.35 = (f32[2,512,128]{2,1,0:T(8,128)}, f32[2,512,128]{2,1,0:T(8,128)}, u32[]{:S(2)}, u32[]{:S(2)}) collective-permute-start(f32[2,512,128]{2,1,0:T(8,128)} %collective-permute-done.29.refs_4_.refs_10_), channel_id=1, source_target_pairs={{0,1},{1,0},{2,3},{3,2},{4,5},{5,4},{6,7},{7,6},{8,9},{9,8},{10,11... | collective-permute-start | bytes 1572872 | tf_op jit(solution)/shard_map/ppermute | solution.py:221
  247.0 5.7 %collective-permute-start.30 = (f32[128,128]{1,0:T(8,128)S(1)}, f32[128,128]{1,0:T(8,128)S(1)}, u32[]{:S(2)}, u32[]{:S(2)}) collective-permute-start(f32[128,128]{1,0:T(8,128)S(1)} %add_add_fusion.1), channel_id=1, source_target_pairs={{0,2},{1,3},{2,0},{3,1},{4,6},{5,7},{6,4},{7,5},{8,10},{9,11},{10,... | collective-permute-start | bytes 196616 | tf_op jit(solution)/shard_map/ppermute | solution.py:367
  247.0 7.7 %collective-permute-start.31 = (f32[128,128]{1,0:T(8,128)S(1)}, f32[128,128]{1,0:T(8,128)S(1)}, u32[]{:S(2)}, u32[]{:S(2)}) collective-permute-start(f32[128,128]{1,0:T(8,128)S(1)} %add_add_fusion.1), channel_id=1, source_target_pairs={{0,4},{1,5},{2,6},{3,7},{4,0},{5,1},{6,2},{7,3},{8,12},{9,13},{10,... | collective-permute-start | bytes 196616 | tf_op jit(solution)/shard_map/ppermute | solution.py:367
  252.7 6.1 %collective-permute-start.32 = (f32[128,128]{1,0:T(8,128)S(1)}, f32[128,128]{1,0:T(8,128)S(1)}, u32[]{:S(2)}, u32[]{:S(2)}) collective-permute-start(f32[128,128]{1,0:T(8,128)S(1)} %add_add_fusion.1), channel_id=1, source_target_pairs={{0,6},{1,7},{2,4},{3,5},{4,2},{5,3},{6,0},{7,1},{8,14},{9,15},{10,... | collective-permute-start | bytes 196616 | tf_op jit(solution)/shard_map/ppermute | solution.py:367
  268.9 5.8 %collective-permute-start.37 = (f32[128,128]{1,0:T(8,128)S(1)}, f32[128,128]{1,0:T(8,128)S(1)}, u32[]{:S(2)}, u32[]{:S(2)}) collective-permute-start(f32[128,128]{1,0:T(8,128)S(1)} %get-tuple-element.216), channel_id=1, source_target_pairs={{0,8},{8,0},{16,24},{24,16},{1,9},{9,1},{17,25},{25,17},{2,10},{10... | collective-permute-start | bytes 196616 | tf_op jit(solution)/shard_map/ppermute | solution.py:377
  274.0 5.2 %collective-permute-start.39 = (f32[128,128]{1,0:T(8,128)S(1)}, f32[128,128]{1,0:T(8,128)S(1)}, u32[]{:S(2)}, u32[]{:S(2)}) collective-permute-start(f32[128,128]{1,0:T(8,128)S(1)} %get-tuple-element.217), channel_id=1, source_target_pairs={{0,24},{8,16},{16,8},{24,0},{1,25},{9,17},{17,9},{25,1},{2,26},{10... | collective-permute-start | bytes 196616 | tf_op jit(solution)/shard_map/ppermute | solution.py:377
  280.0 14.6 %collective-permute-start.50 = (f32[512,128]{1,0:T(8,128)S(1)}, f32[512,128]{1,0:T(8,128)S(1)}, u32[]{:S(2)}, u32[]{:S(2)}) collective-permute-start(f32[512,128]{1,0:T(8,128)S(1)} %pad_maximum_fusion.3.refs_0_), channel_id=1, source_target_pairs={{8,0},{9,1},{10,2},{11,3},{12,4},{13,5},{14,6},{15,7}} | collective-permute-start | bytes 786440 | tf_op jit(solution)/shard_map/ppermute | solution.py:448
  281.3 14.2 %collective-permute-start.51 = (f32[512,128]{1,0:T(8,128)S(1)}, f32[512,128]{1,0:T(8,128)S(1)}, u32[]{:S(2)}, u32[]{:S(2)}) collective-permute-start(f32[512,128]{1,0:T(8,128)S(1)} %pad_maximum_fusion.3.refs_0_), channel_id=1, source_target_pairs={{16,0},{17,1},{18,2},{19,3},{20,4},{21,5},{22,6},{23,7}} | collective-permute-start | bytes 786440 | tf_op jit(solution)/shard_map/ppermute | solution.py:448
  282.6 12.9 %collective-permute-start.52 = (f32[512,128]{1,0:T(8,128)S(1)}, f32[512,128]{1,0:T(8,128)S(1)}, u32[]{:S(2)}, u32[]{:S(2)}) collective-permute-start(f32[512,128]{1,0:T(8,128)S(1)} %pad_maximum_fusion.3.refs_0_), channel_id=1, source_target_pairs={{24,0},{25,1},{26,2},{27,3},{28,4},{29,5},{30,6},{31,7}} | collective-permute-start | bytes 786440 | tf_op jit(solution)/shard_map/ppermute | solution.py:448
  284.1 4.3 %collective-permute-start.40 = (f32[128,128]{1,0:T(8,128)S(1)}, f32[128,128]{1,0:T(8,128)S(1)}, u32[]{:S(2)}, u32[]{:S(2)}) collective-permute-start(f32[128,128]{1,0:T(8,128)S(1)} %bitcast_subtract_fusion.1), channel_id=1, source_target_pairs={{0,2},{1,3},{2,0},{3,1},{4,6},{5,7},{6,4},{7,5},{8,10},{9,11},{10,... | collective-permute-start | bytes 196616 | tf_op jit(solution)/shard_map/ppermute | solution.py:367
  284.2 6.3 %collective-permute-start.41 = (f32[128,128]{1,0:T(8,128)S(1)}, f32[128,128]{1,0:T(8,128)S(1)}, u32[]{:S(2)}, u32[]{:S(2)}) collective-permute-start(f32[128,128]{1,0:T(8,128)S(1)} %bitcast_subtract_fusion.1), channel_id=1, source_target_pairs={{0,4},{1,5},{2,6},{3,7},{4,0},{5,1},{6,2},{7,3},{8,12},{9,13},{10,... | collective-permute-start | bytes 196616 | tf_op jit(solution)/shard_map/ppermute | solution.py:367
  288.4 6.1 %collective-permute-start.42 = (f32[128,128]{1,0:T(8,128)S(1)}, f32[128,128]{1,0:T(8,128)S(1)}, u32[]{:S(2)}, u32[]{:S(2)}) collective-permute-start(f32[128,128]{1,0:T(8,128)S(1)} %bitcast_subtract_fusion.1), channel_id=1, source_target_pairs={{0,6},{1,7},{2,4},{3,5},{4,2},{5,3},{6,0},{7,1},{8,14},{9,15},{10,... | collective-permute-start | bytes 196616 | tf_op jit(solution)/shard_map/ppermute | solution.py:367
  295.5 19.8 %collective-permute-start.53 = (f32[4,512,128]{2,1,0:T(8,128)S(1)}, f32[4,512,128]{2,1,0:T(8,128)}, u32[]{:S(2)}, u32[]{:S(2)}) collective-permute-start(f32[4,512,128]{2,1,0:T(8,128)S(1)} %pad_maximum_fusion), channel_id=1, source_target_pairs={{0,1},{1,0},{2,3},{3,2},{4,5},{5,4},{6,7},{7,6},{8,9},{9,8},{10,11... | collective-permute-start | bytes 3145736 | tf_op jit(solution)/shard_map/ppermute | solution.py:221
  298.7 5.7 %collective-permute-start.45 = (f32[128,128]{1,0:T(8,128)S(1)}, f32[128,128]{1,0:T(8,128)S(1)}, u32[]{:S(2)}, u32[]{:S(2)}) collective-permute-start(f32[128,128]{1,0:T(8,128)S(1)} %get-tuple-element.215), channel_id=1, source_target_pairs={{0,16},{8,24},{16,0},{24,8},{1,17},{9,25},{17,1},{25,9},{2,18},{10... | collective-permute-start | bytes 196616 | tf_op jit(solution)/shard_map/ppermute | solution.py:377
  301.4 5.2 %collective-permute-start.46 = (f32[128,128]{1,0:T(8,128)S(1)}, f32[128,128]{1,0:T(8,128)S(1)}, u32[]{:S(2)}, u32[]{:S(2)}) collective-permute-start(f32[128,128]{1,0:T(8,128)S(1)} %get-tuple-element.214), channel_id=1, source_target_pairs={{0,24},{8,16},{16,8},{24,0},{1,25},{9,17},{17,9},{25,1},{2,26},{10... | collective-permute-start | bytes 196616 | tf_op jit(solution)/shard_map/ppermute | solution.py:377
  306.5 4.5 %collective-permute-start.47 = (f32[128,128]{1,0:T(8,128)S(1)}, f32[128,128]{1,0:T(8,128)S(1)}, u32[]{:S(2)}, u32[]{:S(2)}) collective-permute-start(f32[128,128]{1,0:T(8,128)S(1)} %add_add_fusion), channel_id=1, source_target_pairs={{0,2},{1,3},{2,0},{3,1},{4,6},{5,7},{6,4},{7,5},{8,10},{9,11},{10,... | collective-permute-start | bytes 196616 | tf_op jit(solution)/shard_map/ppermute | solution.py:367
  306.6 6.6 %collective-permute-start.48 = (f32[128,128]{1,0:T(8,128)S(1)}, f32[128,128]{1,0:T(8,128)S(1)}, u32[]{:S(2)}, u32[]{:S(2)}) collective-permute-start(f32[128,128]{1,0:T(8,128)S(1)} %add_add_fusion), channel_id=1, source_target_pairs={{0,4},{1,5},{2,6},{3,7},{4,0},{5,1},{6,2},{7,3},{8,12},{9,13},{10,... | collective-permute-start | bytes 196616 | tf_op jit(solution)/shard_map/ppermute | solution.py:367
  309.2 6.1 %collective-permute-start.49 = (f32[128,128]{1,0:T(8,128)S(1)}, f32[128,128]{1,0:T(8,128)S(1)}, u32[]{:S(2)}, u32[]{:S(2)}) collective-permute-start(f32[128,128]{1,0:T(8,128)S(1)} %add_add_fusion), channel_id=1, source_target_pairs={{0,6},{1,7},{2,4},{3,5},{4,2},{5,3},{6,0},{7,1},{8,14},{9,15},{10,... | collective-permute-start | bytes 196616 | tf_op jit(solution)/shard_map/ppermute | solution.py:367
  328.0 4.6 %collective-permute-start.55 = (f32[128,128]{1,0:T(8,128)S(1)}, f32[128,128]{1,0:T(8,128)S(1)}, u32[]{:S(2)}, u32[]{:S(2)}) collective-permute-start(f32[128,128]{1,0:T(8,128)S(1)} %get-tuple-element.210), channel_id=1, source_target_pairs={{0,8},{8,0},{16,24},{24,16},{1,9},{9,1},{17,25},{25,17},{2,10},{10... | collective-permute-start | bytes 196616 | tf_op jit(solution)/shard_map/ppermute | solution.py:377
  328.1 5.7 %collective-permute-start.56 = (f32[128,128]{1,0:T(8,128)S(1)}, f32[128,128]{1,0:T(8,128)S(1)}, u32[]{:S(2)}, u32[]{:S(2)}) collective-permute-start(f32[128,128]{1,0:T(8,128)S(1)} %get-tuple-element.212), channel_id=1, source_target_pairs={{0,16},{8,24},{16,0},{24,8},{1,17},{9,25},{17,1},{25,9},{2,18},{10... | collective-permute-start | bytes 196616 | tf_op jit(solution)/shard_map/ppermute | solution.py:377
  328.6 5.2 %collective-permute-start.57 = (f32[128,128]{1,0:T(8,128)S(1)}, f32[128,128]{1,0:T(8,128)S(1)}, u32[]{:S(2)}, u32[]{:S(2)}) collective-permute-start(f32[128,128]{1,0:T(8,128)S(1)} %get-tuple-element.211), channel_id=1, source_target_pairs={{0,24},{8,16},{16,8},{24,0},{1,25},{9,17},{17,9},{25,1},{2,26},{10... | collective-permute-start | bytes 196616 | tf_op jit(solution)/shard_map/ppermute | solution.py:377
  334.7 8.0 %collective-permute-start.58 = (f32[128,128]{1,0:T(8,128)S(1)}, f32[128,128]{1,0:T(8,128)S(1)}, u32[]{:S(2)}, u32[]{:S(2)}) collective-permute-start(f32[128,128]{1,0:T(8,128)S(1)} %bitcast_subtract_fusion.2), channel_id=1, source_target_pairs={{0,2},{1,3},{2,0},{3,1},{4,6},{5,7},{6,4},{7,5},{8,10},{9,11},{10,... | collective-permute-start | bytes 196616 | tf_op jit(solution)/shard_map/ppermute | solution.py:367
  334.8 7.9 %collective-permute-start.59 = (f32[128,128]{1,0:T(8,128)S(1)}, f32[128,128]{1,0:T(8,128)S(1)}, u32[]{:S(2)}, u32[]{:S(2)}) collective-permute-start(f32[128,128]{1,0:T(8,128)S(1)} %bitcast_subtract_fusion.2), channel_id=1, source_target_pairs={{0,4},{1,5},{2,6},{3,7},{4,0},{5,1},{6,2},{7,3},{8,12},{9,13},{10,... | collective-permute-start | bytes 196616 | tf_op jit(solution)/shard_map/ppermute | solution.py:367
  337.1 6.1 %collective-permute-start.60 = (f32[128,128]{1,0:T(8,128)S(1)}, f32[128,128]{1,0:T(8,128)S(1)}, u32[]{:S(2)}, u32[]{:S(2)}) collective-permute-start(f32[128,128]{1,0:T(8,128)S(1)} %bitcast_subtract_fusion.2), channel_id=1, source_target_pairs={{0,6},{1,7},{2,4},{3,5},{4,2},{5,3},{6,0},{7,1},{8,14},{9,15},{10,... | collective-permute-start | bytes 196616 | tf_op jit(solution)/shard_map/ppermute | solution.py:367
  339.1 5.7 %collective-permute-start.61 = (f32[2,128,128]{2,1,0:T(8,128)S(1)}, f32[2,128,128]{2,1,0:T(8,128)S(1)}, u32[]{:S(2)}, u32[]{:S(2)}) collective-permute-start(f32[2,128,128]{2,1,0:T(8,128)S(1)} %pad_maximum_fusion.7), channel_id=1, source_target_pairs={{0,8},{8,0},{16,24},{24,16},{1,9},{9,1},{17,25},{25,17},{2,10},{10... | collective-permute-start | bytes 393224 | tf_op jit(solution)/shard_map/ppermute | solution.py:381
  340.9 5.5 %collective-permute-start.62 = (f32[2,128,128]{2,1,0:T(8,128)S(1)}, f32[2,128,128]{2,1,0:T(8,128)S(1)}, u32[]{:S(2)}, u32[]{:S(2)}) collective-permute-start(f32[2,128,128]{2,1,0:T(8,128)S(1)} %pad_maximum_fusion.7), channel_id=1, source_target_pairs={{0,16},{8,24},{16,0},{24,8},{1,17},{9,25},{17,1},{25,9},{2,18},{10... | collective-permute-start | bytes 393224 | tf_op jit(solution)/shard_map/ppermute | solution.py:381
  342.7 5.9 %collective-permute-start.63 = (f32[2,128,128]{2,1,0:T(8,128)S(1)}, f32[2,128,128]{2,1,0:T(8,128)S(1)}, u32[]{:S(2)}, u32[]{:S(2)}) collective-permute-start(f32[2,128,128]{2,1,0:T(8,128)S(1)} %pad_maximum_fusion.7), channel_id=1, source_target_pairs={{0,24},{8,16},{16,8},{24,0},{1,25},{9,17},{17,9},{25,1},{2,26},{10... | collective-permute-start | bytes 393224 | tf_op jit(solution)/shard_map/ppermute | solution.py:381
  351.3 4.6 %collective-permute-start.65 = (f32[128,128]{1,0:T(8,128)S(1)}, f32[128,128]{1,0:T(8,128)S(1)}, u32[]{:S(2)}, u32[]{:S(2)}) collective-permute-start(f32[128,128]{1,0:T(8,128)S(1)} %get-tuple-element.207), channel_id=1, source_target_pairs={{0,8},{8,0},{16,24},{24,16},{1,9},{9,1},{17,25},{25,17},{2,10},{10... | collective-permute-start | bytes 196616 | tf_op jit(solution)/shard_map/ppermute | solution.py:377
  351.4 5.0 %collective-permute-start.66 = (f32[128,128]{1,0:T(8,128)S(1)}, f32[128,128]{1,0:T(8,128)S(1)}, u32[]{:S(2)}, u32[]{:S(2)}) collective-permute-start(f32[128,128]{1,0:T(8,128)S(1)} %get-tuple-element.209), channel_id=1, source_target_pairs={{0,16},{8,24},{16,0},{24,8},{1,17},{9,25},{17,1},{25,9},{2,18},{10... | collective-permute-start | bytes 196616 | tf_op jit(solution)/shard_map/ppermute | solution.py:377
  351.9 5.2 %collective-permute-start.67 = (f32[128,128]{1,0:T(8,128)S(1)}, f32[128,128]{1,0:T(8,128)S(1)}, u32[]{:S(2)}, u32[]{:S(2)}) collective-permute-start(f32[128,128]{1,0:T(8,128)S(1)} %get-tuple-element.208), channel_id=1, source_target_pairs={{0,24},{8,16},{16,8},{24,0},{1,25},{9,17},{17,9},{25,1},{2,26},{10... | collective-permute-start | bytes 196616 | tf_op jit(solution)/shard_map/ppermute | solution.py:377
  357.1 4.6 %collective-permute-start.68 = (f32[1,128,128]{2,1,0:T(8,128)S(1)}, f32[1,128,128]{2,1,0:T(8,128)S(1)}, u32[]{:S(2)}, u32[]{:S(2)}) collective-permute-start(f32[1,128,128]{2,1,0:T(8,128)S(1)} %add_bitcast_fusion), channel_id=1, source_target_pairs={{0,8},{8,0},{16,24},{24,16},{1,9},{9,1},{17,25},{25,17},{2,10},{10... | collective-permute-start | bytes 196616 | tf_op jit(solution)/shard_map/ppermute | solution.py:381
  359.1 4.6 %collective-permute-start.69 = (f32[1,128,128]{2,1,0:T(8,128)S(1)}, f32[1,128,128]{2,1,0:T(8,128)S(1)}, u32[]{:S(2)}, u32[]{:S(2)}) collective-permute-start(f32[1,128,128]{2,1,0:T(8,128)S(1)} %add_bitcast_fusion), channel_id=1, source_target_pairs={{0,16},{8,24},{16,0},{24,8},{1,17},{9,25},{17,1},{25,9},{2,18},{10... | collective-permute-start | bytes 196616 | tf_op jit(solution)/shard_map/ppermute | solution.py:381
  360.7 5.2 %collective-permute-start.70 = (f32[1,128,128]{2,1,0:T(8,128)S(1)}, f32[1,128,128]{2,1,0:T(8,128)S(1)}, u32[]{:S(2)}, u32[]{:S(2)}) collective-permute-start(f32[1,128,128]{2,1,0:T(8,128)S(1)} %add_bitcast_fusion), channel_id=1, source_target_pairs={{0,24},{8,16},{16,8},{24,0},{1,25},{9,17},{17,9},{25,1},{2,26},{10... | collective-permute-start | bytes 196616 | tf_op jit(solution)/shard_map/ppermute | solution.py:381
  (28 other events, 185.8 us)

commit v6 on v5

--- a/solution.py
+++ b/solution.py
@@ -148,6 +148,10 @@
             vector[...] = ordered(where[0], pieces[2 * i][0], pieces[2 * i + 1][0])
 
     out[...] += product(weights[0], [vector[...]])
+
+
+def part_kernel(which, source, out):
+    out[...] = source[0]
 
 
 def columns_kernel(where, *refs):
@@ -446,7 +450,11 @@
     right_side, two, old, both = tie((right_side, two, mine, both))
     mine = gather_near(right_side)
     nears = [old] + [lax.ppermute(old, "lag", [(j, 0)]) for j in range(1, groups)]
-    mine, two = tie((mine, two))
+    field = call(
+        part_kernel, group.astype(jnp.int32).reshape(1), (1,), (excitation,),
+        [pl.BlockSpec((1, part, width), lambda i, w: (STEPS - 1, w[0], 0))], 1, (part, width), (0, 8 * part * width),
+    )[0]
+    mine, two, field = tie((mine, two, field))
     carried = multiply(head_columns, mine)
     density = sum_parts(carried)
     fars = other_core(jnp.stack(nears))
@@ -456,7 +464,7 @@
     mine = gather_near(density)
     two = add_second(two, nears, both, fars)
     mine, two = tie((mine, two))
-    right_side = own_part(excitation[2]) - sum_parts(two + multiply(first_columns, mine))
+    right_side = field - sum_parts(two + multiply(first_columns, mine))
 
     right_side, results = tie((right_side, results))
     mine = gather_near(right_side)

time: 368 us -> 366 us (level)
    pallas_call x4 -> x5, Pallas kernels: 24 us -> 25.6 us  [call(): pl.pallas_call(kernel, out_shape=[jax.ShapeDtypeStruct(shape, F32)] * cou...]
where the time goes in v6:
time: 366 us; the launch traced here: 365 us
  waiting for transfers between devices  164 us (45%)
  starting transfers between devices  99.3 us (27%)
  Pallas kernels  76.6 us (21%)
  other arithmetic  8.32 us (2%)
  matrix products  8.11 us (2%)
  local copies, waits for them, and re-layouts  8.07 us (2%)
    ppermute x18, waiting for transfers between devices, sum_parts(): result = result + lax.ppermute(sent, 'lag', pairs(groups, mask))  91 us
    pallas_call x2, Pallas kernels, add_chip(): pl.pallas_call(chip_kernel, out_shape=[jax.ShapeDtypeStruct(square, F32)]...  26.7 us
    ppermute x15, waiting for transfers between devices, gather_near(): lax.ppermute(value, 'row', pairs(devices, 2 * k))  26.2 us
    pallas_call x5, Pallas kernels, call(): pl.pallas_call(kernel, out_shape=[jax.ShapeDtypeStruct(shape, F32)] * cou...  25.6 us
    ppermute x6, waiting for transfers between devices, along(): lax.ppermute(value, 'row', [(2 * i + c, 2 * (i + step) + c) for i in sour...  22.7 us
    ppermute x18, starting transfers between devices, sum_parts(): result = result + lax.ppermute(sent, 'lag', pairs(groups, mask))  22.6 us
    ppermute x15, starting transfers between devices, gather_near(): lax.ppermute(value, 'row', pairs(devices, 2 * k))  20.1 us
    ppermute x4, starting transfers between devices, enter(): return lax.ppermute(tail, 'lag', [(i, i + 1) for i in range(groups - 1)])  16.1 us
  transfers between devices with their start and end apart: 71, of which 40 were waited for; matrix products, arithmetic and copies ran while one was open for 3% of the time, Pallas kernels for 17%

profile of v6, /device:TPU:0, one launch (start us, length us, event | category | flops | bytes accessed | tf_op | source)
XLA Modules:
  0.0 365.1 jit_solution(11026666223324792016)
XLA Ops:
  0.0 5.0 %collective-permute-start = (f32[4,512,128]{2,1,0:T(8,128)}, f32[4,512,128]{2,1,0:T(8,128)S(1)}, u32[]{:S(2)}, u32[]{:S(2)}) collective-permute-start(f32[4,512,128]{2,1,0:T(8,128)} %refs_0_.2), channel_id=1, source_target_pairs={{0,2},{1,3},{2,4},{3,5},{4,6},{5,7},{8,10},{9,11},{10,12},{11,13},... | collective-permute-start | bytes 3145736 | tf_op jit(solution)/shard_map/ppermute | solution.py:228
  7.5 4.2 %collective-permute-start.2 = (f32[2,512,128]{2,1,0:T(8,128)S(1)}, f32[2,512,128]{2,1,0:T(8,128)}, u32[]{:S(2)}, u32[]{:S(2)}) collective-permute-start(f32[2,512,128]{2,1,0:T(8,128)S(1)} %slice_select_fusion), channel_id=1, source_target_pairs={{0,8},{8,16},{16,24},{1,9},{9,17},{17,25},{2,10},{10,18},{18,26},{... | collective-permute-start | bytes 1572872 | tf_op jit(solution)/shard_map/ppermute | solution.py:389
  12.5 5.8 %columns.2 = f32[512,1024]{1,0:T(8,128)} custom-call(s32[2,5,4]{2,1,0:T(8,128)} %concatenate.43.where, f32[1,512,4096]{2,1,0:T(8,128)} %bitcast.35, f32[1,512,4096]{2,1,0:T(8,128)} %bitcast.36, f32[1,512,4096]{2,1,0:T(8,128)} %bitcast.37, f32[1,512,4096]{2,1,0:T(8,128)} %bitcast.38), custom_call_target="tpu_custom_call" | custom-call | bytes 16777216 | tf_op jit(solution)/shard_map/columns/pallas_call | solution.py:340
  18.3 4.4 %collective-permute-done.2.refs_0_.refs_4_ = f32[2,512,128]{2,1,0:T(8,128)} collective-permute-done((f32[2,512,128]{2,1,0:T(8,128)S(1)}, f32[2,512,128]{2,1,0:T(8,128)}, u32[]{:S(2)}, u32[]{:S(2)}) %collective-permute-start.2) | collective-permute-done | bytes 524320 | tf_op jit(solution)/shard_map/ppermute | solution.py:389
  22.7 5.0 %collective-permute-done = f32[4,512,128]{2,1,0:T(8,128)S(1)} collective-permute-done((f32[4,512,128]{2,1,0:T(8,128)}, f32[4,512,128]{2,1,0:T(8,128)S(1)}, u32[]{:S(2)}, u32[]{:S(2)}) %collective-permute-start) | collective-permute-done | bytes 1048608 | tf_op jit(solution)/shard_map/ppermute | solution.py:228
  27.7 4.1 %collective-permute-done.1 = f32[4,512,128]{2,1,0:T(8,128)S(1)} collective-permute-done((f32[4,512,128]{2,1,0:T(8,128)}, f32[4,512,128]{2,1,0:T(8,128)S(1)}, u32[]{:S(2)}, u32[]{:S(2)}) %collective-permute-start.1) | collective-permute-done | bytes 1048608 | tf_op jit(solution)/shard_map/ppermute | solution.py:228
  34.0 7.1 %columns.3 = (f32[512,1024]{1,0:T(8,128)}, f32[512,1024]{1,0:T(8,128)}, f32[512,1024]{1,0:T(8,128)}, f32[512,512]{1,0:T(8,128)}, f32[512,512]{1,0:T(8,128)}) custom-call(s32[2,5,4]{2,1,0:T(8,128)} %concatenate.43.where, f32[4,512,4096]{2,1,0:T(8,128)} %weights.13, f32[4,512,4096]{2,1,0:T(8,128)} %weights.13, f32[4,512,4096]{2,1,0:T(8,128)} %weights.13, ...), custom_call_target="tpu_custom_call" | custom-call | bytes 16777216 | tf_op jit(solution)/shard_map/columns/pallas_call | solution.py:340
  41.1 4.5 %collective-permute-start.9 = (f32[512,512]{1,0:T(8,128)}, f32[512,512]{1,0:T(8,128)}, u32[]{:S(2)}, u32[]{:S(2)}) collective-permute-start(f32[512,512]{1,0:T(8,128)} %get-tuple-element.112), channel_id=1, source_target_pairs={{0,16},{1,17},{2,18},{3,19},{4,20},{5,21},{6,22},{7,23}} | collective-permute-start | bytes 3145736 | tf_op jit(solution)/shard_map/ppermute | solution.py:400
  46.2 16.6 %chip.2 = (f32[512,128]{1,0:T(8,128)}, f32[512,128]{1,0:T(8,128)}, f32[512,128]{1,0:T(8,128)}, f32[2,512,128]{2,1,0:T(8,128)}) custom-call(s32[10]{0:T(128)} %stack.100.where, f32[4,512,4096]{2,1,0:T(8,128)} %weights.13, f32[4,512,128]{2,1,0:T(8,128)} %refs_0_.2, f32[4,512,128]{2,1,0:T(8,128)} %collective-permute-done.3.refs_1_, f32[4,512,128]{2,1,0:T(8,128)} %copy-done.7, ...), custom_call_target="tpu_custom_call" | custom-call | flops 9663676416 | bytes 16777216 | tf_op jit(solution)/shard_map/chip/pallas_call | solution.py:269
  62.9 1.7 select_select_fusion.1.refs_0_
  64.7 3.2 collective-permute-done.9
  67.9 1.6 collective-permute-start.7
  71.4 10.1 %chip.3 = (f32[512,128]{1,0:T(8,128)}, f32[512,128]{1,0:T(8,128)}, f32[512,128]{1,0:T(8,128)}, f32[2,512,128]{2,1,0:T(8,128)}) custom-call(s32[10]{0:T(128)} %stack.100.where, f32[4,512,4096]{2,1,0:T(8,128)} %weights.13, f32[4,512,128]{2,1,0:T(8,128)} %copy-done.6, ...), custom_call_target="tpu_custom_call", output_to_operand_aliasing={{0}: (4, {}), {1}: (5, {}), {2}: (6, {})} | custom-call | flops 4831838208 | bytes 8388608 | tf_op jit(solution)/shard_map/chip/pallas_call | solution.py:269
  82.3 3.6 shard_map.46
  85.9 13.7 %collective-permute-done.8 = f32[4,512,128]{2,1,0:T(8,128)} collective-permute-done((f32[4,512,128]{2,1,0:T(8,128)}, f32[4,512,128]{2,1,0:T(8,128)}, u32[]{:S(2)}, u32[]{:S(2)}) %collective-permute-start.8) | collective-permute-done | bytes 1048608 | tf_op jit(solution)/shard_map/ppermute | solution.py:228
  101.1 2.8 collective-permute-start.19
  103.9 5.1 %collective-permute-start.20 = (f32[512,1024]{1,0:T(8,128)}, f32[512,1024]{1,0:T(8,128)}, u32[]{:S(2)}, u32[]{:S(2)}) collective-permute-start(f32[512,1024]{1,0:T(8,128)} %get-tuple-element.141), channel_id=1, source_target_pairs={{0,16},{1,17},{2,18},{3,19},{4,20},{5,21},{6,22},{7,23}} | collective-permute-start | bytes 6291464 | tf_op jit(solution)/shard_map/ppermute | solution.py:401
  110.0 7.5 %first.1 = (f32[512,128]{1,0:T(8,128)}, f32[2,512,128]{2,1,0:T(8,128)}) custom-call(s32[10]{0:T(128)} %stack.100.where, f32[4,512,4096]{2,1,0:T(8,128)} %weights.13, f32[4,512,128]{2,1,0:T(8,128)} %copy-done.1, f32[4,512,128]{2,1,0:T(8,128)} %copy-done.3, f32[512,128]{1,0:T(8,128)} %get-tuple-element.127.total), custom_call_target="tpu_custom_call", output_to_operand_aliasing={{0}: (4, {})} | custom-call | flops 1610612736 | bytes 8388608 | tf_op jit(solution)/shard_map/first/pallas_call | solution.py:289
  118.6 1.7 collective-permute-start.22
  120.3 29.6 %collective-permute-done.13 = f32[128,128]{1,0:T(8,128)S(1)} collective-permute-done((f32[128,128]{1,0:T(8,128)S(1)}, f32[128,128]{1,0:T(8,128)S(1)}, u32[]{:S(2)}, u32[]{:S(2)}) %collective-permute-start.13) | collective-permute-done | bytes 65568 | tf_op jit(solution)/shard_map/ppermute | solution.py:381
  149.8 2.3 collective-permute-start.21
  152.1 2.7 collective-permute-done.14
  155.6 19.9 %collective-permute-done.15 = f32[128,128]{1,0:T(8,128)S(1)} collective-permute-done((f32[128,128]{1,0:T(8,128)S(1)}, f32[128,128]{1,0:T(8,128)S(1)}, u32[]{:S(2)}, u32[]{:S(2)}) %collective-permute-start.15) | collective-permute-done | bytes 65568 | tf_op jit(solution)/shard_map/ppermute | solution.py:381
  176.5 4.3 %collective-permute-done.16 = f32[128,128]{1,0:T(8,128)S(1)} collective-permute-done((f32[128,128]{1,0:T(8,128)S(1)}, f32[128,128]{1,0:T(8,128)S(1)}, u32[]{:S(2)}, u32[]{:S(2)}) %collective-permute-start.16) | collective-permute-done | bytes 65568 | tf_op jit(solution)/shard_map/ppermute | solution.py:371
  181.0 5.7 %collective-permute-done.17 = f32[128,128]{1,0:T(8,128)S(1)} collective-permute-done((f32[128,128]{1,0:T(8,128)S(1)}, f32[128,128]{1,0:T(8,128)S(1)}, u32[]{:S(2)}, u32[]{:S(2)}) %collective-permute-start.17) | collective-permute-done | bytes 65568 | tf_op jit(solution)/shard_map/ppermute | solution.py:371
  186.7 1.8 collective-permute-start.18
  188.5 7.7 %shard_map.47 = (f32[512,128]{1,0:T(8,128)}, f32[512,128]{1,0:T(8,128)}) custom-call(s32[10]{0:T(128)} %stack.100.where, f32[4,512,4096]{2,1,0:T(8,128)} %weights.13, f32[4,512,128]{2,1,0:T(8,128)} %copy-done.1, f32[4,512,128]{2,1,0:T(8,128)} %copy-done.1, f32[4,512,128]{2,1,0:T(8,128)} %copy-done.3, ...), custom_call_target="tpu_custom_call", output_to_operand_aliasing={{0}: (6, {}), {1}: (7, {})} | custom-call | flops 3221225472 | bytes 8388608 | tf_op jit(solution)/shard_map/pallas_call | solution.py:193
  199.0 9.2 %collective-permute-start.29 = (f32[2,512,128]{2,1,0:T(8,128)}, f32[2,512,128]{2,1,0:T(8,128)}, u32[]{:S(2)}, u32[]{:S(2)}) collective-permute-start(f32[2,512,128]{2,1,0:T(8,128)} %get-tuple-element.153), channel_id=1, source_target_pairs={{0,8},{8,16},{16,24},{1,9},{9,17},{17,25},{2,10},{10,18},{18,26},{... | collective-permute-start | bytes 1572872 | tf_op jit(solution)/shard_map/ppermute | solution.py:389
  209.9 23.9 %collective-permute-done.24 = f32[128,128]{1,0:T(8,128)S(1)} collective-permute-done((f32[128,128]{1,0:T(8,128)S(1)}, f32[128,128]{1,0:T(8,128)S(1)}, u32[]{:S(2)}, u32[]{:S(2)}) %collective-permute-start.24) | collective-permute-done | bytes 65568 | tf_op jit(solution)/shard_map/ppermute | solution.py:381
  233.8 6.1 %collective-permute-start.26 = (f32[128,128]{1,0:T(8,128)}, f32[128,128]{1,0:T(8,128)}, u32[]{:S(2)}, u32[]{:S(2)}) collective-permute-start(f32[128,128]{1,0:T(8,128)} %get-tuple-element.221), channel_id=1, source_target_pairs={{0,24},{8,16},{16,8},{24,0},{1,25},{9,17},{17,9},{25,1},{2,26},{10... | collective-permute-start | bytes 196616 | tf_op jit(solution)/shard_map/ppermute | solution.py:381
  239.9 3.9 %pick.1 = f32[512,1024]{1,0:T(8,128)} custom-call(s32[1]{0:T(128)} %bitcast.12.which, f32[512,1024]{1,0:T(8,128)} %get-tuple-element.147.refs_0_, f32[512,1024]{1,0:T(8,128)} %collective-permute-done.19.refs_1_, f32[512,1024]{1,0:T(8,128)} %collective-permute-done.20.refs_2_, f32[512,512]{1,0:T(8,128)} %collective-permute-done.21.refs_3_, ...), custom_call_target="tpu_custom_call" | custom-call | bytes 8388608 | tf_op jit(solution)/shard_map/pick/pallas_call | solution.py:356
  246.1 2.5 collective-permute-start.31
  248.6 3.1 collective-permute-done.30
  251.8 2.0 collective-permute-start.32
  253.7 4.1 %collective-permute-done.32 = f32[128,128]{1,0:T(8,128)S(1)} collective-permute-done((f32[128,128]{1,0:T(8,128)S(1)}, f32[128,128]{1,0:T(8,128)S(1)}, u32[]{:S(2)}, u32[]{:S(2)}) %collective-permute-start.32) | collective-permute-done | bytes 65568 | tf_op jit(solution)/shard_map/ppermute | solution.py:371
  259.5 4.3 %shard_map.48 = (f32[512,128]{1,0:T(8,128)}, f32[512,128]{1,0:T(8,128)}) custom-call(s32[10]{0:T(128)} %stack.100.where, f32[4,512,4096]{2,1,0:T(8,128)} %weights.13, f32[2,512,128]{2,1,0:T(8,128)} %copy-done.12, f32[2,512,128]{2,1,0:T(8,128)} %copy-done.14, f32[2,512,128]{2,1,0:T(8,128)} %copy-done.13, ...), custom_call_target="tpu_custom_call", output_to_operand_aliasing={{0}: (8, {}), {1}: (9, {})} | custom-call | flops 2415919104 | bytes 6291456 | tf_op jit(solution)/shard_map/pallas_call | solution.py:193
  265.4 2.6 fusion.4
  268.0 3.4 collective-permute-start.37
  273.9 1.9 collective-permute-done.38
  275.7 2.5 collective-permute-done.39
  283.3 2.5 collective-permute-start.41
  285.8 1.7 collective-permute-done.40
  287.6 2.0 collective-permute-start.42
  291.0 2.6 collective-permute-done.42
  297.8 2.7 collective-permute-start.45
  300.6 2.9 collective-permute-done.45
  303.5 2.2 collective-permute-done.46
  305.7 2.5 collective-permute-start.48
  308.3 1.8 collective-permute-start.49
  310.1 2.3 collective-permute-done.48
  312.4 2.0 collective-permute-done.49
  314.4 8.5 %shard_map.50 = f32[512,128]{1,0:T(8,128)} custom-call(s32[10]{0:T(128)} %stack.100.where, f32[4,512,4096]{2,1,0:T(8,128)} %weights.13, f32[512,128]{1,0:T(8,128)} %copy-done.5, f32[512,128]{1,0:T(8,128)} %copy-done.16, f32[512,128]{1,0:T(8,128)} %copy-done.17, f32[512,128]{1,0:T(8,128)} %copy-done.18, ...), custom_call_target="tpu_custom_call", output_to_operand_aliasing={{}: (15, {})} | custom-call | flops 1610612736 | bytes 8388608 | tf_op jit(solution)/shard_map/pallas_call | solution.py:193
  324.5 2.6 fusion.12
  327.7 2.9 collective-permute-start.57
  333.0 2.4 collective-permute-start.59
  335.4 2.0 collective-permute-start.60
  337.4 1.8 collective-permute-start.61
  339.2 1.7 collective-permute-start.62
  341.5 1.6 collective-permute-done.61
  344.7 2.1 collective-permute-done.63
  350.2 2.9 collective-permute-start.67
  355.4 2.0 collective-permute-start.68
  360.1 2.0 collective-permute-done.69
  362.1 2.1 collective-permute-done.70
  (174 shorter events, 53.4 us)
Async XLA Ops:
  0.0 27.7 %collective-permute-start = (f32[4,512,128]{2,1,0:T(8,128)}, f32[4,512,128]{2,1,0:T(8,128)S(1)}, u32[]{:S(2)}, u32[]{:S(2)}) collective-permute-start(f32[4,512,128]{2,1,0:T(8,128)} %refs_0_.2), channel_id=1, source_target_pairs={{0,2},{1,3},{2,4},{3,5},{4,6},{5,7},{8,10},{9,11},{10,12},{11,13},... | collective-permute-start | bytes 3145736 | tf_op jit(solution)/shard_map/ppermute | solution.py:228
  5.0 26.7 %collective-permute-start.1 = (f32[4,512,128]{2,1,0:T(8,128)}, f32[4,512,128]{2,1,0:T(8,128)S(1)}, u32[]{:S(2)}, u32[]{:S(2)}) collective-permute-start(f32[4,512,128]{2,1,0:T(8,128)} %refs_0_.2), channel_id=1, source_target_pairs={{2,0},{3,1},{4,2},{5,3},{6,4},{7,5},{10,8},{11,9},{12,10},{13,11},... | collective-permute-start | bytes 3145736 | tf_op jit(solution)/shard_map/ppermute | solution.py:228
  6.3 25.4 %collective-permute-start.3 = (f32[4,512,128]{2,1,0:T(8,128)}, f32[4,512,128]{2,1,0:T(8,128)}, u32[]{:S(2)}, u32[]{:S(2)}) collective-permute-start(f32[4,512,128]{2,1,0:T(8,128)} %refs_0_.2), channel_id=1, source_target_pairs={{0,1},{1,0},{2,3},{3,2},{4,5},{5,4},{6,7},{7,6},{8,9},{9,8},{10,11... | collective-permute-start | bytes 3145736 | tf_op jit(solution)/shard_map/ppermute | solution.py:225
  7.5 15.2 %collective-permute-start.2 = (f32[2,512,128]{2,1,0:T(8,128)S(1)}, f32[2,512,128]{2,1,0:T(8,128)}, u32[]{:S(2)}, u32[]{:S(2)}) collective-permute-start(f32[2,512,128]{2,1,0:T(8,128)S(1)} %slice_select_fusion), channel_id=1, source_target_pairs={{0,8},{8,16},{16,24},{1,9},{9,17},{17,25},{2,10},{10,18},{18,26},{... | collective-permute-start | bytes 1572872 | tf_op jit(solution)/shard_map/ppermute | solution.py:389
  31.9 14.4 %collective-permute-start.6 = (f32[4,512,128]{2,1,0:T(8,128)S(1)}, f32[4,512,128]{2,1,0:T(8,128)}, u32[]{:S(2)}, u32[]{:S(2)}) collective-permute-start(f32[4,512,128]{2,1,0:T(8,128)S(1)} %broadcast_select_fusion.refs_2_), channel_id=1, source_target_pairs={{0,1},{1,0},{2,3},{3,2},{4,5},{5,4},{6,7},{7,6},{8,9},{9,8},{10,11... | collective-permute-start | bytes 3145736 | tf_op jit(solution)/shard_map/ppermute | solution.py:225
  32.0 30.9 %collective-permute-start.4 = (f32[4,512,128]{2,1,0:T(8,128)}, f32[4,512,128]{2,1,0:T(8,128)S(1)}, u32[]{:S(2)}, u32[]{:S(2)}) collective-permute-start(f32[4,512,128]{2,1,0:T(8,128)} %copy-done.19), channel_id=1, source_target_pairs={{2,4},{3,5},{4,6},{5,7},{10,12},{11,13},{12,14},{13,15},{18,20},{1... | collective-permute-start | bytes 3145736 | tf_op jit(solution)/shard_map/ppermute | solution.py:228
  32.7 30.2 %collective-permute-start.5 = (f32[4,512,128]{2,1,0:T(8,128)S(1)}, f32[4,512,128]{2,1,0:T(8,128)}, u32[]{:S(2)}, u32[]{:S(2)}) collective-permute-start(f32[4,512,128]{2,1,0:T(8,128)S(1)} %collective-permute-done.1), channel_id=1, source_target_pairs={{2,0},{3,1},{4,2},{5,3},{10,8},{11,9},{12,10},{13,11},{18,16},{19,... | collective-permute-start | bytes 3145736 | tf_op jit(solution)/shard_map/ppermute | solution.py:228
  41.1 26.8 %collective-permute-start.9 = (f32[512,512]{1,0:T(8,128)}, f32[512,512]{1,0:T(8,128)}, u32[]{:S(2)}, u32[]{:S(2)}) collective-permute-start(f32[512,512]{1,0:T(8,128)} %get-tuple-element.112), channel_id=1, source_target_pairs={{0,16},{1,17},{2,18},{3,19},{4,20},{5,21},{6,22},{7,23}} | collective-permute-start | bytes 3145736 | tf_op jit(solution)/shard_map/ppermute | solution.py:400
  67.9 18.0 %collective-permute-start.7 = (f32[4,512,128]{2,1,0:T(8,128)S(1)}, f32[4,512,128]{2,1,0:T(8,128)}, u32[]{:S(2)}, u32[]{:S(2)}) collective-permute-start(f32[4,512,128]{2,1,0:T(8,128)S(1)} %collective-permute-done.4), channel_id=1, source_target_pairs={{4,6},{5,7},{12,14},{13,15},{20,22},{21,23},{28,30},{29,31}} | collective-permute-start | bytes 3145736 | tf_op jit(solution)/shard_map/ppermute | solution.py:228
  69.5 30.1 %collective-permute-start.8 = (f32[4,512,128]{2,1,0:T(8,128)}, f32[4,512,128]{2,1,0:T(8,128)}, u32[]{:S(2)}, u32[]{:S(2)}) collective-permute-start(f32[4,512,128]{2,1,0:T(8,128)} %collective-permute-done.5), channel_id=1, source_target_pairs={{2,0},{3,1},{10,8},{11,9},{18,16},{19,17},{26,24},{27,25}} | collective-permute-start | bytes 3145736 | tf_op jit(solution)/shard_map/ppermute | solution.py:228
  70.8 10.7 %collective-permute-start.11 = (f32[2,512,128]{2,1,0:T(8,128)}, f32[2,512,128]{2,1,0:T(8,128)S(1)}, u32[]{:S(2)}, u32[]{:S(2)}) collective-permute-start(f32[2,512,128]{2,1,0:T(8,128)} %collective-permute-done.2.refs_0_.refs_4_), channel_id=1, source_target_pairs={{0,1},{1,0},{2,3},{3,2},{4,5},{5,4},{6,7},{7,6},{8,9},{9,8},{10,11... | collective-permute-start | bytes 1572872 | tf_op jit(solution)/shard_map/ppermute | solution.py:225
  101.1 8.0 %collective-permute-start.12 = (f32[4,512,128]{2,1,0:T(8,128)S(1)}, f32[4,512,128]{2,1,0:T(8,128)S(1)}, u32[]{:S(2)}, u32[]{:S(2)}) collective-permute-start(f32[4,512,128]{2,1,0:T(8,128)S(1)} %select_select_fusion.near.near_before), channel_id=1, source_target_pairs={{0,1},{1,0},{2,3},{3,2},{4,5},{5,4},{6,7},{7,6},{8,9},{9,8},{10,11... | collective-permute-start | bytes 3145736 | tf_op jit(solution)/shard_map/ppermute | solution.py:225
  101.1 95.0 %collective-permute-start.19 = (f32[512,1024]{1,0:T(8,128)}, f32[512,1024]{1,0:T(8,128)}, u32[]{:S(2)}, u32[]{:S(2)}) collective-permute-start(f32[512,1024]{1,0:T(8,128)} %get-tuple-element.140), channel_id=1, source_target_pairs={{0,8},{1,9},{2,10},{3,11},{4,12},{5,13},{6,14},{7,15}} | collective-permute-start | bytes 6291464 | tf_op jit(solution)/shard_map/ppermute | solution.py:401
  103.9 92.3 %collective-permute-start.20 = (f32[512,1024]{1,0:T(8,128)}, f32[512,1024]{1,0:T(8,128)}, u32[]{:S(2)}, u32[]{:S(2)}) collective-permute-start(f32[512,1024]{1,0:T(8,128)} %get-tuple-element.141), channel_id=1, source_target_pairs={{0,16},{1,17},{2,18},{3,19},{4,20},{5,21},{6,22},{7,23}} | collective-permute-start | bytes 6291464 | tf_op jit(solution)/shard_map/ppermute | solution.py:401
  118.5 31.4 %collective-permute-start.13 = (f32[128,128]{1,0:T(8,128)S(1)}, f32[128,128]{1,0:T(8,128)S(1)}, u32[]{:S(2)}, u32[]{:S(2)}) collective-permute-start(f32[128,128]{1,0:T(8,128)S(1)} %get-tuple-element.223), channel_id=1, source_target_pairs={{0,8},{8,0},{16,24},{24,16},{1,9},{9,1},{17,25},{25,17},{2,10},{10... | collective-permute-start | bytes 196616 | tf_op jit(solution)/shard_map/ppermute | solution.py:381
  118.5 36.3 %collective-permute-start.14 = (f32[128,128]{1,0:T(8,128)S(1)}, f32[128,128]{1,0:T(8,128)S(1)}, u32[]{:S(2)}, u32[]{:S(2)}) collective-permute-start(f32[128,128]{1,0:T(8,128)S(1)} %get-tuple-element.225), channel_id=1, source_target_pairs={{0,16},{8,24},{16,0},{24,8},{1,17},{9,25},{17,1},{25,9},{2,18},{10... | collective-permute-start | bytes 196616 | tf_op jit(solution)/shard_map/ppermute | solution.py:381
  118.6 77.6 %collective-permute-start.22 = (f32[512,512]{1,0:T(8,128)}, f32[512,512]{1,0:T(8,128)}, u32[]{:S(2)}, u32[]{:S(2)}) collective-permute-start(f32[512,512]{1,0:T(8,128)} %collective-permute-done.9), channel_id=1, source_target_pairs={{16,24},{17,25},{18,26},{19,27},{20,28},{21,29},{22,30},{23,31}} | collective-permute-start | bytes 3145736 | tf_op jit(solution)/shard_map/ppermute | solution.py:410
  149.8 46.4 %collective-permute-start.21 = (f32[512,512]{1,0:T(8,128)}, f32[512,512]{1,0:T(8,128)}, u32[]{:S(2)}, u32[]{:S(2)}) collective-permute-start(f32[512,512]{1,0:T(8,128)} %get-tuple-element.144), channel_id=1, source_target_pairs={{0,24},{1,25},{2,26},{3,27},{4,28},{5,29},{6,30},{7,31}} | collective-permute-start | bytes 3145736 | tf_op jit(solution)/shard_map/ppermute | solution.py:421
  154.8 20.7 %collective-permute-start.15 = (f32[128,128]{1,0:T(8,128)S(1)}, f32[128,128]{1,0:T(8,128)S(1)}, u32[]{:S(2)}, u32[]{:S(2)}) collective-permute-start(f32[128,128]{1,0:T(8,128)S(1)} %get-tuple-element.224), channel_id=1, source_target_pairs={{0,24},{8,16},{16,8},{24,0},{1,25},{9,17},{17,9},{25,1},{2,26},{10... | collective-permute-start | bytes 196616 | tf_op jit(solution)/shard_map/ppermute | solution.py:381
  176.4 4.3 %collective-permute-start.16 = (f32[128,128]{1,0:T(8,128)S(1)}, f32[128,128]{1,0:T(8,128)S(1)}, u32[]{:S(2)}, u32[]{:S(2)}) collective-permute-start(f32[128,128]{1,0:T(8,128)S(1)} %bitcast_subtract_fusion), channel_id=1, source_target_pairs={{0,2},{1,3},{2,0},{3,1},{4,6},{5,7},{6,4},{7,5},{8,10},{9,11},{10,... | collective-permute-start | bytes 196616 | tf_op jit(solution)/shard_map/ppermute | solution.py:371
  180.7 6.0 %collective-permute-start.17 = (f32[128,128]{1,0:T(8,128)S(1)}, f32[128,128]{1,0:T(8,128)S(1)}, u32[]{:S(2)}, u32[]{:S(2)}) collective-permute-start(f32[128,128]{1,0:T(8,128)S(1)} %bitcast_subtract_fusion), channel_id=1, source_target_pairs={{0,4},{1,5},{2,6},{3,7},{4,0},{5,1},{6,2},{7,3},{8,12},{9,13},{10,... | collective-permute-start | bytes 196616 | tf_op jit(solution)/shard_map/ppermute | solution.py:371
  186.7 9.4 %collective-permute-start.18 = (f32[128,128]{1,0:T(8,128)S(1)}, f32[128,128]{1,0:T(8,128)S(1)}, u32[]{:S(2)}, u32[]{:S(2)}) collective-permute-start(f32[128,128]{1,0:T(8,128)S(1)} %bitcast_subtract_fusion), channel_id=1, source_target_pairs={{0,6},{1,7},{2,4},{3,5},{4,2},{5,3},{6,0},{7,1},{8,14},{9,15},{10,... | collective-permute-start | bytes 196616 | tf_op jit(solution)/shard_map/ppermute | solution.py:371
  196.2 12.0 %collective-permute-start.23 = (f32[512,128]{1,0:T(8,128)S(1)}, f32[512,128]{1,0:T(8,128)S(1)}, u32[]{:S(2)}, u32[]{:S(2)}) collective-permute-start(f32[512,128]{1,0:T(8,128)S(1)} %pad_maximum_fusion.2), channel_id=1, source_target_pairs={{0,1},{1,0},{2,3},{3,2},{4,5},{5,4},{6,7},{7,6},{8,9},{9,8},{10,11... | collective-permute-start | bytes 786440 | tf_op jit(solution)/shard_map/ppermute | solution.py:225
  196.3 49.1 %collective-permute-start.27 = (f32[2,512,128]{2,1,0:T(8,128)}, f32[2,512,128]{2,1,0:T(8,128)S(1)}, u32[]{:S(2)}, u32[]{:S(2)}) collective-permute-start(f32[2,512,128]{2,1,0:T(8,128)} %get-tuple-element.143), channel_id=1, source_target_pairs={{0,8},{8,16},{16,24},{1,9},{9,17},{17,25},{2,10},{10,18},{18,26},{... | collective-permute-start | bytes 1572872 | tf_op jit(solution)/shard_map/ppermute | solution.py:389
  197.6 47.8 %collective-permute-start.28 = (f32[2,512,128]{2,1,0:T(8,128)}, f32[2,512,128]{2,1,0:T(8,128)S(1)}, u32[]{:S(2)}, u32[]{:S(2)}) collective-permute-start(f32[2,512,128]{2,1,0:T(8,128)} %get-tuple-element.152), channel_id=1, source_target_pairs={{0,8},{8,16},{16,24},{1,9},{9,17},{17,25},{2,10},{10,18},{18,26},{... | collective-permute-start | bytes 1572872 | tf_op jit(solution)/shard_map/ppermute | solution.py:389
  199.0 46.5 %collective-permute-start.29 = (f32[2,512,128]{2,1,0:T(8,128)}, f32[2,512,128]{2,1,0:T(8,128)}, u32[]{:S(2)}, u32[]{:S(2)}) collective-permute-start(f32[2,512,128]{2,1,0:T(8,128)} %get-tuple-element.153), channel_id=1, source_target_pairs={{0,8},{8,16},{16,24},{1,9},{9,17},{17,25},{2,10},{10,18},{18,26},{... | collective-permute-start | bytes 1572872 | tf_op jit(solution)/shard_map/ppermute | solution.py:389
  209.9 23.9 %collective-permute-start.24 = (f32[128,128]{1,0:T(8,128)S(1)}, f32[128,128]{1,0:T(8,128)S(1)}, u32[]{:S(2)}, u32[]{:S(2)}) collective-permute-start(f32[128,128]{1,0:T(8,128)S(1)} %get-tuple-element.220), channel_id=1, source_target_pairs={{0,8},{8,0},{16,24},{24,16},{1,9},{9,1},{17,25},{25,17},{2,10},{10... | collective-permute-start | bytes 196616 | tf_op jit(solution)/shard_map/ppermute | solution.py:381
  209.9 34.0 %collective-permute-start.25 = (f32[128,128]{1,0:T(8,128)}, f32[128,128]{1,0:T(8,128)S(1)}, u32[]{:S(2)}, u32[]{:S(2)}) collective-permute-start(f32[128,128]{1,0:T(8,128)} %get-tuple-element.222), channel_id=1, source_target_pairs={{0,16},{8,24},{16,0},{24,8},{1,17},{9,25},{17,1},{25,9},{2,18},{10... | collective-permute-start | bytes 196616 | tf_op jit(solution)/shard_map/ppermute | solution.py:381
  233.8 10.7 %collective-permute-start.26 = (f32[128,128]{1,0:T(8,128)}, f32[128,128]{1,0:T(8,128)}, u32[]{:S(2)}, u32[]{:S(2)}) collective-permute-start(f32[128,128]{1,0:T(8,128)} %get-tuple-element.221), channel_id=1, source_target_pairs={{0,24},{8,16},{16,8},{24,0},{1,25},{9,17},{17,9},{25,1},{2,26},{10... | collective-permute-start | bytes 196616 | tf_op jit(solution)/shard_map/ppermute | solution.py:381
  245.4 12.4 %collective-permute-start.33 = (f32[2,512,128]{2,1,0:T(8,128)S(1)}, f32[2,512,128]{2,1,0:T(8,128)S(1)}, u32[]{:S(2)}, u32[]{:S(2)}) collective-permute-start(f32[2,512,128]{2,1,0:T(8,128)S(1)} %collective-permute-done.27.refs_0_.refs_6_), channel_id=1, source_target_pairs={{0,1},{1,0},{2,3},{3,2},{4,5},{5,4},{6,7},{7,6},{8,9},{9,8},{10,11... | collective-permute-start | bytes 1572872 | tf_op jit(solution)/shard_map/ppermute | solution.py:225
  245.5 12.4 %collective-permute-start.34 = (f32[2,512,128]{2,1,0:T(8,128)S(1)}, f32[2,512,128]{2,1,0:T(8,128)S(1)}, u32[]{:S(2)}, u32[]{:S(2)}) collective-permute-start(f32[2,512,128]{2,1,0:T(8,128)S(1)} %collective-permute-done.28.refs_2_.refs_8_), channel_id=1, source_target_pairs={{0,1},{1,0},{2,3},{3,2},{4,5},{5,4},{6,7},{7,6},{8,9},{9,8},{10,11... | collective-permute-start | bytes 1572872 | tf_op jit(solution)/shard_map/ppermute | solution.py:225
  246.0 13.5 %collective-permute-start.35 = (f32[2,512,128]{2,1,0:T(8,128)}, f32[2,512,128]{2,1,0:T(8,128)}, u32[]{:S(2)}, u32[]{:S(2)}) collective-permute-start(f32[2,512,128]{2,1,0:T(8,128)} %collective-permute-done.29.refs_4_.refs_10_), channel_id=1, source_target_pairs={{0,1},{1,0},{2,3},{3,2},{4,5},{5,4},{6,7},{7,6},{8,9},{9,8},{10,11... | collective-permute-start | bytes 1572872 | tf_op jit(solution)/shard_map/ppermute | solution.py:225
  246.1 5.7 %collective-permute-start.30 = (f32[128,128]{1,0:T(8,128)S(1)}, f32[128,128]{1,0:T(8,128)S(1)}, u32[]{:S(2)}, u32[]{:S(2)}) collective-permute-start(f32[128,128]{1,0:T(8,128)S(1)} %add_add_fusion.1), channel_id=1, source_target_pairs={{0,2},{1,3},{2,0},{3,1},{4,6},{5,7},{6,4},{7,5},{8,10},{9,11},{10,... | collective-permute-start | bytes 196616 | tf_op jit(solution)/shard_map/ppermute | solution.py:371
  246.1 7.6 %collective-permute-start.31 = (f32[128,128]{1,0:T(8,128)S(1)}, f32[128,128]{1,0:T(8,128)S(1)}, u32[]{:S(2)}, u32[]{:S(2)}) collective-permute-start(f32[128,128]{1,0:T(8,128)S(1)} %add_add_fusion.1), channel_id=1, source_target_pairs={{0,4},{1,5},{2,6},{3,7},{4,0},{5,1},{6,2},{7,3},{8,12},{9,13},{10,... | collective-permute-start | bytes 196616 | tf_op jit(solution)/shard_map/ppermute | solution.py:371
  251.8 6.1 %collective-permute-start.32 = (f32[128,128]{1,0:T(8,128)S(1)}, f32[128,128]{1,0:T(8,128)S(1)}, u32[]{:S(2)}, u32[]{:S(2)}) collective-permute-start(f32[128,128]{1,0:T(8,128)S(1)} %add_add_fusion.1), channel_id=1, source_target_pairs={{0,6},{1,7},{2,4},{3,5},{4,2},{5,3},{6,0},{7,1},{8,14},{9,15},{10,... | collective-permute-start | bytes 196616 | tf_op jit(solution)/shard_map/ppermute | solution.py:371
  268.0 5.8 %collective-permute-start.37 = (f32[128,128]{1,0:T(8,128)S(1)}, f32[128,128]{1,0:T(8,128)S(1)}, u32[]{:S(2)}, u32[]{:S(2)}) collective-permute-start(f32[128,128]{1,0:T(8,128)S(1)} %get-tuple-element.217), channel_id=1, source_target_pairs={{0,8},{8,0},{16,24},{24,16},{1,9},{9,1},{17,25},{25,17},{2,10},{10... | collective-permute-start | bytes 196616 | tf_op jit(solution)/shard_map/ppermute | solution.py:381
  273.1 5.2 %collective-permute-start.39 = (f32[128,128]{1,0:T(8,128)S(1)}, f32[128,128]{1,0:T(8,128)S(1)}, u32[]{:S(2)}, u32[]{:S(2)}) collective-permute-start(f32[128,128]{1,0:T(8,128)S(1)} %get-tuple-element.218), channel_id=1, source_target_pairs={{0,24},{8,16},{16,8},{24,0},{1,25},{9,17},{17,9},{25,1},{2,26},{10... | collective-permute-start | bytes 196616 | tf_op jit(solution)/shard_map/ppermute | solution.py:381
  279.1 14.6 %collective-permute-start.50 = (f32[512,128]{1,0:T(8,128)S(1)}, f32[512,128]{1,0:T(8,128)S(1)}, u32[]{:S(2)}, u32[]{:S(2)}) collective-permute-start(f32[512,128]{1,0:T(8,128)S(1)} %pad_maximum_fusion.3.refs_0_), channel_id=1, source_target_pairs={{8,0},{9,1},{10,2},{11,3},{12,4},{13,5},{14,6},{15,7}} | collective-permute-start | bytes 786440 | tf_op jit(solution)/shard_map/ppermute | solution.py:452
  280.4 14.1 %collective-permute-start.51 = (f32[512,128]{1,0:T(8,128)S(1)}, f32[512,128]{1,0:T(8,128)S(1)}, u32[]{:S(2)}, u32[]{:S(2)}) collective-permute-start(f32[512,128]{1,0:T(8,128)S(1)} %pad_maximum_fusion.3.refs_0_), channel_id=1, source_target_pairs={{16,0},{17,1},{18,2},{19,3},{20,4},{21,5},{22,6},{23,7}} | collective-permute-start | bytes 786440 | tf_op jit(solution)/shard_map/ppermute | solution.py:452
  281.7 12.9 %collective-permute-start.52 = (f32[512,128]{1,0:T(8,128)S(1)}, f32[512,128]{1,0:T(8,128)S(1)}, u32[]{:S(2)}, u32[]{:S(2)}) collective-permute-start(f32[512,128]{1,0:T(8,128)S(1)} %pad_maximum_fusion.3.refs_0_), channel_id=1, source_target_pairs={{24,0},{25,1},{26,2},{27,3},{28,4},{29,5},{30,6},{31,7}} | collective-permute-start | bytes 786440 | tf_op jit(solution)/shard_map/ppermute | solution.py:452
  283.2 4.3 %collective-permute-start.40 = (f32[128,128]{1,0:T(8,128)S(1)}, f32[128,128]{1,0:T(8,128)S(1)}, u32[]{:S(2)}, u32[]{:S(2)}) collective-permute-start(f32[128,128]{1,0:T(8,128)S(1)} %bitcast_subtract_fusion.1), channel_id=1, source_target_pairs={{0,2},{1,3},{2,0},{3,1},{4,6},{5,7},{6,4},{7,5},{8,10},{9,11},{10,... | collective-permute-start | bytes 196616 | tf_op jit(solution)/shard_map/ppermute | solution.py:371
  283.3 7.7 %collective-permute-start.41 = (f32[128,128]{1,0:T(8,128)S(1)}, f32[128,128]{1,0:T(8,128)S(1)}, u32[]{:S(2)}, u32[]{:S(2)}) collective-permute-start(f32[128,128]{1,0:T(8,128)S(1)} %bitcast_subtract_fusion.1), channel_id=1, source_target_pairs={{0,4},{1,5},{2,6},{3,7},{4,0},{5,1},{6,2},{7,3},{8,12},{9,13},{10,... | collective-permute-start | bytes 196616 | tf_op jit(solution)/shard_map/ppermute | solution.py:371
  287.6 6.1 %collective-permute-start.42 = (f32[128,128]{1,0:T(8,128)S(1)}, f32[128,128]{1,0:T(8,128)S(1)}, u32[]{:S(2)}, u32[]{:S(2)}) collective-permute-start(f32[128,128]{1,0:T(8,128)S(1)} %bitcast_subtract_fusion.1), channel_id=1, source_target_pairs={{0,6},{1,7},{2,4},{3,5},{4,2},{5,3},{6,0},{7,1},{8,14},{9,15},{10,... | collective-permute-start | bytes 196616 | tf_op jit(solution)/shard_map/ppermute | solution.py:371
  294.6 19.7 %collective-permute-start.53 = (f32[4,512,128]{2,1,0:T(8,128)S(1)}, f32[4,512,128]{2,1,0:T(8,128)}, u32[]{:S(2)}, u32[]{:S(2)}) collective-permute-start(f32[4,512,128]{2,1,0:T(8,128)S(1)} %pad_maximum_fusion), channel_id=1, source_target_pairs={{0,1},{1,0},{2,3},{3,2},{4,5},{5,4},{6,7},{7,6},{8,9},{9,8},{10,11... | collective-permute-start | bytes 3145736 | tf_op jit(solution)/shard_map/ppermute | solution.py:225
  297.8 5.7 %collective-permute-start.45 = (f32[128,128]{1,0:T(8,128)S(1)}, f32[128,128]{1,0:T(8,128)S(1)}, u32[]{:S(2)}, u32[]{:S(2)}) collective-permute-start(f32[128,128]{1,0:T(8,128)S(1)} %get-tuple-element.216), channel_id=1, source_target_pairs={{0,16},{8,24},{16,0},{24,8},{1,17},{9,25},{17,1},{25,9},{2,18},{10... | collective-permute-start | bytes 196616 | tf_op jit(solution)/shard_map/ppermute | solution.py:381
  300.5 5.2 %collective-permute-start.46 = (f32[128,128]{1,0:T(8,128)S(1)}, f32[128,128]{1,0:T(8,128)S(1)}, u32[]{:S(2)}, u32[]{:S(2)}) collective-permute-start(f32[128,128]{1,0:T(8,128)S(1)} %get-tuple-element.215), channel_id=1, source_target_pairs={{0,24},{8,16},{16,8},{24,0},{1,25},{9,17},{17,9},{25,1},{2,26},{10... | collective-permute-start | bytes 196616 | tf_op jit(solution)/shard_map/ppermute | solution.py:381
  305.7 4.5 %collective-permute-start.47 = (f32[128,128]{1,0:T(8,128)S(1)}, f32[128,128]{1,0:T(8,128)S(1)}, u32[]{:S(2)}, u32[]{:S(2)}) collective-permute-start(f32[128,128]{1,0:T(8,128)S(1)} %add_add_fusion), channel_id=1, source_target_pairs={{0,2},{1,3},{2,0},{3,1},{4,6},{5,7},{6,4},{7,5},{8,10},{9,11},{10,... | collective-permute-start | bytes 196616 | tf_op jit(solution)/shard_map/ppermute | solution.py:371
  305.7 6.6 %collective-permute-start.48 = (f32[128,128]{1,0:T(8,128)S(1)}, f32[128,128]{1,0:T(8,128)S(1)}, u32[]{:S(2)}, u32[]{:S(2)}) collective-permute-start(f32[128,128]{1,0:T(8,128)S(1)} %add_add_fusion), channel_id=1, source_target_pairs={{0,4},{1,5},{2,6},{3,7},{4,0},{5,1},{6,2},{7,3},{8,12},{9,13},{10,... | collective-permute-start | bytes 196616 | tf_op jit(solution)/shard_map/ppermute | solution.py:371
  308.3 6.1 %collective-permute-start.49 = (f32[128,128]{1,0:T(8,128)S(1)}, f32[128,128]{1,0:T(8,128)S(1)}, u32[]{:S(2)}, u32[]{:S(2)}) collective-permute-start(f32[128,128]{1,0:T(8,128)S(1)} %add_add_fusion), channel_id=1, source_target_pairs={{0,6},{1,7},{2,4},{3,5},{4,2},{5,3},{6,0},{7,1},{8,14},{9,15},{10,... | collective-permute-start | bytes 196616 | tf_op jit(solution)/shard_map/ppermute | solution.py:371
  327.1 4.6 %collective-permute-start.55 = (f32[128,128]{1,0:T(8,128)S(1)}, f32[128,128]{1,0:T(8,128)S(1)}, u32[]{:S(2)}, u32[]{:S(2)}) collective-permute-start(f32[128,128]{1,0:T(8,128)S(1)} %get-tuple-element.211), channel_id=1, source_target_pairs={{0,8},{8,0},{16,24},{24,16},{1,9},{9,1},{17,25},{25,17},{2,10},{10... | collective-permute-start | bytes 196616 | tf_op jit(solution)/shard_map/ppermute | solution.py:381
  327.2 5.7 %collective-permute-start.56 = (f32[128,128]{1,0:T(8,128)S(1)}, f32[128,128]{1,0:T(8,128)S(1)}, u32[]{:S(2)}, u32[]{:S(2)}) collective-permute-start(f32[128,128]{1,0:T(8,128)S(1)} %get-tuple-element.213), channel_id=1, source_target_pairs={{0,16},{8,24},{16,0},{24,8},{1,17},{9,25},{17,1},{25,9},{2,18},{10... | collective-permute-start | bytes 196616 | tf_op jit(solution)/shard_map/ppermute | solution.py:381
  327.7 5.2 %collective-permute-start.57 = (f32[128,128]{1,0:T(8,128)S(1)}, f32[128,128]{1,0:T(8,128)S(1)}, u32[]{:S(2)}, u32[]{:S(2)}) collective-permute-start(f32[128,128]{1,0:T(8,128)S(1)} %get-tuple-element.212), channel_id=1, source_target_pairs={{0,24},{8,16},{16,8},{24,0},{1,25},{9,17},{17,9},{25,1},{2,26},{10... | collective-permute-start | bytes 196616 | tf_op jit(solution)/shard_map/ppermute | solution.py:381
  333.0 8.0 %collective-permute-start.58 = (f32[128,128]{1,0:T(8,128)S(1)}, f32[128,128]{1,0:T(8,128)S(1)}, u32[]{:S(2)}, u32[]{:S(2)}) collective-permute-start(f32[128,128]{1,0:T(8,128)S(1)} %add_subtract_fusion), channel_id=1, source_target_pairs={{0,2},{1,3},{2,0},{3,1},{4,6},{5,7},{6,4},{7,5},{8,10},{9,11},{10,... | collective-permute-start | bytes 196616 | tf_op jit(solution)/shard_map/ppermute | solution.py:371
  333.0 7.9 %collective-permute-start.59 = (f32[128,128]{1,0:T(8,128)S(1)}, f32[128,128]{1,0:T(8,128)S(1)}, u32[]{:S(2)}, u32[]{:S(2)}) collective-permute-start(f32[128,128]{1,0:T(8,128)S(1)} %add_subtract_fusion), channel_id=1, source_target_pairs={{0,4},{1,5},{2,6},{3,7},{4,0},{5,1},{6,2},{7,3},{8,12},{9,13},{10,... | collective-permute-start | bytes 196616 | tf_op jit(solution)/shard_map/ppermute | solution.py:371
  335.4 6.1 %collective-permute-start.60 = (f32[128,128]{1,0:T(8,128)S(1)}, f32[128,128]{1,0:T(8,128)S(1)}, u32[]{:S(2)}, u32[]{:S(2)}) collective-permute-start(f32[128,128]{1,0:T(8,128)S(1)} %add_subtract_fusion), channel_id=1, source_target_pairs={{0,6},{1,7},{2,4},{3,5},{4,2},{5,3},{6,0},{7,1},{8,14},{9,15},{10,... | collective-permute-start | bytes 196616 | tf_op jit(solution)/shard_map/ppermute | solution.py:371
  337.4 5.7 %collective-permute-start.61 = (f32[2,128,128]{2,1,0:T(8,128)S(1)}, f32[2,128,128]{2,1,0:T(8,128)S(1)}, u32[]{:S(2)}, u32[]{:S(2)}) collective-permute-start(f32[2,128,128]{2,1,0:T(8,128)S(1)} %pad_maximum_fusion.7), channel_id=1, source_target_pairs={{0,8},{8,0},{16,24},{24,16},{1,9},{9,1},{17,25},{25,17},{2,10},{10... | collective-permute-start | bytes 393224 | tf_op jit(solution)/shard_map/ppermute | solution.py:385
  339.2 5.5 %collective-permute-start.62 = (f32[2,128,128]{2,1,0:T(8,128)S(1)}, f32[2,128,128]{2,1,0:T(8,128)S(1)}, u32[]{:S(2)}, u32[]{:S(2)}) collective-permute-start(f32[2,128,128]{2,1,0:T(8,128)S(1)} %pad_maximum_fusion.7), channel_id=1, source_target_pairs={{0,16},{8,24},{16,0},{24,8},{1,17},{9,25},{17,1},{25,9},{2,18},{10... | collective-permute-start | bytes 393224 | tf_op jit(solution)/shard_map/ppermute | solution.py:385
  341.0 5.9 %collective-permute-start.63 = (f32[2,128,128]{2,1,0:T(8,128)S(1)}, f32[2,128,128]{2,1,0:T(8,128)S(1)}, u32[]{:S(2)}, u32[]{:S(2)}) collective-permute-start(f32[2,128,128]{2,1,0:T(8,128)S(1)} %pad_maximum_fusion.7), channel_id=1, source_target_pairs={{0,24},{8,16},{16,8},{24,0},{1,25},{9,17},{17,9},{25,1},{2,26},{10... | collective-permute-start | bytes 393224 | tf_op jit(solution)/shard_map/ppermute | solution.py:385
  349.6 4.6 %collective-permute-start.65 = (f32[128,128]{1,0:T(8,128)S(1)}, f32[128,128]{1,0:T(8,128)S(1)}, u32[]{:S(2)}, u32[]{:S(2)}) collective-permute-start(f32[128,128]{1,0:T(8,128)S(1)} %get-tuple-element.208), channel_id=1, source_target_pairs={{0,8},{8,0},{16,24},{24,16},{1,9},{9,1},{17,25},{25,17},{2,10},{10... | collective-permute-start | bytes 196616 | tf_op jit(solution)/shard_map/ppermute | solution.py:381
  349.7 5.0 %collective-permute-start.66 = (f32[128,128]{1,0:T(8,128)S(1)}, f32[128,128]{1,0:T(8,128)S(1)}, u32[]{:S(2)}, u32[]{:S(2)}) collective-permute-start(f32[128,128]{1,0:T(8,128)S(1)} %get-tuple-element.210), channel_id=1, source_target_pairs={{0,16},{8,24},{16,0},{24,8},{1,17},{9,25},{17,1},{25,9},{2,18},{10... | collective-permute-start | bytes 196616 | tf_op jit(solution)/shard_map/ppermute | solution.py:381
  350.2 5.2 %collective-permute-start.67 = (f32[128,128]{1,0:T(8,128)S(1)}, f32[128,128]{1,0:T(8,128)S(1)}, u32[]{:S(2)}, u32[]{:S(2)}) collective-permute-start(f32[128,128]{1,0:T(8,128)S(1)} %get-tuple-element.209), channel_id=1, source_target_pairs={{0,24},{8,16},{16,8},{24,0},{1,25},{9,17},{17,9},{25,1},{2,26},{10... | collective-permute-start | bytes 196616 | tf_op jit(solution)/shard_map/ppermute | solution.py:381
  355.4 4.6 %collective-permute-start.68 = (f32[1,128,128]{2,1,0:T(8,128)S(1)}, f32[1,128,128]{2,1,0:T(8,128)S(1)}, u32[]{:S(2)}, u32[]{:S(2)}) collective-permute-start(f32[1,128,128]{2,1,0:T(8,128)S(1)} %add_bitcast_fusion), channel_id=1, source_target_pairs={{0,8},{8,0},{16,24},{24,16},{1,9},{9,1},{17,25},{25,17},{2,10},{10... | collective-permute-start | bytes 196616 | tf_op jit(solution)/shard_map/ppermute | solution.py:385
  357.4 4.6 %collective-permute-start.69 = (f32[1,128,128]{2,1,0:T(8,128)S(1)}, f32[1,128,128]{2,1,0:T(8,128)S(1)}, u32[]{:S(2)}, u32[]{:S(2)}) collective-permute-start(f32[1,128,128]{2,1,0:T(8,128)S(1)} %add_bitcast_fusion), channel_id=1, source_target_pairs={{0,16},{8,24},{16,0},{24,8},{1,17},{9,25},{17,1},{25,9},{2,18},{10... | collective-permute-start | bytes 196616 | tf_op jit(solution)/shard_map/ppermute | solution.py:385
  359.0 5.2 %collective-permute-start.70 = (f32[1,128,128]{2,1,0:T(8,128)S(1)}, f32[1,128,128]{2,1,0:T(8,128)S(1)}, u32[]{:S(2)}, u32[]{:S(2)}) collective-permute-start(f32[1,128,128]{2,1,0:T(8,128)S(1)} %add_bitcast_fusion), channel_id=1, source_target_pairs={{0,24},{8,16},{16,8},{24,0},{1,25},{9,17},{17,9},{25,1},{2,26},{10... | collective-permute-start | bytes 196616 | tf_op jit(solution)/shard_map/ppermute | solution.py:385
  (29 other events, 239.9 us)

commit v7 on v6

--- a/solution.py
+++ b/solution.py
@@ -387,6 +387,12 @@
 
     def enter(tail):
         return lax.ppermute(tail, "lag", [(i, i + 1) for i in range(groups - 1)])
+
+    def field_part(step):
+        return call(
+            part_kernel, group.astype(jnp.int32).reshape(1), (1,), (excitation,),
+            [pl.BlockSpec((1, part, width), lambda i, w: (step, w[0], 0))], 1, (part, width), (0, 8 * part * width),
+        )[0]
 
     def multiply(matrix, mine):
         vector = jnp.concatenate([mine, other_core(mine)], axis=0)
@@ -430,10 +436,12 @@
     far = other_core(near)
     first, tail = add_first(first, near, far, chips - 1)
 
-    right_side = own_part(excitation[0]) - sum_parts(first)
-    right_side, waiting, tail, near, far, one, two = tie((right_side, waiting, tail, near, far, one, two))
+    entered.append(enter(waiting))
+    field = field_part(0)
+    right_side = field - sum_parts(first)
+    right_side, tail, near, far, one, two = tie((right_side, tail, near, far, one, two))
     mine = gather_near(right_side)
-    entered += [enter(waiting), enter(tail)]
+    entered.append(enter(tail))
     one, two = add_rest(one, two, near, far, chips - 1)
     mine, one, two, sent = tie((mine, one, two, sent))
     density = sum_parts(multiply(head_columns, mine))
@@ -450,10 +458,7 @@
     right_side, two, old, both = tie((right_side, two, mine, both))
     mine = gather_near(right_side)
     nears = [old] + [lax.ppermute(old, "lag", [(j, 0)]) for j in range(1, groups)]
-    field = call(
-        part_kernel, group.astype(jnp.int32).reshape(1), (1,), (excitation,),
-        [pl.BlockSpec((1, part, width), lambda i, w: (STEPS - 1, w[0], 0))], 1, (part, width), (0, 8 * part * width),
-    )[0]
+    field = field_part(2)
     mine, two, field = tie((mine, two, field))
     carried = multiply(head_columns, mine)
     density = sum_parts(carried)

time: 366 us -> 370 us (1.011)
    ppermute x18, waiting for transfers between devices: 91 us -> 99.2 us  [sum_parts(): result = result + lax.ppermute(sent, 'lag', pairs(groups, mask))]
    ppermute x15, starting transfers between devices: 20.1 us -> 25.8 us  [gather_near(): lax.ppermute(value, 'row', pairs(devices, 2 * k))]
    ppermute x15, waiting for transfers between devices: 26.2 us -> 20.6 us  [gather_near(): lax.ppermute(value, 'row', pairs(devices, 2 * k))]
    pallas_call x5 -> x6, Pallas kernels: 25.6 us -> 27 us  [call(): pl.pallas_call(kernel, out_shape=[jax.ShapeDtypeStruct(shape, F32)] * cou...]
  transfers between devices with their start and end apart: 71 -> 71, of which waited for: 40 -> 41; matrix products, arithmetic and copies ran while one was open for 3% -> 2% of each run, Pallas kernels for 17% -> 18%
where the time goes in v7:
time: 370 us; the launch traced here: 369 us
  waiting for transfers between devices  167 us (45%)
  starting transfers between devices  102 us (28%)
  Pallas kernels  78 us (21%)
  matrix products  8.12 us (2%)
  other arithmetic  6.64 us (2%)
  local copies, waits for them, and re-layouts  6.03 us (2%)
    ppermute x18, waiting for transfers between devices, sum_parts(): result = result + lax.ppermute(sent, 'lag', pairs(groups, mask))  99.2 us
    pallas_call x6, Pallas kernels, call(): pl.pallas_call(kernel, out_shape=[jax.ShapeDtypeStruct(shape, F32)] * cou...  27 us
    pallas_call x2, Pallas kernels, add_chip(): pl.pallas_call(chip_kernel, out_shape=[jax.ShapeDtypeStruct(square, F32)]...  26.7 us
    ppermute x15, starting transfers between devices, gather_near(): lax.ppermute(value, 'row', pairs(devices, 2 * k))  25.8 us
    ppermute x6, waiting for transfers between devices, along(): lax.ppermute(value, 'row', [(2 * i + c, 2 * (i + step) + c) for i in sour...  22.7 us
    ppermute x18, starting transfers between devices, sum_parts(): result = result + lax.ppermute(sent, 'lag', pairs(groups, mask))  21.4 us
    ppermute x15, waiting for transfers between devices, gather_near(): lax.ppermute(value, 'row', pairs(devices, 2 * k))  20.6 us
    ppermute x4, starting transfers between devices, enter(): return lax.ppermute(tail, 'lag', [(i, i + 1) for i in range(groups - 1)])  14.6 us
  transfers between devices with their start and end apart: 71, of which 41 were waited for; matrix products, arithmetic and copies ran while one was open for 2% of the time, Pallas kernels for 18%

profile of v7, /device:TPU:0, one launch (start us, length us, event | category | flops | bytes accessed | tf_op | source)
XLA Modules:
  0.0 369.1 jit_solution(1312962275408653397)
XLA Ops:
  0.0 5.0 %collective-permute-start = (f32[4,512,128]{2,1,0:T(8,128)}, f32[4,512,128]{2,1,0:T(8,128)S(1)}, u32[]{:S(2)}, u32[]{:S(2)}) collective-permute-start(f32[4,512,128]{2,1,0:T(8,128)} %refs_0_.2), channel_id=1, source_target_pairs={{0,2},{1,3},{2,4},{3,5},{4,6},{5,7},{8,10},{9,11},{10,12},{11,13},... | collective-permute-start | bytes 3145736 | tf_op jit(solution)/shard_map/ppermute | solution.py:228
  7.5 4.2 %collective-permute-start.2 = (f32[2,512,128]{2,1,0:T(8,128)S(1)}, f32[2,512,128]{2,1,0:T(8,128)}, u32[]{:S(2)}, u32[]{:S(2)}) collective-permute-start(f32[2,512,128]{2,1,0:T(8,128)S(1)} %slice_select_fusion), channel_id=1, source_target_pairs={{0,8},{8,16},{16,24},{1,9},{9,17},{17,25},{2,10},{10,18},{18,26},{... | collective-permute-start | bytes 1572872 | tf_op jit(solution)/shard_map/ppermute | solution.py:389
  12.5 5.8 %columns.2 = f32[512,1024]{1,0:T(8,128)} custom-call(s32[2,5,4]{2,1,0:T(8,128)} %concatenate.43.where, f32[1,512,4096]{2,1,0:T(8,128)} %bitcast.33, f32[1,512,4096]{2,1,0:T(8,128)} %bitcast.34, f32[1,512,4096]{2,1,0:T(8,128)} %bitcast.35, f32[1,512,4096]{2,1,0:T(8,128)} %bitcast.36), custom_call_target="tpu_custom_call" | custom-call | bytes 16777216 | tf_op jit(solution)/shard_map/columns/pallas_call | solution.py:340
  18.3 4.4 %collective-permute-done.2.refs_0_.refs_4_ = f32[2,512,128]{2,1,0:T(8,128)} collective-permute-done((f32[2,512,128]{2,1,0:T(8,128)S(1)}, f32[2,512,128]{2,1,0:T(8,128)}, u32[]{:S(2)}, u32[]{:S(2)}) %collective-permute-start.2) | collective-permute-done | bytes 524320 | tf_op jit(solution)/shard_map/ppermute | solution.py:389
  22.7 5.0 %collective-permute-done = f32[4,512,128]{2,1,0:T(8,128)S(1)} collective-permute-done((f32[4,512,128]{2,1,0:T(8,128)}, f32[4,512,128]{2,1,0:T(8,128)S(1)}, u32[]{:S(2)}, u32[]{:S(2)}) %collective-permute-start) | collective-permute-done | bytes 1048608 | tf_op jit(solution)/shard_map/ppermute | solution.py:228
  27.7 4.1 %collective-permute-done.1 = f32[4,512,128]{2,1,0:T(8,128)S(1)} collective-permute-done((f32[4,512,128]{2,1,0:T(8,128)}, f32[4,512,128]{2,1,0:T(8,128)S(1)}, u32[]{:S(2)}, u32[]{:S(2)}) %collective-permute-start.1) | collective-permute-done | bytes 1048608 | tf_op jit(solution)/shard_map/ppermute | solution.py:228
  34.0 7.1 %columns.3 = (f32[512,1024]{1,0:T(8,128)}, f32[512,1024]{1,0:T(8,128)}, f32[512,1024]{1,0:T(8,128)}, f32[512,512]{1,0:T(8,128)}, f32[512,512]{1,0:T(8,128)}) custom-call(s32[2,5,4]{2,1,0:T(8,128)} %concatenate.43.where, f32[4,512,4096]{2,1,0:T(8,128)} %weights.13, f32[4,512,4096]{2,1,0:T(8,128)} %weights.13, f32[4,512,4096]{2,1,0:T(8,128)} %weights.13, ...), custom_call_target="tpu_custom_call" | custom-call | bytes 16777216 | tf_op jit(solution)/shard_map/columns/pallas_call | solution.py:340
  41.1 4.4 %collective-permute-start.9 = (f32[512,512]{1,0:T(8,128)}, f32[512,512]{1,0:T(8,128)}, u32[]{:S(2)}, u32[]{:S(2)}) collective-permute-start(f32[512,512]{1,0:T(8,128)} %get-tuple-element.111), channel_id=1, source_target_pairs={{0,16},{1,17},{2,18},{3,19},{4,20},{5,21},{6,22},{7,23}} | collective-permute-start | bytes 3145736 | tf_op jit(solution)/shard_map/ppermute | solution.py:406
  46.1 16.6 %chip.2 = (f32[512,128]{1,0:T(8,128)}, f32[512,128]{1,0:T(8,128)}, f32[512,128]{1,0:T(8,128)}, f32[2,512,128]{2,1,0:T(8,128)}) custom-call(s32[10]{0:T(128)} %stack.97.where, f32[4,512,4096]{2,1,0:T(8,128)} %weights.13, f32[4,512,128]{2,1,0:T(8,128)} %refs_0_.2, f32[4,512,128]{2,1,0:T(8,128)} %collective-permute-done.3.refs_1_, f32[4,512,128]{2,1,0:T(8,128)} %copy-done.7, ...), custom_call_target="tpu_custom_call" | custom-call | flops 9663676416 | bytes 16777216 | tf_op jit(solution)/shard_map/chip/pallas_call | solution.py:269
  62.8 1.7 select_select_fusion.1.refs_0_
  64.5 3.3 collective-permute-done.9
  67.9 1.6 collective-permute-start.7
  71.4 10.1 %chip.3 = (f32[512,128]{1,0:T(8,128)}, f32[512,128]{1,0:T(8,128)}, f32[512,128]{1,0:T(8,128)}, f32[2,512,128]{2,1,0:T(8,128)}) custom-call(s32[10]{0:T(128)} %stack.97.where, f32[4,512,4096]{2,1,0:T(8,128)} %weights.13, f32[4,512,128]{2,1,0:T(8,128)} %copy-done.6, ...), custom_call_target="tpu_custom_call", output_to_operand_aliasing={{0}: (4, {}), {1}: (5, {}), {2}: (6, {})} | custom-call | flops 4831838208 | bytes 8388608 | tf_op jit(solution)/shard_map/chip/pallas_call | solution.py:269
  82.3 3.6 shard_map.47
  85.9 13.7 %collective-permute-done.8 = f32[4,512,128]{2,1,0:T(8,128)} collective-permute-done((f32[4,512,128]{2,1,0:T(8,128)}, f32[4,512,128]{2,1,0:T(8,128)}, u32[]{:S(2)}, u32[]{:S(2)}) %collective-permute-start.8) | collective-permute-done | bytes 1048608 | tf_op jit(solution)/shard_map/ppermute | solution.py:228
  101.1 2.8 collective-permute-start.19
  103.9 5.1 %collective-permute-start.20 = (f32[512,1024]{1,0:T(8,128)}, f32[512,1024]{1,0:T(8,128)}, u32[]{:S(2)}, u32[]{:S(2)}) collective-permute-start(f32[512,1024]{1,0:T(8,128)} %get-tuple-element.139), channel_id=1, source_target_pairs={{0,16},{1,17},{2,18},{3,19},{4,20},{5,21},{6,22},{7,23}} | collective-permute-start | bytes 6291464 | tf_op jit(solution)/shard_map/ppermute | solution.py:407
  109.0 1.7 collective-permute-start.22
  110.7 2.3 collective-permute-start.21
  114.0 7.5 %first.1 = (f32[512,128]{1,0:T(8,128)}, f32[2,512,128]{2,1,0:T(8,128)}) custom-call(s32[10]{0:T(128)} %stack.97.where, f32[4,512,4096]{2,1,0:T(8,128)} %weights.13, f32[4,512,128]{2,1,0:T(8,128)} %copy-done.1, f32[4,512,128]{2,1,0:T(8,128)} %copy-done.3, f32[512,128]{1,0:T(8,128)} %get-tuple-element.126.total), custom_call_target="tpu_custom_call", output_to_operand_aliasing={{0}: (4, {})} | custom-call | flops 1610612736 | bytes 8388608 | tf_op jit(solution)/shard_map/first/pallas_call | solution.py:289
  122.5 49.8 %collective-permute-done.13 = f32[128,128]{1,0:T(8,128)S(1)} collective-permute-done((f32[128,128]{1,0:T(8,128)S(1)}, f32[128,128]{1,0:T(8,128)S(1)}, u32[]{:S(2)}, u32[]{:S(2)}) %collective-permute-start.13) | collective-permute-done | bytes 65568 | tf_op jit(solution)/shard_map/ppermute | solution.py:381
  172.3 4.3 %collective-permute-done.14 = f32[128,128]{1,0:T(8,128)S(1)} collective-permute-done((f32[128,128]{1,0:T(8,128)S(1)}, f32[128,128]{1,0:T(8,128)S(1)}, u32[]{:S(2)}, u32[]{:S(2)}) %collective-permute-start.14) | collective-permute-done | bytes 65568 | tf_op jit(solution)/shard_map/ppermute | solution.py:381
  176.6 1.9 collective-permute-start.15
  180.0 1.8 collective-permute-done.15
  182.7 4.3 %collective-permute-done.16 = f32[128,128]{1,0:T(8,128)S(1)} collective-permute-done((f32[128,128]{1,0:T(8,128)S(1)}, f32[128,128]{1,0:T(8,128)S(1)}, u32[]{:S(2)}, u32[]{:S(2)}) %collective-permute-start.16) | collective-permute-done | bytes 65568 | tf_op jit(solution)/shard_map/ppermute | solution.py:371
  187.3 6.0 %collective-permute-done.17 = f32[128,128]{1,0:T(8,128)S(1)} collective-permute-done((f32[128,128]{1,0:T(8,128)S(1)}, f32[128,128]{1,0:T(8,128)S(1)}, u32[]{:S(2)}, u32[]{:S(2)}) %collective-permute-start.17) | collective-permute-done | bytes 65568 | tf_op jit(solution)/shard_map/ppermute | solution.py:371
  194.1 7.6 %shard_map.48 = (f32[512,128]{1,0:T(8,128)}, f32[512,128]{1,0:T(8,128)}) custom-call(s32[10]{0:T(128)} %stack.97.where, f32[4,512,4096]{2,1,0:T(8,128)} %weights.13, f32[4,512,128]{2,1,0:T(8,128)} %copy-done.1, f32[4,512,128]{2,1,0:T(8,128)} %copy-done.1, f32[4,512,128]{2,1,0:T(8,128)} %copy-done.3, ...), custom_call_target="tpu_custom_call", output_to_operand_aliasing={{0}: (6, {}), {1}: (7, {})} | custom-call | flops 3221225472 | bytes 8388608 | tf_op jit(solution)/shard_map/pallas_call | solution.py:193
  201.9 4.4 %collective-permute-start.27 = (f32[2,512,128]{2,1,0:T(8,128)}, f32[2,512,128]{2,1,0:T(8,128)S(1)}, u32[]{:S(2)}, u32[]{:S(2)}) collective-permute-start(f32[2,512,128]{2,1,0:T(8,128)} %get-tuple-element.141), channel_id=1, source_target_pairs={{0,8},{8,16},{16,24},{1,9},{9,17},{17,25},{2,10},{10,18},{18,26},{... | collective-permute-start | bytes 1572872 | tf_op jit(solution)/shard_map/ppermute | solution.py:389
  206.3 2.7 collective-permute-start.28
  209.0 3.3 collective-permute-start.29
  213.5 29.5 %collective-permute-done.24 = f32[128,128]{1,0:T(8,128)S(1)} collective-permute-done((f32[128,128]{1,0:T(8,128)S(1)}, f32[128,128]{1,0:T(8,128)S(1)}, u32[]{:S(2)}, u32[]{:S(2)}) %collective-permute-start.24) | collective-permute-done | bytes 65568 | tf_op jit(solution)/shard_map/ppermute | solution.py:381
  244.1 3.9 %pick.1 = f32[512,1024]{1,0:T(8,128)} custom-call(s32[1]{0:T(128)} %bitcast.10.which, f32[512,1024]{1,0:T(8,128)} %get-tuple-element.145.refs_0_, f32[512,1024]{1,0:T(8,128)} %collective-permute-done.19.refs_1_, f32[512,1024]{1,0:T(8,128)} %collective-permute-done.20.refs_2_, f32[512,512]{1,0:T(8,128)} %collective-permute-done.21.refs_3_, ...), custom_call_target="tpu_custom_call" | custom-call | bytes 8388608 | tf_op jit(solution)/shard_map/pick/pallas_call | solution.py:356
  248.9 3.7 collective-permute-start.31
  253.3 4.3 %collective-permute-start.32 = (f32[128,128]{1,0:T(8,128)S(1)}, f32[128,128]{1,0:T(8,128)S(1)}, u32[]{:S(2)}, u32[]{:S(2)}) collective-permute-start(f32[128,128]{1,0:T(8,128)S(1)} %add_add_fusion.1), channel_id=1, source_target_pairs={{0,6},{1,7},{2,4},{3,5},{4,2},{5,3},{6,0},{7,1},{8,14},{9,15},{10,... | collective-permute-start | bytes 196616 | tf_op jit(solution)/shard_map/ppermute | solution.py:371
  257.6 2.2 collective-permute-done.32
  261.6 4.3 %shard_map.49 = (f32[512,128]{1,0:T(8,128)}, f32[512,128]{1,0:T(8,128)}) custom-call(s32[10]{0:T(128)} %stack.97.where, f32[4,512,4096]{2,1,0:T(8,128)} %weights.13, f32[2,512,128]{2,1,0:T(8,128)} %copy-done.11, f32[2,512,128]{2,1,0:T(8,128)} %copy-done.12, ...), custom_call_target="tpu_custom_call", output_to_operand_aliasing={{0}: (8, {}), {1}: (9, {})} | custom-call | flops 2415919104 | bytes 6291456 | tf_op jit(solution)/shard_map/pallas_call | solution.py:193
  266.0 1.5 collective-permute-done.36
  267.5 2.6 fusion.4
  270.2 5.3 %collective-permute-start.37 = (f32[128,128]{1,0:T(8,128)S(1)}, f32[128,128]{1,0:T(8,128)S(1)}, u32[]{:S(2)}, u32[]{:S(2)}) collective-permute-start(f32[128,128]{1,0:T(8,128)S(1)} %get-tuple-element.213), channel_id=1, source_target_pairs={{0,8},{8,0},{16,24},{24,16},{1,9},{9,1},{17,25},{25,17},{2,10},{10... | collective-permute-start | bytes 196616 | tf_op jit(solution)/shard_map/ppermute | solution.py:381
  277.9 2.6 collective-permute-done.38
  285.4 4.4 %collective-permute-start.41 = (f32[128,128]{1,0:T(8,128)S(1)}, f32[128,128]{1,0:T(8,128)S(1)}, u32[]{:S(2)}, u32[]{:S(2)}) collective-permute-start(f32[128,128]{1,0:T(8,128)S(1)} %bitcast_subtract_fusion), channel_id=1, source_target_pairs={{0,4},{1,5},{2,6},{3,7},{4,0},{5,1},{6,2},{7,3},{8,12},{9,13},{10,... | collective-permute-start | bytes 196616 | tf_op jit(solution)/shard_map/ppermute | solution.py:371
  290.2 3.3 collective-permute-start.42
  300.4 2.7 collective-permute-start.45
  303.2 2.8 collective-permute-done.45
  306.1 2.1 collective-permute-done.46
  308.3 3.9 %collective-permute-start.48 = (f32[128,128]{1,0:T(8,128)S(1)}, f32[128,128]{1,0:T(8,128)S(1)}, u32[]{:S(2)}, u32[]{:S(2)}) collective-permute-start(f32[128,128]{1,0:T(8,128)S(1)} %add_add_fusion), channel_id=1, source_target_pairs={{0,4},{1,5},{2,6},{3,7},{4,0},{5,1},{6,2},{7,3},{8,12},{9,13},{10,... | collective-permute-start | bytes 196616 | tf_op jit(solution)/shard_map/ppermute | solution.py:371
  312.7 3.1 collective-permute-done.48
  315.9 2.4 collective-permute-done.49
  318.3 8.5 %shard_map.51 = f32[512,128]{1,0:T(8,128)} custom-call(s32[10]{0:T(128)} %stack.97.where, f32[4,512,4096]{2,1,0:T(8,128)} %weights.13, f32[512,128]{1,0:T(8,128)} %copy-done.5, f32[512,128]{1,0:T(8,128)} %copy-done.14, f32[512,128]{1,0:T(8,128)} %copy-done.15, f32[512,128]{1,0:T(8,128)} %copy-done.16, ...), custom_call_target="tpu_custom_call", output_to_operand_aliasing={{}: (15, {})} | custom-call | flops 1610612736 | bytes 8388608 | tf_op jit(solution)/shard_map/pallas_call | solution.py:193
  326.9 1.5 collective-permute-done.54
  328.4 2.6 fusion.12
  331.7 2.9 collective-permute-start.57
  338.4 3.0 collective-permute-start.60
  341.4 1.8 collective-permute-start.61
  343.2 1.7 collective-permute-start.62
  345.0 2.1 collective-permute-done.61
  347.1 1.5 collective-permute-done.62
  348.6 2.1 collective-permute-done.63
  351.0 1.5 collective-permute-done.64
  354.2 2.9 collective-permute-start.67
  359.4 2.0 collective-permute-start.68
  361.4 1.5 collective-permute-start.69
  364.0 2.0 collective-permute-done.69
  366.0 2.1 collective-permute-done.70
  (170 shorter events, 47.6 us)
Async XLA Ops:
  0.0 27.7 %collective-permute-start = (f32[4,512,128]{2,1,0:T(8,128)}, f32[4,512,128]{2,1,0:T(8,128)S(1)}, u32[]{:S(2)}, u32[]{:S(2)}) collective-permute-start(f32[4,512,128]{2,1,0:T(8,128)} %refs_0_.2), channel_id=1, source_target_pairs={{0,2},{1,3},{2,4},{3,5},{4,6},{5,7},{8,10},{9,11},{10,12},{11,13},... | collective-permute-start | bytes 3145736 | tf_op jit(solution)/shard_map/ppermute | solution.py:228
  5.0 26.7 %collective-permute-start.1 = (f32[4,512,128]{2,1,0:T(8,128)}, f32[4,512,128]{2,1,0:T(8,128)S(1)}, u32[]{:S(2)}, u32[]{:S(2)}) collective-permute-start(f32[4,512,128]{2,1,0:T(8,128)} %refs_0_.2), channel_id=1, source_target_pairs={{2,0},{3,1},{4,2},{5,3},{6,4},{7,5},{10,8},{11,9},{12,10},{13,11},... | collective-permute-start | bytes 3145736 | tf_op jit(solution)/shard_map/ppermute | solution.py:228
  6.3 25.4 %collective-permute-start.3 = (f32[4,512,128]{2,1,0:T(8,128)}, f32[4,512,128]{2,1,0:T(8,128)}, u32[]{:S(2)}, u32[]{:S(2)}) collective-permute-start(f32[4,512,128]{2,1,0:T(8,128)} %refs_0_.2), channel_id=1, source_target_pairs={{0,1},{1,0},{2,3},{3,2},{4,5},{5,4},{6,7},{7,6},{8,9},{9,8},{10,11... | collective-permute-start | bytes 3145736 | tf_op jit(solution)/shard_map/ppermute | solution.py:225
  7.5 15.2 %collective-permute-start.2 = (f32[2,512,128]{2,1,0:T(8,128)S(1)}, f32[2,512,128]{2,1,0:T(8,128)}, u32[]{:S(2)}, u32[]{:S(2)}) collective-permute-start(f32[2,512,128]{2,1,0:T(8,128)S(1)} %slice_select_fusion), channel_id=1, source_target_pairs={{0,8},{8,16},{16,24},{1,9},{9,17},{17,25},{2,10},{10,18},{18,26},{... | collective-permute-start | bytes 1572872 | tf_op jit(solution)/shard_map/ppermute | solution.py:389
  31.9 14.2 %collective-permute-start.6 = (f32[4,512,128]{2,1,0:T(8,128)S(1)}, f32[4,512,128]{2,1,0:T(8,128)}, u32[]{:S(2)}, u32[]{:S(2)}) collective-permute-start(f32[4,512,128]{2,1,0:T(8,128)S(1)} %broadcast_select_fusion.refs_2_), channel_id=1, source_target_pairs={{0,1},{1,0},{2,3},{3,2},{4,5},{5,4},{6,7},{7,6},{8,9},{9,8},{10,11... | collective-permute-start | bytes 3145736 | tf_op jit(solution)/shard_map/ppermute | solution.py:225
  32.0 30.8 %collective-permute-start.4 = (f32[4,512,128]{2,1,0:T(8,128)}, f32[4,512,128]{2,1,0:T(8,128)S(1)}, u32[]{:S(2)}, u32[]{:S(2)}) collective-permute-start(f32[4,512,128]{2,1,0:T(8,128)} %copy-done.17), channel_id=1, source_target_pairs={{2,4},{3,5},{4,6},{5,7},{10,12},{11,13},{12,14},{13,15},{18,20},{1... | collective-permute-start | bytes 3145736 | tf_op jit(solution)/shard_map/ppermute | solution.py:228
  32.7 30.1 %collective-permute-start.5 = (f32[4,512,128]{2,1,0:T(8,128)S(1)}, f32[4,512,128]{2,1,0:T(8,128)}, u32[]{:S(2)}, u32[]{:S(2)}) collective-permute-start(f32[4,512,128]{2,1,0:T(8,128)S(1)} %collective-permute-done.1), channel_id=1, source_target_pairs={{2,0},{3,1},{4,2},{5,3},{10,8},{11,9},{12,10},{13,11},{18,16},{19,... | collective-permute-start | bytes 3145736 | tf_op jit(solution)/shard_map/ppermute | solution.py:228
  41.1 26.8 %collective-permute-start.9 = (f32[512,512]{1,0:T(8,128)}, f32[512,512]{1,0:T(8,128)}, u32[]{:S(2)}, u32[]{:S(2)}) collective-permute-start(f32[512,512]{1,0:T(8,128)} %get-tuple-element.111), channel_id=1, source_target_pairs={{0,16},{1,17},{2,18},{3,19},{4,20},{5,21},{6,22},{7,23}} | collective-permute-start | bytes 3145736 | tf_op jit(solution)/shard_map/ppermute | solution.py:406
  67.9 18.0 %collective-permute-start.7 = (f32[4,512,128]{2,1,0:T(8,128)S(1)}, f32[4,512,128]{2,1,0:T(8,128)}, u32[]{:S(2)}, u32[]{:S(2)}) collective-permute-start(f32[4,512,128]{2,1,0:T(8,128)S(1)} %collective-permute-done.4), channel_id=1, source_target_pairs={{4,6},{5,7},{12,14},{13,15},{20,22},{21,23},{28,30},{29,31}} | collective-permute-start | bytes 3145736 | tf_op jit(solution)/shard_map/ppermute | solution.py:228
  69.5 30.1 %collective-permute-start.8 = (f32[4,512,128]{2,1,0:T(8,128)}, f32[4,512,128]{2,1,0:T(8,128)}, u32[]{:S(2)}, u32[]{:S(2)}) collective-permute-start(f32[4,512,128]{2,1,0:T(8,128)} %collective-permute-done.5), channel_id=1, source_target_pairs={{2,0},{3,1},{10,8},{11,9},{18,16},{19,17},{26,24},{27,25}} | collective-permute-start | bytes 3145736 | tf_op jit(solution)/shard_map/ppermute | solution.py:228
  70.8 10.7 %collective-permute-start.11 = (f32[2,512,128]{2,1,0:T(8,128)}, f32[2,512,128]{2,1,0:T(8,128)S(1)}, u32[]{:S(2)}, u32[]{:S(2)}) collective-permute-start(f32[2,512,128]{2,1,0:T(8,128)} %collective-permute-done.2.refs_0_.refs_4_), channel_id=1, source_target_pairs={{0,1},{1,0},{2,3},{3,2},{4,5},{5,4},{6,7},{7,6},{8,9},{9,8},{10,11... | collective-permute-start | bytes 1572872 | tf_op jit(solution)/shard_map/ppermute | solution.py:225
  101.1 11.9 %collective-permute-start.12 = (f32[4,512,128]{2,1,0:T(8,128)S(1)}, f32[4,512,128]{2,1,0:T(8,128)S(1)}, u32[]{:S(2)}, u32[]{:S(2)}) collective-permute-start(f32[4,512,128]{2,1,0:T(8,128)S(1)} %select_select_fusion.near.near_before), channel_id=1, source_target_pairs={{0,1},{1,0},{2,3},{3,2},{4,5},{5,4},{6,7},{7,6},{8,9},{9,8},{10,11... | collective-permute-start | bytes 3145736 | tf_op jit(solution)/shard_map/ppermute | solution.py:225
  101.1 100.6 %collective-permute-start.19 = (f32[512,1024]{1,0:T(8,128)}, f32[512,1024]{1,0:T(8,128)}, u32[]{:S(2)}, u32[]{:S(2)}) collective-permute-start(f32[512,1024]{1,0:T(8,128)} %get-tuple-element.138), channel_id=1, source_target_pairs={{0,8},{1,9},{2,10},{3,11},{4,12},{5,13},{6,14},{7,15}} | collective-permute-start | bytes 6291464 | tf_op jit(solution)/shard_map/ppermute | solution.py:407
  103.9 97.9 %collective-permute-start.20 = (f32[512,1024]{1,0:T(8,128)}, f32[512,1024]{1,0:T(8,128)}, u32[]{:S(2)}, u32[]{:S(2)}) collective-permute-start(f32[512,1024]{1,0:T(8,128)} %get-tuple-element.139), channel_id=1, source_target_pairs={{0,16},{1,17},{2,18},{3,19},{4,20},{5,21},{6,22},{7,23}} | collective-permute-start | bytes 6291464 | tf_op jit(solution)/shard_map/ppermute | solution.py:407
  109.0 92.8 %collective-permute-start.22 = (f32[512,512]{1,0:T(8,128)}, f32[512,512]{1,0:T(8,128)}, u32[]{:S(2)}, u32[]{:S(2)}) collective-permute-start(f32[512,512]{1,0:T(8,128)} %collective-permute-done.9), channel_id=1, source_target_pairs={{16,24},{17,25},{18,26},{19,27},{20,28},{21,29},{22,30},{23,31}} | collective-permute-start | bytes 3145736 | tf_op jit(solution)/shard_map/ppermute | solution.py:416
  110.7 91.1 %collective-permute-start.21 = (f32[512,512]{1,0:T(8,128)}, f32[512,512]{1,0:T(8,128)}, u32[]{:S(2)}, u32[]{:S(2)}) collective-permute-start(f32[512,512]{1,0:T(8,128)} %get-tuple-element.142), channel_id=1, source_target_pairs={{0,24},{1,25},{2,26},{3,27},{4,28},{5,29},{6,30},{7,31}} | collective-permute-start | bytes 3145736 | tf_op jit(solution)/shard_map/ppermute | solution.py:427
  122.4 49.9 %collective-permute-start.13 = (f32[128,128]{1,0:T(8,128)S(1)}, f32[128,128]{1,0:T(8,128)S(1)}, u32[]{:S(2)}, u32[]{:S(2)}) collective-permute-start(f32[128,128]{1,0:T(8,128)S(1)} %get-tuple-element.219), channel_id=1, source_target_pairs={{0,8},{8,0},{16,24},{24,16},{1,9},{9,1},{17,25},{25,17},{2,10},{10... | collective-permute-start | bytes 196616 | tf_op jit(solution)/shard_map/ppermute | solution.py:381
  176.6 5.2 %collective-permute-start.15 = (f32[128,128]{1,0:T(8,128)S(1)}, f32[128,128]{1,0:T(8,128)S(1)}, u32[]{:S(2)}, u32[]{:S(2)}) collective-permute-start(f32[128,128]{1,0:T(8,128)S(1)} %get-tuple-element.220), channel_id=1, source_target_pairs={{0,24},{8,16},{16,8},{24,0},{1,25},{9,17},{17,9},{25,1},{2,26},{10... | collective-permute-start | bytes 196616 | tf_op jit(solution)/shard_map/ppermute | solution.py:381
  182.7 4.3 %collective-permute-start.16 = (f32[128,128]{1,0:T(8,128)S(1)}, f32[128,128]{1,0:T(8,128)S(1)}, u32[]{:S(2)}, u32[]{:S(2)}) collective-permute-start(f32[128,128]{1,0:T(8,128)S(1)} %add_subtract_fusion.1), channel_id=1, source_target_pairs={{0,2},{1,3},{2,0},{3,1},{4,6},{5,7},{6,4},{7,5},{8,10},{9,11},{10,... | collective-permute-start | bytes 196616 | tf_op jit(solution)/shard_map/ppermute | solution.py:371
  187.0 6.4 %collective-permute-start.17 = (f32[128,128]{1,0:T(8,128)S(1)}, f32[128,128]{1,0:T(8,128)S(1)}, u32[]{:S(2)}, u32[]{:S(2)}) collective-permute-start(f32[128,128]{1,0:T(8,128)S(1)} %add_subtract_fusion.1), channel_id=1, source_target_pairs={{0,4},{1,5},{2,6},{3,7},{4,0},{5,1},{6,2},{7,3},{8,12},{9,13},{10,... | collective-permute-start | bytes 196616 | tf_op jit(solution)/shard_map/ppermute | solution.py:371
  193.4 8.4 %collective-permute-start.18 = (f32[128,128]{1,0:T(8,128)S(1)}, f32[128,128]{1,0:T(8,128)S(1)}, u32[]{:S(2)}, u32[]{:S(2)}) collective-permute-start(f32[128,128]{1,0:T(8,128)S(1)} %add_subtract_fusion.1), channel_id=1, source_target_pairs={{0,6},{1,7},{2,4},{3,5},{4,2},{5,3},{6,0},{7,1},{8,14},{9,15},{10,... | collective-permute-start | bytes 196616 | tf_op jit(solution)/shard_map/ppermute | solution.py:371
  201.8 10.5 %collective-permute-start.23 = (f32[512,128]{1,0:T(8,128)S(1)}, f32[512,128]{1,0:T(8,128)S(1)}, u32[]{:S(2)}, u32[]{:S(2)}) collective-permute-start(f32[512,128]{1,0:T(8,128)S(1)} %pad_maximum_fusion.2), channel_id=1, source_target_pairs={{0,1},{1,0},{2,3},{3,2},{4,5},{5,4},{6,7},{7,6},{8,9},{9,8},{10,11... | collective-permute-start | bytes 786440 | tf_op jit(solution)/shard_map/ppermute | solution.py:225
  201.9 46.3 %collective-permute-start.27 = (f32[2,512,128]{2,1,0:T(8,128)}, f32[2,512,128]{2,1,0:T(8,128)S(1)}, u32[]{:S(2)}, u32[]{:S(2)}) collective-permute-start(f32[2,512,128]{2,1,0:T(8,128)} %get-tuple-element.141), channel_id=1, source_target_pairs={{0,8},{8,16},{16,24},{1,9},{9,17},{17,25},{2,10},{10,18},{18,26},{... | collective-permute-start | bytes 1572872 | tf_op jit(solution)/shard_map/ppermute | solution.py:389
  206.3 41.9 %collective-permute-start.28 = (f32[2,512,128]{2,1,0:T(8,128)}, f32[2,512,128]{2,1,0:T(8,128)}, u32[]{:S(2)}, u32[]{:S(2)}) collective-permute-start(f32[2,512,128]{2,1,0:T(8,128)} %get-tuple-element.150), channel_id=1, source_target_pairs={{0,8},{8,16},{16,24},{1,9},{9,17},{17,25},{2,10},{10,18},{18,26},{... | collective-permute-start | bytes 1572872 | tf_op jit(solution)/shard_map/ppermute | solution.py:389
  209.0 39.2 %collective-permute-start.29 = (f32[2,512,128]{2,1,0:T(8,128)}, f32[2,512,128]{2,1,0:T(8,128)}, u32[]{:S(2)}, u32[]{:S(2)}) collective-permute-start(f32[2,512,128]{2,1,0:T(8,128)} %get-tuple-element.151), channel_id=1, source_target_pairs={{0,8},{8,16},{16,24},{1,9},{9,17},{17,25},{2,10},{10,18},{18,26},{... | collective-permute-start | bytes 1572872 | tf_op jit(solution)/shard_map/ppermute | solution.py:389
  213.4 29.6 %collective-permute-start.24 = (f32[128,128]{1,0:T(8,128)S(1)}, f32[128,128]{1,0:T(8,128)S(1)}, u32[]{:S(2)}, u32[]{:S(2)}) collective-permute-start(f32[128,128]{1,0:T(8,128)S(1)} %get-tuple-element.216), channel_id=1, source_target_pairs={{0,8},{8,0},{16,24},{24,16},{1,9},{9,1},{17,25},{25,17},{2,10},{10... | collective-permute-start | bytes 196616 | tf_op jit(solution)/shard_map/ppermute | solution.py:381
  213.4 34.5 %collective-permute-start.25 = (f32[128,128]{1,0:T(8,128)S(1)}, f32[128,128]{1,0:T(8,128)S(1)}, u32[]{:S(2)}, u32[]{:S(2)}) collective-permute-start(f32[128,128]{1,0:T(8,128)S(1)} %get-tuple-element.218), channel_id=1, source_target_pairs={{0,16},{8,24},{16,0},{24,8},{1,17},{9,25},{17,1},{25,9},{2,18},{10... | collective-permute-start | bytes 196616 | tf_op jit(solution)/shard_map/ppermute | solution.py:381
  243.0 5.2 %collective-permute-start.26 = (f32[128,128]{1,0:T(8,128)S(1)}, f32[128,128]{1,0:T(8,128)S(1)}, u32[]{:S(2)}, u32[]{:S(2)}) collective-permute-start(f32[128,128]{1,0:T(8,128)S(1)} %get-tuple-element.217), channel_id=1, source_target_pairs={{0,24},{8,16},{16,8},{24,0},{1,25},{9,17},{17,9},{25,1},{2,26},{10... | collective-permute-start | bytes 196616 | tf_op jit(solution)/shard_map/ppermute | solution.py:381
  248.2 11.7 %collective-permute-start.33 = (f32[2,512,128]{2,1,0:T(8,128)S(1)}, f32[2,512,128]{2,1,0:T(8,128)S(1)}, u32[]{:S(2)}, u32[]{:S(2)}) collective-permute-start(f32[2,512,128]{2,1,0:T(8,128)S(1)} %collective-permute-done.27.refs_0_.refs_6_), channel_id=1, source_target_pairs={{0,1},{1,0},{2,3},{3,2},{4,5},{5,4},{6,7},{7,6},{8,9},{9,8},{10,11... | collective-permute-start | bytes 1572872 | tf_op jit(solution)/shard_map/ppermute | solution.py:225
  248.3 12.5 %collective-permute-start.34 = (f32[2,512,128]{2,1,0:T(8,128)}, f32[2,512,128]{2,1,0:T(8,128)S(1)}, u32[]{:S(2)}, u32[]{:S(2)}) collective-permute-start(f32[2,512,128]{2,1,0:T(8,128)} %collective-permute-done.28.refs_2_.refs_8_), channel_id=1, source_target_pairs={{0,1},{1,0},{2,3},{3,2},{4,5},{5,4},{6,7},{7,6},{8,9},{9,8},{10,11... | collective-permute-start | bytes 1572872 | tf_op jit(solution)/shard_map/ppermute | solution.py:225
  248.8 12.8 %collective-permute-start.35 = (f32[2,512,128]{2,1,0:T(8,128)}, f32[2,512,128]{2,1,0:T(8,128)}, u32[]{:S(2)}, u32[]{:S(2)}) collective-permute-start(f32[2,512,128]{2,1,0:T(8,128)} %collective-permute-done.29.refs_4_.refs_10_), channel_id=1, source_target_pairs={{0,1},{1,0},{2,3},{3,2},{4,5},{5,4},{6,7},{7,6},{8,9},{9,8},{10,11... | collective-permute-start | bytes 1572872 | tf_op jit(solution)/shard_map/ppermute | solution.py:225
  248.9 4.4 %collective-permute-start.30 = (f32[128,128]{1,0:T(8,128)S(1)}, f32[128,128]{1,0:T(8,128)S(1)}, u32[]{:S(2)}, u32[]{:S(2)}) collective-permute-start(f32[128,128]{1,0:T(8,128)S(1)} %add_add_fusion.1), channel_id=1, source_target_pairs={{0,2},{1,3},{2,0},{3,1},{4,6},{5,7},{6,4},{7,5},{8,10},{9,11},{10,... | collective-permute-start | bytes 196616 | tf_op jit(solution)/shard_map/ppermute | solution.py:371
  248.9 8.8 %collective-permute-start.31 = (f32[128,128]{1,0:T(8,128)S(1)}, f32[128,128]{1,0:T(8,128)S(1)}, u32[]{:S(2)}, u32[]{:S(2)}) collective-permute-start(f32[128,128]{1,0:T(8,128)S(1)} %add_add_fusion.1), channel_id=1, source_target_pairs={{0,4},{1,5},{2,6},{3,7},{4,0},{5,1},{6,2},{7,3},{8,12},{9,13},{10,... | collective-permute-start | bytes 196616 | tf_op jit(solution)/shard_map/ppermute | solution.py:371
  253.3 6.6 %collective-permute-start.32 = (f32[128,128]{1,0:T(8,128)S(1)}, f32[128,128]{1,0:T(8,128)S(1)}, u32[]{:S(2)}, u32[]{:S(2)}) collective-permute-start(f32[128,128]{1,0:T(8,128)S(1)} %add_add_fusion.1), channel_id=1, source_target_pairs={{0,6},{1,7},{2,4},{3,5},{4,2},{5,3},{6,0},{7,1},{8,14},{9,15},{10,... | collective-permute-start | bytes 196616 | tf_op jit(solution)/shard_map/ppermute | solution.py:371
  270.2 7.7 %collective-permute-start.37 = (f32[128,128]{1,0:T(8,128)S(1)}, f32[128,128]{1,0:T(8,128)S(1)}, u32[]{:S(2)}, u32[]{:S(2)}) collective-permute-start(f32[128,128]{1,0:T(8,128)S(1)} %get-tuple-element.213), channel_id=1, source_target_pairs={{0,8},{8,0},{16,24},{24,16},{1,9},{9,1},{17,25},{25,17},{2,10},{10... | collective-permute-start | bytes 196616 | tf_op jit(solution)/shard_map/ppermute | solution.py:381
  275.5 5.0 %collective-permute-start.38 = (f32[128,128]{1,0:T(8,128)S(1)}, f32[128,128]{1,0:T(8,128)S(1)}, u32[]{:S(2)}, u32[]{:S(2)}) collective-permute-start(f32[128,128]{1,0:T(8,128)S(1)} %get-tuple-element.215), channel_id=1, source_target_pairs={{0,16},{8,24},{16,0},{24,8},{1,17},{9,25},{17,1},{25,9},{2,18},{10... | collective-permute-start | bytes 196616 | tf_op jit(solution)/shard_map/ppermute | solution.py:381
  276.0 5.2 %collective-permute-start.39 = (f32[128,128]{1,0:T(8,128)S(1)}, f32[128,128]{1,0:T(8,128)S(1)}, u32[]{:S(2)}, u32[]{:S(2)}) collective-permute-start(f32[128,128]{1,0:T(8,128)S(1)} %get-tuple-element.214), channel_id=1, source_target_pairs={{0,24},{8,16},{16,8},{24,0},{1,25},{9,17},{17,9},{25,1},{2,26},{10... | collective-permute-start | bytes 196616 | tf_op jit(solution)/shard_map/ppermute | solution.py:381
  281.2 15.1 %collective-permute-start.50 = (f32[512,128]{1,0:T(8,128)S(1)}, f32[512,128]{1,0:T(8,128)S(1)}, u32[]{:S(2)}, u32[]{:S(2)}) collective-permute-start(f32[512,128]{1,0:T(8,128)S(1)} %pad_maximum_fusion.3.refs_0_), channel_id=1, source_target_pairs={{8,0},{9,1},{10,2},{11,3},{12,4},{13,5},{14,6},{15,7}} | collective-permute-start | bytes 786440 | tf_op jit(solution)/shard_map/ppermute | solution.py:460
  282.5 14.6 %collective-permute-start.51 = (f32[512,128]{1,0:T(8,128)S(1)}, f32[512,128]{1,0:T(8,128)S(1)}, u32[]{:S(2)}, u32[]{:S(2)}) collective-permute-start(f32[512,128]{1,0:T(8,128)S(1)} %pad_maximum_fusion.3.refs_0_), channel_id=1, source_target_pairs={{16,0},{17,1},{18,2},{19,3},{20,4},{21,5},{22,6},{23,7}} | collective-permute-start | bytes 786440 | tf_op jit(solution)/shard_map/ppermute | solution.py:460
  283.8 13.3 %collective-permute-start.52 = (f32[512,128]{1,0:T(8,128)S(1)}, f32[512,128]{1,0:T(8,128)S(1)}, u32[]{:S(2)}, u32[]{:S(2)}) collective-permute-start(f32[512,128]{1,0:T(8,128)S(1)} %pad_maximum_fusion.3.refs_0_), channel_id=1, source_target_pairs={{24,0},{25,1},{26,2},{27,3},{28,4},{29,5},{30,6},{31,7}} | collective-permute-start | bytes 786440 | tf_op jit(solution)/shard_map/ppermute | solution.py:460
  285.3 4.9 %collective-permute-start.40 = (f32[128,128]{1,0:T(8,128)S(1)}, f32[128,128]{1,0:T(8,128)S(1)}, u32[]{:S(2)}, u32[]{:S(2)}) collective-permute-start(f32[128,128]{1,0:T(8,128)S(1)} %bitcast_subtract_fusion), channel_id=1, source_target_pairs={{0,2},{1,3},{2,0},{3,1},{4,6},{5,7},{6,4},{7,5},{8,10},{9,11},{10,... | collective-permute-start | bytes 196616 | tf_op jit(solution)/shard_map/ppermute | solution.py:371
  285.4 9.6 %collective-permute-start.41 = (f32[128,128]{1,0:T(8,128)S(1)}, f32[128,128]{1,0:T(8,128)S(1)}, u32[]{:S(2)}, u32[]{:S(2)}) collective-permute-start(f32[128,128]{1,0:T(8,128)S(1)} %bitcast_subtract_fusion), channel_id=1, source_target_pairs={{0,4},{1,5},{2,6},{3,7},{4,0},{5,1},{6,2},{7,3},{8,12},{9,13},{10,... | collective-permute-start | bytes 196616 | tf_op jit(solution)/shard_map/ppermute | solution.py:371
  290.2 6.1 %collective-permute-start.42 = (f32[128,128]{1,0:T(8,128)S(1)}, f32[128,128]{1,0:T(8,128)S(1)}, u32[]{:S(2)}, u32[]{:S(2)}) collective-permute-start(f32[128,128]{1,0:T(8,128)S(1)} %bitcast_subtract_fusion), channel_id=1, source_target_pairs={{0,6},{1,7},{2,4},{3,5},{4,2},{5,3},{6,0},{7,1},{8,14},{9,15},{10,... | collective-permute-start | bytes 196616 | tf_op jit(solution)/shard_map/ppermute | solution.py:371
  297.2 21.1 %collective-permute-start.53 = (f32[4,512,128]{2,1,0:T(8,128)S(1)}, f32[4,512,128]{2,1,0:T(8,128)}, u32[]{:S(2)}, u32[]{:S(2)}) collective-permute-start(f32[4,512,128]{2,1,0:T(8,128)S(1)} %pad_maximum_fusion), channel_id=1, source_target_pairs={{0,1},{1,0},{2,3},{3,2},{4,5},{5,4},{6,7},{7,6},{8,9},{9,8},{10,11... | collective-permute-start | bytes 3145736 | tf_op jit(solution)/shard_map/ppermute | solution.py:225
  300.4 5.7 %collective-permute-start.45 = (f32[128,128]{1,0:T(8,128)S(1)}, f32[128,128]{1,0:T(8,128)S(1)}, u32[]{:S(2)}, u32[]{:S(2)}) collective-permute-start(f32[128,128]{1,0:T(8,128)S(1)} %get-tuple-element.212), channel_id=1, source_target_pairs={{0,16},{8,24},{16,0},{24,8},{1,17},{9,25},{17,1},{25,9},{2,18},{10... | collective-permute-start | bytes 196616 | tf_op jit(solution)/shard_map/ppermute | solution.py:381
  303.0 5.2 %collective-permute-start.46 = (f32[128,128]{1,0:T(8,128)S(1)}, f32[128,128]{1,0:T(8,128)S(1)}, u32[]{:S(2)}, u32[]{:S(2)}) collective-permute-start(f32[128,128]{1,0:T(8,128)S(1)} %get-tuple-element.211), channel_id=1, source_target_pairs={{0,24},{8,16},{16,8},{24,0},{1,25},{9,17},{17,9},{25,1},{2,26},{10... | collective-permute-start | bytes 196616 | tf_op jit(solution)/shard_map/ppermute | solution.py:381
  308.2 4.5 %collective-permute-start.47 = (f32[128,128]{1,0:T(8,128)S(1)}, f32[128,128]{1,0:T(8,128)S(1)}, u32[]{:S(2)}, u32[]{:S(2)}) collective-permute-start(f32[128,128]{1,0:T(8,128)S(1)} %add_add_fusion), channel_id=1, source_target_pairs={{0,2},{1,3},{2,0},{3,1},{4,6},{5,7},{6,4},{7,5},{8,10},{9,11},{10,... | collective-permute-start | bytes 196616 | tf_op jit(solution)/shard_map/ppermute | solution.py:371
  308.3 7.6 %collective-permute-start.48 = (f32[128,128]{1,0:T(8,128)S(1)}, f32[128,128]{1,0:T(8,128)S(1)}, u32[]{:S(2)}, u32[]{:S(2)}) collective-permute-start(f32[128,128]{1,0:T(8,128)S(1)} %add_add_fusion), channel_id=1, source_target_pairs={{0,4},{1,5},{2,6},{3,7},{4,0},{5,1},{6,2},{7,3},{8,12},{9,13},{10,... | collective-permute-start | bytes 196616 | tf_op jit(solution)/shard_map/ppermute | solution.py:371
  312.2 6.1 %collective-permute-start.49 = (f32[128,128]{1,0:T(8,128)S(1)}, f32[128,128]{1,0:T(8,128)S(1)}, u32[]{:S(2)}, u32[]{:S(2)}) collective-permute-start(f32[128,128]{1,0:T(8,128)S(1)} %add_add_fusion), channel_id=1, source_target_pairs={{0,6},{1,7},{2,4},{3,5},{4,2},{5,3},{6,0},{7,1},{8,14},{9,15},{10,... | collective-permute-start | bytes 196616 | tf_op jit(solution)/shard_map/ppermute | solution.py:371
  331.1 4.6 %collective-permute-start.55 = (f32[128,128]{1,0:T(8,128)S(1)}, f32[128,128]{1,0:T(8,128)S(1)}, u32[]{:S(2)}, u32[]{:S(2)}) collective-permute-start(f32[128,128]{1,0:T(8,128)S(1)} %get-tuple-element.207), channel_id=1, source_target_pairs={{0,8},{8,0},{16,24},{24,16},{1,9},{9,1},{17,25},{25,17},{2,10},{10... | collective-permute-start | bytes 196616 | tf_op jit(solution)/shard_map/ppermute | solution.py:381
  331.2 5.7 %collective-permute-start.56 = (f32[128,128]{1,0:T(8,128)S(1)}, f32[128,128]{1,0:T(8,128)S(1)}, u32[]{:S(2)}, u32[]{:S(2)}) collective-permute-start(f32[128,128]{1,0:T(8,128)S(1)} %get-tuple-element.209), channel_id=1, source_target_pairs={{0,16},{8,24},{16,0},{24,8},{1,17},{9,25},{17,1},{25,9},{2,18},{10... | collective-permute-start | bytes 196616 | tf_op jit(solution)/shard_map/ppermute | solution.py:381
  331.7 5.2 %collective-permute-start.57 = (f32[128,128]{1,0:T(8,128)S(1)}, f32[128,128]{1,0:T(8,128)S(1)}, u32[]{:S(2)}, u32[]{:S(2)}) collective-permute-start(f32[128,128]{1,0:T(8,128)S(1)} %get-tuple-element.208), channel_id=1, source_target_pairs={{0,24},{8,16},{16,8},{24,0},{1,25},{9,17},{17,9},{25,1},{2,26},{10... | collective-permute-start | bytes 196616 | tf_op jit(solution)/shard_map/ppermute | solution.py:381
  336.9 8.0 %collective-permute-start.58 = (f32[128,128]{1,0:T(8,128)S(1)}, f32[128,128]{1,0:T(8,128)S(1)}, u32[]{:S(2)}, u32[]{:S(2)}) collective-permute-start(f32[128,128]{1,0:T(8,128)S(1)} %add_subtract_fusion), channel_id=1, source_target_pairs={{0,2},{1,3},{2,0},{3,1},{4,6},{5,7},{6,4},{7,5},{8,10},{9,11},{10,... | collective-permute-start | bytes 196616 | tf_op jit(solution)/shard_map/ppermute | solution.py:371
  337.0 7.9 %collective-permute-start.59 = (f32[128,128]{1,0:T(8,128)S(1)}, f32[128,128]{1,0:T(8,128)S(1)}, u32[]{:S(2)}, u32[]{:S(2)}) collective-permute-start(f32[128,128]{1,0:T(8,128)S(1)} %add_subtract_fusion), channel_id=1, source_target_pairs={{0,4},{1,5},{2,6},{3,7},{4,0},{5,1},{6,2},{7,3},{8,12},{9,13},{10,... | collective-permute-start | bytes 196616 | tf_op jit(solution)/shard_map/ppermute | solution.py:371
  338.4 6.6 %collective-permute-start.60 = (f32[128,128]{1,0:T(8,128)S(1)}, f32[128,128]{1,0:T(8,128)S(1)}, u32[]{:S(2)}, u32[]{:S(2)}) collective-permute-start(f32[128,128]{1,0:T(8,128)S(1)} %add_subtract_fusion), channel_id=1, source_target_pairs={{0,6},{1,7},{2,4},{3,5},{4,2},{5,3},{6,0},{7,1},{8,14},{9,15},{10,... | collective-permute-start | bytes 196616 | tf_op jit(solution)/shard_map/ppermute | solution.py:371
  341.4 5.7 %collective-permute-start.61 = (f32[2,128,128]{2,1,0:T(8,128)S(1)}, f32[2,128,128]{2,1,0:T(8,128)S(1)}, u32[]{:S(2)}, u32[]{:S(2)}) collective-permute-start(f32[2,128,128]{2,1,0:T(8,128)S(1)} %pad_maximum_fusion.7), channel_id=1, source_target_pairs={{0,8},{8,0},{16,24},{24,16},{1,9},{9,1},{17,25},{25,17},{2,10},{10... | collective-permute-start | bytes 393224 | tf_op jit(solution)/shard_map/ppermute | solution.py:385
  343.2 5.5 %collective-permute-start.62 = (f32[2,128,128]{2,1,0:T(8,128)S(1)}, f32[2,128,128]{2,1,0:T(8,128)S(1)}, u32[]{:S(2)}, u32[]{:S(2)}) collective-permute-start(f32[2,128,128]{2,1,0:T(8,128)S(1)} %pad_maximum_fusion.7), channel_id=1, source_target_pairs={{0,16},{8,24},{16,0},{24,8},{1,17},{9,25},{17,1},{25,9},{2,18},{10... | collective-permute-start | bytes 393224 | tf_op jit(solution)/shard_map/ppermute | solution.py:385
  344.9 5.9 %collective-permute-start.63 = (f32[2,128,128]{2,1,0:T(8,128)S(1)}, f32[2,128,128]{2,1,0:T(8,128)S(1)}, u32[]{:S(2)}, u32[]{:S(2)}) collective-permute-start(f32[2,128,128]{2,1,0:T(8,128)S(1)} %pad_maximum_fusion.7), channel_id=1, source_target_pairs={{0,24},{8,16},{16,8},{24,0},{1,25},{9,17},{17,9},{25,1},{2,26},{10... | collective-permute-start | bytes 393224 | tf_op jit(solution)/shard_map/ppermute | solution.py:385
  353.5 4.6 %collective-permute-start.65 = (f32[128,128]{1,0:T(8,128)S(1)}, f32[128,128]{1,0:T(8,128)S(1)}, u32[]{:S(2)}, u32[]{:S(2)}) collective-permute-start(f32[128,128]{1,0:T(8,128)S(1)} %get-tuple-element.204), channel_id=1, source_target_pairs={{0,8},{8,0},{16,24},{24,16},{1,9},{9,1},{17,25},{25,17},{2,10},{10... | collective-permute-start | bytes 196616 | tf_op jit(solution)/shard_map/ppermute | solution.py:381
  353.7 5.0 %collective-permute-start.66 = (f32[128,128]{1,0:T(8,128)S(1)}, f32[128,128]{1,0:T(8,128)S(1)}, u32[]{:S(2)}, u32[]{:S(2)}) collective-permute-start(f32[128,128]{1,0:T(8,128)S(1)} %get-tuple-element.206), channel_id=1, source_target_pairs={{0,16},{8,24},{16,0},{24,8},{1,17},{9,25},{17,1},{25,9},{2,18},{10... | collective-permute-start | bytes 196616 | tf_op jit(solution)/shard_map/ppermute | solution.py:381
  354.2 5.2 %collective-permute-start.67 = (f32[128,128]{1,0:T(8,128)S(1)}, f32[128,128]{1,0:T(8,128)S(1)}, u32[]{:S(2)}, u32[]{:S(2)}) collective-permute-start(f32[128,128]{1,0:T(8,128)S(1)} %get-tuple-element.205), channel_id=1, source_target_pairs={{0,24},{8,16},{16,8},{24,0},{1,25},{9,17},{17,9},{25,1},{2,26},{10... | collective-permute-start | bytes 196616 | tf_op jit(solution)/shard_map/ppermute | solution.py:381
  359.4 4.6 %collective-permute-start.68 = (f32[1,128,128]{2,1,0:T(8,128)S(1)}, f32[1,128,128]{2,1,0:T(8,128)S(1)}, u32[]{:S(2)}, u32[]{:S(2)}) collective-permute-start(f32[1,128,128]{2,1,0:T(8,128)S(1)} %add_bitcast_fusion), channel_id=1, source_target_pairs={{0,8},{8,0},{16,24},{24,16},{1,9},{9,1},{17,25},{25,17},{2,10},{10... | collective-permute-start | bytes 196616 | tf_op jit(solution)/shard_map/ppermute | solution.py:385
  361.4 4.6 %collective-permute-start.69 = (f32[1,128,128]{2,1,0:T(8,128)S(1)}, f32[1,128,128]{2,1,0:T(8,128)S(1)}, u32[]{:S(2)}, u32[]{:S(2)}) collective-permute-start(f32[1,128,128]{2,1,0:T(8,128)S(1)} %add_bitcast_fusion), channel_id=1, source_target_pairs={{0,16},{8,24},{16,0},{24,8},{1,17},{9,25},{17,1},{25,9},{2,18},{10... | collective-permute-start | bytes 196616 | tf_op jit(solution)/shard_map/ppermute | solution.py:385
  362.9 5.2 %collective-permute-start.70 = (f32[1,128,128]{2,1,0:T(8,128)S(1)}, f32[1,128,128]{2,1,0:T(8,128)S(1)}, u32[]{:S(2)}, u32[]{:S(2)}) collective-permute-start(f32[1,128,128]{2,1,0:T(8,128)S(1)} %add_bitcast_fusion), channel_id=1, source_target_pairs={{0,24},{8,16},{16,8},{24,0},{1,25},{9,17},{17,9},{25,1},{2,26},{10... | collective-permute-start | bytes 196616 | tf_op jit(solution)/shard_map/ppermute | solution.py:385
  (27 other events, 196.8 us)

commit v8 on v7

--- a/solution.py
+++ b/solution.py
@@ -159,6 +159,9 @@
     sources, outs = refs[:fold], refs[fold:]
     part = sources[0].shape[2] // groups
     take = lambda j: jnp.concatenate([s[0, :, j * part : (j + 1) * part] for s in sources], axis=1)
+    if len(outs) == 1 and sources[0].shape[2] * fold == outs[0].shape[1]:
+        outs[0][...] = jnp.concatenate([s[0] for s in sources], axis=1)
+        return
     if len(outs) == 1:
         for j in range(groups):
 
@@ -336,6 +339,10 @@
         numbers = jnp.concatenate([numbers, jnp.full((2, 1, groups), group, jnp.int32)], axis=1)
         whole = pl.BlockSpec((rows, meet // 2), lambda s, w: (0, s))
         half = pl.BlockSpec((rows, meet // 2), lambda s, w: (0, 0))
+        if every or part % 128:
+            specs = [pl.BlockSpec((1, rows, rows), lambda s, w, i=i: (0, 0, w[s, i, 0])) for i in range(fold)]
+        else:
+            specs = [pl.BlockSpec((1, rows, part), lambda s, w, i=i: (0, 0, w[s, i, 0] * groups + w[s, fold, 0])) for i in range(fold)]
         shape = lambda size: jax.ShapeDtypeStruct((rows, size), F32)
         return pl.pallas_call(
             columns_kernel,
@@ -343,7 +350,7 @@
             grid_spec=pltpu.PrefetchScalarGridSpec(
                 num_scalar_prefetch=1,
                 grid=(2,),
-                in_specs=[pl.BlockSpec((1, rows, rows), lambda s, w, i=i: (0, 0, w[s, i, 0])) for i in range(fold)],
+                in_specs=specs,
                 out_specs=[whole] * (groups - 1) + [half] * 2 if every else [whole],
             ),
             cost_estimate=pl.CostEstimate(flops=0, bytes_accessed=8 * rows * order, transcendentals=0),
@@ -355,12 +362,12 @@
         spec = lambda j: pl.BlockSpec((rows, meet // 2), lambda s, w: (0, jnp.where(w[0] == j, s, 0)))
         return pl.pallas_call(
             pick_kernel,
-            out_shape=jax.ShapeDtypeStruct((rows, meet), F32),
+            out_shape=pltpu.VMEM((rows, meet), F32),
             grid_spec=pltpu.PrefetchScalarGridSpec(
                 num_scalar_prefetch=1,
                 grid=(2,),
                 in_specs=[spec(j) for j in range(groups - 1)] + [all_of((rows, meet // 2))] * 2,
-                out_specs=pl.BlockSpec((rows, meet // 2), lambda s, w: (0, s)),
+                out_specs=pl.BlockSpec((rows, meet // 2), lambda s, w: (0, s), memory_space=pltpu.VMEM),
             ),
             cost_estimate=pl.CostEstimate(flops=0, bytes_accessed=16 * rows * meet, transcendentals=0),
             compiler_params=pltpu.CompilerParams(dimension_semantics=("arbitrary",)),

time: 370 us -> 367 us (level)
  waiting for transfers between devices: 167 us -> 171 us
  transfers between devices with their start and end apart: 71 -> 71, of which waited for: 41 -> 40; matrix products, arithmetic and copies ran while one was open for 2% -> 2% of each run, Pallas kernels for 18% -> 17%
where the time goes in v8:
time: 367 us; the launch traced here: 366 us
  waiting for transfers between devices  171 us (47%)
  starting transfers between devices  102 us (28%)
  Pallas kernels  74.9 us (20%)
  other arithmetic  6.64 us (2%)
  local copies, waits for them, and re-layouts  6.05 us (2%)
  matrix products  4.93 us (1%)
    ppermute x18, waiting for transfers between devices, sum_parts(): result = result + lax.ppermute(sent, 'lag', pairs(groups, mask))  101 us
    pallas_call x6, Pallas kernels, call(): pl.pallas_call(kernel, out_shape=[jax.ShapeDtypeStruct(shape, F32)] * cou...  27.1 us
    pallas_call x2, Pallas kernels, add_chip(): pl.pallas_call(chip_kernel, out_shape=[jax.ShapeDtypeStruct(square, F32)]...  26.7 us
    ppermute x15, starting transfers between devices, gather_near(): lax.ppermute(value, 'row', pairs(devices, 2 * k))  25.3 us
    ppermute x6, waiting for transfers between devices, along(): lax.ppermute(value, 'row', [(2 * i + c, 2 * (i + step) + c) for i in sour...  22.7 us
    ppermute x18, starting transfers between devices, sum_parts(): result = result + lax.ppermute(sent, 'lag', pairs(groups, mask))  21.5 us
    ppermute x15, waiting for transfers between devices, gather_near(): lax.ppermute(value, 'row', pairs(devices, 2 * k))  20.4 us
    ppermute x4, starting transfers between devices, enter(): return lax.ppermute(tail, 'lag', [(i, i + 1) for i in range(groups - 1)])  14.6 us
  transfers between devices with their start and end apart: 71, of which 40 were waited for; matrix products, arithmetic and copies ran while one was open for 2% of the time, Pallas kernels for 17%

profile of v8, /device:TPU:0, one launch (start us, length us, event | category | flops | bytes accessed | tf_op | source)
XLA Modules:
  0.0 365.6 jit_solution(18109580009987525590)
XLA Ops:
  0.0 5.0 %collective-permute-start = (f32[4,512,128]{2,1,0:T(8,128)}, f32[4,512,128]{2,1,0:T(8,128)S(1)}, u32[]{:S(2)}, u32[]{:S(2)}) collective-permute-start(f32[4,512,128]{2,1,0:T(8,128)} %refs_0_.2), channel_id=1, source_target_pairs={{0,2},{1,3},{2,4},{3,5},{4,6},{5,7},{8,10},{9,11},{10,12},{11,13},... | collective-permute-start | bytes 3145736 | tf_op jit(solution)/shard_map/ppermute | solution.py:231
  7.5 4.2 %collective-permute-start.2 = (f32[2,512,128]{2,1,0:T(8,128)S(1)}, f32[2,512,128]{2,1,0:T(8,128)}, u32[]{:S(2)}, u32[]{:S(2)}) collective-permute-start(f32[2,512,128]{2,1,0:T(8,128)S(1)} %slice_select_fusion), channel_id=1, source_target_pairs={{0,8},{8,16},{16,24},{1,9},{9,17},{17,25},{2,10},{10,18},{18,26},{... | collective-permute-start | bytes 1572872 | tf_op jit(solution)/shard_map/ppermute | solution.py:396
  12.5 3.4 columns.2
  16.0 6.7 %collective-permute-done.2.refs_0_.refs_4_ = f32[2,512,128]{2,1,0:T(8,128)} collective-permute-done((f32[2,512,128]{2,1,0:T(8,128)S(1)}, f32[2,512,128]{2,1,0:T(8,128)}, u32[]{:S(2)}, u32[]{:S(2)}) %collective-permute-start.2) | collective-permute-done | bytes 524320 | tf_op jit(solution)/shard_map/ppermute | solution.py:396
  22.7 5.0 %collective-permute-done = f32[4,512,128]{2,1,0:T(8,128)S(1)} collective-permute-done((f32[4,512,128]{2,1,0:T(8,128)}, f32[4,512,128]{2,1,0:T(8,128)S(1)}, u32[]{:S(2)}, u32[]{:S(2)}) %collective-permute-start) | collective-permute-done | bytes 1048608 | tf_op jit(solution)/shard_map/ppermute | solution.py:231
  27.7 4.1 %collective-permute-done.1 = f32[4,512,128]{2,1,0:T(8,128)S(1)} collective-permute-done((f32[4,512,128]{2,1,0:T(8,128)}, f32[4,512,128]{2,1,0:T(8,128)S(1)}, u32[]{:S(2)}, u32[]{:S(2)}) %collective-permute-start.1) | collective-permute-done | bytes 1048608 | tf_op jit(solution)/shard_map/ppermute | solution.py:231
  34.0 7.1 %columns.3 = (f32[512,1024]{1,0:T(8,128)}, f32[512,1024]{1,0:T(8,128)}, f32[512,1024]{1,0:T(8,128)}, f32[512,512]{1,0:T(8,128)}, f32[512,512]{1,0:T(8,128)}) custom-call(s32[2,5,4]{2,1,0:T(8,128)} %concatenate.43.where, f32[4,512,4096]{2,1,0:T(8,128)} %weights.13, f32[4,512,4096]{2,1,0:T(8,128)} %weights.13, f32[4,512,4096]{2,1,0:T(8,128)} %weights.13, ...), custom_call_target="tpu_custom_call" | custom-call | bytes 16777216 | tf_op jit(solution)/shard_map/columns/pallas_call | solution.py:347
  41.1 4.5 %collective-permute-start.9 = (f32[512,512]{1,0:T(8,128)}, f32[512,512]{1,0:T(8,128)}, u32[]{:S(2)}, u32[]{:S(2)}) collective-permute-start(f32[512,512]{1,0:T(8,128)} %get-tuple-element.111), channel_id=1, source_target_pairs={{0,16},{1,17},{2,18},{3,19},{4,20},{5,21},{6,22},{7,23}} | collective-permute-start | bytes 3145736 | tf_op jit(solution)/shard_map/ppermute | solution.py:413
  46.2 16.6 %chip.2 = (f32[512,128]{1,0:T(8,128)}, f32[512,128]{1,0:T(8,128)}, f32[512,128]{1,0:T(8,128)}, f32[2,512,128]{2,1,0:T(8,128)}) custom-call(s32[10]{0:T(128)} %stack.97.where, f32[4,512,4096]{2,1,0:T(8,128)} %weights.13, f32[4,512,128]{2,1,0:T(8,128)} %refs_0_.2, f32[4,512,128]{2,1,0:T(8,128)} %collective-permute-done.3.refs_1_, f32[4,512,128]{2,1,0:T(8,128)} %copy-done.9, ...), custom_call_target="tpu_custom_call" | custom-call | flops 9663676416 | bytes 16777216 | tf_op jit(solution)/shard_map/chip/pallas_call | solution.py:272
  62.8 1.7 select_select_fusion.1.refs_0_
  64.6 3.3 collective-permute-done.9
  67.9 1.6 collective-permute-start.7
  71.4 10.1 %chip.3 = (f32[512,128]{1,0:T(8,128)}, f32[512,128]{1,0:T(8,128)}, f32[512,128]{1,0:T(8,128)}, f32[2,512,128]{2,1,0:T(8,128)}) custom-call(s32[10]{0:T(128)} %stack.97.where, f32[4,512,4096]{2,1,0:T(8,128)} %weights.13, f32[4,512,128]{2,1,0:T(8,128)} %copy-done.8, ...), custom_call_target="tpu_custom_call", output_to_operand_aliasing={{0}: (4, {}), {1}: (5, {}), {2}: (6, {})} | custom-call | flops 4831838208 | bytes 8388608 | tf_op jit(solution)/shard_map/chip/pallas_call | solution.py:272
  82.3 3.6 shard_map.47
  85.9 13.7 %collective-permute-done.8 = f32[4,512,128]{2,1,0:T(8,128)} collective-permute-done((f32[4,512,128]{2,1,0:T(8,128)}, f32[4,512,128]{2,1,0:T(8,128)}, u32[]{:S(2)}, u32[]{:S(2)}) %collective-permute-start.8) | collective-permute-done | bytes 1048608 | tf_op jit(solution)/shard_map/ppermute | solution.py:231
  101.1 2.6 collective-permute-start.19
  103.8 5.1 %collective-permute-start.20 = (f32[512,1024]{1,0:T(8,128)}, f32[512,1024]{1,0:T(8,128)}, u32[]{:S(2)}, u32[]{:S(2)}) collective-permute-start(f32[512,1024]{1,0:T(8,128)} %get-tuple-element.139), channel_id=1, source_target_pairs={{0,16},{1,17},{2,18},{3,19},{4,20},{5,21},{6,22},{7,23}} | collective-permute-start | bytes 6291464 | tf_op jit(solution)/shard_map/ppermute | solution.py:414
  108.9 1.6 collective-permute-start.22
  110.5 2.3 collective-permute-start.21
  113.8 7.5 %first.1 = (f32[512,128]{1,0:T(8,128)}, f32[2,512,128]{2,1,0:T(8,128)}) custom-call(s32[10]{0:T(128)} %stack.97.where, f32[4,512,4096]{2,1,0:T(8,128)} %weights.13, f32[4,512,128]{2,1,0:T(8,128)} %copy-done.3, f32[4,512,128]{2,1,0:T(8,128)} %copy-done.5, f32[512,128]{1,0:T(8,128)} %get-tuple-element.126.total), custom_call_target="tpu_custom_call", output_to_operand_aliasing={{0}: (4, {})} | custom-call | flops 1610612736 | bytes 8388608 | tf_op jit(solution)/shard_map/first/pallas_call | solution.py:292
  122.3 50.0 %collective-permute-done.13 = f32[128,128]{1,0:T(8,128)S(1)} collective-permute-done((f32[128,128]{1,0:T(8,128)S(1)}, f32[128,128]{1,0:T(8,128)S(1)}, u32[]{:S(2)}, u32[]{:S(2)}) %collective-permute-start.13) | collective-permute-done | bytes 65568 | tf_op jit(solution)/shard_map/ppermute | solution.py:388
  172.3 4.3 %collective-permute-done.14 = f32[128,128]{1,0:T(8,128)S(1)} collective-permute-done((f32[128,128]{1,0:T(8,128)S(1)}, f32[128,128]{1,0:T(8,128)S(1)}, u32[]{:S(2)}, u32[]{:S(2)}) %collective-permute-start.14) | collective-permute-done | bytes 65568 | tf_op jit(solution)/shard_map/ppermute | solution.py:388
  176.6 1.9 collective-permute-start.15
  180.0 1.8 collective-permute-done.15
  182.7 4.3 %collective-permute-done.16 = f32[128,128]{1,0:T(8,128)S(1)} collective-permute-done((f32[128,128]{1,0:T(8,128)S(1)}, f32[128,128]{1,0:T(8,128)S(1)}, u32[]{:S(2)}, u32[]{:S(2)}) %collective-permute-start.16) | collective-permute-done | bytes 65568 | tf_op jit(solution)/shard_map/ppermute | solution.py:378
  187.4 6.0 %collective-permute-done.17 = f32[128,128]{1,0:T(8,128)S(1)} collective-permute-done((f32[128,128]{1,0:T(8,128)S(1)}, f32[128,128]{1,0:T(8,128)S(1)}, u32[]{:S(2)}, u32[]{:S(2)}) %collective-permute-start.17) | collective-permute-done | bytes 65568 | tf_op jit(solution)/shard_map/ppermute | solution.py:378
  194.1 7.7 %shard_map.48 = (f32[512,128]{1,0:T(8,128)}, f32[512,128]{1,0:T(8,128)}) custom-call(s32[10]{0:T(128)} %stack.97.where, f32[4,512,4096]{2,1,0:T(8,128)} %weights.13, f32[4,512,128]{2,1,0:T(8,128)} %copy-done.3, f32[4,512,128]{2,1,0:T(8,128)} %copy-done.3, f32[4,512,128]{2,1,0:T(8,128)} %copy-done.5, ...), custom_call_target="tpu_custom_call", output_to_operand_aliasing={{0}: (6, {}), {1}: (7, {})} | custom-call | flops 3221225472 | bytes 8388608 | tf_op jit(solution)/shard_map/pallas_call | solution.py:196
  202.0 4.4 %collective-permute-start.27 = (f32[2,512,128]{2,1,0:T(8,128)}, f32[2,512,128]{2,1,0:T(8,128)S(1)}, u32[]{:S(2)}, u32[]{:S(2)}) collective-permute-start(f32[2,512,128]{2,1,0:T(8,128)} %get-tuple-element.141), channel_id=1, source_target_pairs={{0,8},{8,16},{16,24},{1,9},{9,17},{17,25},{2,10},{10,18},{18,26},{... | collective-permute-start | bytes 1572872 | tf_op jit(solution)/shard_map/ppermute | solution.py:396
  206.4 2.7 collective-permute-start.28
  209.1 3.3 collective-permute-start.29
  213.6 29.5 %collective-permute-done.24 = f32[128,128]{1,0:T(8,128)S(1)} collective-permute-done((f32[128,128]{1,0:T(8,128)S(1)}, f32[128,128]{1,0:T(8,128)S(1)}, u32[]{:S(2)}, u32[]{:S(2)}) %collective-permute-start.24) | collective-permute-done | bytes 65568 | tf_op jit(solution)/shard_map/ppermute | solution.py:388
  244.1 3.0 pick.1
  248.9 3.5 collective-permute-start.31
  253.4 4.2 %collective-permute-start.32 = (f32[128,128]{1,0:T(8,128)S(1)}, f32[128,128]{1,0:T(8,128)S(1)}, u32[]{:S(2)}, u32[]{:S(2)}) collective-permute-start(f32[128,128]{1,0:T(8,128)S(1)} %add_add_fusion.1), channel_id=1, source_target_pairs={{0,6},{1,7},{2,4},{3,5},{4,2},{5,3},{6,0},{7,1},{8,14},{9,15},{10,... | collective-permute-start | bytes 196616 | tf_op jit(solution)/shard_map/ppermute | solution.py:378
  257.6 2.2 collective-permute-done.32
  261.6 4.3 %shard_map.49 = (f32[512,128]{1,0:T(8,128)}, f32[512,128]{1,0:T(8,128)}) custom-call(s32[10]{0:T(128)} %stack.97.where, f32[4,512,4096]{2,1,0:T(8,128)} %weights.13, f32[2,512,128]{2,1,0:T(8,128)} %copy-done.13, f32[2,512,128]{2,1,0:T(8,128)} %copy-done.14, ...), custom_call_target="tpu_custom_call", output_to_operand_aliasing={{0}: (8, {}), {1}: (9, {})} | custom-call | flops 2415919104 | bytes 6291456 | tf_op jit(solution)/shard_map/pallas_call | solution.py:196
  266.0 1.5 collective-permute-done.36
  268.6 5.3 %collective-permute-start.37 = (f32[128,128]{1,0:T(8,128)S(1)}, f32[128,128]{1,0:T(8,128)S(1)}, u32[]{:S(2)}, u32[]{:S(2)}) collective-permute-start(f32[128,128]{1,0:T(8,128)S(1)} %get-tuple-element.213), channel_id=1, source_target_pairs={{0,8},{8,0},{16,24},{24,16},{1,9},{9,1},{17,25},{25,17},{2,10},{10... | collective-permute-start | bytes 196616 | tf_op jit(solution)/shard_map/ppermute | solution.py:388
  276.2 2.6 collective-permute-done.38
  282.3 1.5 collective-permute-start.52
  283.9 4.0 %collective-permute-start.41 = (f32[128,128]{1,0:T(8,128)S(1)}, f32[128,128]{1,0:T(8,128)S(1)}, u32[]{:S(2)}, u32[]{:S(2)}) collective-permute-start(f32[128,128]{1,0:T(8,128)S(1)} %bitcast_subtract_fusion), channel_id=1, source_target_pairs={{0,4},{1,5},{2,6},{3,7},{4,0},{5,1},{6,2},{7,3},{8,12},{9,13},{10,... | collective-permute-start | bytes 196616 | tf_op jit(solution)/shard_map/ppermute | solution.py:378
  288.1 3.4 collective-permute-start.42
  296.9 1.6 collective-permute-start.44
  298.5 2.7 collective-permute-start.45
  301.2 3.0 collective-permute-done.45
  304.2 2.2 collective-permute-done.46
  306.5 3.8 %collective-permute-start.48 = (f32[128,128]{1,0:T(8,128)S(1)}, f32[128,128]{1,0:T(8,128)S(1)}, u32[]{:S(2)}, u32[]{:S(2)}) collective-permute-start(f32[128,128]{1,0:T(8,128)S(1)} %add_add_fusion), channel_id=1, source_target_pairs={{0,4},{1,5},{2,6},{3,7},{4,0},{5,1},{6,2},{7,3},{8,12},{9,13},{10,... | collective-permute-start | bytes 196616 | tf_op jit(solution)/shard_map/ppermute | solution.py:378
  310.9 3.0 collective-permute-done.48
  314.0 2.4 collective-permute-done.49
  316.4 8.5 %shard_map.51 = f32[512,128]{1,0:T(8,128)} custom-call(s32[10]{0:T(128)} %stack.97.where, f32[4,512,4096]{2,1,0:T(8,128)} %weights.13, f32[512,128]{1,0:T(8,128)} %copy-done.7, f32[512,128]{1,0:T(8,128)} %copy-done.16, f32[512,128]{1,0:T(8,128)} %copy-done.17, f32[512,128]{1,0:T(8,128)} %copy-done.18, ...), custom_call_target="tpu_custom_call", output_to_operand_aliasing={{}: (15, {})} | custom-call | flops 1610612736 | bytes 8388608 | tf_op jit(solution)/shard_map/pallas_call | solution.py:196
  325.0 1.5 collective-permute-done.54
  328.2 2.9 collective-permute-start.57
  334.9 3.0 collective-permute-start.60
  337.9 1.8 collective-permute-start.61
  339.7 1.7 collective-permute-start.62
  341.5 2.2 collective-permute-done.61
  343.6 1.5 collective-permute-done.62
  345.2 2.1 collective-permute-done.63
  347.5 1.5 collective-permute-done.64
  350.7 2.9 collective-permute-start.67
  355.9 2.0 collective-permute-start.68
  357.9 1.5 collective-permute-start.69
  360.5 2.0 collective-permute-done.69
  362.5 2.0 collective-permute-done.70
  (174 shorter events, 47.6 us)
Async XLA Ops:
  0.0 27.7 %collective-permute-start = (f32[4,512,128]{2,1,0:T(8,128)}, f32[4,512,128]{2,1,0:T(8,128)S(1)}, u32[]{:S(2)}, u32[]{:S(2)}) collective-permute-start(f32[4,512,128]{2,1,0:T(8,128)} %refs_0_.2), channel_id=1, source_target_pairs={{0,2},{1,3},{2,4},{3,5},{4,6},{5,7},{8,10},{9,11},{10,12},{11,13},... | collective-permute-start | bytes 3145736 | tf_op jit(solution)/shard_map/ppermute | solution.py:231
  5.0 26.7 %collective-permute-start.1 = (f32[4,512,128]{2,1,0:T(8,128)}, f32[4,512,128]{2,1,0:T(8,128)S(1)}, u32[]{:S(2)}, u32[]{:S(2)}) collective-permute-start(f32[4,512,128]{2,1,0:T(8,128)} %refs_0_.2), channel_id=1, source_target_pairs={{2,0},{3,1},{4,2},{5,3},{6,4},{7,5},{10,8},{11,9},{12,10},{13,11},... | collective-permute-start | bytes 3145736 | tf_op jit(solution)/shard_map/ppermute | solution.py:231
  6.3 25.4 %collective-permute-start.3 = (f32[4,512,128]{2,1,0:T(8,128)}, f32[4,512,128]{2,1,0:T(8,128)}, u32[]{:S(2)}, u32[]{:S(2)}) collective-permute-start(f32[4,512,128]{2,1,0:T(8,128)} %refs_0_.2), channel_id=1, source_target_pairs={{0,1},{1,0},{2,3},{3,2},{4,5},{5,4},{6,7},{7,6},{8,9},{9,8},{10,11... | collective-permute-start | bytes 3145736 | tf_op jit(solution)/shard_map/ppermute | solution.py:228
  7.5 15.2 %collective-permute-start.2 = (f32[2,512,128]{2,1,0:T(8,128)S(1)}, f32[2,512,128]{2,1,0:T(8,128)}, u32[]{:S(2)}, u32[]{:S(2)}) collective-permute-start(f32[2,512,128]{2,1,0:T(8,128)S(1)} %slice_select_fusion), channel_id=1, source_target_pairs={{0,8},{8,16},{16,24},{1,9},{9,17},{17,25},{2,10},{10,18},{18,26},{... | collective-permute-start | bytes 1572872 | tf_op jit(solution)/shard_map/ppermute | solution.py:396
  31.9 14.3 %collective-permute-start.6 = (f32[4,512,128]{2,1,0:T(8,128)S(1)}, f32[4,512,128]{2,1,0:T(8,128)}, u32[]{:S(2)}, u32[]{:S(2)}) collective-permute-start(f32[4,512,128]{2,1,0:T(8,128)S(1)} %broadcast_select_fusion.refs_2_), channel_id=1, source_target_pairs={{0,1},{1,0},{2,3},{3,2},{4,5},{5,4},{6,7},{7,6},{8,9},{9,8},{10,11... | collective-permute-start | bytes 3145736 | tf_op jit(solution)/shard_map/ppermute | solution.py:228
  32.0 30.9 %collective-permute-start.4 = (f32[4,512,128]{2,1,0:T(8,128)}, f32[4,512,128]{2,1,0:T(8,128)S(1)}, u32[]{:S(2)}, u32[]{:S(2)}) collective-permute-start(f32[4,512,128]{2,1,0:T(8,128)} %copy-done.19), channel_id=1, source_target_pairs={{2,4},{3,5},{4,6},{5,7},{10,12},{11,13},{12,14},{13,15},{18,20},{1... | collective-permute-start | bytes 3145736 | tf_op jit(solution)/shard_map/ppermute | solution.py:231
  32.7 30.1 %collective-permute-start.5 = (f32[4,512,128]{2,1,0:T(8,128)S(1)}, f32[4,512,128]{2,1,0:T(8,128)}, u32[]{:S(2)}, u32[]{:S(2)}) collective-permute-start(f32[4,512,128]{2,1,0:T(8,128)S(1)} %collective-permute-done.1), channel_id=1, source_target_pairs={{2,0},{3,1},{4,2},{5,3},{10,8},{11,9},{12,10},{13,11},{18,16},{19,... | collective-permute-start | bytes 3145736 | tf_op jit(solution)/shard_map/ppermute | solution.py:231
  41.1 26.8 %collective-permute-start.9 = (f32[512,512]{1,0:T(8,128)}, f32[512,512]{1,0:T(8,128)}, u32[]{:S(2)}, u32[]{:S(2)}) collective-permute-start(f32[512,512]{1,0:T(8,128)} %get-tuple-element.111), channel_id=1, source_target_pairs={{0,16},{1,17},{2,18},{3,19},{4,20},{5,21},{6,22},{7,23}} | collective-permute-start | bytes 3145736 | tf_op jit(solution)/shard_map/ppermute | solution.py:413
  67.9 18.0 %collective-permute-start.7 = (f32[4,512,128]{2,1,0:T(8,128)S(1)}, f32[4,512,128]{2,1,0:T(8,128)}, u32[]{:S(2)}, u32[]{:S(2)}) collective-permute-start(f32[4,512,128]{2,1,0:T(8,128)S(1)} %collective-permute-done.4), channel_id=1, source_target_pairs={{4,6},{5,7},{12,14},{13,15},{20,22},{21,23},{28,30},{29,31}} | collective-permute-start | bytes 3145736 | tf_op jit(solution)/shard_map/ppermute | solution.py:231
  69.5 30.1 %collective-permute-start.8 = (f32[4,512,128]{2,1,0:T(8,128)}, f32[4,512,128]{2,1,0:T(8,128)}, u32[]{:S(2)}, u32[]{:S(2)}) collective-permute-start(f32[4,512,128]{2,1,0:T(8,128)} %collective-permute-done.5), channel_id=1, source_target_pairs={{2,0},{3,1},{10,8},{11,9},{18,16},{19,17},{26,24},{27,25}} | collective-permute-start | bytes 3145736 | tf_op jit(solution)/shard_map/ppermute | solution.py:231
  70.8 10.7 %collective-permute-start.11 = (f32[2,512,128]{2,1,0:T(8,128)}, f32[2,512,128]{2,1,0:T(8,128)S(1)}, u32[]{:S(2)}, u32[]{:S(2)}) collective-permute-start(f32[2,512,128]{2,1,0:T(8,128)} %collective-permute-done.2.refs_0_.refs_4_), channel_id=1, source_target_pairs={{0,1},{1,0},{2,3},{3,2},{4,5},{5,4},{6,7},{7,6},{8,9},{9,8},{10,11... | collective-permute-start | bytes 1572872 | tf_op jit(solution)/shard_map/ppermute | solution.py:228
  101.1 11.7 %collective-permute-start.12 = (f32[4,512,128]{2,1,0:T(8,128)S(1)}, f32[4,512,128]{2,1,0:T(8,128)S(1)}, u32[]{:S(2)}, u32[]{:S(2)}) collective-permute-start(f32[4,512,128]{2,1,0:T(8,128)S(1)} %select_select_fusion.near.near_before), channel_id=1, source_target_pairs={{0,1},{1,0},{2,3},{3,2},{4,5},{5,4},{6,7},{7,6},{8,9},{9,8},{10,11... | collective-permute-start | bytes 3145736 | tf_op jit(solution)/shard_map/ppermute | solution.py:228
  101.1 100.7 %collective-permute-start.19 = (f32[512,1024]{1,0:T(8,128)}, f32[512,1024]{1,0:T(8,128)}, u32[]{:S(2)}, u32[]{:S(2)}) collective-permute-start(f32[512,1024]{1,0:T(8,128)} %get-tuple-element.138), channel_id=1, source_target_pairs={{0,8},{1,9},{2,10},{3,11},{4,12},{5,13},{6,14},{7,15}} | collective-permute-start | bytes 6291464 | tf_op jit(solution)/shard_map/ppermute | solution.py:414
  103.8 98.1 %collective-permute-start.20 = (f32[512,1024]{1,0:T(8,128)}, f32[512,1024]{1,0:T(8,128)}, u32[]{:S(2)}, u32[]{:S(2)}) collective-permute-start(f32[512,1024]{1,0:T(8,128)} %get-tuple-element.139), channel_id=1, source_target_pairs={{0,16},{1,17},{2,18},{3,19},{4,20},{5,21},{6,22},{7,23}} | collective-permute-start | bytes 6291464 | tf_op jit(solution)/shard_map/ppermute | solution.py:414
  108.9 93.0 %collective-permute-start.22 = (f32[512,512]{1,0:T(8,128)}, f32[512,512]{1,0:T(8,128)}, u32[]{:S(2)}, u32[]{:S(2)}) collective-permute-start(f32[512,512]{1,0:T(8,128)} %collective-permute-done.9), channel_id=1, source_target_pairs={{16,24},{17,25},{18,26},{19,27},{20,28},{21,29},{22,30},{23,31}} | collective-permute-start | bytes 3145736 | tf_op jit(solution)/shard_map/ppermute | solution.py:423
  110.5 91.4 %collective-permute-start.21 = (f32[512,512]{1,0:T(8,128)}, f32[512,512]{1,0:T(8,128)}, u32[]{:S(2)}, u32[]{:S(2)}) collective-permute-start(f32[512,512]{1,0:T(8,128)} %get-tuple-element.142), channel_id=1, source_target_pairs={{0,24},{1,25},{2,26},{3,27},{4,28},{5,29},{6,30},{7,31}} | collective-permute-start | bytes 3145736 | tf_op jit(solution)/shard_map/ppermute | solution.py:434
  122.2 50.1 %collective-permute-start.13 = (f32[128,128]{1,0:T(8,128)S(1)}, f32[128,128]{1,0:T(8,128)S(1)}, u32[]{:S(2)}, u32[]{:S(2)}) collective-permute-start(f32[128,128]{1,0:T(8,128)S(1)} %get-tuple-element.219), channel_id=1, source_target_pairs={{0,8},{8,0},{16,24},{24,16},{1,9},{9,1},{17,25},{25,17},{2,10},{10... | collective-permute-start | bytes 196616 | tf_op jit(solution)/shard_map/ppermute | solution.py:388
  176.6 5.2 %collective-permute-start.15 = (f32[128,128]{1,0:T(8,128)S(1)}, f32[128,128]{1,0:T(8,128)S(1)}, u32[]{:S(2)}, u32[]{:S(2)}) collective-permute-start(f32[128,128]{1,0:T(8,128)S(1)} %get-tuple-element.220), channel_id=1, source_target_pairs={{0,24},{8,16},{16,8},{24,0},{1,25},{9,17},{17,9},{25,1},{2,26},{10... | collective-permute-start | bytes 196616 | tf_op jit(solution)/shard_map/ppermute | solution.py:388
  187.0 6.4 %collective-permute-start.17 = (f32[128,128]{1,0:T(8,128)S(1)}, f32[128,128]{1,0:T(8,128)S(1)}, u32[]{:S(2)}, u32[]{:S(2)}) collective-permute-start(f32[128,128]{1,0:T(8,128)S(1)} %add_subtract_fusion.1), channel_id=1, source_target_pairs={{0,4},{1,5},{2,6},{3,7},{4,0},{5,1},{6,2},{7,3},{8,12},{9,13},{10,... | collective-permute-start | bytes 196616 | tf_op jit(solution)/shard_map/ppermute | solution.py:378
  193.4 8.5 %collective-permute-start.18 = (f32[128,128]{1,0:T(8,128)S(1)}, f32[128,128]{1,0:T(8,128)S(1)}, u32[]{:S(2)}, u32[]{:S(2)}) collective-permute-start(f32[128,128]{1,0:T(8,128)S(1)} %add_subtract_fusion.1), channel_id=1, source_target_pairs={{0,6},{1,7},{2,4},{3,5},{4,2},{5,3},{6,0},{7,1},{8,14},{9,15},{10,... | collective-permute-start | bytes 196616 | tf_op jit(solution)/shard_map/ppermute | solution.py:378
  201.9 10.5 %collective-permute-start.23 = (f32[512,128]{1,0:T(8,128)S(1)}, f32[512,128]{1,0:T(8,128)S(1)}, u32[]{:S(2)}, u32[]{:S(2)}) collective-permute-start(f32[512,128]{1,0:T(8,128)S(1)} %pad_maximum_fusion.2), channel_id=1, source_target_pairs={{0,1},{1,0},{2,3},{3,2},{4,5},{5,4},{6,7},{7,6},{8,9},{9,8},{10,11... | collective-permute-start | bytes 786440 | tf_op jit(solution)/shard_map/ppermute | solution.py:228
  202.0 46.3 %collective-permute-start.27 = (f32[2,512,128]{2,1,0:T(8,128)}, f32[2,512,128]{2,1,0:T(8,128)S(1)}, u32[]{:S(2)}, u32[]{:S(2)}) collective-permute-start(f32[2,512,128]{2,1,0:T(8,128)} %get-tuple-element.141), channel_id=1, source_target_pairs={{0,8},{8,16},{16,24},{1,9},{9,17},{17,25},{2,10},{10,18},{18,26},{... | collective-permute-start | bytes 1572872 | tf_op jit(solution)/shard_map/ppermute | solution.py:396
  206.4 41.9 %collective-permute-start.28 = (f32[2,512,128]{2,1,0:T(8,128)}, f32[2,512,128]{2,1,0:T(8,128)}, u32[]{:S(2)}, u32[]{:S(2)}) collective-permute-start(f32[2,512,128]{2,1,0:T(8,128)} %get-tuple-element.150), channel_id=1, source_target_pairs={{0,8},{8,16},{16,24},{1,9},{9,17},{17,25},{2,10},{10,18},{18,26},{... | collective-permute-start | bytes 1572872 | tf_op jit(solution)/shard_map/ppermute | solution.py:396
  209.1 39.2 %collective-permute-start.29 = (f32[2,512,128]{2,1,0:T(8,128)}, f32[2,512,128]{2,1,0:T(8,128)}, u32[]{:S(2)}, u32[]{:S(2)}) collective-permute-start(f32[2,512,128]{2,1,0:T(8,128)} %get-tuple-element.151), channel_id=1, source_target_pairs={{0,8},{8,16},{16,24},{1,9},{9,17},{17,25},{2,10},{10,18},{18,26},{... | collective-permute-start | bytes 1572872 | tf_op jit(solution)/shard_map/ppermute | solution.py:396
  213.4 29.6 %collective-permute-start.24 = (f32[128,128]{1,0:T(8,128)S(1)}, f32[128,128]{1,0:T(8,128)S(1)}, u32[]{:S(2)}, u32[]{:S(2)}) collective-permute-start(f32[128,128]{1,0:T(8,128)S(1)} %get-tuple-element.216), channel_id=1, source_target_pairs={{0,8},{8,0},{16,24},{24,16},{1,9},{9,1},{17,25},{25,17},{2,10},{10... | collective-permute-start | bytes 196616 | tf_op jit(solution)/shard_map/ppermute | solution.py:388
  213.5 33.6 %collective-permute-start.25 = (f32[128,128]{1,0:T(8,128)S(1)}, f32[128,128]{1,0:T(8,128)S(1)}, u32[]{:S(2)}, u32[]{:S(2)}) collective-permute-start(f32[128,128]{1,0:T(8,128)S(1)} %get-tuple-element.218), channel_id=1, source_target_pairs={{0,16},{8,24},{16,0},{24,8},{1,17},{9,25},{17,1},{25,9},{2,18},{10... | collective-permute-start | bytes 196616 | tf_op jit(solution)/shard_map/ppermute | solution.py:388
  243.0 5.2 %collective-permute-start.26 = (f32[128,128]{1,0:T(8,128)S(1)}, f32[128,128]{1,0:T(8,128)S(1)}, u32[]{:S(2)}, u32[]{:S(2)}) collective-permute-start(f32[128,128]{1,0:T(8,128)S(1)} %get-tuple-element.217), channel_id=1, source_target_pairs={{0,24},{8,16},{16,8},{24,0},{1,25},{9,17},{17,9},{25,1},{2,26},{10... | collective-permute-start | bytes 196616 | tf_op jit(solution)/shard_map/ppermute | solution.py:388
  248.3 11.6 %collective-permute-start.33 = (f32[2,512,128]{2,1,0:T(8,128)S(1)}, f32[2,512,128]{2,1,0:T(8,128)S(1)}, u32[]{:S(2)}, u32[]{:S(2)}) collective-permute-start(f32[2,512,128]{2,1,0:T(8,128)S(1)} %collective-permute-done.27.refs_0_.refs_6_), channel_id=1, source_target_pairs={{0,1},{1,0},{2,3},{3,2},{4,5},{5,4},{6,7},{7,6},{8,9},{9,8},{10,11... | collective-permute-start | bytes 1572872 | tf_op jit(solution)/shard_map/ppermute | solution.py:228
  248.4 12.4 %collective-permute-start.34 = (f32[2,512,128]{2,1,0:T(8,128)}, f32[2,512,128]{2,1,0:T(8,128)S(1)}, u32[]{:S(2)}, u32[]{:S(2)}) collective-permute-start(f32[2,512,128]{2,1,0:T(8,128)} %collective-permute-done.28.refs_2_.refs_8_), channel_id=1, source_target_pairs={{0,1},{1,0},{2,3},{3,2},{4,5},{5,4},{6,7},{7,6},{8,9},{9,8},{10,11... | collective-permute-start | bytes 1572872 | tf_op jit(solution)/shard_map/ppermute | solution.py:228
  248.9 12.7 %collective-permute-start.35 = (f32[2,512,128]{2,1,0:T(8,128)}, f32[2,512,128]{2,1,0:T(8,128)}, u32[]{:S(2)}, u32[]{:S(2)}) collective-permute-start(f32[2,512,128]{2,1,0:T(8,128)} %collective-permute-done.29.refs_4_.refs_10_), channel_id=1, source_target_pairs={{0,1},{1,0},{2,3},{3,2},{4,5},{5,4},{6,7},{7,6},{8,9},{9,8},{10,11... | collective-permute-start | bytes 1572872 | tf_op jit(solution)/shard_map/ppermute | solution.py:228
  248.9 4.4 %collective-permute-start.30 = (f32[128,128]{1,0:T(8,128)S(1)}, f32[128,128]{1,0:T(8,128)S(1)}, u32[]{:S(2)}, u32[]{:S(2)}) collective-permute-start(f32[128,128]{1,0:T(8,128)S(1)} %add_add_fusion.1), channel_id=1, source_target_pairs={{0,2},{1,3},{2,0},{3,1},{4,6},{5,7},{6,4},{7,5},{8,10},{9,11},{10,... | collective-permute-start | bytes 196616 | tf_op jit(solution)/shard_map/ppermute | solution.py:378
  248.9 8.6 %collective-permute-start.31 = (f32[128,128]{1,0:T(8,128)S(1)}, f32[128,128]{1,0:T(8,128)S(1)}, u32[]{:S(2)}, u32[]{:S(2)}) collective-permute-start(f32[128,128]{1,0:T(8,128)S(1)} %add_add_fusion.1), channel_id=1, source_target_pairs={{0,4},{1,5},{2,6},{3,7},{4,0},{5,1},{6,2},{7,3},{8,12},{9,13},{10,... | collective-permute-start | bytes 196616 | tf_op jit(solution)/shard_map/ppermute | solution.py:378
  253.4 6.4 %collective-permute-start.32 = (f32[128,128]{1,0:T(8,128)S(1)}, f32[128,128]{1,0:T(8,128)S(1)}, u32[]{:S(2)}, u32[]{:S(2)}) collective-permute-start(f32[128,128]{1,0:T(8,128)S(1)} %add_add_fusion.1), channel_id=1, source_target_pairs={{0,6},{1,7},{2,4},{3,5},{4,2},{5,3},{6,0},{7,1},{8,14},{9,15},{10,... | collective-permute-start | bytes 196616 | tf_op jit(solution)/shard_map/ppermute | solution.py:378
  268.6 7.7 %collective-permute-start.37 = (f32[128,128]{1,0:T(8,128)S(1)}, f32[128,128]{1,0:T(8,128)S(1)}, u32[]{:S(2)}, u32[]{:S(2)}) collective-permute-start(f32[128,128]{1,0:T(8,128)S(1)} %get-tuple-element.213), channel_id=1, source_target_pairs={{0,8},{8,0},{16,24},{24,16},{1,9},{9,1},{17,25},{25,17},{2,10},{10... | collective-permute-start | bytes 196616 | tf_op jit(solution)/shard_map/ppermute | solution.py:388
  273.8 5.0 %collective-permute-start.38 = (f32[128,128]{1,0:T(8,128)S(1)}, f32[128,128]{1,0:T(8,128)S(1)}, u32[]{:S(2)}, u32[]{:S(2)}) collective-permute-start(f32[128,128]{1,0:T(8,128)S(1)} %get-tuple-element.215), channel_id=1, source_target_pairs={{0,16},{8,24},{16,0},{24,8},{1,17},{9,25},{17,1},{25,9},{2,18},{10... | collective-permute-start | bytes 196616 | tf_op jit(solution)/shard_map/ppermute | solution.py:388
  274.5 5.2 %collective-permute-start.39 = (f32[128,128]{1,0:T(8,128)S(1)}, f32[128,128]{1,0:T(8,128)S(1)}, u32[]{:S(2)}, u32[]{:S(2)}) collective-permute-start(f32[128,128]{1,0:T(8,128)S(1)} %get-tuple-element.214), channel_id=1, source_target_pairs={{0,24},{8,16},{16,8},{24,0},{1,25},{9,17},{17,9},{25,1},{2,26},{10... | collective-permute-start | bytes 196616 | tf_op jit(solution)/shard_map/ppermute | solution.py:388
  279.7 14.6 %collective-permute-start.50 = (f32[512,128]{1,0:T(8,128)S(1)}, f32[512,128]{1,0:T(8,128)S(1)}, u32[]{:S(2)}, u32[]{:S(2)}) collective-permute-start(f32[512,128]{1,0:T(8,128)S(1)} %pad_maximum_fusion.3.refs_0_), channel_id=1, source_target_pairs={{8,0},{9,1},{10,2},{11,3},{12,4},{13,5},{14,6},{15,7}} | collective-permute-start | bytes 786440 | tf_op jit(solution)/shard_map/ppermute | solution.py:467
  281.0 14.3 %collective-permute-start.51 = (f32[512,128]{1,0:T(8,128)S(1)}, f32[512,128]{1,0:T(8,128)S(1)}, u32[]{:S(2)}, u32[]{:S(2)}) collective-permute-start(f32[512,128]{1,0:T(8,128)S(1)} %pad_maximum_fusion.3.refs_0_), channel_id=1, source_target_pairs={{16,0},{17,1},{18,2},{19,3},{20,4},{21,5},{22,6},{23,7}} | collective-permute-start | bytes 786440 | tf_op jit(solution)/shard_map/ppermute | solution.py:467
  282.3 13.0 %collective-permute-start.52 = (f32[512,128]{1,0:T(8,128)S(1)}, f32[512,128]{1,0:T(8,128)S(1)}, u32[]{:S(2)}, u32[]{:S(2)}) collective-permute-start(f32[512,128]{1,0:T(8,128)S(1)} %pad_maximum_fusion.3.refs_0_), channel_id=1, source_target_pairs={{24,0},{25,1},{26,2},{27,3},{28,4},{29,5},{30,6},{31,7}} | collective-permute-start | bytes 786440 | tf_op jit(solution)/shard_map/ppermute | solution.py:467
  283.8 4.4 %collective-permute-start.40 = (f32[128,128]{1,0:T(8,128)S(1)}, f32[128,128]{1,0:T(8,128)S(1)}, u32[]{:S(2)}, u32[]{:S(2)}) collective-permute-start(f32[128,128]{1,0:T(8,128)S(1)} %bitcast_subtract_fusion), channel_id=1, source_target_pairs={{0,2},{1,3},{2,0},{3,1},{4,6},{5,7},{6,4},{7,5},{8,10},{9,11},{10,... | collective-permute-start | bytes 196616 | tf_op jit(solution)/shard_map/ppermute | solution.py:378
  283.9 9.2 %collective-permute-start.41 = (f32[128,128]{1,0:T(8,128)S(1)}, f32[128,128]{1,0:T(8,128)S(1)}, u32[]{:S(2)}, u32[]{:S(2)}) collective-permute-start(f32[128,128]{1,0:T(8,128)S(1)} %bitcast_subtract_fusion), channel_id=1, source_target_pairs={{0,4},{1,5},{2,6},{3,7},{4,0},{5,1},{6,2},{7,3},{8,12},{9,13},{10,... | collective-permute-start | bytes 196616 | tf_op jit(solution)/shard_map/ppermute | solution.py:378
  288.1 6.1 %collective-permute-start.42 = (f32[128,128]{1,0:T(8,128)S(1)}, f32[128,128]{1,0:T(8,128)S(1)}, u32[]{:S(2)}, u32[]{:S(2)}) collective-permute-start(f32[128,128]{1,0:T(8,128)S(1)} %bitcast_subtract_fusion), channel_id=1, source_target_pairs={{0,6},{1,7},{2,4},{3,5},{4,2},{5,3},{6,0},{7,1},{8,14},{9,15},{10,... | collective-permute-start | bytes 196616 | tf_op jit(solution)/shard_map/ppermute | solution.py:378
  295.3 21.1 %collective-permute-start.53 = (f32[4,512,128]{2,1,0:T(8,128)S(1)}, f32[4,512,128]{2,1,0:T(8,128)}, u32[]{:S(2)}, u32[]{:S(2)}) collective-permute-start(f32[4,512,128]{2,1,0:T(8,128)S(1)} %pad_maximum_fusion), channel_id=1, source_target_pairs={{0,1},{1,0},{2,3},{3,2},{4,5},{5,4},{6,7},{7,6},{8,9},{9,8},{10,11... | collective-permute-start | bytes 3145736 | tf_op jit(solution)/shard_map/ppermute | solution.py:228
  296.9 4.4 %collective-permute-start.44 = (f32[128,128]{1,0:T(8,128)S(1)}, f32[128,128]{1,0:T(8,128)S(1)}, u32[]{:S(2)}, u32[]{:S(2)}) collective-permute-start(f32[128,128]{1,0:T(8,128)S(1)} %get-tuple-element.210), channel_id=1, source_target_pairs={{0,8},{8,0},{16,24},{24,16},{1,9},{9,1},{17,25},{25,17},{2,10},{10... | collective-permute-start | bytes 196616 | tf_op jit(solution)/shard_map/ppermute | solution.py:388
  298.5 5.7 %collective-permute-start.45 = (f32[128,128]{1,0:T(8,128)S(1)}, f32[128,128]{1,0:T(8,128)S(1)}, u32[]{:S(2)}, u32[]{:S(2)}) collective-permute-start(f32[128,128]{1,0:T(8,128)S(1)} %get-tuple-element.212), channel_id=1, source_target_pairs={{0,16},{8,24},{16,0},{24,8},{1,17},{9,25},{17,1},{25,9},{2,18},{10... | collective-permute-start | bytes 196616 | tf_op jit(solution)/shard_map/ppermute | solution.py:388
  301.2 5.2 %collective-permute-start.46 = (f32[128,128]{1,0:T(8,128)S(1)}, f32[128,128]{1,0:T(8,128)S(1)}, u32[]{:S(2)}, u32[]{:S(2)}) collective-permute-start(f32[128,128]{1,0:T(8,128)S(1)} %get-tuple-element.211), channel_id=1, source_target_pairs={{0,24},{8,16},{16,8},{24,0},{1,25},{9,17},{17,9},{25,1},{2,26},{10... | collective-permute-start | bytes 196616 | tf_op jit(solution)/shard_map/ppermute | solution.py:388
  306.4 4.5 %collective-permute-start.47 = (f32[128,128]{1,0:T(8,128)S(1)}, f32[128,128]{1,0:T(8,128)S(1)}, u32[]{:S(2)}, u32[]{:S(2)}) collective-permute-start(f32[128,128]{1,0:T(8,128)S(1)} %add_add_fusion), channel_id=1, source_target_pairs={{0,2},{1,3},{2,0},{3,1},{4,6},{5,7},{6,4},{7,5},{8,10},{9,11},{10,... | collective-permute-start | bytes 196616 | tf_op jit(solution)/shard_map/ppermute | solution.py:378
  306.5 7.5 %collective-permute-start.48 = (f32[128,128]{1,0:T(8,128)S(1)}, f32[128,128]{1,0:T(8,128)S(1)}, u32[]{:S(2)}, u32[]{:S(2)}) collective-permute-start(f32[128,128]{1,0:T(8,128)S(1)} %add_add_fusion), channel_id=1, source_target_pairs={{0,4},{1,5},{2,6},{3,7},{4,0},{5,1},{6,2},{7,3},{8,12},{9,13},{10,... | collective-permute-start | bytes 196616 | tf_op jit(solution)/shard_map/ppermute | solution.py:378
  310.3 6.1 %collective-permute-start.49 = (f32[128,128]{1,0:T(8,128)S(1)}, f32[128,128]{1,0:T(8,128)S(1)}, u32[]{:S(2)}, u32[]{:S(2)}) collective-permute-start(f32[128,128]{1,0:T(8,128)S(1)} %add_add_fusion), channel_id=1, source_target_pairs={{0,6},{1,7},{2,4},{3,5},{4,2},{5,3},{6,0},{7,1},{8,14},{9,15},{10,... | collective-permute-start | bytes 196616 | tf_op jit(solution)/shard_map/ppermute | solution.py:378
  327.6 4.6 %collective-permute-start.55 = (f32[128,128]{1,0:T(8,128)S(1)}, f32[128,128]{1,0:T(8,128)S(1)}, u32[]{:S(2)}, u32[]{:S(2)}) collective-permute-start(f32[128,128]{1,0:T(8,128)S(1)} %get-tuple-element.207), channel_id=1, source_target_pairs={{0,8},{8,0},{16,24},{24,16},{1,9},{9,1},{17,25},{25,17},{2,10},{10... | collective-permute-start | bytes 196616 | tf_op jit(solution)/shard_map/ppermute | solution.py:388
  327.7 5.7 %collective-permute-start.56 = (f32[128,128]{1,0:T(8,128)S(1)}, f32[128,128]{1,0:T(8,128)S(1)}, u32[]{:S(2)}, u32[]{:S(2)}) collective-permute-start(f32[128,128]{1,0:T(8,128)S(1)} %get-tuple-element.209), channel_id=1, source_target_pairs={{0,16},{8,24},{16,0},{24,8},{1,17},{9,25},{17,1},{25,9},{2,18},{10... | collective-permute-start | bytes 196616 | tf_op jit(solution)/shard_map/ppermute | solution.py:388
  328.2 5.2 %collective-permute-start.57 = (f32[128,128]{1,0:T(8,128)S(1)}, f32[128,128]{1,0:T(8,128)S(1)}, u32[]{:S(2)}, u32[]{:S(2)}) collective-permute-start(f32[128,128]{1,0:T(8,128)S(1)} %get-tuple-element.208), channel_id=1, source_target_pairs={{0,24},{8,16},{16,8},{24,0},{1,25},{9,17},{17,9},{25,1},{2,26},{10... | collective-permute-start | bytes 196616 | tf_op jit(solution)/shard_map/ppermute | solution.py:388
  333.4 8.0 %collective-permute-start.58 = (f32[128,128]{1,0:T(8,128)S(1)}, f32[128,128]{1,0:T(8,128)S(1)}, u32[]{:S(2)}, u32[]{:S(2)}) collective-permute-start(f32[128,128]{1,0:T(8,128)S(1)} %add_subtract_fusion), channel_id=1, source_target_pairs={{0,2},{1,3},{2,0},{3,1},{4,6},{5,7},{6,4},{7,5},{8,10},{9,11},{10,... | collective-permute-start | bytes 196616 | tf_op jit(solution)/shard_map/ppermute | solution.py:378
  333.5 7.9 %collective-permute-start.59 = (f32[128,128]{1,0:T(8,128)S(1)}, f32[128,128]{1,0:T(8,128)S(1)}, u32[]{:S(2)}, u32[]{:S(2)}) collective-permute-start(f32[128,128]{1,0:T(8,128)S(1)} %add_subtract_fusion), channel_id=1, source_target_pairs={{0,4},{1,5},{2,6},{3,7},{4,0},{5,1},{6,2},{7,3},{8,12},{9,13},{10,... | collective-permute-start | bytes 196616 | tf_op jit(solution)/shard_map/ppermute | solution.py:378
  334.9 6.6 %collective-permute-start.60 = (f32[128,128]{1,0:T(8,128)S(1)}, f32[128,128]{1,0:T(8,128)S(1)}, u32[]{:S(2)}, u32[]{:S(2)}) collective-permute-start(f32[128,128]{1,0:T(8,128)S(1)} %add_subtract_fusion), channel_id=1, source_target_pairs={{0,6},{1,7},{2,4},{3,5},{4,2},{5,3},{6,0},{7,1},{8,14},{9,15},{10,... | collective-permute-start | bytes 196616 | tf_op jit(solution)/shard_map/ppermute | solution.py:378
  337.9 5.7 %collective-permute-start.61 = (f32[2,128,128]{2,1,0:T(8,128)S(1)}, f32[2,128,128]{2,1,0:T(8,128)S(1)}, u32[]{:S(2)}, u32[]{:S(2)}) collective-permute-start(f32[2,128,128]{2,1,0:T(8,128)S(1)} %pad_maximum_fusion.7), channel_id=1, source_target_pairs={{0,8},{8,0},{16,24},{24,16},{1,9},{9,1},{17,25},{25,17},{2,10},{10... | collective-permute-start | bytes 393224 | tf_op jit(solution)/shard_map/ppermute | solution.py:392
  339.7 5.5 %collective-permute-start.62 = (f32[2,128,128]{2,1,0:T(8,128)S(1)}, f32[2,128,128]{2,1,0:T(8,128)S(1)}, u32[]{:S(2)}, u32[]{:S(2)}) collective-permute-start(f32[2,128,128]{2,1,0:T(8,128)S(1)} %pad_maximum_fusion.7), channel_id=1, source_target_pairs={{0,16},{8,24},{16,0},{24,8},{1,17},{9,25},{17,1},{25,9},{2,18},{10... | collective-permute-start | bytes 393224 | tf_op jit(solution)/shard_map/ppermute | solution.py:392
  341.4 5.9 %collective-permute-start.63 = (f32[2,128,128]{2,1,0:T(8,128)S(1)}, f32[2,128,128]{2,1,0:T(8,128)S(1)}, u32[]{:S(2)}, u32[]{:S(2)}) collective-permute-start(f32[2,128,128]{2,1,0:T(8,128)S(1)} %pad_maximum_fusion.7), channel_id=1, source_target_pairs={{0,24},{8,16},{16,8},{24,0},{1,25},{9,17},{17,9},{25,1},{2,26},{10... | collective-permute-start | bytes 393224 | tf_op jit(solution)/shard_map/ppermute | solution.py:392
  350.0 4.6 %collective-permute-start.65 = (f32[128,128]{1,0:T(8,128)S(1)}, f32[128,128]{1,0:T(8,128)S(1)}, u32[]{:S(2)}, u32[]{:S(2)}) collective-permute-start(f32[128,128]{1,0:T(8,128)S(1)} %get-tuple-element.204), channel_id=1, source_target_pairs={{0,8},{8,0},{16,24},{24,16},{1,9},{9,1},{17,25},{25,17},{2,10},{10... | collective-permute-start | bytes 196616 | tf_op jit(solution)/shard_map/ppermute | solution.py:388
  350.2 5.0 %collective-permute-start.66 = (f32[128,128]{1,0:T(8,128)S(1)}, f32[128,128]{1,0:T(8,128)S(1)}, u32[]{:S(2)}, u32[]{:S(2)}) collective-permute-start(f32[128,128]{1,0:T(8,128)S(1)} %get-tuple-element.206), channel_id=1, source_target_pairs={{0,16},{8,24},{16,0},{24,8},{1,17},{9,25},{17,1},{25,9},{2,18},{10... | collective-permute-start | bytes 196616 | tf_op jit(solution)/shard_map/ppermute | solution.py:388
  350.7 5.2 %collective-permute-start.67 = (f32[128,128]{1,0:T(8,128)S(1)}, f32[128,128]{1,0:T(8,128)S(1)}, u32[]{:S(2)}, u32[]{:S(2)}) collective-permute-start(f32[128,128]{1,0:T(8,128)S(1)} %get-tuple-element.205), channel_id=1, source_target_pairs={{0,24},{8,16},{16,8},{24,0},{1,25},{9,17},{17,9},{25,1},{2,26},{10... | collective-permute-start | bytes 196616 | tf_op jit(solution)/shard_map/ppermute | solution.py:388
  355.9 4.6 %collective-permute-start.68 = (f32[1,128,128]{2,1,0:T(8,128)S(1)}, f32[1,128,128]{2,1,0:T(8,128)S(1)}, u32[]{:S(2)}, u32[]{:S(2)}) collective-permute-start(f32[1,128,128]{2,1,0:T(8,128)S(1)} %add_bitcast_fusion), channel_id=1, source_target_pairs={{0,8},{8,0},{16,24},{24,16},{1,9},{9,1},{17,25},{25,17},{2,10},{10... | collective-permute-start | bytes 196616 | tf_op jit(solution)/shard_map/ppermute | solution.py:392
  357.9 4.6 %collective-permute-start.69 = (f32[1,128,128]{2,1,0:T(8,128)S(1)}, f32[1,128,128]{2,1,0:T(8,128)S(1)}, u32[]{:S(2)}, u32[]{:S(2)}) collective-permute-start(f32[1,128,128]{2,1,0:T(8,128)S(1)} %add_bitcast_fusion), channel_id=1, source_target_pairs={{0,16},{8,24},{16,0},{24,8},{1,17},{9,25},{17,1},{25,9},{2,18},{10... | collective-permute-start | bytes 196616 | tf_op jit(solution)/shard_map/ppermute | solution.py:392
  359.4 5.2 %collective-permute-start.70 = (f32[1,128,128]{2,1,0:T(8,128)S(1)}, f32[1,128,128]{2,1,0:T(8,128)S(1)}, u32[]{:S(2)}, u32[]{:S(2)}) collective-permute-start(f32[1,128,128]{2,1,0:T(8,128)S(1)} %add_bitcast_fusion), channel_id=1, source_target_pairs={{0,24},{8,16},{16,8},{24,0},{1,25},{9,17},{17,9},{25,1},{2,26},{10... | collective-permute-start | bytes 196616 | tf_op jit(solution)/shard_map/ppermute | solution.py:392
  (29 other events, 212.3 us)
